TPU v7x, 32 devices: a whole 2x2x4 slice. The times are simulated.
32 devices in a mesh: batch: 8 (over z, x), seq: 4 (over y, core).
Axes of the slice: x: 2, y: 2, z: 4, core: 2. Of those that a mesh axis runs over, the one named last changes fastest.
Arguments:
- target: bfloat16 [8, 512, 1024], P('batch', 'seq'), may hold values from -6 to 6
- memory: bfloat16 [8, 256, 1024], P('batch', 'seq'), may hold values from -6 to 6
- cotangent: bfloat16 [8, 512, 1024], P('batch', 'seq'), may hold values from -6 to 6
- target_segments: int32 [8, 512], P('batch'), may hold values from 0 to 3, never falling along the last dimension, each value on 1 to 256 neighbouring positions
- memory_segments: int32 [8, 256], P('batch'), may hold values from 0 to 3, never falling along the last dimension, each value on 1 to 128 neighbouring positions
- bucket_ids: int32 [512], replicated, may hold values from 0 to 31
- self_norm_gain: bfloat16 [1024], P(('batch', 'seq')), may hold values from 0.099609375 to 1.8984375
- self_query: bfloat16 [1024, 1024], P(('batch', 'seq')), may hold values from -0.09375 to 0.09375
- self_key: bfloat16 [1024, 1024], P(('batch', 'seq')), may hold values from -0.09375 to 0.09375
- self_value: bfloat16 [1024, 1024], P(('batch', 'seq')), may hold values from -0.1875 to 0.1875
- self_output: bfloat16 [1024, 1024], P(('batch', 'seq')), may hold values from -0.75 to 0.75
- bias_table: bfloat16 [32, 16], P('batch', 'seq'), may hold values from -4 to 4
- cross_norm_gain: bfloat16 [1024], P(('batch', 'seq')), may hold values from 0.099609375 to 1.8984375
- cross_query: bfloat16 [1024, 1024], P(('batch', 'seq')), may hold values from -0.09375 to 0.09375
- cross_key: bfloat16 [1024, 1024], P(('batch', 'seq')), may hold values from -0.09375 to 0.09375
- cross_value: bfloat16 [1024, 1024], P(('batch', 'seq')), may hold values from -0.1875 to 0.1875
- cross_output: bfloat16 [1024, 1024], P(('batch', 'seq')), may hold values from -0.75 to 0.75
- ffn_norm_gain: bfloat16 [1024], P(('batch', 'seq')), may hold values from 0.099609375 to 1.8984375
- ffn_gate: bfloat16 [1024, 2816], P(('batch', 'seq')), may hold values from -0.1875 to 0.1875
- ffn_up: bfloat16 [1024, 2816], P(('batch', 'seq')), may hold values from -0.1875 to 0.1875
- ffn_down: bfloat16 [2816, 1024], P(('batch', 'seq')), may hold values from -0.109375 to 0.109375
Outputs:
- activations: bfloat16 [8, 512, 1024], P('batch', 'seq')
- target_grad: float32 [8, 512, 1024], P('batch', 'seq')
- memory_grad: float32 [8, 256, 1024], P('batch', 'seq')
- self_norm_gain_grad: float32 [1024], P(('batch', 'seq'))
- self_query_grad: float32 [1024, 1024], P(('batch', 'seq'))
- self_key_grad: float32 [1024, 1024], P(('batch', 'seq'))
- self_value_grad: float32 [1024, 1024], P(('batch', 'seq'))
- self_output_grad: float32 [1024, 1024], P(('batch', 'seq'))
- bias_table_grad: float32 [32, 16], P('batch', 'seq')
- cross_norm_gain_grad: float32 [1024], P(('batch', 'seq'))
- cross_query_grad: float32 [1024, 1024], P(('batch', 'seq'))
- cross_key_grad: float32 [1024, 1024], P(('batch', 'seq'))
- cross_value_grad: float32 [1024, 1024], P(('batch', 'seq'))
- cross_output_grad: float32 [1024, 1024], P(('batch', 'seq'))
- ffn_norm_gain_grad: float32 [1024], P(('batch', 'seq'))
- ffn_gate_grad: float32 [1024, 2816], P(('batch', 'seq'))
- ffn_up_grad: float32 [1024, 2816], P(('batch', 'seq'))
- ffn_down_grad: float32 [2816, 1024], P(('batch', 'seq'))
Inputs may be any that keep to these rules, and one draw needn't show every extreme that they name: `target_segments`: in each target sequence the ids never fall, every id 0 to 3 occurs, and the longest document has 256 tokens. `memory_segments`: in each sequence the ids never fall and every id 0 to 3 occurs, so every target document has encoder rows of its own id; the longest has 128 rows. `bucket_ids`: entry d is the bucket of a key d positions before its query.
All inputs are finite; a program needn't handle non-finite values.
Results may differ from a plain program's by a relative error of at most 0.02.
The roundings to bfloat16 on the way count: a program that leaves them out, or rounds other values in their place, can miss the bound.
Values may be sent and summed in bfloat16 or wider, within the bound.
No kernel may reach another device: no remote copies, remote signals or barrier semaphores. Data moves between devices by JAX's collectives and lax.ppermute only.
A program may use at most 256 MiB of HBM per device.

v0:
```python
import jax
import jax.numpy as jnp
from jax import lax
from jax.sharding import PartitionSpec as P

HD = 64


EPSILON = 1e-06
MASKED = -1e30
HIGHEST = lax.Precision.HIGHEST
GROUP_HEADS = 4


def norm_gain(values, gain):
    return values * lax.rsqrt(jnp.mean(values * values, axis=-1, keepdims=True) + EPSILON) * gain


def norm_back(values, gain, grad_out):
    _, pullback = jax.vjp(norm_gain, values, gain)
    return pullback(grad_out)


def gated_unit(gate_act, up_act):
    return jax.nn.gelu(gate_act, approximate=True) * up_act


def project(acts, weight):
    return jnp.dot(acts, weight, preferred_element_type=jnp.float32)


def project_back(grad_out, weight):
    return jnp.einsum("bte,de->btd", grad_out, weight, preferred_element_type=jnp.float32)


def weight_grad(acts, grad_out):
    return jnp.einsum("btd,bte->de", acts, grad_out, preferred_element_type=jnp.float32)


def unfold_table(flat, rows_local, cols_local, batch_size, seq_size):
    blocks = flat.reshape(batch_size, seq_size, rows_local, cols_local)
    return jnp.transpose(blocks, (0, 2, 1, 3)).reshape(
        batch_size * rows_local, seq_size * cols_local
    )


def fold_table(table_full, rows_local, cols_local, batch_size, seq_size):
    blocks = table_full.reshape(batch_size, rows_local, seq_size, cols_local)
    return jnp.transpose(blocks, (0, 2, 1, 3)).reshape(-1)


def head_part(tensor, group_index, heads_per_group, head_size):
    group_width = heads_per_group * head_size
    piece = lax.dynamic_slice_in_dim(tensor, group_index * group_width, group_width, 2)
    return piece.reshape(piece.shape[0], piece.shape[1], heads_per_group, head_size)


def merge_heads(stacked):
    moved = jnp.transpose(stacked, (1, 2, 0, 3, 4))
    return moved.reshape(moved.shape[0], moved.shape[1], -1)


def group_scores(query_part, key_part, bias_info, allowed, group_index, heads_per_group):
    scores = jnp.einsum("bqhd,bkhd->bhqk", query_part, key_part, preferred_element_type=jnp.float32)
    if bias_info is not None:
        head_bias = bias_info[0]
        group_bias = lax.dynamic_slice_in_dim(
            head_bias, group_index * heads_per_group, heads_per_group, 0
        )
        scores = scores + group_bias[None]
    return jnp.where(allowed[:, None], scores, MASKED)


def attend(queries, keys_all, values_all, bias_info, allowed, head_size):
    heads_per_group = GROUP_HEADS
    group_count = queries.shape[2] // (heads_per_group * head_size)

    def one_group(group_index):
        query_part = head_part(queries, group_index, heads_per_group, head_size)
        key_part = head_part(keys_all, group_index, heads_per_group, head_size)
        value_part = head_part(values_all, group_index, heads_per_group, head_size)
        scores = group_scores(
            query_part, key_part, bias_info, allowed, group_index, heads_per_group
        )
        log_total = jax.nn.logsumexp(scores, axis=-1)
        weights = jnp.exp(scores - log_total[..., None]).astype(jnp.bfloat16)
        attended = jnp.einsum(
            "bhqk,bkhd->bqhd", weights, value_part, preferred_element_type=jnp.float32
        )
        return (attended, log_total)

    attended, log_totals = lax.map(one_group, jnp.arange(group_count, dtype=jnp.int32))
    return (merge_heads(attended), log_totals)


def attend_back(
    queries, keys_all, values_all, bias_info, allowed, log_totals, grad_attended, head_size
):
    heads_per_group = GROUP_HEADS
    group_count = queries.shape[2] // (heads_per_group * head_size)

    def one_group(group_index):
        query_part = head_part(queries, group_index, heads_per_group, head_size)
        key_part = head_part(keys_all, group_index, heads_per_group, head_size)
        value_part = head_part(values_all, group_index, heads_per_group, head_size)
        grad_part = head_part(grad_attended, group_index, heads_per_group, head_size)
        scores = group_scores(
            query_part, key_part, bias_info, allowed, group_index, heads_per_group
        )
        weights = jnp.exp(scores - log_totals[group_index][..., None])
        grad_weights = jnp.einsum(
            "bqhd,bkhd->bhqk", grad_part, value_part, preferred_element_type=jnp.float32
        )
        inner_sum = jnp.sum(weights * grad_weights, axis=-1, keepdims=True)
        grad_scores = weights * (grad_weights - inner_sum)
        low_scores = grad_scores.astype(jnp.bfloat16)
        grad_query = jnp.einsum(
            "bhqk,bkhd->bqhd", low_scores, key_part, preferred_element_type=jnp.float32
        )
        grad_key = jnp.einsum(
            "bhqk,bqhd->bkhd", low_scores, query_part, preferred_element_type=jnp.float32
        )
        grad_value = jnp.einsum(
            "bhqk,bqhd->bkhd",
            weights.astype(jnp.bfloat16),
            grad_part,
            preferred_element_type=jnp.float32,
        )
        if bias_info is None:
            grad_bias = jnp.zeros((heads_per_group, 1), jnp.float32)
        else:
            pair_onehot = bias_info[1]
            summed = jnp.sum(grad_scores, axis=0).reshape(heads_per_group, -1)
            grad_bias = jnp.dot(summed, pair_onehot, precision=HIGHEST)
        return (grad_query, grad_key, grad_value, grad_bias)

    grad_queries, grad_keys, grad_values, grad_biases = lax.map(
        one_group, jnp.arange(group_count, dtype=jnp.int32)
    )
    grad_biases = grad_biases.reshape(-1, grad_biases.shape[-1])
    return (
        merge_heads(grad_queries),
        merge_heads(grad_keys),
        merge_heads(grad_values),
        grad_biases,
    )


def per_device(
    target,
    memory,
    cotangent,
    target_segments,
    memory_segments,
    bucket_ids,
    self_norm_gain,
    self_query,
    self_key,
    self_value,
    self_output,
    bias_table,
    cross_norm_gain,
    cross_query,
    cross_key,
    cross_value,
    cross_output,
    ffn_norm_gain,
    ffn_gate,
    ffn_up,
    ffn_down,
):
    batch_size = lax.axis_size("batch")
    seq_size = lax.axis_size("seq")
    rows_local, cols_local = bias_table.shape
    head_size = HD
    shards = (
        self_query,
        self_key,
        self_value,
        self_output,
        cross_query,
        cross_key,
        cross_value,
        cross_output,
        ffn_gate,
        ffn_up,
        ffn_down,
        self_norm_gain,
        cross_norm_gain,
        ffn_norm_gain,
        bias_table.reshape(-1),
    )
    gathered = (
        lax.all_gather(shards[0], ("batch", "seq"), axis=0, tiled=True),
        lax.all_gather(shards[1], ("batch", "seq"), axis=0, tiled=True),
        lax.all_gather(shards[2], ("batch", "seq"), axis=0, tiled=True),
        lax.all_gather(shards[3], ("batch", "seq"), axis=0, tiled=True),
        lax.all_gather(shards[4], ("batch", "seq"), axis=0, tiled=True),
        lax.all_gather(shards[5], ("batch", "seq"), axis=0, tiled=True),
        lax.all_gather(shards[6], ("batch", "seq"), axis=0, tiled=True),
        lax.all_gather(shards[7], ("batch", "seq"), axis=0, tiled=True),
        lax.all_gather(shards[8], ("batch", "seq"), axis=0, tiled=True),
        lax.all_gather(shards[9], ("batch", "seq"), axis=0, tiled=True),
        lax.all_gather(shards[10], ("batch", "seq"), axis=0, tiled=True),
        lax.all_gather(shards[11], ("batch", "seq"), axis=0, tiled=True),
        lax.all_gather(shards[12], ("batch", "seq"), axis=0, tiled=True),
        lax.all_gather(shards[13], ("batch", "seq"), axis=0, tiled=True),
        lax.all_gather(shards[14], ("batch", "seq"), axis=0, tiled=True),
    )
    (
        query_self,
        key_self,
        value_self,
        out_self,
        query_cross,
        key_cross,
        value_cross,
        out_cross,
        gate_full,
        up_full,
        down_full,
        gain_self,
        gain_cross,
        gain_ffn,
        table_flat,
    ) = gathered
    bias_full = unfold_table(table_flat, rows_local, cols_local, batch_size, seq_size).astype(
        jnp.float32
    )
    bucket_count = bias_full.shape[0]
    head_count = bias_full.shape[1]
    seq_index = lax.axis_index("seq")
    tok_local = target.shape[1]
    length = target_segments.shape[1]
    positions = seq_index * tok_local + jnp.arange(tok_local, dtype=jnp.int32)
    key_positions = jnp.arange(length, dtype=jnp.int32)
    causal = positions[:, None] >= key_positions[None, :]
    query_segments = lax.dynamic_slice_in_dim(target_segments, seq_index * tok_local, tok_local, 1)
    self_allowed = causal[None] & (query_segments[:, :, None] == target_segments[:, None, :])
    cross_allowed = query_segments[:, :, None] == memory_segments[:, None, :]
    bucket_range = jnp.arange(bucket_count, dtype=jnp.int32)
    bucket_onehot = (bucket_ids[:, None] == bucket_range[None, :]).astype(jnp.float32)
    spread_offsets = jnp.clip(length - jnp.arange(2 * length, dtype=jnp.int32), 0, length - 1)
    offset_select = (spread_offsets[:, None] == key_positions[None, :]).astype(jnp.float32)
    spread_onehot = jnp.dot(offset_select, bucket_onehot, precision=HIGHEST)

    def query_row(position):
        return lax.dynamic_slice_in_dim(spread_onehot, length - position, length, 0)

    pair_onehot = jax.vmap(query_row)(positions).reshape(tok_local * length, bucket_count)
    pair_bias = jnp.dot(pair_onehot, bias_full, precision=HIGHEST)
    head_bias = pair_bias.T.reshape(head_count, tok_local, length)
    bias_info = (head_bias, pair_onehot)
    target_float = target.astype(jnp.float32)
    normed_one = norm_gain(target_float, gain_self.astype(jnp.float32)).astype(jnp.bfloat16)
    queries = project(normed_one, query_self).astype(jnp.bfloat16)
    keys_local = project(normed_one, key_self).astype(jnp.bfloat16)
    values_local = project(normed_one, value_self).astype(jnp.bfloat16)
    keys_all, values_all = (
        lax.all_gather(keys_local, "seq", axis=1, tiled=True),
        lax.all_gather(values_local, "seq", axis=1, tiled=True),
    )
    attended, log_self = attend(queries, keys_all, values_all, bias_info, self_allowed, head_size)
    attended = attended.astype(jnp.bfloat16)
    hidden_one = target_float + project(attended, out_self)
    normed_two = norm_gain(hidden_one, gain_cross.astype(jnp.float32)).astype(jnp.bfloat16)
    cross_queries = project(normed_two, query_cross).astype(jnp.bfloat16)
    memory_all = lax.all_gather(memory, "seq", axis=1, tiled=True)
    cross_keys = project(memory_all, key_cross).astype(jnp.bfloat16)
    cross_values = project(memory_all, value_cross).astype(jnp.bfloat16)
    cross_attended, log_cross = attend(
        cross_queries, cross_keys, cross_values, None, cross_allowed, head_size
    )
    cross_attended = cross_attended.astype(jnp.bfloat16)
    hidden_two = hidden_one + project(cross_attended, out_cross)
    normed_three = norm_gain(hidden_two, gain_ffn.astype(jnp.float32)).astype(jnp.bfloat16)
    gate_act = project(normed_three, gate_full)
    up_act = project(normed_three, up_full)
    inner_act, gated_pull = jax.vjp(gated_unit, gate_act, up_act)
    inner_low = inner_act.astype(jnp.bfloat16)
    output = hidden_two + project(inner_low, down_full)
    activations = output.astype(jnp.bfloat16)
    (
        query_self,
        key_self,
        value_self,
        out_self,
        query_cross,
        key_cross,
        value_cross,
        out_cross,
        gate_full,
        up_full,
        down_full,
        gain_self,
        gain_cross,
        gain_ffn,
        table_flat,
    ) = gathered
    grad_out = cotangent.astype(jnp.float32)
    grad_down = weight_grad(inner_low, cotangent)
    grad_inner = project_back(cotangent, down_full)
    grad_gate, grad_up = gated_pull(grad_inner)
    grad_gate = grad_gate.astype(jnp.bfloat16)
    grad_up = grad_up.astype(jnp.bfloat16)
    grad_gate_weight = weight_grad(normed_three, grad_gate)
    grad_up_weight = weight_grad(normed_three, grad_up)
    grad_normed_three = project_back(grad_gate, gate_full) + project_back(grad_up, up_full)
    grad_through_three, grad_gain_ffn = norm_back(
        hidden_two, gain_ffn.astype(jnp.float32), grad_normed_three
    )
    grad_hidden_two = grad_out + grad_through_three
    low_two = grad_hidden_two.astype(jnp.bfloat16)
    grad_out_cross = weight_grad(cross_attended, low_two)
    grad_cross_attended = project_back(low_two, out_cross).astype(jnp.bfloat16)
    grad_cross_queries, grad_cross_keys, grad_cross_values, _ = attend_back(
        cross_queries,
        cross_keys,
        cross_values,
        None,
        cross_allowed,
        log_cross,
        grad_cross_attended,
        head_size,
    )
    grad_cross_queries = grad_cross_queries.astype(jnp.bfloat16)
    cross_key_rows, cross_value_rows = (
        lax.psum_scatter(
            grad_cross_keys.astype(jnp.bfloat16), "seq", scatter_dimension=1, tiled=True
        ).astype(jnp.float32),
        lax.psum_scatter(
            grad_cross_values.astype(jnp.bfloat16), "seq", scatter_dimension=1, tiled=True
        ).astype(jnp.float32),
    )
    cross_key_rows = cross_key_rows.astype(jnp.bfloat16)
    cross_value_rows = cross_value_rows.astype(jnp.bfloat16)
    grad_key_cross = weight_grad(memory, cross_key_rows)
    grad_value_cross = weight_grad(memory, cross_value_rows)
    memory_grad = project_back(cross_key_rows, key_cross) + project_back(
        cross_value_rows, value_cross
    )
    grad_query_cross = weight_grad(normed_two, grad_cross_queries)
    grad_normed_two = project_back(grad_cross_queries, query_cross)
    grad_through_two, grad_gain_cross = norm_back(
        hidden_one, gain_cross.astype(jnp.float32), grad_normed_two
    )
    grad_hidden_one = grad_hidden_two + grad_through_two
    low_one = grad_hidden_one.astype(jnp.bfloat16)
    grad_out_self = weight_grad(attended, low_one)
    grad_self_attended = project_back(low_one, out_self).astype(jnp.bfloat16)
    grad_queries, grad_keys, grad_values, grad_heads_bias = attend_back(
        queries,
        keys_all,
        values_all,
        bias_info,
        self_allowed,
        log_self,
        grad_self_attended,
        head_size,
    )
    grad_queries = grad_queries.astype(jnp.bfloat16)
    key_rows, value_rows = (
        lax.psum_scatter(
            grad_keys.astype(jnp.bfloat16), "seq", scatter_dimension=1, tiled=True
        ).astype(jnp.float32),
        lax.psum_scatter(
            grad_values.astype(jnp.bfloat16), "seq", scatter_dimension=1, tiled=True
        ).astype(jnp.float32),
    )
    key_rows = key_rows.astype(jnp.bfloat16)
    value_rows = value_rows.astype(jnp.bfloat16)
    grad_query_self = weight_grad(normed_one, grad_queries)
    grad_key_self = weight_grad(normed_one, key_rows)
    grad_value_self = weight_grad(normed_one, value_rows)
    grad_normed_one = (
        project_back(grad_queries, query_self)
        + project_back(key_rows, key_self)
        + project_back(value_rows, value_self)
    )
    grad_through_one, grad_gain_self = norm_back(
        target_float, gain_self.astype(jnp.float32), grad_normed_one
    )
    target_grad = grad_hidden_one + grad_through_one
    table_folded = fold_table(grad_heads_bias.T, rows_local, cols_local, batch_size, seq_size)
    reduced = (
        lax.psum_scatter(grad_query_self, ("batch", "seq"), scatter_dimension=0, tiled=True),
        lax.psum_scatter(grad_key_self, ("batch", "seq"), scatter_dimension=0, tiled=True),
        lax.psum_scatter(grad_value_self, ("batch", "seq"), scatter_dimension=0, tiled=True),
        lax.psum_scatter(grad_out_self, ("batch", "seq"), scatter_dimension=0, tiled=True),
        lax.psum_scatter(grad_query_cross, ("batch", "seq"), scatter_dimension=0, tiled=True),
        lax.psum_scatter(grad_key_cross, ("batch", "seq"), scatter_dimension=0, tiled=True),
        lax.psum_scatter(grad_value_cross, ("batch", "seq"), scatter_dimension=0, tiled=True),
        lax.psum_scatter(grad_out_cross, ("batch", "seq"), scatter_dimension=0, tiled=True),
        lax.psum_scatter(grad_gate_weight, ("batch", "seq"), scatter_dimension=0, tiled=True),
        lax.psum_scatter(grad_up_weight, ("batch", "seq"), scatter_dimension=0, tiled=True),
        lax.psum_scatter(grad_down, ("batch", "seq"), scatter_dimension=0, tiled=True),
        lax.psum_scatter(grad_gain_self, ("batch", "seq"), scatter_dimension=0, tiled=True),
        lax.psum_scatter(grad_gain_cross, ("batch", "seq"), scatter_dimension=0, tiled=True),
        lax.psum_scatter(grad_gain_ffn, ("batch", "seq"), scatter_dimension=0, tiled=True),
        lax.psum_scatter(table_folded, ("batch", "seq"), scatter_dimension=0, tiled=True),
    )
    return (
        activations,
        target_grad,
        memory_grad,
        reduced[11],
        reduced[0],
        reduced[1],
        reduced[2],
        reduced[3],
        reduced[14].reshape(rows_local, cols_local),
        reduced[12],
        reduced[4],
        reduced[5],
        reduced[6],
        reduced[7],
        reduced[13],
        reduced[8],
        reduced[9],
        reduced[10],
    )


def solution(mesh):
    return jax.shard_map(
        per_device,
        mesh=mesh,
        in_specs=(
            P("batch", "seq", None),
            P("batch", "seq", None),
            P("batch", "seq", None),
            P("batch", None),
            P("batch", None),
            P(),
            P(("batch", "seq")),
            P(("batch", "seq"), None),
            P(("batch", "seq"), None),
            P(("batch", "seq"), None),
            P(("batch", "seq"), None),
            P("batch", "seq"),
            P(("batch", "seq")),
            P(("batch", "seq"), None),
            P(("batch", "seq"), None),
            P(("batch", "seq"), None),
            P(("batch", "seq"), None),
            P(("batch", "seq")),
            P(("batch", "seq"), None),
            P(("batch", "seq"), None),
            P(("batch", "seq"), None),
        ),
        out_specs=(
            P("batch", "seq", None),
            P("batch", "seq", None),
            P("batch", "seq", None),
            P(("batch", "seq")),
            P(("batch", "seq"), None),
            P(("batch", "seq"), None),
            P(("batch", "seq"), None),
            P(("batch", "seq"), None),
            P("batch", "seq"),
            P(("batch", "seq")),
            P(("batch", "seq"), None),
            P(("batch", "seq"), None),
            P(("batch", "seq"), None),
            P(("batch", "seq"), None),
            P(("batch", "seq")),
            P(("batch", "seq"), None),
            P(("batch", "seq"), None),
            P(("batch", "seq"), None),
        ),
        check_vma=False,
    )
```

profile of v0, /device:TPU:0, one launch (start us, length us, event | category | flops | bytes accessed | tf_op | source)
XLA Modules:
  0.0 2570.8 jit_solution(16468681649490801421)
XLA Ops:
  14.1 42.1 %all-reduce.10 = (bf16[1024]{0:T(1024)(128)(2,1)S(1)}, bf16[512]{0:T(512)(128)(2,1)S(1)}, bf16[1024]{0:T(1024)(128)(2,1)S(1)}, bf16[1024]{0:T(1024)(128)(2,1)S(1)}) all-reduce(bf16[1024]{0:T(1024)(128)(2,1)S(1)} %dynamic-update-slice.2, bf16[512]{0:T(512)(128)(2,1)S(1)} %dynamic-update-slice.3, ...), channel_id=1, replica_groups=mesh['batch'=8,'seq'=4] {'batch','seq'}, use_global_device_ids=true, to_apply=%add.1 | all-reduce | flops 3584 | bytes 14336
  57.4 12.7 all-gather.16.cloned.1.call-done
  73.0 55.2 %all-gather.20.cloned.1.call-done = bf16[1024,1024]{1,0:T(8,128)(2,1)} async-done(((bf16[32,1024]{1,0:T(8,128)(2,1)}), bf16[1024,1024]{1,0:T(8,128)(2,1)}) %all-gather.20.cloned.1.call-update) | async-done | bytes 2097168 | tf_op jit(solution)/shard_map/all_gather | solution.py:195
  136.4 251.7 %while.59 = (s32[]{:T(128)}, f32[1024,32]{1,0:T(8,128)S(1)}, s32[128,2]{0,1:T(2,128)S(1)}, f32[128,512,32]{2,1,0:T(8,128)}, s32[]{:T(128)}) while((s32[]{:T(128)}, f32[1024,32]{1,0:T(8,128)S(1)}, s32[128,2]{0,1:T(2,128)S(1)}, f32[128,512,32]{2,1,0:T(8,128)}, s32[]{:T(128)}) %tuple.139), condition=%wide.while_cond, body=%wide.while_body.sunk | while | flops 2 | bytes 328293 | solution.py:248
  388.2 20.9 fusion.123
  415.7 7.2 all_gather.62
  436.2 22.2 while.60
  463.1 13.3 while.61
  476.5 38.4 %all-gather.30.cloned.1.call-done = bf16[1024,1024]{1,0:T(8,128)(2,1)} async-done(((bf16[32,1024]{1,0:T(8,128)(2,1)}), bf16[1024,1024]{1,0:T(8,128)(2,1)}) %all-gather.30.cloned.1.call-update) | async-done | bytes 2097168 | tf_op jit(solution)/shard_map/all_gather | solution.py:201
  517.2 66.7 %all-gather.32.cloned.1.call-done = bf16[1024,2816]{1,0:T(8,128)(2,1)} async-done(((bf16[32,2816]{1,0:T(8,128)(2,1)}), bf16[1024,2816]{1,0:T(8,128)(2,1)}) %all-gather.32.cloned.1.call-update) | async-done | bytes 5767184 | tf_op jit(solution)/shard_map/all_gather | solution.py:202
  588.6 64.4 %all-gather.34.cloned.1.call-done = bf16[1024,2816]{1,0:T(8,128)(2,1)} async-done(((bf16[32,2816]{1,0:T(8,128)(2,1)}), bf16[1024,2816]{1,0:T(8,128)(2,1)}) %all-gather.34.cloned.1.call-update) | async-done | bytes 5767184 | tf_op jit(solution)/shard_map/all_gather | solution.py:203
  657.6 64.5 %all-gather.36.cloned.1.call-done = bf16[2816,1024]{1,0:T(8,128)(2,1)} async-done(((bf16[88,1024]{1,0:T(8,128)(2,1)}), bf16[2816,1024]{1,0:T(8,128)(2,1)}) %all-gather.36.cloned.1.call-update) | async-done | bytes 5767184 | tf_op jit(solution)/shard_map/all_gather | solution.py:204
  722.1 7.1 multiply_convert_fusion.1
  739.6 36.3 %while.62 = (s32[]{:T(128)}, bf16[4,1,128,4,64]{2,4,3,1,0:T(8,128)(2,1)}, bf16[4,1,256,4,64]{2,4,3,1,0:T(8,128)(2,1)}, bf16[4,1,256,4,64]{2,4,3,1,0:T(8,128)(2,1...) while((s32[]{:T(128)}, ...), condition=%wide.region_14.15_spmd.clone, body=%wide.region_12.14_spmd.clone.sunk | while | flops 84966912 | bytes 14626701 | solution.py:137
  793.1 123.3 %while.63 = (s32[]{:T(128)}, bf16[4,1,128,4,64]{2,4,3,1,0:T(8,128)(2,1)}, bf16[4,1,512,4,64]{2,4,3,1,0:T(8,128)(2,1)}, bf16[4,1,512,4,64]{2,4,3,1,0:T(8,128)(2,1...) while((s32[]{:T(128)}, ...), condition=%wide.region_18.19_spmd.clone, body=%wide.region_16.18_spmd.clone.sunk | while | flops 270990848 | bytes 46284380 | solution.py:137
  803.8 20.0 fusion.295
  834.6 20.0 fusion.295
  865.4 20.0 fusion.295
  896.3 20.0 fusion.295
  969.9 7.0 reduce-scatter.48.cloned.1.call-done
  1015.8 39.8 %all-reduce.9 = (f32[1024]{0:T(1024)S(1)}, f32[512]{0:T(512)S(1)}, f32[1024]{0:T(1024)S(1)}, f32[1024]{0:T(1024)S(1)}) all-reduce(f32[1024]{0:T(1024)S(1)} %get-tuple-element.590, f32[512]{0:T(512)S(1)} %reshape.887, f32[1024]{0:T(1024)S(1)} %copy-done.54, ...), channel_id=8, replica_groups=mesh['batch'=8,'seq'=4] {'batch','seq'}, use_global_device_ids=true, to_apply=%region_25.26.clone | all-reduce | flops 3584 | bytes 28672
  1059.1 61.6 %reduce-scatter.28.cloned.1.call-done = f32[32,1024]{1,0:T(8,128)} async-done(((f32[1024,1024]{1,0:T(8,128)}), f32[32,1024]{1,0:T(8,128)}) %reduce-scatter.28.cloned.1.call-update) | async-done | bytes 131088 | tf_op jit(solution)/shard_map/reduce_scatter | solution.py:386
  1120.7 139.7 %reduce-scatter.34.cloned.1.call-done = f32[32,1024]{1,0:T(8,128)} async-done(((f32[1024,1024]{1,0:T(8,128)}), f32[32,1024]{1,0:T(8,128)}) %reduce-scatter.34.cloned.1.call-update) | async-done | bytes 131088 | tf_op jit(solution)/shard_map/reduce_scatter | solution.py:389
  1260.4 139.4 %reduce-scatter.36.cloned.1.call-done = f32[32,1024]{1,0:T(8,128)} async-done(((f32[1024,1024]{1,0:T(8,128)}), f32[32,1024]{1,0:T(8,128)}) %reduce-scatter.36.cloned.1.call-update) | async-done | bytes 131088 | tf_op jit(solution)/shard_map/reduce_scatter | solution.py:390
  1399.8 139.6 %reduce-scatter.38.cloned.1.call-done = f32[32,1024]{1,0:T(8,128)} async-done(((f32[1024,1024]{1,0:T(8,128)}), f32[32,1024]{1,0:T(8,128)}) %reduce-scatter.38.cloned.1.call-update) | async-done | bytes 131088 | tf_op jit(solution)/shard_map/reduce_scatter | solution.py:393
  1539.5 140.0 %reduce-scatter.54.cloned.1.call-done = f32[32,1024]{1,0:T(8,128)} async-done(((f32[1024,1024]{1,0:T(8,128)}), f32[32,1024]{1,0:T(8,128)}) %reduce-scatter.54.cloned.1.call-update) | async-done | bytes 131088
  1679.5 139.7 %reduce-scatter.56.cloned.1.call-done = f32[32,1024]{1,0:T(8,128)} async-done(((f32[1024,1024]{1,0:T(8,128)}), f32[32,1024]{1,0:T(8,128)}) %reduce-scatter.56.cloned.1.call-update) | async-done | bytes 131088
  1819.2 139.6 %reduce-scatter.30.cloned.1.call-done = f32[32,1024]{1,0:T(8,128)} async-done(((f32[1024,1024]{1,0:T(8,128)}), f32[32,1024]{1,0:T(8,128)}) %reduce-scatter.30.cloned.1.call-update) | async-done | bytes 131088 | tf_op jit(solution)/shard_map/reduce_scatter | solution.py:387
  1958.8 140.0 %reduce-scatter.32.cloned.1.call-done = f32[32,1024]{1,0:T(8,128)} async-done(((f32[1024,1024]{1,0:T(8,128)}), f32[32,1024]{1,0:T(8,128)}) %reduce-scatter.32.cloned.1.call-update) | async-done | bytes 131088 | tf_op jit(solution)/shard_map/reduce_scatter | solution.py:388
  2098.8 153.5 %reduce-scatter.40.cloned.1.call-done = f32[32,2816]{1,0:T(8,128)} async-done(((f32[1024,2816]{1,0:T(8,128)}), f32[32,2816]{1,0:T(8,128)}) %reduce-scatter.40.cloned.1.call-update) | async-done | bytes 360464 | tf_op jit(solution)/shard_map/reduce_scatter | solution.py:394
  2252.3 155.5 %reduce-scatter.42.cloned.1.call-done = f32[32,2816]{1,0:T(8,128)} async-done(((f32[1024,2816]{1,0:T(8,128)}), f32[32,2816]{1,0:T(8,128)}) %reduce-scatter.42.cloned.1.call-update) | async-done | bytes 360464 | tf_op jit(solution)/shard_map/reduce_scatter | solution.py:395
  2407.8 155.7 %reduce-scatter.44.cloned.1.call-done = f32[88,1024]{1,0:T(8,128)} async-done(((f32[2816,1024]{1,0:T(8,128)}), f32[88,1024]{1,0:T(8,128)}) %reduce-scatter.44.cloned.1.call-update) | async-done | bytes 360464 | tf_op jit(solution)/shard_map/reduce_scatter | solution.py:396
  (939 shorter events, 511.5 us)
Async XLA Ops:
  7.2 62.9 %all-gather.16.cloned.1.call-start = ((), (), s32[]{:S(2)}) async-start(), calls=%async_computation.15 | async-start | bytes 2162688 | tf_op jit(solution)/shard_map/all_gather | solution.py:196
  7.9 120.3 %all-gather.20.cloned.1.call-start = ((), (), s32[]{:S(2)}) async-start(), calls=%async_computation.17 | async-start | bytes 2162688 | tf_op jit(solution)/shard_map/all_gather | solution.py:195
  8.7 414.3 %all-gather.18.cloned.1.call-start = ((), (), s32[]{:S(2)}) async-start(), calls=%async_computation.16 | async-start | bytes 2162688 | tf_op jit(solution)/shard_map/all_gather | solution.py:194
  9.4 415.9 %all-gather.24.cloned.1.call-start = ((), (), s32[]{:S(2)}) async-start(), calls=%async_computation.19 | async-start | bytes 2162688 | tf_op jit(solution)/shard_map/all_gather | solution.py:200
  10.0 418.6 %all-gather.28.cloned.1.call-start = ((), (), s32[]{:S(2)}) async-start(), calls=%async_computation.21 | async-start | bytes 2162688 | tf_op jit(solution)/shard_map/all_gather | solution.py:199
  10.6 421.4 %all-gather.38.cloned.1.call-start = ((), (), s32[]{:S(2)}) async-start(), calls=%async_computation.35 | async-start | bytes 1310720 | tf_op jit(solution)/shard_map/all_gather | solution.py:261
  56.3 366.7 %copy-start.47 = (f32[1024]{0:T(1024)}, f32[1024]{0:T(1024)S(1)}, u32[]{:S(2)}) copy-start(f32[1024]{0:T(1024)S(1)} %convert_element_type.260) | copy-start | bytes 12292
  57.4 365.6 %copy-start.51 = (f32[128]{0:T(128)}, f32[128]{0:T(128)S(1)}, u32[]{:S(2)}) copy-start(f32[128]{0:T(128)S(1)} %fusion.106) | copy-start | bytes 1540
  73.0 360.8 %all-gather.40.cloned.1.call-start = ((), (), s32[]{:S(2)}) async-start(), calls=%async_computation.36 | async-start | bytes 1310720 | tf_op jit(solution)/shard_map/all_gather | solution.py:260
  131.1 327.3 %all-gather.22.cloned.1.call-start = ((), (), s32[]{:S(2)}) async-start(), calls=%async_computation.18 | async-start | bytes 2162688 | tf_op jit(solution)/shard_map/all_gather | solution.py:197
  131.8 328.9 %all-gather.26.cloned.1.call-start = ((), (), s32[]{:S(2)}) async-start(), calls=%async_computation.20 | async-start | bytes 2162688 | tf_op jit(solution)/shard_map/all_gather | solution.py:198
  132.5 382.3 %all-gather.30.cloned.1.call-start = ((), (), s32[]{:S(2)}) async-start(), calls=%async_computation.22 | async-start | bytes 2162688 | tf_op jit(solution)/shard_map/all_gather | solution.py:201
  133.1 450.8 %all-gather.32.cloned.1.call-start = ((), (), s32[]{:S(2)}) async-start(), calls=%async_computation.23 | async-start | bytes 5947392 | tf_op jit(solution)/shard_map/all_gather | solution.py:202
  133.9 519.1 %all-gather.34.cloned.1.call-start = ((), (), s32[]{:S(2)}) async-start(), calls=%async_computation.24 | async-start | bytes 5947392 | tf_op jit(solution)/shard_map/all_gather | solution.py:203
  134.4 587.6 %all-gather.36.cloned.1.call-start = ((), (), s32[]{:S(2)}) async-start(), calls=%async_computation.25 | async-start | bytes 5947392 | tf_op jit(solution)/shard_map/all_gather | solution.py:204
  135.2 811.5 %reduce-scatter.50.cloned.1.call-start = ((), (), s32[]{:S(2)}) async-start(), calls=%async_computation.39 | async-start | bytes 655360
  517.0 220.0 %copy-start.2 = (f32[1,128,1024]{2,1,0:T(8,128)}, f32[1,128,1024]{2,1,0:T(8,128)S(1)}, u32[]{:S(2)}) copy-start(f32[1,128,1024]{2,1,0:T(8,128)S(1)} %get-tuple-element.728) | copy-start | bytes 1572868
  517.2 135.8 %copy-start.4 = (bf16[128,1024]{1,0:T(8,128)(2,1)}, bf16[128,1024]{1,0:T(8,128)(2,1)S(1)}, u32[]{:S(2)}) copy-start(bf16[128,1024]{1,0:T(8,128)(2,1)S(1)} %fusion.76) | copy-start | bytes 786436
  781.7 174.3 %reduce-scatter.52.cloned.1.call-start = ((), (), s32[]{:S(2)}) async-start(), calls=%async_computation.40 | async-start | bytes 655360
  789.7 175.7 %reduce-scatter.46.cloned.1.call-start = ((), (), s32[]{:S(2)}) async-start(), calls=%async_computation.37 | async-start | bytes 1310720
  925.4 51.5 %reduce-scatter.48.cloned.1.call-start = ((), (), s32[]{:S(2)}) async-start(), calls=%async_computation.38 | async-start | bytes 1310720
  932.5 188.2 %reduce-scatter.28.cloned.1.call-start = ((), (), s32[]{:S(2)}) async-start(), calls=%async_computation.26 | async-start | bytes 4325376 | tf_op jit(solution)/shard_map/reduce_scatter | solution.py:386
  935.3 325.1 %reduce-scatter.34.cloned.1.call-start = ((), (), s32[]{:S(2)}) async-start(), calls=%async_computation.29 | async-start | bytes 4325376 | tf_op jit(solution)/shard_map/reduce_scatter | solution.py:389
  939.1 460.8 %reduce-scatter.36.cloned.1.call-start = ((), (), s32[]{:S(2)}) async-start(), calls=%async_computation.30 | async-start | bytes 4325376 | tf_op jit(solution)/shard_map/reduce_scatter | solution.py:390
  942.8 596.7 %reduce-scatter.38.cloned.1.call-start = ((), (), s32[]{:S(2)}) async-start(), calls=%async_computation.31 | async-start | bytes 4325376 | tf_op jit(solution)/shard_map/reduce_scatter | solution.py:393
  946.6 732.9 %reduce-scatter.54.cloned.1.call-start = ((), (), s32[]{:S(2)}) async-start(), calls=%async_computation.41 | async-start | bytes 4325376
  955.9 863.3 %reduce-scatter.56.cloned.1.call-start = ((), (), s32[]{:S(2)}) async-start(), calls=%async_computation.42 | async-start | bytes 4325376
  965.3 993.4 %reduce-scatter.30.cloned.1.call-start = ((), (), s32[]{:S(2)}) async-start(), calls=%async_computation.27 | async-start | bytes 4325376 | tf_op jit(solution)/shard_map/reduce_scatter | solution.py:387
  969.9 1128.9 %reduce-scatter.32.cloned.1.call-start = ((), (), s32[]{:S(2)}) async-start(), calls=%async_computation.28 | async-start | bytes 4325376 | tf_op jit(solution)/shard_map/reduce_scatter | solution.py:388
  981.4 1270.9 %reduce-scatter.40.cloned.1.call-start = ((), (), s32[]{:S(2)}) async-start(), calls=%async_computation.32 | async-start | bytes 11894784 | tf_op jit(solution)/shard_map/reduce_scatter | solution.py:394
  988.5 1419.3 %reduce-scatter.42.cloned.1.call-start = ((), (), s32[]{:S(2)}) async-start(), calls=%async_computation.33 | async-start | bytes 11894784 | tf_op jit(solution)/shard_map/reduce_scatter | solution.py:395
  995.5 1568.0 %reduce-scatter.44.cloned.1.call-start = ((), (), s32[]{:S(2)}) async-start(), calls=%async_computation.34 | async-start | bytes 11894784 | tf_op jit(solution)/shard_map/reduce_scatter | solution.py:396
  (90 other events, 844.9 us)
Sparse Core Ops, SparseCore 0:
  10.9 59.1 all-gather.15
  72.9 55.2 all-gather.19
  131.1 55.2 all-gather.17
  189.1 55.3 all-gather.23
  247.3 55.3 all-gather.27
  304.7 15.5 all-gather.37
  322.4 16.8 all-gather.39
  342.1 56.4 all-gather.21
  401.5 55.2 all-gather.25
  459.5 55.3 all-gather.29
  517.8 66.1 all-gather.31
  586.7 66.2 all-gather.33
  655.8 66.2 all-gather.35
  781.9 20.6 reduce-scatter.49
  805.0 21.6 reduce-scatter.51
  925.5 23.9 reduce-scatter.45
  952.0 24.8 reduce-scatter.47
  979.6 141.0 reduce-scatter.27
  1123.6 136.8 reduce-scatter.33
  1263.1 136.6 reduce-scatter.35
  1402.7 136.7 reduce-scatter.37
  1542.3 137.1 reduce-scatter.53
  1682.4 136.7 reduce-scatter.55
  1821.9 136.8 reduce-scatter.29
  1961.6 137.1 reduce-scatter.31
  2101.5 150.6 reduce-scatter.39
  2255.0 152.7 reduce-scatter.41
  2410.7 152.7 reduce-scatter.43
where the time goes:
time: 2580 us; the launch traced here: 2570 us
  waiting for transfers between devices  1820 us (71%)
  local copies, waits for them, and re-layouts  370 us (14%)
  matrix products  232 us (9%)
  blocking collectives  89.2 us (3%)
  loops' own time  33.1 us (1%)
    unnamed x34, waiting for transfers between devices  294 us
    gather x384, local copies, waits for them, and re-layouts  252 us
    reduce_scatter x1, waiting for transfers between devices, per_device(): lax.psum_scatter(grad_down, ('batch', 'seq'), scatter_dimension=0, tiled=...  156 us
    reduce_scatter x1, waiting for transfers between devices, per_device(): lax.psum_scatter(grad_up_weight, ('batch', 'seq'), scatter_dimension=0, t...  156 us
    reduce_scatter x1, waiting for transfers between devices, per_device(): lax.psum_scatter(grad_gate_weight, ('batch', 'seq'), scatter_dimension=0,...  153 us
    reduce_scatter x1, waiting for transfers between devices, per_device(): lax.psum_scatter(grad_value_self, ('batch', 'seq'), scatter_dimension=0,...  140 us
    reduce_scatter x1, waiting for transfers between devices, per_device(): lax.psum_scatter(grad_out_self, ('batch', 'seq'), scatter_dimension=0, ti...  140 us
    reduce_scatter x1, waiting for transfers between devices, per_device(): lax.psum_scatter(grad_out_cross, ('batch', 'seq'), scatter_dimension=0, t...  140 us
  transfers between devices with their start and end apart: 28, of which 18 were waited for; matrix products, arithmetic and copies ran while one was open for 21% of the time, Pallas kernels for 0%

commit v1 on v0

v1 whole, which is shorter than its diff:
```python
import functools

import jax
import jax.numpy as jnp
from jax import lax
from jax.experimental import pallas as pl
from jax.experimental.pallas import tpu as pltpu
from jax.sharding import PartitionSpec as P

HD = 64
LANES = 128
SUBLANES = 8
EPSILON = 1e-06
MASKED = -1e30
BF = jnp.bfloat16
F32 = jnp.float32
AXES = ("batch", "seq")
NT = (((1,), (1,)), ((), ()))
TN = (((0,), (0,)), ((), ()))
NN = (((1,), (0,)), ((), ()))


def mm(left, right, dims=NN):
    return lax.dot_general(left, right, dims, preferred_element_type=F32)


def norm_gain(values, gain):
    return values * lax.rsqrt(jnp.mean(values * values, axis=-1, keepdims=True) + EPSILON) * gain


def norm_back(values, gain, grad_out):
    _, pullback = jax.vjp(norm_gain, values, gain)
    return pullback(grad_out)


def gated_unit(gate_act, up_act):
    return jax.nn.gelu(gate_act, approximate=True) * up_act


def head_only(pair, head):
    lane = lax.broadcasted_iota(jnp.int32, pair.shape, 1)
    return jnp.where((lane // HD) == head, pair, jnp.zeros_like(pair))


def pick_heads(first, second):
    lane = lax.broadcasted_iota(jnp.int32, first.shape, 1)
    return jnp.where(lane < HD, first, second)


def spread(window, rows):
    wide = jnp.broadcast_to(window, (rows, window.shape[1]))
    rolled = pltpu.roll(wide, 0, 1, stride=1, stride_axis=0)
    return rolled[:, rows:]


def unspread(grads, rows):
    wide = jnp.concatenate([jnp.zeros((rows, rows), F32), grads], axis=1)
    width = wide.shape[1]
    total = wide[:SUBLANES]
    for start in range(SUBLANES, rows, SUBLANES):
        total = total + pltpu.roll(wide[start : start + SUBLANES], width - start, 1)
    row = lax.broadcasted_iota(jnp.int32, total.shape, 0)
    for bit in (1, 2, 4):
        total = jnp.where((row & bit) != 0, pltpu.roll(total, width - bit, 1), total)
    return jnp.sum(total, axis=0, keepdims=True)


def allowed_pairs(position, query_segments, key_segments, causal):
    rows, keys = query_segments.shape[0], key_segments.shape[1]
    allowed = query_segments == key_segments
    if causal:
        own = lax.broadcasted_iota(jnp.int32, (rows, keys), 0) + position
        other = lax.broadcasted_iota(jnp.int32, (rows, keys), 1)
        allowed = allowed & (own >= other)
    return allowed


def pair_probs(query, key, bias_ref, allowed, head, causal):
    scores = mm(head_only(query, head), key, NT)
    if causal:
        scores = scores + spread(bias_ref[0, head : head + 1, :], query.shape[0])
    scores = jnp.where(allowed, scores, MASKED)
    top = jnp.max(scores, axis=1, keepdims=True)
    grown = jnp.exp(scores - top)
    return grown / jnp.sum(grown, axis=1, keepdims=True)


def attend_body(causal, pos_ref, q_ref, k_ref, v_ref, bias_ref, qseg_ref, kseg_ref, out_ref):
    query, key, value = q_ref[...], k_ref[...], v_ref[...]
    allowed = allowed_pairs(pos_ref[0], qseg_ref[...], kseg_ref[...], causal)
    parts = []
    for head in range(2):
        probs = pair_probs(query, key, bias_ref, allowed, head, causal)
        parts.append(mm(probs.astype(BF), value))
    out_ref[...] = pick_heads(*parts).astype(BF)


def attend_back_body(
    causal, pos_ref, q_ref, k_ref, v_ref, do_ref, bias_ref, qseg_ref, kseg_ref,
    dq_ref, dk_ref, dv_ref, dbias_ref,
):
    query, key, value, grad = q_ref[...], k_ref[...], v_ref[...], do_ref[...]
    allowed = allowed_pairs(pos_ref[0], qseg_ref[...], kseg_ref[...], causal)
    grad_query, grad_key, grad_value = [], 0.0, 0.0
    for head in range(2):
        probs = pair_probs(query, key, bias_ref, allowed, head, causal)
        grad_head = head_only(grad, head)
        grad_probs = mm(grad_head, value, NT)
        inner = jnp.sum(probs * grad_probs, axis=1, keepdims=True)
        grad_scores = probs * (grad_probs - inner)
        low_scores = grad_scores.astype(BF)
        grad_query.append(mm(low_scores, key))
        grad_key = grad_key + mm(low_scores, head_only(query, head), TN)
        grad_value = grad_value + mm(probs.astype(BF), grad_head, TN)
        if causal:
            dbias_ref[0, head : head + 1, :] = unspread(grad_scores, query.shape[0])
    if not causal:
        dbias_ref[...] = jnp.zeros_like(dbias_ref)
    dq_ref[...] = pick_heads(*grad_query).astype(BF)
    dk_ref[...] = grad_key.astype(BF)
    dv_ref[...] = grad_value.astype(BF)


def attention_specs(rows, keys, width):
    pair = lambda count: pl.BlockSpec((count, LANES), lambda step: (0, step))
    whole = lambda shape: pl.BlockSpec(shape, lambda step: (0, 0))
    smem = pl.BlockSpec(memory_space=pltpu.SMEM)
    bias = pl.BlockSpec((1, 2, width), lambda step: (step, 0, 0))
    return pair, bias, smem, [whole((rows, 1)), whole((1, keys))]


PARAMS = pltpu.CompilerParams(dimension_semantics=("arbitrary",), vmem_limit_bytes=48 << 20)


def attend(position, query, key, value, windows, qseg, kseg, causal):
    rows, inner = query.shape
    keys = key.shape[0]
    pair, bias, smem, segs = attention_specs(rows, keys, windows.shape[2])
    return pl.pallas_call(
        functools.partial(attend_body, causal),
        grid=(inner // LANES,),
        in_specs=[smem, pair(rows), pair(keys), pair(keys), bias] + segs,
        out_specs=pair(rows),
        out_shape=jax.ShapeDtypeStruct((rows, inner), BF),
        compiler_params=PARAMS,
        name="attend_self" if causal else "attend_cross",
    )(position, query, key, value, windows, qseg, kseg)


def attend_back(position, query, key, value, grad, windows, qseg, kseg, causal):
    rows, inner = query.shape
    keys = key.shape[0]
    pair, bias, smem, segs = attention_specs(rows, keys, windows.shape[2])
    return pl.pallas_call(
        functools.partial(attend_back_body, causal),
        grid=(inner // LANES,),
        in_specs=[smem, pair(rows), pair(keys), pair(keys), pair(rows), bias] + segs,
        out_specs=[pair(rows), pair(keys), pair(keys), bias],
        out_shape=[
            jax.ShapeDtypeStruct((rows, inner), BF),
            jax.ShapeDtypeStruct((keys, inner), BF),
            jax.ShapeDtypeStruct((keys, inner), BF),
            jax.ShapeDtypeStruct(windows.shape, F32),
        ],
        compiler_params=PARAMS,
        name="attend_self_back" if causal else "attend_cross_back",
    )(position, query, key, value, grad, windows, qseg, kseg)


def seq_perm(size, step):
    return [(i, (i + step) % size) for i in range(size)]


def seq_gather(rows):
    size, own = lax.axis_size("seq"), lax.axis_index("seq")
    full = jnp.zeros((size,) + rows.shape, rows.dtype)
    full = lax.dynamic_update_slice_in_dim(full, rows[None], own, 0)
    for step in range(1, size):
        piece = lax.ppermute(rows, "seq", seq_perm(size, step))
        full = lax.dynamic_update_slice_in_dim(full, piece[None], (own - step) % size, 0)
    return full


def seq_scatter(parts):
    size, own = lax.axis_size("seq"), lax.axis_index("seq")
    total = lax.dynamic_index_in_dim(parts, own, 0, False)
    low = parts.astype(BF)
    for step in range(1, size):
        piece = lax.dynamic_index_in_dim(low, (own + step) % size, 0, False)
        total = total + lax.ppermute(piece, "seq", seq_perm(size, step)).astype(F32)
    return total


def gather_all(shard):
    return lax.all_gather(shard, AXES, axis=0, tiled=True)


def scatter_all(grads):
    return lax.psum_scatter(grads, AXES, scatter_dimension=0, tiled=True).astype(F32)


def per_device(
    target, memory, cotangent, target_segments, memory_segments, bucket_ids,
    self_norm_gain, self_query, self_key, self_value, self_output, bias_table,
    cross_norm_gain, cross_query, cross_key, cross_value, cross_output,
    ffn_norm_gain, ffn_gate, ffn_up, ffn_down,
):
    batch_size, seq_size = lax.axis_size("batch"), lax.axis_size("seq")
    devices = batch_size * seq_size
    seq_index = lax.axis_index("seq")
    rows, width = target.shape[1], target.shape[2]
    length, enc = target_segments.shape[1], memory_segments.shape[1]
    enc_rows = memory.shape[1]
    inner = self_query.shape[1]
    hidden = ffn_gate.shape[1]
    table_rows, table_cols = bias_table.shape
    weight_rows = self_query.shape[0]
    table_size = table_rows * table_cols

    small = jnp.concatenate(
        [self_norm_gain, cross_norm_gain, ffn_norm_gain, bias_table.reshape(-1)]
    )
    small = jnp.pad(small[None], ((0, weight_rows - 1), (0, LANES - small.shape[0])))
    first = gather_all(jnp.concatenate([self_query, self_key, self_value, small], axis=1))
    second = gather_all(
        jnp.concatenate([self_output, cross_query, cross_key, cross_value, cross_output], axis=1)
    )
    third = gather_all(jnp.concatenate([ffn_gate, ffn_up], axis=1))
    down = gather_all(ffn_down)
    w_query, w_kv = first[:, :inner], first[:, inner : 3 * inner]
    smalls = first[:, 3 * inner :].reshape(devices, weight_rows, LANES)[:, 0, :].astype(F32)
    gains = [smalls[:, i * weight_rows : (i + 1) * weight_rows].reshape(1, width) for i in range(3)]
    gain_self, gain_cross, gain_ffn = gains
    table = smalls[:, 3 * weight_rows : 3 * weight_rows + table_size]
    table = table.reshape(batch_size, seq_size, table_rows, table_cols)
    table = jnp.transpose(table, (0, 2, 1, 3)).reshape(batch_size * table_rows, seq_size * table_cols)
    w_out, w_cq, w_ckv, w_co = (
        second[:, :inner],
        second[:, inner : 2 * inner],
        second[:, 2 * inner : 4 * inner],
        second[:, 4 * inner :],
    )

    both = seq_gather(jnp.concatenate([target[0], memory[0]], axis=0))
    target_all = both[:, :rows].reshape(length, width)
    memory_all = both[:, rows:].reshape(enc, width)

    position = seq_index * rows
    heads = table.shape[1]
    distance = position + rows - jnp.arange(rows + length, dtype=jnp.int32)
    near = (distance >= 0) & (distance < length)
    bucket = jnp.take(bucket_ids, jnp.clip(distance, 0, length - 1))
    bucket_range = jnp.arange(table.shape[0], dtype=jnp.int32)
    onehot = ((bucket[:, None] == bucket_range[None, :]) & near[:, None]).astype(BF)
    windows = mm(table.astype(BF), onehot, (((0,), (1,)), ((), ())))
    windows = windows.reshape(heads // 2, 2, rows + length)
    no_windows = jnp.zeros((heads // 2, 2, LANES), F32)

    position1 = position.reshape(1)
    qseg = lax.dynamic_slice_in_dim(target_segments, position, rows, 1).reshape(rows, 1)
    kseg, mseg = target_segments, memory_segments

    target_float = target[0].astype(F32)
    normed_all = norm_gain(target_all.astype(F32), gain_self).astype(BF)
    normed_one = norm_gain(target_float, gain_self).astype(BF)
    queries = mm(normed_one, w_query).astype(BF)
    kv = mm(normed_all, w_kv).astype(BF)
    keys, values = kv[:, :inner], kv[:, inner:]
    attended = attend(position1, queries, keys, values, windows, qseg, kseg, True)
    hidden_one = target_float + mm(attended, w_out)
    normed_two = norm_gain(hidden_one, gain_cross).astype(BF)
    cross_queries = mm(normed_two, w_cq).astype(BF)
    cross_kv = mm(memory_all, w_ckv).astype(BF)
    cross_keys, cross_values = cross_kv[:, :inner], cross_kv[:, inner:]
    cross_attended = attend(
        position1, cross_queries, cross_keys, cross_values, no_windows, qseg, mseg, False
    )
    hidden_two = hidden_one + mm(cross_attended, w_co)
    normed_three = norm_gain(hidden_two, gain_ffn).astype(BF)
    gate_up = mm(normed_three, third)
    inner_act, gated_pull = jax.vjp(gated_unit, gate_up[:, :hidden], gate_up[:, hidden:])
    inner_low = inner_act.astype(BF)
    activations = (hidden_two + mm(inner_low, down)).astype(BF)

    cot = cotangent[0]
    grad_down = mm(inner_low, cot, TN).astype(BF)
    grad_gate, grad_up = gated_pull(mm(cot, down, NT))
    grad_gate_up = jnp.concatenate([grad_gate.astype(BF), grad_up.astype(BF)], axis=1)
    grad_third = mm(normed_three, grad_gate_up, TN).astype(BF)
    down_out = scatter_all(grad_down)
    third_out = scatter_all(grad_third)
    through, grad_gain_ffn = norm_back(hidden_two, gain_ffn, mm(grad_gate_up, third, NT))
    grad_hidden_two = cot.astype(F32) + through

    low_two = grad_hidden_two.astype(BF)
    grad_cross_attended = mm(low_two, w_co, NT).astype(BF)
    grad_cq, grad_ck, grad_cv, _ = attend_back(
        position1, cross_queries, cross_keys, cross_values, grad_cross_attended,
        no_windows, qseg, mseg, False,
    )
    grad_ckv = jnp.concatenate([grad_ck, grad_cv], axis=1)
    cross_out = scatter_all(
        jnp.concatenate(
            [
                mm(normed_two, grad_cq, TN).astype(BF),
                mm(memory_all, grad_ckv, TN).astype(BF),
                mm(cross_attended, low_two, TN).astype(BF),
            ],
            axis=1,
        )
    )
    memory_grad = seq_scatter(mm(grad_ckv, w_ckv, NT).reshape(seq_size, enc_rows, width))
    through, grad_gain_cross = norm_back(hidden_one, gain_cross, mm(grad_cq, w_cq, NT))
    grad_hidden_one = grad_hidden_two + through

    low_one = grad_hidden_one.astype(BF)
    grad_attended = mm(low_one, w_out, NT).astype(BF)
    grad_q, grad_k, grad_v, grad_windows = attend_back(
        position1, queries, keys, values, grad_attended, windows, qseg, kseg, True
    )
    grad_kv = jnp.concatenate([grad_k, grad_v], axis=1)
    normed_grad = seq_scatter(mm(grad_kv, w_kv, NT).reshape(seq_size, rows, width))
    normed_grad = normed_grad + mm(grad_q, w_query, NT)
    through, grad_gain_self = norm_back(target_float, gain_self, normed_grad)
    target_grad = grad_hidden_one + through

    grad_windows = grad_windows.reshape(heads, rows + length)
    grad_table = lax.dot_general(
        onehot.astype(F32), grad_windows, (((0,), (1,)), ((), ())), precision=lax.Precision.HIGHEST
    )
    grad_table = grad_table.reshape(batch_size, table_rows, seq_size, table_cols)
    grad_table = jnp.transpose(grad_table, (0, 2, 1, 3)).reshape(devices, table_size)
    gain_parts = [g.reshape(devices, weight_rows) for g in (grad_gain_self, grad_gain_cross, grad_gain_ffn)]
    small_grad = jnp.concatenate(gain_parts + [grad_table], axis=1)
    small_grad = jnp.pad(
        small_grad[:, None], ((0, 0), (0, weight_rows - 1), (0, LANES - small_grad.shape[1]))
    ).reshape(devices * weight_rows, LANES)
    self_out = scatter_all(
        jnp.concatenate(
            [
                mm(normed_one, grad_q, TN).astype(BF),
                mm(normed_all, grad_kv, TN).astype(BF),
                mm(attended, low_one, TN).astype(BF),
                small_grad.astype(BF),
            ],
            axis=1,
        )
    )
    cut = lambda packed, i: packed[:, i * inner : (i + 1) * inner]
    small_out = self_out[0, 4 * inner :]
    gain_out = [small_out[i * weight_rows : (i + 1) * weight_rows] for i in range(3)]
    table_out = small_out[3 * weight_rows : 3 * weight_rows + table_size]
    return (
        activations[None],
        target_grad[None],
        memory_grad[None],
        gain_out[0],
        cut(self_out, 0),
        cut(self_out, 1),
        cut(self_out, 2),
        cut(self_out, 3),
        table_out.reshape(table_rows, table_cols),
        gain_out[1],
        cut(cross_out, 0),
        cut(cross_out, 1),
        cut(cross_out, 2),
        cut(cross_out, 3),
        gain_out[2],
        third_out[:, :hidden],
        third_out[:, hidden:],
        down_out,
    )


def solution(mesh):
    rows3 = P("batch", "seq", None)
    seg = P("batch", None)
    gain = P(AXES)
    weight = P(AXES, None)
    table = P("batch", "seq")
    return jax.shard_map(
        per_device,
        mesh=mesh,
        in_specs=(
            rows3, rows3, rows3, seg, seg, P(),
            gain, weight, weight, weight, weight, table,
            gain, weight, weight, weight, weight,
            gain, weight, weight, weight,
        ),
        out_specs=(
            rows3, rows3, rows3,
            gain, weight, weight, weight, weight, table,
            gain, weight, weight, weight, weight,
            gain, weight, weight, weight,
        ),
        check_vma=False,
    )
```

time: 2580 us -> 946 us (0.37)
  waiting for transfers between devices: 1820 us -> 734 us
  local copies, waits for them, and re-layouts: 370 us -> 33.5 us
  matrix products: 232 us -> 88.5 us
  blocking collectives: 89.2 us -> 0 us
  Pallas kernels: 0 us -> 38.1 us
  loops' own time: 33.1 us -> 0 us
    reduce_scatter x9 -> x4, waiting for transfers between devices: 1220 us -> 457 us  [scatter_all(): lax.psum_scatter(grads, AXES, scatter_dimension=0, tiled=True).astype(F32)]
    unnamed x34 -> x8, waiting for transfers between devices: 294 us -> 0.64 us
    gather x384 -> x1, local copies, waits for them, and re-layouts: 252 us -> 4.31 us  [per_device(): bucket = jnp.take(bucket_ids, jnp.clip(distance, 0, length - 1))]
    dot_general x95 -> x26, matrix products: 232 us -> 88.5 us  [the longest x25 87.9 us: mm(): return lax.dot_general(left, right, dims, preferred_element_type=F32)]
    unnamed x2 -> x0, blocking collectives: 82 us -> none
    unnamed x129 -> x126, local copies, waits for them, and re-layouts: 68.1 us -> 10.9 us
    all_gather x13 -> x4, waiting for transfers between devices: 302 us -> 252 us  [gather_all(): return lax.all_gather(shard, AXES, axis=0, tiled=True)]
    pallas_call x0 -> x4, Pallas kernels: none -> 38.1 us  [the longest x2 22.8 us: attend_back(): pl.pallas_call(functools.partial(attend_back_body, causal), grid=(inner /...]
  transfers between devices with their start and end apart: 28 -> 17, of which waited for: 18 -> 14; matrix products, arithmetic and copies ran while one was open for 21% -> 13% of each run, Pallas kernels for 0% -> 4%
where the time goes in v1:
time: 946 us; the launch traced here: 939 us
  waiting for transfers between devices  734 us (78%)
  matrix products  88.5 us (9%)
  Pallas kernels  38.1 us (4%)
  local copies, waits for them, and re-layouts  33.5 us (4%)
  other arithmetic  21.1 us (2%)
  between operations  15.5 us (2%)
    reduce_scatter x4, waiting for transfers between devices, scatter_all(): lax.psum_scatter(grads, AXES, scatter_dimension=0, tiled=True).astype(F32)  457 us
    all_gather x4, waiting for transfers between devices, gather_all(): return lax.all_gather(shard, AXES, axis=0, tiled=True)  252 us
    dot_general x25, matrix products, mm(): return lax.dot_general(left, right, dims, preferred_element_type=F32)  87.9 us
    pallas_call x2, Pallas kernels, attend_back(): pl.pallas_call(functools.partial(attend_back_body, causal), grid=(inner /...  22.8 us
  transfers between devices with their start and end apart: 17, of which 14 were waited for; matrix products, arithmetic and copies ran while one was open for 13% of the time, Pallas kernels for 4%

profile of v1, /device:TPU:0, one launch (start us, length us, event | category | flops | bytes accessed | tf_op | source)
XLA Modules:
  0.0 938.8 jit_solution(3150465886255393845)
XLA Ops:
  22.6 4.3 gather_fusion
  27.6 3.2 collective-permute-done
  32.6 7.3 collective-permute-done.2
  40.5 45.7 %all-gather.5.cloned.1.call-done = bf16[1024,3200]{1,0:T(8,128)(2,1)} async-done(((bf16[32,3200]{1,0:T(8,128)(2,1)}), bf16[1024,3200]{1,0:T(8,128)(2,1)}) %all-gather.5.cloned.1.call-update) | async-done | bytes 6553616 | tf_op jit(solution)/shard_map/all_gather | solution.py:195
  90.7 4.9 fusion.8
  95.8 7.9 attend_self.1
  103.7 71.3 %all-gather.7.cloned.1.call-done = bf16[1024,5120]{1,0:T(8,128)(2,1)} async-done(((bf16[32,5120]{1,0:T(8,128)(2,1)}), bf16[1024,5120]{1,0:T(8,128)(2,1)}) %all-gather.7.cloned.1.call-update) | async-done | bytes 10485776 | tf_op jit(solution)/shard_map/all_gather | solution.py:195
  177.2 3.6 fusion.11
  183.0 7.4 attend_cross.1
  190.4 3.0 multiply_reduce_fusion.5
  193.9 74.6 %all-gather.9.cloned.1.call-done = bf16[1024,5632]{1,0:T(8,128)(2,1)} async-done(((bf16[32,5632]{1,0:T(8,128)(2,1)}), bf16[1024,5632]{1,0:T(8,128)(2,1)}) %all-gather.9.cloned.1.call-update) | async-done | bytes 11534352 | tf_op jit(solution)/shard_map/all_gather | solution.py:195
  268.5 7.8 fusion.117
  276.3 60.6 %all-gather.11.cloned.1.call-done = bf16[2816,1024]{1,0:T(8,128)(2,1)} async-done(((bf16[88,1024]{1,0:T(8,128)(2,1)}), bf16[2816,1024]{1,0:T(8,128)(2,1)}) %all-gather.11.cloned.1.call-update) | async-done | bytes 5767184 | tf_op jit(solution)/shard_map/all_gather | solution.py:195
  336.9 7.4 fusion.38
  345.2 4.2 convolution_convert_fusion.1
  350.1 8.8 multiply_reduce_fusion.1
  361.8 8.8 attend_cross_back.1
  370.7 3.1 multiply_reduce_fusion.2
  377.4 14.0 %attend_self_back.1 = (bf16[128,1024]{1,0:T(8,128)(2,1)S(1)}, bf16[512,1024]{1,0:T(8,128)(2,1)S(1)}, bf16[512,1024]{1,0:T(8,128)(2,1)S(1)}, f32[8,2,640]{2,1,0:T(2,128)S(1)}) custom-call(s32[1]{0:T(128)} %bitcast.1.pos_ref, bf16[128,1024]{1,0:T(8,128)(2,1)S(1)} %fusion.46.q_ref, bf16[512,1024]{1,0:T(8,128)(2,1)S(1)} %get-tuple-element.43.k_ref, ...), custom_call_target="tpu_custom_call" | custom-call | tf_op jit(solution)/shard_map/attend_self_back/pallas_call | solution.py:154
  403.6 6.3 convolution_convert_fusion.3
  412.0 5.7 collective-permute-done.4
  417.7 3.6 fusion.64
  421.6 6.6 pad_maximum_fusion
  436.4 3.7 pad_maximum_fusion.1
  441.6 6.2 convolution_convert_fusion
  447.7 3.5 fusion
  453.2 4.4 fusion.58
  457.6 6.0 collective-permute-done.7
  465.5 27.3 %reduce-scatter.11.cloned.1.call-done = bf16[88,1024]{1,0:T(8,128)(2,1)} async-done(((bf16[2816,1024]{1,0:T(8,128)(2,1)}), bf16[88,1024]{1,0:T(8,128)(2,1)}) %reduce-scatter.11.cloned.1.call-update) | async-done | bytes 180240 | tf_op jit(solution)/shard_map/reduce_scatter | solution.py:199
  494.5 131.9 %reduce-scatter.5.cloned.1.call-done = bf16[32,4224]{1,0:T(8,128)(2,1)} async-done(((bf16[1024,4224]{1,0:T(8,128)(2,1)}), bf16[32,4224]{1,0:T(8,128)(2,1)}) %reduce-scatter.5.cloned.1.call-update) | async-done | bytes 270352 | tf_op jit(solution)/shard_map/reduce_scatter | solution.py:199
  630.4 146.4 %reduce-scatter.7.cloned.1.call-done = bf16[32,4096]{1,0:T(8,128)(2,1)} async-done(((bf16[1024,4096]{1,0:T(8,128)(2,1)}), bf16[32,4096]{1,0:T(8,128)(2,1)}) %reduce-scatter.7.cloned.1.call-update) | async-done | bytes 262160 | tf_op jit(solution)/shard_map/reduce_scatter | solution.py:199
  778.5 151.3 %reduce-scatter.9.cloned.1.call-done = bf16[32,5632]{1,0:T(8,128)(2,1)} async-done(((bf16[1024,5632]{1,0:T(8,128)(2,1)}), bf16[32,5632]{1,0:T(8,128)(2,1)}) %reduce-scatter.9.cloned.1.call-update) | async-done | bytes 360464 | tf_op jit(solution)/shard_map/reduce_scatter | solution.py:199
  (243 shorter events, 72.7 us)
Async XLA Ops:
  7.2 15.4 %copy-start = (s32[512]{0:T(512)S(1)}, s32[512]{0:T(512)}, u32[]{:S(2)}) copy-start(s32[512]{0:T(512)} %param.26) | copy-start | bytes 6148
  7.2 79.0 %all-gather.5.cloned.1.call-start = ((), (), s32[]{:S(2)}) async-start(), calls=%async_computation.4 | async-start | bytes 6758400 | tf_op jit(solution)/shard_map/all_gather | solution.py:195
  10.5 164.5 %all-gather.7.cloned.1.call-start = ((), (), s32[]{:S(2)}) async-start(), calls=%async_computation.5 | async-start | bytes 10813440 | tf_op jit(solution)/shard_map/all_gather | solution.py:195
  15.5 253.0 %all-gather.9.cloned.1.call-start = ((), (), s32[]{:S(2)}) async-start(), calls=%async_computation.6 | async-start | bytes 11894784 | tf_op jit(solution)/shard_map/all_gather | solution.py:195
  17.4 319.6 %all-gather.11.cloned.1.call-start = ((), (), s32[]{:S(2)}) async-start(), calls=%async_computation.7 | async-start | bytes 5947392 | tf_op jit(solution)/shard_map/all_gather | solution.py:195
  17.9 474.9 %reduce-scatter.11.cloned.1.call-start = ((), (), s32[]{:S(2)}) async-start(), calls=%async_computation.11 | async-start | bytes 5947392 | tf_op jit(solution)/shard_map/reduce_scatter | solution.py:199
  18.0 12.7 %collective-permute-start = (bf16[192,1024]{1,0:T(8,128)(2,1)S(1)}, bf16[192,1024]{1,0:T(8,128)(2,1)S(1)}, u32[]{:S(2)}, u32[]{:S(2)}) collective-permute-start(bf16[192,1024]{1,0:T(8,128)(2,1)S(1)} %pad_maximum_fusion.5), channel_id=1, source_target_pairs={{0,1},{1,2},{2,3},{3,0},{4,5},{5,6},{6,7},{7,4},{8,9},{9,10},{10,1... | collective-permute-start | bytes 1179656 | tf_op jit(solution)/shard_map/ppermute | solution.py:179
  18.5 14.0 %collective-permute-start.1 = (bf16[192,1024]{1,0:T(8,128)(2,1)S(1)}, bf16[192,1024]{1,0:T(8,128)(2,1)S(1)}, u32[]{:S(2)}, u32[]{:S(2)}) collective-permute-start(bf16[192,1024]{1,0:T(8,128)(2,1)S(1)} %pad_maximum_fusion.5), channel_id=1, source_target_pairs={{0,2},{1,3},{2,0},{3,1},{4,6},{5,7},{6,4},{7,5},{8,10},{9,11},{10,... | collective-permute-start | bytes 1179656 | tf_op jit(solution)/shard_map/ppermute | solution.py:179
  21.1 18.8 %collective-permute-start.2 = (bf16[192,1024]{1,0:T(8,128)(2,1)S(1)}, bf16[192,1024]{1,0:T(8,128)(2,1)S(1)}, u32[]{:S(2)}, u32[]{:S(2)}) collective-permute-start(bf16[192,1024]{1,0:T(8,128)(2,1)S(1)} %pad_maximum_fusion.5), channel_id=1, source_target_pairs={{0,3},{1,0},{2,1},{3,2},{4,7},{5,4},{6,5},{7,6},{8,11},{9,8},{10,9... | collective-permute-start | bytes 1179656 | tf_op jit(solution)/shard_map/ppermute | solution.py:179
  27.0 12.9 %copy-start.51 = (f32[128]{0:T(128)}, f32[128]{0:T(128)S(1)}, u32[]{:S(2)}) copy-start(f32[128]{0:T(128)S(1)} %fusion.69) | copy-start | bytes 1540
  27.1 61.3 %copy-start.44 = (f32[128]{0:T(128)}, f32[128]{0:T(128)S(1)}, u32[]{:S(2)}) copy-start(f32[128]{0:T(128)S(1)} %fusion.110) | copy-start | bytes 1540
  27.1 60.9 %copy-start.49 = (pred[640]{0:T(1024)(128)(4,1)}, pred[640]{0:T(1024)(128)(4,1)S(1)}, u32[]{:S(2)}) copy-start(pred[640]{0:T(1024)(128)(4,1)S(1)} %fusion.107) | copy-start | bytes 1924
  40.0 137.2 %copy-start.28 = (bf16[4,64,1024]{2,1,0:T(8,128)(2,1)}, bf16[4,64,1024]{2,1,0:T(8,128)(2,1)S(1)}, u32[]{:S(2)}) copy-start(bf16[4,64,1024]{2,1,0:T(8,128)(2,1)S(1)} %slice.169) | copy-start | bytes 1572868
  103.7 73.4 %copy-start.2 = (bf16[128,1024]{1,0:T(8,128)(2,1)}, bf16[128,1024]{1,0:T(8,128)(2,1)S(1)}, u32[]{:S(2)}) copy-start(bf16[128,1024]{1,0:T(8,128)(2,1)S(1)} %attend_self.1) | copy-start | bytes 786436
  177.1 13.3 %copy-start.33 = (f32[128,1024]{1,0:T(8,128)}, f32[128,1024]{1,0:T(8,128)S(1)}, u32[]{:S(2)}) copy-start(f32[128,1024]{1,0:T(8,128)S(1)} %get-tuple-element.69) | copy-start | bytes 1572868
  349.4 277.0 %reduce-scatter.5.cloned.1.call-start = ((), (), s32[]{:S(2)}) async-start(), calls=%async_computation.8 | async-start | bytes 8921088 | tf_op jit(solution)/shard_map/reduce_scatter | solution.py:199
  359.2 14.6 %copy-start.26 = (f32[128,1024]{1,0:T(8,128)}, f32[128,1024]{1,0:T(8,128)S(1)}, u32[]{:S(2)}) copy-start(f32[128,1024]{1,0:T(8,128)S(1)} %fusion.65) | copy-start | bytes 1572868
  359.2 11.5 %copy-start.34 = (f32[128,1024]{1,0:T(8,128)S(1)}, f32[128,1024]{1,0:T(8,128)}, u32[]{:S(2)}) copy-start(f32[128,1024]{1,0:T(8,128)} %copy-done.33) | copy-start | bytes 1572868
  370.7 21.0 %slice-start = ((s8[6553600]{0:T(1024)(128)(4,1)}), s8[4194304]{0:T(1024)(128)(4,1)S(1)}, s32[]{:S(2)}) async-start(s8[6553600]{0:T(1024)(128)(4,1)} %bitcast.154), calls=%async_computation.12 | async-start | bytes 8388608
  374.8 16.8 %slice-start.1 = ((s8[6553600]{0:T(1024)(128)(4,1)}), s8[2359296]{0:T(1024)(128)(4,1)S(1)}, s32[]{:S(2)}) async-start(s8[6553600]{0:T(1024)(128)(4,1)} %bitcast.154), calls=%async_computation.13 | async-start | bytes 4718592
  395.6 16.4 %collective-permute-start.5 = (bf16[128,1024]{1,0:T(8,128)(2,1)}, bf16[128,1024]{1,0:T(8,128)(2,1)}, u32[]{:S(2)}, u32[]{:S(2)}) collective-permute-start(bf16[128,1024]{1,0:T(8,128)(2,1)} %get-tuple-element.45), channel_id=1, source_target_pairs={{0,3},{1,0},{2,1},{3,2},{4,7},{5,4},{6,5},{7,6},{8,11},{9,8},{10,9... | collective-permute-start | bytes 786440 | tf_op jit(solution)/shard_map/ppermute | solution.py:190
  396.9 20.8 %collective-permute-start.4 = (bf16[128,1024]{1,0:T(8,128)(2,1)}, bf16[128,1024]{1,0:T(8,128)(2,1)}, u32[]{:S(2)}, u32[]{:S(2)}) collective-permute-start(bf16[128,1024]{1,0:T(8,128)(2,1)} %get-tuple-element.46), channel_id=1, source_target_pairs={{0,2},{1,3},{2,0},{3,1},{4,6},{5,7},{6,4},{7,5},{8,10},{9,11},{10,... | collective-permute-start | bytes 786440 | tf_op jit(solution)/shard_map/ppermute | solution.py:190
  397.5 20.2 %collective-permute-start.3 = (bf16[128,1024]{1,0:T(8,128)(2,1)S(1)}, bf16[128,1024]{1,0:T(8,128)(2,1)}, u32[]{:S(2)}, u32[]{:S(2)}) collective-permute-start(bf16[128,1024]{1,0:T(8,128)(2,1)S(1)} %get-tuple-element.44), channel_id=1, source_target_pairs={{0,1},{1,2},{2,3},{3,0},{4,5},{5,6},{6,7},{7,4},{8,9},{9,10},{10,1... | collective-permute-start | bytes 786440 | tf_op jit(solution)/shard_map/ppermute | solution.py:190
  428.2 348.6 %reduce-scatter.7.cloned.1.call-start = ((), (), s32[]{:S(2)}) async-start(), calls=%async_computation.9 | async-start | bytes 8650752 | tf_op jit(solution)/shard_map/reduce_scatter | solution.py:199
  440.1 489.8 %reduce-scatter.9.cloned.1.call-start = ((), (), s32[]{:S(2)}) async-start(), calls=%async_computation.10 | async-start | bytes 11894784 | tf_op jit(solution)/shard_map/reduce_scatter | solution.py:199
  451.4 6.2 collective-permute-start.8
  451.5 12.2 %collective-permute-start.7 = (bf16[64,1024]{1,0:T(8,128)(2,1)S(1)}, bf16[64,1024]{1,0:T(8,128)(2,1)S(1)}, u32[]{:S(2)}, u32[]{:S(2)}) collective-permute-start(bf16[64,1024]{1,0:T(8,128)(2,1)S(1)} %get-tuple-element.54), channel_id=1, source_target_pairs={{0,2},{1,3},{2,0},{3,1},{4,6},{5,7},{6,4},{7,5},{8,10},{9,11},{10,... | collective-permute-start | bytes 393224 | tf_op jit(solution)/shard_map/ppermute | solution.py:190
  453.0 11.5 %copy-start.52 = (f32[128]{0:T(128)S(1)}, f32[128]{0:T(128)}, u32[]{:S(2)}) copy-start(f32[128]{0:T(128)} %copy-done.51) | copy-start | bytes 1540
  453.0 11.5 %copy-start.25 = (f32[128,1024]{1,0:T(8,128)S(1)}, f32[128,1024]{1,0:T(8,128)}, u32[]{:S(2)}) copy-start(f32[128,1024]{1,0:T(8,128)} %copy-done.23) | copy-start | bytes 1572868
  453.0 11.5 %copy-start.39 = (f32[128,1024]{1,0:T(8,128)S(1)}, f32[128,1024]{1,0:T(8,128)}, u32[]{:S(2)}) copy-start(f32[128,1024]{1,0:T(8,128)} %get-tuple-element.38) | copy-start | bytes 1572868
  453.0 10.7 %collective-permute-start.6 = (bf16[64,1024]{1,0:T(8,128)(2,1)S(1)}, bf16[64,1024]{1,0:T(8,128)(2,1)S(1)}, u32[]{:S(2)}, u32[]{:S(2)}) collective-permute-start(bf16[64,1024]{1,0:T(8,128)(2,1)S(1)} %get-tuple-element.52), channel_id=1, source_target_pairs={{0,1},{1,2},{2,3},{3,0},{4,5},{5,6},{6,7},{7,4},{8,9},{9,10},{10,1... | collective-permute-start | bytes 393224 | tf_op jit(solution)/shard_map/ppermute | solution.py:190
  492.8 438.9 %copy-start.1 = (s32[512]{0:T(512)S(1)}, s32[512]{0:T(512)}, u32[]{:S(2)}) copy-start(s32[512]{0:T(512)} %param.26) | copy-start | bytes 6148
  (44 other events, 171.8 us)
Sparse Core Ops, SparseCore 0:
  11.5 74.6 all-gather.4
  89.6 85.2 all-gather.6
  178.4 90.0 all-gather.8
  271.3 65.6 all-gather.10
  349.6 143.2 reduce-scatter.10
  498.6 127.7 reduce-scatter.4
  628.7 148.0 reduce-scatter.6
  779.1 150.6 reduce-scatter.8

commit v2 on v1

--- a/solution.py
+++ b/solution.py
@@ -199,6 +199,227 @@
     return lax.psum_scatter(grads, AXES, scatter_dimension=0, tiled=True).astype(F32)
 
 
+class Links:
+    def __init__(self):
+        self.batch, self.seq = lax.axis_size("batch"), lax.axis_size("seq")
+        self.depth = self.batch // 2
+        z_x, y_c = lax.axis_index("batch"), lax.axis_index("seq")
+        self.z, self.x = z_x // 2, z_x % 2
+        self.y, self.core = y_c // 2, y_c % 2
+        self.lead = self.core == 0
+        self.place = jnp.stack([self.z, self.x, self.y, self.core]).astype(jnp.int32)
+
+    def move(self, value, target):
+        pairs = []
+        for source in range(self.batch * self.seq):
+            z_x, y_c = source // self.seq, source % self.seq
+            z, x, y, core = target(z_x // 2, z_x % 2, y_c // 2, y_c % 2)
+            pairs.append((source, (z * 2 + x) * self.seq + y * 2 + core))
+        return lax.ppermute(value, AXES, pairs)
+
+    def over_core(self, value):
+        return self.move(value, lambda z, x, y, core: (z, x, y, 1 - core))
+
+    def over_near(self, value):
+        return self.move(
+            value, lambda z, x, y, c: (z, x, 1 - y, c) if c else (z, 1 - x, y, c)
+        )
+
+    def over_far(self, value):
+        return self.move(
+            value, lambda z, x, y, c: (z, 1 - x, y, c) if c else (z, x, 1 - y, c)
+        )
+
+    def over_z(self, value, step):
+        depth = self.depth
+        return self.move(value, lambda z, x, y, core: ((z - step) % depth, x, y, core))
+
+
+def in_order(first, own, other):
+    return jnp.concatenate([jnp.where(first, own, other), jnp.where(first, other, own)], axis=0)
+
+
+def gather_core(links, left, right):
+    own = jnp.where(links.lead, left, right)
+    other = links.over_core(jnp.where(links.lead, right, left))
+    return in_order(links.lead, own, other)
+
+
+def z_steps(links, value, steps):
+    return [links.over_z(value, step) for step in steps]
+
+
+def gather_near(links, value):
+    return jnp.stack([value, links.over_near(value)])
+
+
+def assemble(links, near, far, near_other, far_other):
+    depth, rows, cols = near.shape[1:]
+
+    def body(place_ref, *refs):
+        sources, out_ref, sem = refs[:4], refs[4], refs[5]
+        z, x, y, core = [place_ref[i] for i in range(4)]
+        for which, source in enumerate(sources):
+            half = core if which < 2 else 1 - core
+            far_step = which % 2
+            for near_step in range(2):
+                step_x = jnp.where(half == 0, near_step, far_step)
+                step_y = jnp.where(half == 0, far_step, near_step)
+                for step in range(depth):
+                    chip = (((z + step) % depth) * 2 + (x ^ step_x)) * 2 + (y ^ step_y)
+                    target = out_ref.at[
+                        pl.ds(pl.multiple_of(chip * rows, 16), rows),
+                        pl.ds(pl.multiple_of(half * cols, LANES), cols),
+                    ]
+                    pltpu.make_async_copy(source.at[near_step, step], target, sem).start()
+        pltpu.make_async_copy(out_ref, out_ref, sem).wait()
+
+    anywhere = pl.BlockSpec(memory_space=pl.ANY)
+    return pl.pallas_call(
+        body,
+        in_specs=[pl.BlockSpec(memory_space=pltpu.SMEM)] + [anywhere] * 4,
+        out_specs=pl.BlockSpec(memory_space=pltpu.VMEM),
+        out_shape=jax.ShapeDtypeStruct((depth * 4 * rows, 2 * cols), near.dtype),
+        scratch_shapes=[pltpu.SemaphoreType.DMA(())],
+        compiler_params=pltpu.CompilerParams(vmem_limit_bytes=48 << 20),
+        name="assemble",
+    )(links.place, near, far, near_other, far_other)
+
+
+def weight_grad(links, core, terms, extra=None):
+    depth, total_rows = links.depth, terms[0][0].shape[1]
+    rows = total_rows // (depth * 4)
+    widths = [term[1].shape[1] for term in terms]
+    extra_width = 0 if extra is None else extra.shape[1]
+    total = sum(widths) + extra_width
+    tile = 1408 if total % 1408 == 0 else 512
+
+    def body(place_ref, *refs):
+        inputs, out_ref, stage, sems = refs[:-3], refs[-3], refs[-2], refs[-1]
+        z, x, y, left = place_ref[0], place_ref[1], place_ref[2], place_ref[3] == 0
+        places = []
+        for chip in range(depth * 4):
+            step_x, step_y = (chip // 2 % 2) ^ x, (chip % 2) ^ y
+            near, far = jnp.where(left, step_x, step_y), jnp.where(left, step_y, step_x)
+            spot = (near * 2 + far) * depth + (chip // 4 - z) % depth
+            places.append(pl.multiple_of(spot * rows, 8))
+        copies, start = [], 0
+
+        def emit(start, value, width):
+            for chip, spot in enumerate(places):
+                stage[pl.ds(spot, rows), start : start + width] = value[
+                    chip * rows : (chip + 1) * rows
+                ].astype(BF)
+            copies.append(
+                pltpu.make_async_copy(
+                    stage.at[:, pl.ds(start, width)],
+                    out_ref.at[:, pl.ds(start, width)],
+                    sems.at[len(copies)],
+                )
+            )
+            copies[-1].start()
+
+        for index, width in enumerate(widths):
+            acts_l, grad_l, acts_r, grad_r = inputs[4 * index : 4 * index + 4]
+            acts = jnp.where(left, acts_l[...], acts_r[...])
+            for offset in range(0, width, tile):
+                cols = slice(offset, offset + tile)
+                grad = jnp.where(left, grad_l[:, cols], grad_r[:, cols])
+                emit(start, mm(acts, grad, TN), tile)
+                start += tile
+        if extra is not None:
+            small = inputs[-1][...]
+            emit(start, jnp.where(left, small, jnp.zeros_like(small)), extra_width)
+        for copy in copies:
+            copy.wait()
+
+    place = links.place.at[3].set(core)
+    operands = [array for term in terms for array in term] + ([] if extra is None else [extra])
+    count = sum(width // tile for width in widths) + (extra is not None)
+    vmem = pl.BlockSpec(memory_space=pltpu.VMEM)
+    return pl.pallas_call(
+        body,
+        in_specs=[pl.BlockSpec(memory_space=pltpu.SMEM)] + [vmem] * len(operands),
+        out_specs=pl.BlockSpec(memory_space=pl.ANY),
+        out_shape=jax.ShapeDtypeStruct((total_rows, total), BF),
+        scratch_shapes=[pltpu.VMEM((total_rows, total), BF), pltpu.SemaphoreType.DMA((count,))],
+        compiler_params=pltpu.CompilerParams(vmem_limit_bytes=48 << 20),
+        name="weight_grad",
+    )(place, *operands)
+
+
+class Scatter:
+    def __init__(self, links):
+        self.links, self.parts = links, []
+
+    def core(self, sent):
+        self.rows = sent.shape[0]
+        self.parts.append(self.links.over_core(sent))
+
+    def keep(self, kept):
+        self.parts.append(kept)
+
+    def total(self, start, count):
+        return sum(part[start : start + count].astype(F32) for part in self.parts)
+
+    def halve(self):
+        self.rows //= 2
+        return self.total(self.rows, self.rows).astype(BF)
+
+    def near(self, send):
+        self.parts.append(self.links.over_near(send))
+
+    def far(self, send):
+        self.parts.append(self.links.over_far(send))
+
+    def z_sends(self):
+        self.rows //= self.links.depth
+        return [
+            self.total(step * self.rows, self.rows).astype(BF)
+            for step in range(1, self.links.depth)
+        ]
+
+    def z(self, sends):
+        depth = self.links.depth
+        for step, send in enumerate(sends, 1):
+            self.parts.append(self.links.over_z(send, depth - step))
+
+    def own(self):
+        return self.total(0, self.rows)
+
+    def last(self, total):
+        links, half = self.links, self.rows // 2
+        above, below = total[:half], total[half:]
+        own = jnp.where(links.lead, above, below)
+        other = links.over_core(jnp.where(links.lead, below, above))
+        return jnp.where(links.lead, own, other), jnp.where(links.lead, other, own)
+
+
+class PlainScatter:
+    def core(self, sent):
+        self.sent = sent
+
+    def keep(self, kept):
+        self.kept = kept
+
+    def halve(self):
+        return self.sent
+
+    def near(self, send):
+        self.sent = send
+
+    far = z = near
+    z_sends = own = halve
+
+    def last(self, total):
+        whole = scatter_all(self.kept)
+        return jnp.split(whole, 2, axis=1)
+
+
+def phase(*values):
+    return lax.optimization_barrier(values)
+
+
 def per_device(
     target, memory, cotangent, target_segments, memory_segments, bucket_ids,
     self_norm_gain, self_query, self_key, self_value, self_output, bias_table,
@@ -217,33 +438,76 @@
     weight_rows = self_query.shape[0]
     table_size = table_rows * table_cols
 
+    links = Links()
+    core, lead, depth = links.core, links.lead, links.depth
     small = jnp.concatenate(
         [self_norm_gain, cross_norm_gain, ffn_norm_gain, bias_table.reshape(-1)]
     )
-    small = jnp.pad(small[None], ((0, weight_rows - 1), (0, LANES - small.shape[0])))
-    first = gather_all(jnp.concatenate([self_query, self_key, self_value, small], axis=1))
-    second = gather_all(
-        jnp.concatenate([self_output, cross_query, cross_key, cross_value, cross_output], axis=1)
-    )
-    third = gather_all(jnp.concatenate([ffn_gate, ffn_up], axis=1))
-    down = gather_all(ffn_down)
+    small = jnp.pad(small[None], ((0, weight_rows - 1), (0, 2 * LANES - small.shape[0])))
+    groups = [
+        [self_query, self_key, self_value, small],
+        [self_output, cross_query, cross_key, cross_value, cross_output],
+        [ffn_gate, ffn_up],
+    ]
+    groups = [jnp.concatenate(group, axis=1) for group in groups]
+    cuts = [group.shape[1] // 2 for group in groups]
+    left = jnp.concatenate([group[:, :cut] for group, cut in zip(groups, cuts)], axis=1)
+    right = jnp.concatenate([group[:, cut:] for group, cut in zip(groups, cuts)], axis=1)
+    down_cut = width // 2
+    steps = list(range(1, depth))
+    some, rest = steps[:1], steps[1:]
+
+    moved = gather_core(links, left, right)
+    direct = 2 * ffn_down.shape[0] % 16 == 0
+    if direct:
+        down0 = gather_core(links, ffn_down[:, :down_cut], ffn_down[:, down_cut:])
+    else:
+        down0 = gather_all(ffn_down)
+    rows_own = jnp.concatenate([target[0], memory[0]], axis=0)
+    rows_other = [
+        lax.ppermute(rows_own, "seq", seq_perm(seq_size, step)) for step in range(1, seq_size)
+    ]
+    moved, down0 = phase(moved, down0)
+    first0 = moved[:, : cuts[0]]
+    second0 = moved[:, cuts[0] : cuts[0] + cuts[1]]
+    third0 = moved[:, cuts[0] + cuts[1] :]
+
+    first_z = z_steps(links, first0, steps)
+    first_z = jnp.stack([first0] + first_z)
+    first_z, second0, third0, rows_other = phase(first_z, second0, third0, rows_other)
+
+    first_near = gather_near(links, first_z)
+    second_z = z_steps(links, second0, some)
+    both = jnp.zeros((seq_size,) + rows_own.shape, rows_own.dtype)
+    for step, piece in enumerate([rows_own] + rows_other):
+        both = lax.dynamic_update_slice_in_dim(both, piece[None], (seq_index - step) % seq_size, 0)
+    target_all = both[:, :rows].reshape(length, width)
+    memory_all = both[:, rows:].reshape(enc, width)
+    first_near, second_z, second0, target_all, memory_all = phase(
+        first_near, second_z, second0, target_all, memory_all
+    )
+
+    first_far = links.over_far(first_near)
+    first_near_other = links.over_core(first_near)
+    second_z = jnp.stack([second0] + second_z + z_steps(links, second0, rest))
+    first_far, first_near_other, second_z, third0 = phase(
+        first_far, first_near_other, second_z, third0
+    )
+
+    second_near = gather_near(links, second_z)
+    third_z = z_steps(links, third0, some)
+    first = assemble(
+        links, first_near, first_far, first_near_other, links.over_core(first_far)
+    )
+    first, second_near, third_z, third0, down0 = phase(first, second_near, third_z, third0, down0)
+
     w_query, w_kv = first[:, :inner], first[:, inner : 3 * inner]
-    smalls = first[:, 3 * inner :].reshape(devices, weight_rows, LANES)[:, 0, :].astype(F32)
+    smalls = first[:, 3 * inner :].reshape(devices, weight_rows, 2 * LANES)[:, 0, :].astype(F32)
     gains = [smalls[:, i * weight_rows : (i + 1) * weight_rows].reshape(1, width) for i in range(3)]
     gain_self, gain_cross, gain_ffn = gains
     table = smalls[:, 3 * weight_rows : 3 * weight_rows + table_size]
     table = table.reshape(batch_size, seq_size, table_rows, table_cols)
     table = jnp.transpose(table, (0, 2, 1, 3)).reshape(batch_size * table_rows, seq_size * table_cols)
-    w_out, w_cq, w_ckv, w_co = (
-        second[:, :inner],
-        second[:, inner : 2 * inner],
-        second[:, 2 * inner : 4 * inner],
-        second[:, 4 * inner :],
-    )
-
-    both = seq_gather(jnp.concatenate([target[0], memory[0]], axis=0))
-    target_all = both[:, :rows].reshape(length, width)
-    memory_all = both[:, rows:].reshape(enc, width)
 
     position = seq_index * rows
     heads = table.shape[1]
@@ -255,11 +519,13 @@
     windows = mm(table.astype(BF), onehot, (((0,), (1,)), ((), ())))
     windows = windows.reshape(heads // 2, 2, rows + length)
     no_windows = jnp.zeros((heads // 2, 2, LANES), F32)
-
     position1 = position.reshape(1)
     qseg = lax.dynamic_slice_in_dim(target_segments, position, rows, 1).reshape(rows, 1)
     kseg, mseg = target_segments, memory_segments
 
+    second_far = links.over_far(second_near)
+    second_near_other = links.over_core(second_near)
+    third_z = jnp.stack([third0] + third_z + z_steps(links, third0, rest))
     target_float = target[0].astype(F32)
     normed_all = norm_gain(target_all.astype(F32), gain_self).astype(BF)
     normed_one = norm_gain(target_float, gain_self).astype(BF)
@@ -267,6 +533,28 @@
     kv = mm(normed_all, w_kv).astype(BF)
     keys, values = kv[:, :inner], kv[:, inner:]
     attended = attend(position1, queries, keys, values, windows, qseg, kseg, True)
+    attended, second_far, second_near_other, third_z, down0 = phase(
+        attended, second_far, second_near_other, third_z, down0
+    )
+
+    third_near = gather_near(links, third_z)
+    down_z = z_steps(links, down0, some) if direct else down0
+    second = assemble(
+        links, second_near, second_far, second_near_other, links.over_core(second_far)
+    )
+    second, third_near, down_z, down0 = phase(second, third_near, down_z, down0)
+
+    w_out, w_cq, w_ckv, w_co = (
+        second[:, :inner],
+        second[:, inner : 2 * inner],
+        second[:, 2 * inner : 4 * inner],
+        second[:, 4 * inner :],
+    )
+
+    third_far = links.over_far(third_near)
+    third_near_other = links.over_core(third_near)
+    if direct:
+        down_z = jnp.stack([down0] + down_z + z_steps(links, down0, rest))
     hidden_one = target_float + mm(attended, w_out)
     normed_two = norm_gain(hidden_one, gain_cross).astype(BF)
     cross_queries = mm(normed_two, w_cq).astype(BF)
@@ -277,77 +565,145 @@
     )
     hidden_two = hidden_one + mm(cross_attended, w_co)
     normed_three = norm_gain(hidden_two, gain_ffn).astype(BF)
+    normed_three, third_far, third_near_other, down_z = phase(
+        normed_three, third_far, third_near_other, down_z
+    )
+
+    down_near = gather_near(links, down_z) if direct else down_z
+    third = assemble(links, third_near, third_far, third_near_other, links.over_core(third_far))
+    third, down_near = phase(third, down_near)
+
+    down_far = links.over_far(down_near) if direct else down_near
+    down_near_other = links.over_core(down_near) if direct else down_near
     gate_up = mm(normed_three, third)
     inner_act, gated_pull = jax.vjp(gated_unit, gate_up[:, :hidden], gate_up[:, hidden:])
     inner_low = inner_act.astype(BF)
+    inner_low, down_far, down_near_other = phase(inner_low, down_far, down_near_other)
+    if direct:
+        down = assemble(links, down_near, down_far, down_near_other, links.over_core(down_far))
+    else:
+        down = down_near
+
+    cot = cotangent[0]
+    grad_gate, grad_up = gated_pull(mm(cot, down, NT))
+    grad_gate, grad_up = grad_gate.astype(BF), grad_up.astype(BF)
+    ffn_terms = [(normed_three, grad_gate, normed_three, grad_up)]
+    down_terms = [(inner_low, cot[:, :down_cut], inner_low, cot[:, down_cut:])]
+    ffn_sum, down_sum = Scatter(links), Scatter(links) if direct else PlainScatter()
+    ffn_send = weight_grad(links, 1 - core, ffn_terms)
+    ffn_send, grad_gate, grad_up = phase(ffn_send, grad_gate, grad_up)
+
+    ffn_sum.core(ffn_send)
+    down_send = weight_grad(links, 1 - core, down_terms) if direct else inner_low
     activations = (hidden_two + mm(inner_low, down)).astype(BF)
-
-    cot = cotangent[0]
-    grad_down = mm(inner_low, cot, TN).astype(BF)
-    grad_gate, grad_up = gated_pull(mm(cot, down, NT))
-    grad_gate_up = jnp.concatenate([grad_gate.astype(BF), grad_up.astype(BF)], axis=1)
-    grad_third = mm(normed_three, grad_gate_up, TN).astype(BF)
-    down_out = scatter_all(grad_down)
-    third_out = scatter_all(grad_third)
+    grad_gate_up = jnp.concatenate([grad_gate, grad_up], axis=1)
     through, grad_gain_ffn = norm_back(hidden_two, gain_ffn, mm(grad_gate_up, third, NT))
     grad_hidden_two = cot.astype(F32) + through
-
+    ffn_sum.keep(weight_grad(links, core, ffn_terms))
+    ffn_send = ffn_sum.halve()
+    ffn_send, grad_hidden_two, down_send = phase(ffn_send, grad_hidden_two, down_send)
+
+    ffn_sum.near(ffn_send)
+    down_sum.core(down_send)
+    if direct:
+        down_sum.keep(weight_grad(links, core, down_terms))
+    else:
+        down_sum.keep(mm(inner_low, cot, TN).astype(BF))
     low_two = grad_hidden_two.astype(BF)
     grad_cross_attended = mm(low_two, w_co, NT).astype(BF)
     grad_cq, grad_ck, grad_cv, _ = attend_back(
         position1, cross_queries, cross_keys, cross_values, grad_cross_attended,
         no_windows, qseg, mseg, False,
     )
-    grad_ckv = jnp.concatenate([grad_ck, grad_cv], axis=1)
-    cross_out = scatter_all(
-        jnp.concatenate(
-            [
-                mm(normed_two, grad_cq, TN).astype(BF),
-                mm(memory_all, grad_ckv, TN).astype(BF),
-                mm(cross_attended, low_two, TN).astype(BF),
-            ],
-            axis=1,
-        )
-    )
-    memory_grad = seq_scatter(mm(grad_ckv, w_ckv, NT).reshape(seq_size, enc_rows, width))
+    cross_terms = [
+        (normed_two, grad_cq, cross_attended, low_two),
+        (memory_all, grad_ck, memory_all, grad_cv),
+    ]
+    cross_sum = Scatter(links)
+    cross_send = weight_grad(links, 1 - core, cross_terms)
+    ffn_send, down_send = ffn_sum.halve(), down_sum.halve()
+    ffn_send, down_send, cross_send, grad_cq = phase(ffn_send, down_send, cross_send, grad_cq)
+
+    cross_sum.core(cross_send)
+    ffn_sum.far(ffn_send)
+    down_sum.near(down_send)
     through, grad_gain_cross = norm_back(hidden_one, gain_cross, mm(grad_cq, w_cq, NT))
     grad_hidden_one = grad_hidden_two + through
-
     low_one = grad_hidden_one.astype(BF)
     grad_attended = mm(low_one, w_out, NT).astype(BF)
+    cross_sum.keep(weight_grad(links, core, cross_terms))
+    grad_ckv = jnp.concatenate([grad_ck, grad_cv], axis=1)
+    memory_part = mm(grad_ckv, w_ckv, NT).reshape(seq_size, enc_rows, width)
+    cross_send, ffn_sends, down_send = cross_sum.halve(), ffn_sum.z_sends(), down_sum.halve()
+    grad_attended, cross_send, ffn_sends, down_send, memory_part = phase(
+        grad_attended, cross_send, ffn_sends, down_send, memory_part
+    )
+
+    cross_sum.near(cross_send)
+    ffn_sum.z(ffn_sends)
+    down_sum.far(down_send)
     grad_q, grad_k, grad_v, grad_windows = attend_back(
         position1, queries, keys, values, grad_attended, windows, qseg, kseg, True
     )
     grad_kv = jnp.concatenate([grad_k, grad_v], axis=1)
-    normed_grad = seq_scatter(mm(grad_kv, w_kv, NT).reshape(seq_size, rows, width))
-    normed_grad = normed_grad + mm(grad_q, w_query, NT)
-    through, grad_gain_self = norm_back(target_float, gain_self, normed_grad)
-    target_grad = grad_hidden_one + through
-
+    grad_normed_kv = mm(grad_kv, w_kv, NT)
+    grad_normed_q = mm(grad_q, w_query, NT)
     grad_windows = grad_windows.reshape(heads, rows + length)
     grad_table = lax.dot_general(
         onehot.astype(F32), grad_windows, (((0,), (1,)), ((), ())), precision=lax.Precision.HIGHEST
     )
     grad_table = grad_table.reshape(batch_size, table_rows, seq_size, table_cols)
     grad_table = jnp.transpose(grad_table, (0, 2, 1, 3)).reshape(devices, table_size)
+    unit = lambda values: values * lax.rsqrt(
+        jnp.mean(values * values, axis=-1, keepdims=True) + EPSILON
+    )
+    grad_gain_self = jnp.sum(unit(target_all.astype(F32)) * grad_normed_kv, axis=0) + jnp.sum(
+        unit(target_float) * grad_normed_q, axis=0
+    )
     gain_parts = [g.reshape(devices, weight_rows) for g in (grad_gain_self, grad_gain_cross, grad_gain_ffn)]
     small_grad = jnp.concatenate(gain_parts + [grad_table], axis=1)
     small_grad = jnp.pad(
         small_grad[:, None], ((0, 0), (0, weight_rows - 1), (0, LANES - small_grad.shape[1]))
     ).reshape(devices * weight_rows, LANES)
-    self_out = scatter_all(
-        jnp.concatenate(
-            [
-                mm(normed_one, grad_q, TN).astype(BF),
-                mm(normed_all, grad_kv, TN).astype(BF),
-                mm(attended, low_one, TN).astype(BF),
-                small_grad.astype(BF),
-            ],
-            axis=1,
-        )
-    )
-    cut = lambda packed, i: packed[:, i * inner : (i + 1) * inner]
-    small_out = self_out[0, 4 * inner :]
+    self_terms = [
+        (normed_one, grad_q, attended, low_one),
+        (normed_all, grad_k, normed_all, grad_v),
+    ]
+    self_sum = Scatter(links)
+    self_send = weight_grad(links, 1 - core, self_terms, small_grad)
+    ffn_total, cross_send, down_sends = ffn_sum.own(), cross_sum.halve(), down_sum.z_sends()
+    self_send, ffn_total, cross_send, down_sends, grad_normed_kv = phase(
+        self_send, ffn_total, cross_send, down_sends, grad_normed_kv
+    )
+
+    self_sum.core(self_send)
+    cross_sum.far(cross_send)
+    down_sum.z(down_sends)
+    grad_gate, grad_up = ffn_sum.last(ffn_total)
+    self_sum.keep(weight_grad(links, core, self_terms, small_grad))
+    self_send, cross_sends, down_total = self_sum.halve(), cross_sum.z_sends(), down_sum.own()
+    self_send, cross_sends, down_total, grad_gate, grad_up = phase(
+        self_send, cross_sends, down_total, grad_gate, grad_up
+    )
+
+    self_sum.near(self_send)
+    cross_sum.z(cross_sends)
+    down_left, down_right = down_sum.last(down_total)
+    memory_grad = seq_scatter(memory_part)
+    normed_grad = seq_scatter(grad_normed_kv.reshape(seq_size, rows, width)) + grad_normed_q
+    through, _ = norm_back(target_float, gain_self, normed_grad)
+    target_grad = grad_hidden_one + through
+    self_send, cross_total = self_sum.halve(), cross_sum.own()
+    self_send, cross_total, down_left, down_right = phase(
+        self_send, cross_total, down_left, down_right
+    )
+    self_sum.far(self_send)
+    cross_left, cross_right = cross_sum.last(cross_total)
+    self_sum.z(self_sum.z_sends())
+    self_left, self_right = self_sum.last(self_sum.own())
+    down_out = jnp.concatenate([down_left, down_right], axis=1)
+
+    small_out = self_left[0, 2 * inner :]
     gain_out = [small_out[i * weight_rows : (i + 1) * weight_rows] for i in range(3)]
     table_out = small_out[3 * weight_rows : 3 * weight_rows + table_size]
     return (
@@ -355,19 +711,19 @@
         target_grad[None],
         memory_grad[None],
         gain_out[0],
-        cut(self_out, 0),
-        cut(self_out, 1),
-        cut(self_out, 2),
-        cut(self_out, 3),
+        self_left[:, :inner],
+        self_left[:, inner : 2 * inner],
+        self_right[:, inner : 2 * inner],
+        self_right[:, :inner],
         table_out.reshape(table_rows, table_cols),
         gain_out[1],
-        cut(cross_out, 0),
-        cut(cross_out, 1),
-        cut(cross_out, 2),
-        cut(cross_out, 3),
+        cross_left[:, :inner],
+        cross_left[:, inner:],
+        cross_right[:, inner:],
+        cross_right[:, :inner],
         gain_out[2],
-        third_out[:, :hidden],
-        third_out[:, hidden:],
+        grad_gate,
+        grad_up,
         down_out,
     )
 

time: 946 us -> 556 us (0.59)
  waiting for transfers between devices: 734 us -> 223 us
  starting transfers between devices: 8.47 us -> 62.6 us
  Pallas kernels: 38.1 us -> 91.8 us
  other arithmetic: 21.1 us -> 73.8 us
  matrix products: 88.5 us -> 63.4 us
  between operations: 15.5 us -> 2.9 us
    reduce_scatter x4 -> x0, waiting for transfers between devices: 457 us -> none  [scatter_all(): lax.psum_scatter(grads, AXES, scatter_dimension=0, tiled=True).astype(F32)]
    all_gather x4 -> x0, waiting for transfers between devices: 252 us -> none  [gather_all(): return lax.all_gather(shard, AXES, axis=0, tiled=True)]
    ppermute x3 -> x61, waiting for transfers between devices: 12.2 us -> 218 us  [the longest x58 213 us: move(): return lax.ppermute(value, AXES, pairs)]
    pallas_call x0 -> x12, Pallas kernels: none -> 54.2 us  [the longest x4 28.8 us: assemble(): pl.pallas_call(body, in_specs=[pl.BlockSpec(memory_space=pltpu.SMEM)] + [...]
    ppermute x3 -> x61, starting transfers between devices: 4.48 us -> 58.5 us  [the longest x58 56.8 us: move(): return lax.ppermute(value, AXES, pairs)]
    convert_element_type x2 -> x18, other arithmetic: 2.69 us -> 40 us  [the longest x8 25.5 us: halve(): return self.total(self.rows, self.rows).astype(BF)]
    dot_general x25 -> x17, matrix products: 87.9 us -> 62.1 us  [mm(): return lax.dot_general(left, right, dims, preferred_element_type=F32)]
    concatenate x5 -> x6, other arithmetic: 13.6 us -> 2.48 us  [the longest x1 0.85 us: per_device(): groups = [jnp.concatenate(group, axis=1) for group in groups]]
  transfers between devices with their start and end apart: 17 -> 67, of which waited for: 14 -> 33; matrix products, arithmetic and copies ran while one was open for 13% -> 22% of each run, Pallas kernels for 4% -> 11%
where the time goes in v2:
time: 556 us; the launch traced here: 547 us
  waiting for transfers between devices  223 us (40%)
  Pallas kernels  91.8 us (17%)
  other arithmetic  73.8 us (13%)
  matrix products  63.4 us (11%)
  starting transfers between devices  62.6 us (11%)
  local copies, waits for them, and re-layouts  29.8 us (5%)
    ppermute x58, waiting for transfers between devices, move(): return lax.ppermute(value, AXES, pairs)  213 us
    dot_general x17, matrix products, mm(): return lax.dot_general(left, right, dims, preferred_element_type=F32)  62.1 us
    ppermute x58, starting transfers between devices, move(): return lax.ppermute(value, AXES, pairs)  56.8 us
    pallas_call x4, Pallas kernels, assemble(): pl.pallas_call(body, in_specs=[pl.BlockSpec(memory_space=pltpu.SMEM)] + [...  28.8 us
    convert_element_type x8, other arithmetic, halve(): return self.total(self.rows, self.rows).astype(BF)  25.5 us
    pallas_call x8, Pallas kernels, weight_grad(): pl.pallas_call(body, in_specs=[pl.BlockSpec(memory_space=pltpu.SMEM)] + [...  25.5 us
    pallas_call x2, Pallas kernels, attend_back(): pl.pallas_call(functools.partial(attend_back_body, causal), grid=(inner /...  22.9 us
    unnamed x186, local copies, waits for them, and re-layouts  16.2 us
  transfers between devices with their start and end apart: 67, of which 33 were waited for; matrix products, arithmetic and copies ran while one was open for 22% of the time, Pallas kernels for 11%

profile of v2, /device:TPU:0, one launch (start us, length us, event | category | flops | bytes accessed | tf_op | source)
XLA Modules:
  0.0 546.7 jit_solution(8241360900281269693)
XLA Ops:
  17.8 7.2 %collective-permute-done.3 = bf16[64,1664]{1,0:T(8,128)(2,1)S(1)} collective-permute-done((bf16[64,1664]{1,0:T(8,128)(2,1)}, bf16[64,1664]{1,0:T(8,128)(2,1)S(1)}, u32[]{:S(2)}, u32[]{:S(2)}) %collective-permute-start.3) | collective-permute-done | bytes 213024 | tf_op jit(solution)/shard_map/ppermute | solution.py:218
  43.9 6.1 %collective-permute-done.8 = bf16[4,64,1664]{2,1,0:T(8,128)(2,1)S(1)} collective-permute-done((bf16[4,64,1664]{2,1,0:T(8,128)(2,1)S(1)}, bf16[4,64,1664]{2,1,0:T(8,128)(2,1)S(1)}, u32[]{:S(2)}, u32[]{:S(2)}) %collective-permute-start.8) | collective-permute-done | bytes 852000 | tf_op jit(solution)/shard_map/ppermute | solution.py:218
  56.0 8.0 %collective-permute-done.13 = bf16[64,2560]{1,0:T(8,128)(2,1)S(1)} collective-permute-done((bf16[64,2560]{1,0:T(8,128)(2,1)S(1)}, bf16[64,2560]{1,0:T(8,128)(2,1)S(1)}, u32[]{:S(2)}, u32[]{:S(2)}) %collective-permute-start.13) | collective-permute-done | bytes 327712 | tf_op jit(solution)/shard_map/ppermute | solution.py:218
  64.0 13.4 %collective-permute-done.12 = bf16[64,2560]{1,0:T(8,128)(2,1)S(1)} collective-permute-done((bf16[64,2560]{1,0:T(8,128)(2,1)S(1)}, bf16[64,2560]{1,0:T(8,128)(2,1)S(1)}, u32[]{:S(2)}, u32[]{:S(2)}) %collective-permute-start.12) | collective-permute-done | bytes 327712 | tf_op jit(solution)/shard_map/ppermute | solution.py:218
  88.5 9.4 %collective-permute-done.15 = bf16[4,64,2560]{2,1,0:T(8,128)(2,1)} collective-permute-done((bf16[4,64,2560]{2,1,0:T(8,128)(2,1)}, bf16[4,64,2560]{2,1,0:T(8,128)(2,1)}, u32[]{:S(2)}, u32[]{:S(2)}) %collective-permute-start.15) | collective-permute-done | bytes 1310752 | tf_op jit(solution)/shard_map/ppermute | solution.py:218
  101.5 5.8 %assemble.4 = bf16[1024,3328]{1,0:T(8,128)(2,1)} custom-call(s32[4]{0:T(128)S(1)} %pad_add_fusion.place_ref, bf16[2,4,64,1664]{3,2,1,0:T(8,128)(2,1)S(1)} %pad_maximum_fusion.2.refs_0_, bf16[2,4,64,1664]{3,2,1,0:T(8,128)(2,1)} %collective-permute-done.10.refs_1_, bf16[2,4,64,1664]{3,2,1,0:T(8,128)(2,1)S(1)} %copy-done.27, ...), custom_call_target="tpu_custom_call" | custom-call | tf_op jit(solution)/shard_map/assemble/pallas_call | solution.py:278
  121.3 7.9 %attend_self.1.refs_2_ = bf16[128,1024]{1,0:T(8,128)(2,1)S(1)} custom-call(s32[1]{0:T(128)} %bitcast.1.pos_ref, bf16[128,1024]{1,0:T(8,128)(2,1)S(1)} %fusion.56.q_ref, bf16[512,1024]{1,0:T(8,128)(2,1)S(1)} %get-tuple-element.277.k_ref, bf16[512,1024]{1,0:T(8,128)(2,1)S(1)} %get-tuple-element.276.v_ref, f32[8,2,640]{2,1,0:T(2,128)S(1)} %copy.50.bias_ref, ...), custom_call_target="tpu_custom_call" | custom-call | tf_op jit(solution)/shard_map/attend_self/pallas_call | solution.py:139
  129.2 5.7 %collective-permute-done.19 = bf16[64,2816]{1,0:T(8,128)(2,1)} collective-permute-done((bf16[64,2816]{1,0:T(8,128)(2,1)S(1)}, bf16[64,2816]{1,0:T(8,128)(2,1)}, u32[]{:S(2)}, u32[]{:S(2)}) %collective-permute-start.19) | collective-permute-done | bytes 360480 | tf_op jit(solution)/shard_map/ppermute | solution.py:218
  141.1 17.3 %collective-permute-done.22 = bf16[4,64,2816]{2,1,0:T(8,128)(2,1)S(1)} collective-permute-done((bf16[4,64,2816]{2,1,0:T(8,128)(2,1)S(1)}, bf16[4,64,2816]{2,1,0:T(8,128)(2,1)S(1)}, u32[]{:S(2)}, u32[]{:S(2)}) %collective-permute-start.22) | collective-permute-done | bytes 1441824 | tf_op jit(solution)/shard_map/ppermute | solution.py:218
  161.9 8.7 %assemble.5 = bf16[1024,5120]{1,0:T(8,128)(2,1)} custom-call(s32[4]{0:T(128)S(1)} %pad_add_fusion.place_ref, bf16[2,4,64,2560]{3,2,1,0:T(8,128)(2,1)} %pad_maximum_fusion.1.refs_0_, bf16[2,4,64,2560]{3,2,1,0:T(8,128)(2,1)} %collective-permute-done.17.refs_1_, bf16[2,4,64,2560]{3,2,1,0:T(8,128)(2,1)} %collective-permute-done.18.refs_2_, ...), custom_call_target="tpu_custom_call" | custom-call | tf_op jit(solution)/shard_map/assemble/pallas_call | solution.py:278
  182.5 6.9 %attend_cross.1.refs_2_ = bf16[128,1024]{1,0:T(8,128)(2,1)S(1)} custom-call(s32[1]{0:T(128)} %bitcast.1.pos_ref, bf16[128,1024]{1,0:T(8,128)(2,1)S(1)} %fusion.62.q_ref, bf16[256,1024]{1,0:T(8,128)(2,1)S(1)} %get-tuple-element.284.k_ref, bf16[256,1024]{1,0:T(8,128)(2,1)S(1)} %get-tuple-element.283.v_ref, f32[8,2,128]{2,1,0:T(2,128)S(1)} %broadcast_in_dim.67.bias_ref, ...), custom_call_target="tpu_custom_call" | custom-call | tf_op jit(solution)/shard_map/attend_cross/pallas_call | solution.py:139
  193.0 12.6 %collective-permute-done.24.refs_1_ = bf16[2,4,64,2816]{3,2,1,0:T(8,128)(2,1)} collective-permute-done((bf16[2,4,64,2816]{3,2,1,0:T(8,128)(2,1)}, bf16[2,4,64,2816]{3,2,1,0:T(8,128)(2,1)}, u32[]{:S(2)}, u32[]{:S(2)}) %collective-permute-start.24) | collective-permute-done | bytes 2883616 | tf_op jit(solution)/shard_map/ppermute | solution.py:218
  206.1 10.8 %collective-permute-done.29 = bf16[4,176,512]{2,1,0:T(8,128)(2,1)S(1)} collective-permute-done((bf16[4,176,512]{2,1,0:T(8,128)(2,1)S(1)}, bf16[4,176,512]{2,1,0:T(8,128)(2,1)S(1)}, u32[]{:S(2)}, u32[]{:S(2)}) %collective-permute-start.29) | collective-permute-done | bytes 720928 | tf_op jit(solution)/shard_map/ppermute | solution.py:218
  218.7 9.0 %assemble.6 = bf16[1024,5632]{1,0:T(8,128)(2,1)} custom-call(s32[4]{0:T(128)S(1)} %pad_add_fusion.place_ref, bf16[2,4,64,2816]{3,2,1,0:T(8,128)(2,1)} %pad_maximum_fusion.refs_0_, bf16[2,4,64,2816]{3,2,1,0:T(8,128)(2,1)} %collective-permute-done.24.refs_1_, bf16[2,4,64,2816]{3,2,1,0:T(8,128)(2,1)} %collective-permute-done.25.refs_2_, ...), custom_call_target="tpu_custom_call" | custom-call | tf_op jit(solution)/shard_map/assemble/pallas_call | solution.py:278
  229.2 6.0 %fusion.143 = f32[128,5632]{1,0:T(8,128)S(1)} fusion(bf16[128,1024]{1,0:T(8,128)(2,1)S(1)} %multiply_convert_fusion.2.refs_0_.refs_2_, bf16[1024,5632]{1,0:T(8,128)(2,1)} %assemble.6), kind=kOutput, calls=%fused_computation.254 | convolution fusion | flops 1476395008 | bytes 14680064 | tf_op jit(solution)/shard_map/dot_general | solution.py:24
  237.2 9.8 %collective-permute-done.30.refs_1_ = bf16[2,4,176,512]{3,2,1,0:T(8,128)(2,1)} collective-permute-done((bf16[2,4,176,512]{3,2,1,0:T(8,128)(2,1)S(1)}, bf16[2,4,176,512]{3,2,1,0:T(8,128)(2,1)}, u32[]{:S(2)}, u32[]{:S(2)}) %collective-permute-start.30) | collective-permute-done | bytes 1441824 | tf_op jit(solution)/shard_map/ppermute | solution.py:218
  253.3 5.3 assemble.7
  258.6 5.4 multiply_convert_fusion
  274.6 8.3 %multiply_reduce_fusion = (f32[1024]{0:T(1024)S(1)}, f32[128]{0:T(128)S(1)}, f32[128,1024]{1,0:T(8,128)S(1)}) fusion(f32[128,1024]{1,0:T(8,128)S(1)} %copy-done.50, f32[128]{0:T(128)S(1)} %fusion.127, f32[1024]{0:T(1024)S(1)} %mul.285, bf16[1024,5632]{1,0:T(8,128)(2,1)} %assemble.6, bf16[128,2816]{1,0:T(8,128)(2,1)S(1)} %get-tuple-element.214.refs_3_, ...), kind=kOutput, calls=%fused_computation.125 | convolution fusion | flops 1480063872 | bytes 14033920 | tf_op jit(solution)/shard_map/dot_general | solution.py:24
  294.1 8.8 %attend_cross_back.1 = (bf16[128,1024]{1,0:T(8,128)(2,1)S(1)}, bf16[256,1024]{1,0:T(8,128)(2,1)S(1)}, bf16[256,1024]{1,0:T(8,128)(2,1)S(1)}, f32[8,2,128]{2,1,0:T(2,128)}) custom-call(s32[1]{0:T(128)} %bitcast.1.pos_ref, bf16[128,1024]{1,0:T(8,128)(2,1)S(1)} %copy-done.36, bf16[256,1024]{1,0:T(8,128)(2,1)S(1)} %copy-done.10, ...), custom_call_target="tpu_custom_call" | custom-call | tf_op jit(solution)/shard_map/attend_cross_back/pallas_call | solution.py:154
  306.1 16.0 %collective-permute-done.34 = bf16[512,2816]{1,0:T(8,128)(2,1)} collective-permute-done((bf16[512,2816]{1,0:T(8,128)(2,1)}, bf16[512,2816]{1,0:T(8,128)(2,1)}, u32[]{:S(2)}, u32[]{:S(2)}) %collective-permute-start.34) | collective-permute-done | bytes 2883616 | tf_op jit(solution)/shard_map/ppermute | solution.py:218
  347.0 16.5 %collective-permute-done.38 = bf16[1408,512]{1,0:T(8,128)(2,1)} collective-permute-done((bf16[1408,512]{1,0:T(8,128)(2,1)}, bf16[1408,512]{1,0:T(8,128)(2,1)}, u32[]{:S(2)}, u32[]{:S(2)}) %collective-permute-start.38) | collective-permute-done | bytes 1441824 | tf_op jit(solution)/shard_map/ppermute | solution.py:218
  373.9 14.0 %attend_self_back.1 = (bf16[128,1024]{1,0:T(8,128)(2,1)S(1)}, bf16[512,1024]{1,0:T(8,128)(2,1)S(1)}, bf16[512,1024]{1,0:T(8,128)(2,1)S(1)}, f32[8,2,640]{2,1,0:T(2,128)S(1)}) custom-call(s32[1]{0:T(128)} %bitcast.1.pos_ref, bf16[128,1024]{1,0:T(8,128)(2,1)S(1)} %copy-done.31, bf16[512,1024]{1,0:T(8,128)(2,1)S(1)} %copy-done.6, ...), custom_call_target="tpu_custom_call" | custom-call | tf_op jit(solution)/shard_map/attend_self_back/pallas_call | solution.py:154
  395.8 6.6 %fusion.17 = (f32[1024]{0:T(1024)S(1)}, f32[512,1024]{1,0:T(8,128)}) fusion(bf16[512,1024]{1,0:T(8,128)(2,1)} %bitcast.163, f32[512]{0:T(512)S(1)} %add_rsqrt_fusion, bf16[1024,3328]{1,0:T(8,128)(2,1)} %assemble.4, bf16[512,1024]{1,0:T(8,128)(2,1)} %copy-done.11, bf16[512,1024]{1,0:T(8,128)(2,1)S(1)} %get-tuple-element.227.refs_5_), kind=kOutput, calls=%fused_computation.25 | convolution fusion | flops 2153774080 | bytes 9443328 | tf_op jit(solution)/shard_map/dot_general | solution.py:24
  414.3 5.0 collective-permute-done.40
  452.0 5.3 collective-permute-done.51
  469.8 7.2 %collective-permute-done.57 = bf16[64,2048]{1,0:T(8,128)(2,1)S(1)} collective-permute-done((bf16[64,2048]{1,0:T(8,128)(2,1)}, bf16[64,2048]{1,0:T(8,128)(2,1)S(1)}, u32[]{:S(2)}, u32[]{:S(2)}) %collective-permute-start.57) | collective-permute-done | bytes 262176 | tf_op jit(solution)/shard_map/ppermute | solution.py:218
  477.4 10.3 %collective-permute-done.58 = bf16[64,2048]{1,0:T(8,128)(2,1)S(1)} collective-permute-done((bf16[64,2048]{1,0:T(8,128)(2,1)}, bf16[64,2048]{1,0:T(8,128)(2,1)S(1)}, u32[]{:S(2)}, u32[]{:S(2)}) %collective-permute-start.58) | collective-permute-done | bytes 262176 | tf_op jit(solution)/shard_map/ppermute | solution.py:218
  500.3 4.9 collective-permute-done.45
  506.6 10.6 %collective-permute-done.61 = bf16[256,2176]{1,0:T(8,128)(2,1)S(1)} collective-permute-done((bf16[256,2176]{1,0:T(8,128)(2,1)S(1)}, bf16[256,2176]{1,0:T(8,128)(2,1)S(1)}, u32[]{:S(2)}, u32[]{:S(2)}) %collective-permute-start.61) | collective-permute-done | bytes 1114144 | tf_op jit(solution)/shard_map/ppermute | solution.py:218
  524.3 5.0 collective-permute-done.62
  532.5 8.6 %collective-permute-done.63 = bf16[64,2176]{1,0:T(8,128)(2,1)S(1)} collective-permute-done((bf16[64,2176]{1,0:T(8,128)(2,1)S(1)}, bf16[64,2176]{1,0:T(8,128)(2,1)S(1)}, u32[]{:S(2)}, u32[]{:S(2)}) %collective-permute-start.63) | collective-permute-done | bytes 278560 | tf_op jit(solution)/shard_map/ppermute | solution.py:218
  (442 shorter events, 261.5 us)
Async XLA Ops:
  50.2 28.5 %collective-permute-start.11 = (bf16[2,4,64,1664]{3,2,1,0:T(8,128)(2,1)S(1)}, bf16[2,4,64,1664]{3,2,1,0:T(8,128)(2,1)S(1)}, u32[]{:S(2)}, u32[]{:S(2)}) collective-permute-start(bf16[2,4,64,1664]{3,2,1,0:T(8,128)(2,1)S(1)} %pad_maximum_fusion.2.refs_0_), channel_id=1, source_target_pairs={{0,1},{1,0},{2,3},{3,2},{4,5},{5,4},{6,7},{7,6},{8,9},{9,8},{10,11... | collective-permute-start | bytes 5111816 | tf_op jit(solution)/shard_map/ppermute | solution.py:218
  50.2 29.7 %collective-permute-start.10 = (bf16[2,4,64,1664]{3,2,1,0:T(8,128)(2,1)S(1)}, bf16[2,4,64,1664]{3,2,1,0:T(8,128)(2,1)}, u32[]{:S(2)}, u32[]{:S(2)}) collective-permute-start(bf16[2,4,64,1664]{3,2,1,0:T(8,128)(2,1)S(1)} %pad_maximum_fusion.2.refs_0_), channel_id=1, source_target_pairs={{0,2},{1,5},{2,0},{3,7},{4,6},{5,1},{6,4},{7,3},{8,10},{9,13},{10,... | collective-permute-start | bytes 5111816 | tf_op jit(solution)/shard_map/ppermute | solution.py:218
  52.7 24.8 %collective-permute-start.12 = (bf16[64,2560]{1,0:T(8,128)(2,1)S(1)}, bf16[64,2560]{1,0:T(8,128)(2,1)S(1)}, u32[]{:S(2)}, u32[]{:S(2)}) collective-permute-start(bf16[64,2560]{1,0:T(8,128)(2,1)S(1)} %slice.481), channel_id=1, source_target_pairs={{0,16},{1,17},{2,18},{3,19},{4,20},{5,21},{6,22},{7,23},{8,24},{9,... | collective-permute-start | bytes 983048 | tf_op jit(solution)/shard_map/ppermute | solution.py:218
  80.5 21.0 %collective-permute-start.14 = (bf16[2,4,64,1664]{3,2,1,0:T(8,128)(2,1)}, bf16[2,4,64,1664]{3,2,1,0:T(8,128)(2,1)}, u32[]{:S(2)}, u32[]{:S(2)}) collective-permute-start(bf16[2,4,64,1664]{3,2,1,0:T(8,128)(2,1)} %collective-permute-done.10.refs_1_), channel_id=1, source_target_pairs={{0,1},{1,0},{2,3},{3,2},{4,5},{5,4},{6,7},{7,6},{8,9},{9,8},{10,11... | collective-permute-start | bytes 5111816 | tf_op jit(solution)/shard_map/ppermute | solution.py:218
  87.4 19.9 %collective-permute-start.16 = (bf16[64,2816]{1,0:T(8,128)(2,1)S(1)}, bf16[64,2816]{1,0:T(8,128)(2,1)S(1)}, u32[]{:S(2)}, u32[]{:S(2)}) collective-permute-start(bf16[64,2816]{1,0:T(8,128)(2,1)S(1)} %slice.482), channel_id=1, source_target_pairs={{0,24},{1,25},{2,26},{3,27},{4,28},{5,29},{6,30},{7,31},{8,0},{9,1... | collective-permute-start | bytes 1081352 | tf_op jit(solution)/shard_map/ppermute | solution.py:218
  107.3 28.9 %collective-permute-start.18 = (bf16[2,4,64,2560]{3,2,1,0:T(8,128)(2,1)}, bf16[2,4,64,2560]{3,2,1,0:T(8,128)(2,1)}, u32[]{:S(2)}, u32[]{:S(2)}) collective-permute-start(bf16[2,4,64,2560]{3,2,1,0:T(8,128)(2,1)} %pad_maximum_fusion.1.refs_0_), channel_id=1, source_target_pairs={{0,1},{1,0},{2,3},{3,2},{4,5},{5,4},{6,7},{7,6},{8,9},{9,8},{10,11... | collective-permute-start | bytes 7864328 | tf_op jit(solution)/shard_map/ppermute | solution.py:218
  107.4 32.0 %collective-permute-start.17 = (bf16[2,4,64,2560]{3,2,1,0:T(8,128)(2,1)}, bf16[2,4,64,2560]{3,2,1,0:T(8,128)(2,1)}, u32[]{:S(2)}, u32[]{:S(2)}) collective-permute-start(bf16[2,4,64,2560]{3,2,1,0:T(8,128)(2,1)} %pad_maximum_fusion.1.refs_0_), channel_id=1, source_target_pairs={{0,2},{1,5},{2,0},{3,7},{4,6},{5,1},{6,4},{7,3},{8,10},{9,13},{10,... | collective-permute-start | bytes 7864328 | tf_op jit(solution)/shard_map/ppermute | solution.py:218
  108.8 20.4 %collective-permute-start.20 = (bf16[64,2816]{1,0:T(8,128)(2,1)S(1)}, bf16[64,2816]{1,0:T(8,128)(2,1)}, u32[]{:S(2)}, u32[]{:S(2)}) collective-permute-start(bf16[64,2816]{1,0:T(8,128)(2,1)S(1)} %slice.482), channel_id=1, source_target_pairs={{0,8},{1,9},{2,10},{3,11},{4,12},{5,13},{6,14},{7,15},{8,16},{9,17... | collective-permute-start | bytes 1081352 | tf_op jit(solution)/shard_map/ppermute | solution.py:218
  108.8 26.1 %collective-permute-start.19 = (bf16[64,2816]{1,0:T(8,128)(2,1)S(1)}, bf16[64,2816]{1,0:T(8,128)(2,1)}, u32[]{:S(2)}, u32[]{:S(2)}) collective-permute-start(bf16[64,2816]{1,0:T(8,128)(2,1)S(1)} %slice.482), channel_id=1, source_target_pairs={{0,16},{1,17},{2,18},{3,19},{4,20},{5,21},{6,22},{7,23},{8,24},{9,... | collective-permute-start | bytes 1081352 | tf_op jit(solution)/shard_map/ppermute | solution.py:218
  139.4 20.9 %collective-permute-start.21 = (bf16[2,4,64,2560]{3,2,1,0:T(8,128)(2,1)}, bf16[2,4,64,2560]{3,2,1,0:T(8,128)(2,1)S(1)}, u32[]{:S(2)}, u32[]{:S(2)}) collective-permute-start(bf16[2,4,64,2560]{3,2,1,0:T(8,128)(2,1)} %collective-permute-done.17.refs_1_), channel_id=1, source_target_pairs={{0,1},{1,0},{2,3},{3,2},{4,5},{5,4},{6,7},{7,6},{8,9},{9,8},{10,11... | collective-permute-start | bytes 7864328 | tf_op jit(solution)/shard_map/ppermute | solution.py:218
  140.0 30.6 %collective-permute-start.23 = (bf16[176,512]{1,0:T(8,128)(2,1)}, bf16[176,512]{1,0:T(8,128)(2,1)S(1)}, u32[]{:S(2)}, u32[]{:S(2)}) collective-permute-start(bf16[176,512]{1,0:T(8,128)(2,1)} %pad_maximum_fusion.12), channel_id=1, source_target_pairs={{0,24},{1,25},{2,26},{3,27},{4,28},{5,29},{6,30},{7,31},{8,0},{9,1... | collective-permute-start | bytes 540680 | tf_op jit(solution)/shard_map/ppermute | solution.py:218
  170.6 22.4 %collective-permute-start.25 = (bf16[2,4,64,2816]{3,2,1,0:T(8,128)(2,1)}, bf16[2,4,64,2816]{3,2,1,0:T(8,128)(2,1)}, u32[]{:S(2)}, u32[]{:S(2)}) collective-permute-start(bf16[2,4,64,2816]{3,2,1,0:T(8,128)(2,1)} %pad_maximum_fusion.refs_0_), channel_id=1, source_target_pairs={{0,1},{1,0},{2,3},{3,2},{4,5},{5,4},{6,7},{7,6},{8,9},{9,8},{10,11... | collective-permute-start | bytes 8650760 | tf_op jit(solution)/shard_map/ppermute | solution.py:218
  170.7 34.8 %collective-permute-start.24 = (bf16[2,4,64,2816]{3,2,1,0:T(8,128)(2,1)}, bf16[2,4,64,2816]{3,2,1,0:T(8,128)(2,1)}, u32[]{:S(2)}, u32[]{:S(2)}) collective-permute-start(bf16[2,4,64,2816]{3,2,1,0:T(8,128)(2,1)} %pad_maximum_fusion.refs_0_), channel_id=1, source_target_pairs={{0,2},{1,5},{2,0},{3,7},{4,6},{5,1},{6,4},{7,3},{8,10},{9,13},{10,... | collective-permute-start | bytes 8650760 | tf_op jit(solution)/shard_map/ppermute | solution.py:218
  172.2 19.7 %collective-permute-start.27 = (bf16[176,512]{1,0:T(8,128)(2,1)}, bf16[176,512]{1,0:T(8,128)(2,1)S(1)}, u32[]{:S(2)}, u32[]{:S(2)}) collective-permute-start(bf16[176,512]{1,0:T(8,128)(2,1)} %pad_maximum_fusion.12), channel_id=1, source_target_pairs={{0,8},{1,9},{2,10},{3,11},{4,12},{5,13},{6,14},{7,15},{8,16},{9,17... | collective-permute-start | bytes 540680 | tf_op jit(solution)/shard_map/ppermute | solution.py:218
  172.7 19.2 %collective-permute-start.26 = (bf16[176,512]{1,0:T(8,128)(2,1)}, bf16[176,512]{1,0:T(8,128)(2,1)S(1)}, u32[]{:S(2)}, u32[]{:S(2)}) collective-permute-start(bf16[176,512]{1,0:T(8,128)(2,1)} %pad_maximum_fusion.12), channel_id=1, source_target_pairs={{0,16},{1,17},{2,18},{3,19},{4,20},{5,21},{6,22},{7,23},{8,24},{9,... | collective-permute-start | bytes 540680 | tf_op jit(solution)/shard_map/ppermute | solution.py:218
  227.8 19.2 %collective-permute-start.30 = (bf16[2,4,176,512]{3,2,1,0:T(8,128)(2,1)S(1)}, bf16[2,4,176,512]{3,2,1,0:T(8,128)(2,1)}, u32[]{:S(2)}, u32[]{:S(2)}) collective-permute-start(bf16[2,4,176,512]{3,2,1,0:T(8,128)(2,1)S(1)} %pad_maximum_fusion.4.refs_0_), channel_id=1, source_target_pairs={{0,2},{1,5},{2,0},{3,7},{4,6},{5,1},{6,4},{7,3},{8,10},{9,13},{10,... | collective-permute-start | bytes 4325384 | tf_op jit(solution)/shard_map/ppermute | solution.py:218
  287.3 34.8 %collective-permute-start.34 = (bf16[512,2816]{1,0:T(8,128)(2,1)}, bf16[512,2816]{1,0:T(8,128)(2,1)}, u32[]{:S(2)}, u32[]{:S(2)}) collective-permute-start(bf16[512,2816]{1,0:T(8,128)(2,1)} %add_convert_fusion), channel_id=1, source_target_pairs={{0,4},{1,3},{2,6},{3,1},{4,0},{5,7},{6,2},{7,5},{8,12},{9,11},{10,... | collective-permute-start | bytes 8650760 | tf_op jit(solution)/shard_map/ppermute | solution.py:218
  287.8 38.1 %collective-permute-start.35 = (bf16[2816,512]{1,0:T(8,128)(2,1)S(1)}, bf16[2816,512]{1,0:T(8,128)(2,1)}, u32[]{:S(2)}, u32[]{:S(2)}) collective-permute-start(bf16[2816,512]{1,0:T(8,128)(2,1)S(1)} %weight_grad.10), channel_id=1, source_target_pairs={{0,1},{1,0},{2,3},{3,2},{4,5},{5,4},{6,7},{7,6},{8,9},{9,8},{10,11... | collective-permute-start | bytes 8650760 | tf_op jit(solution)/shard_map/ppermute | solution.py:218
  329.0 40.9 %collective-permute-start.36 = (bf16[1024,2048]{1,0:T(8,128)(2,1)}, bf16[1024,2048]{1,0:T(8,128)(2,1)}, u32[]{:S(2)}, u32[]{:S(2)}) collective-permute-start(bf16[1024,2048]{1,0:T(8,128)(2,1)} %weight_grad.12), channel_id=1, source_target_pairs={{0,1},{1,0},{2,3},{3,2},{4,5},{5,4},{6,7},{7,6},{8,9},{9,8},{10,11... | collective-permute-start | bytes 12582920 | tf_op jit(solution)/shard_map/ppermute | solution.py:218
  329.1 37.0 %collective-permute-start.37 = (bf16[256,2816]{1,0:T(8,128)(2,1)}, bf16[256,2816]{1,0:T(8,128)(2,1)}, u32[]{:S(2)}, u32[]{:S(2)}) collective-permute-start(bf16[256,2816]{1,0:T(8,128)(2,1)} %add_convert_fusion.4), channel_id=1, source_target_pairs={{0,2},{1,5},{2,0},{3,7},{4,6},{5,1},{6,4},{7,3},{8,10},{9,13},{10,... | collective-permute-start | bytes 4325384 | tf_op jit(solution)/shard_map/ppermute | solution.py:218
  330.5 33.0 %collective-permute-start.38 = (bf16[1408,512]{1,0:T(8,128)(2,1)}, bf16[1408,512]{1,0:T(8,128)(2,1)}, u32[]{:S(2)}, u32[]{:S(2)}) collective-permute-start(bf16[1408,512]{1,0:T(8,128)(2,1)} %add_convert_fusion.3), channel_id=1, source_target_pairs={{0,4},{1,3},{2,6},{3,1},{4,0},{5,7},{6,2},{7,5},{8,12},{9,11},{10,... | collective-permute-start | bytes 4325384 | tf_op jit(solution)/shard_map/ppermute | solution.py:218
  391.2 23.1 %collective-permute-start.39 = (bf16[64,2816]{1,0:T(8,128)(2,1)}, bf16[64,2816]{1,0:T(8,128)(2,1)}, u32[]{:S(2)}, u32[]{:S(2)}) collective-permute-start(bf16[64,2816]{1,0:T(8,128)(2,1)} %get-tuple-element.230), channel_id=1, source_target_pairs={{0,8},{1,9},{2,10},{3,11},{4,12},{5,13},{6,14},{7,15},{8,16},{9,17... | collective-permute-start | bytes 1081352 | tf_op jit(solution)/shard_map/ppermute | solution.py:218
  391.3 28.0 %collective-permute-start.40 = (bf16[64,2816]{1,0:T(8,128)(2,1)}, bf16[64,2816]{1,0:T(8,128)(2,1)}, u32[]{:S(2)}, u32[]{:S(2)}) collective-permute-start(bf16[64,2816]{1,0:T(8,128)(2,1)} %get-tuple-element.231), channel_id=1, source_target_pairs={{0,16},{1,17},{2,18},{3,19},{4,20},{5,21},{6,22},{7,23},{8,24},{9,... | collective-permute-start | bytes 1081352 | tf_op jit(solution)/shard_map/ppermute | solution.py:218
  393.0 26.3 %collective-permute-start.41 = (bf16[64,2816]{1,0:T(8,128)(2,1)}, bf16[64,2816]{1,0:T(8,128)(2,1)}, u32[]{:S(2)}, u32[]{:S(2)}) collective-permute-start(bf16[64,2816]{1,0:T(8,128)(2,1)} %get-tuple-element.232), channel_id=1, source_target_pairs={{0,24},{1,25},{2,26},{3,27},{4,28},{5,29},{6,30},{7,31},{8,0},{9,1... | collective-permute-start | bytes 1081352 | tf_op jit(solution)/shard_map/ppermute | solution.py:218
  395.3 34.1 %collective-permute-start.42 = (bf16[512,2048]{1,0:T(8,128)(2,1)}, bf16[512,2048]{1,0:T(8,128)(2,1)}, u32[]{:S(2)}, u32[]{:S(2)}) collective-permute-start(bf16[512,2048]{1,0:T(8,128)(2,1)} %add_convert_fusion.2), channel_id=1, source_target_pairs={{0,4},{1,3},{2,6},{3,1},{4,0},{5,7},{6,2},{7,5},{8,12},{9,11},{10,... | collective-permute-start | bytes 6291464 | tf_op jit(solution)/shard_map/ppermute | solution.py:218
  405.9 19.4 %collective-permute-start.43 = (bf16[704,512]{1,0:T(8,128)(2,1)}, bf16[704,512]{1,0:T(8,128)(2,1)S(1)}, u32[]{:S(2)}, u32[]{:S(2)}) collective-permute-start(bf16[704,512]{1,0:T(8,128)(2,1)} %add_convert_fusion.7), channel_id=1, source_target_pairs={{0,2},{1,5},{2,0},{3,7},{4,6},{5,1},{6,4},{7,3},{8,10},{9,13},{10,... | collective-permute-start | bytes 2162696 | tf_op jit(solution)/shard_map/ppermute | solution.py:218
  432.8 27.7 %collective-permute-start.50 = (bf16[1024,2176]{1,0:T(8,128)(2,1)S(1)}, bf16[1024,2176]{1,0:T(8,128)(2,1)S(1)}, u32[]{:S(2)}, u32[]{:S(2)}) collective-permute-start(bf16[1024,2176]{1,0:T(8,128)(2,1)S(1)} %copy-done.56), channel_id=1, source_target_pairs={{0,1},{1,0},{2,3},{3,2},{4,5},{5,4},{6,7},{7,6},{8,9},{9,8},{10,11... | collective-permute-start | bytes 13369352 | tf_op jit(solution)/shard_map/ppermute | solution.py:218
  463.4 27.8 %collective-permute-start.56 = (bf16[512,2176]{1,0:T(8,128)(2,1)}, bf16[512,2176]{1,0:T(8,128)(2,1)}, u32[]{:S(2)}, u32[]{:S(2)}) collective-permute-start(bf16[512,2176]{1,0:T(8,128)(2,1)} %add_convert_fusion.1), channel_id=1, source_target_pairs={{0,4},{1,3},{2,6},{3,1},{4,0},{5,7},{6,2},{7,5},{8,12},{9,11},{10,... | collective-permute-start | bytes 6684680 | tf_op jit(solution)/shard_map/ppermute | solution.py:218
  466.1 21.5 %collective-permute-start.58 = (bf16[64,2048]{1,0:T(8,128)(2,1)}, bf16[64,2048]{1,0:T(8,128)(2,1)S(1)}, u32[]{:S(2)}, u32[]{:S(2)}) collective-permute-start(bf16[64,2048]{1,0:T(8,128)(2,1)} %get-tuple-element.245), channel_id=1, source_target_pairs={{0,16},{1,17},{2,18},{3,19},{4,20},{5,21},{6,22},{7,23},{8,24},{9,... | collective-permute-start | bytes 786440 | tf_op jit(solution)/shard_map/ppermute | solution.py:218
  467.1 22.0 %collective-permute-start.59 = (bf16[64,2048]{1,0:T(8,128)(2,1)}, bf16[64,2048]{1,0:T(8,128)(2,1)S(1)}, u32[]{:S(2)}, u32[]{:S(2)}) collective-permute-start(bf16[64,2048]{1,0:T(8,128)(2,1)} %get-tuple-element.246), channel_id=1, source_target_pairs={{0,24},{1,25},{2,26},{3,27},{4,28},{5,29},{6,30},{7,31},{8,0},{9,1... | collective-permute-start | bytes 786440 | tf_op jit(solution)/shard_map/ppermute | solution.py:218
  469.6 25.0 %collective-permute-start.47 = (bf16[64,1024]{1,0:T(8,128)(2,1)S(1)}, bf16[64,1024]{1,0:T(8,128)(2,1)S(1)}, u32[]{:S(2)}, u32[]{:S(2)}) collective-permute-start(bf16[64,1024]{1,0:T(8,128)(2,1)S(1)} %get-tuple-element.293), channel_id=1, source_target_pairs={{0,1},{1,2},{2,3},{3,0},{4,5},{5,6},{6,7},{7,4},{8,9},{9,10},{10,1... | collective-permute-start | bytes 393224 | tf_op jit(solution)/shard_map/ppermute | solution.py:190
  495.3 21.9 %collective-permute-start.61 = (bf16[256,2176]{1,0:T(8,128)(2,1)S(1)}, bf16[256,2176]{1,0:T(8,128)(2,1)S(1)}, u32[]{:S(2)}, u32[]{:S(2)}) collective-permute-start(bf16[256,2176]{1,0:T(8,128)(2,1)S(1)} %add_convert_fusion.5), channel_id=1, source_target_pairs={{0,2},{1,5},{2,0},{3,7},{4,6},{5,1},{6,4},{7,3},{8,10},{9,13},{10,... | collective-permute-start | bytes 3342344 | tf_op jit(solution)/shard_map/ppermute | solution.py:218
  (127 other events, 1238.7 us)

commit v3 on v2

v3 whole, which is shorter than its diff:
```python
import functools

import jax
import jax.numpy as jnp
import numpy as np
from jax import lax
from jax.experimental import pallas as pl
from jax.experimental.pallas import tpu as pltpu
from jax.sharding import PartitionSpec as P

HD = 64
LANES = 128
SUBLANES = 8
EPSILON = 1e-06
MASKED = -1e30
BF = jnp.bfloat16
F32 = jnp.float32
AXES = ("batch", "seq")
NT = (((1,), (1,)), ((), ()))
TN = (((0,), (0,)), ((), ()))
NN = (((1,), (0,)), ((), ()))


def mm(left, right, dims=NN):
    return lax.dot_general(left, right, dims, preferred_element_type=F32)


def gated_unit(gate_act, up_act):
    return jax.nn.gelu(gate_act, approximate=True) * up_act


def head_only(pair, head):
    lane = lax.broadcasted_iota(jnp.int32, pair.shape, 1)
    return jnp.where((lane // HD) == head, pair, jnp.zeros_like(pair))


def pick_heads(first, second):
    lane = lax.broadcasted_iota(jnp.int32, first.shape, 1)
    return jnp.where(lane < HD, first, second)


def spread(window, rows):
    wide = jnp.broadcast_to(window, (rows, window.shape[1]))
    rolled = pltpu.roll(wide, 0, 1, stride=1, stride_axis=0)
    return rolled[:, rows:]


def unspread(grads, rows):
    wide = jnp.concatenate([jnp.zeros((rows, rows), F32), grads], axis=1)
    width = wide.shape[1]
    total = wide[:SUBLANES]
    for start in range(SUBLANES, rows, SUBLANES):
        total = total + pltpu.roll(wide[start : start + SUBLANES], width - start, 1)
    row = lax.broadcasted_iota(jnp.int32, total.shape, 0)
    for bit in (1, 2, 4):
        total = jnp.where((row & bit) != 0, pltpu.roll(total, width - bit, 1), total)
    return jnp.sum(total, axis=0, keepdims=True)


def allowed_pairs(position, query_segments, key_segments, causal):
    rows, keys = query_segments.shape[0], key_segments.shape[1]
    allowed = query_segments == key_segments
    if causal:
        own = lax.broadcasted_iota(jnp.int32, (rows, keys), 0) + position
        other = lax.broadcasted_iota(jnp.int32, (rows, keys), 1)
        allowed = allowed & (own >= other)
    return allowed


def pair_probs(query, key, bias_ref, allowed, head, causal):
    scores = mm(head_only(query, head), key, NT)
    if causal:
        scores = scores + spread(bias_ref[0, head : head + 1, :], query.shape[0])
    scores = jnp.where(allowed, scores, MASKED)
    top = jnp.max(scores, axis=1, keepdims=True)
    grown = jnp.exp(scores - top)
    return grown / jnp.sum(grown, axis=1, keepdims=True)


def attend_pair(query, key, value, bias_ref, allowed, causal):
    parts = []
    for head in range(2):
        probs = pair_probs(query, key, bias_ref, allowed, head, causal)
        parts.append(mm(probs.astype(BF), value))
    return pick_heads(*parts).astype(BF)


def attend_pair_back(query, key, value, grad, bias_ref, dbias_ref, allowed, causal):
    grad_query, grad_key, grad_value = [], 0.0, 0.0
    for head in range(2):
        probs = pair_probs(query, key, bias_ref, allowed, head, causal)
        grad_head = head_only(grad, head)
        grad_probs = mm(grad_head, value, NT)
        inner = jnp.sum(probs * grad_probs, axis=1, keepdims=True)
        grad_scores = probs * (grad_probs - inner)
        low_scores = grad_scores.astype(BF)
        grad_query.append(mm(low_scores, key))
        grad_key = grad_key + mm(low_scores, head_only(query, head), TN)
        grad_value = grad_value + mm(probs.astype(BF), grad_head, TN)
        if causal:
            dbias_ref[0, head : head + 1, :] = unspread(grad_scores, query.shape[0])
    return pick_heads(*grad_query).astype(BF), grad_key.astype(BF), grad_value.astype(BF)


def scale_of(values):
    return lax.rsqrt(jnp.mean(values * values, axis=-1, keepdims=True) + EPSILON)


def norm_back(values, gain, grad_out):
    scale = scale_of(values)
    unit = values * scale
    lean = jnp.mean(grad_out * gain * unit, axis=-1, keepdims=True)
    grad_gain = jnp.sum(grad_out * unit, axis=0, keepdims=True)
    return scale * (grad_out * gain - unit * lean), grad_gain


def cost(microseconds):
    return pl.CostEstimate(flops=microseconds * 10**9, bytes_accessed=1, transcendentals=0)


PARAMS = pltpu.CompilerParams(dimension_semantics=("arbitrary",), vmem_limit_bytes=48 << 20)
SMEM = pl.BlockSpec(memory_space=pltpu.SMEM)


def whole(array, rows=None):
    shape = array.shape if rows is None else (rows, array.shape[1])
    return pl.BlockSpec(shape, lambda step: (0,) * len(shape))


def pair_cols(rows, offset=0):
    return pl.BlockSpec((rows, LANES), lambda step: (0, offset + step))


def shape_of(*shape, dtype=BF):
    return jax.ShapeDtypeStruct(shape, dtype)


def windows_spec(windows):
    return pl.BlockSpec((1, 2, windows.shape[2]), lambda step: (step, 0, 0))


def self_forward(place, target_all, gain, weights, windows, qseg, kseg):
    (length, width), rows = target_all.shape, qseg.shape[0]
    inner = windows.shape[0] * LANES
    pairs = inner // LANES

    def body(
        pos_ref, rows_ref, gain_ref, wq_ref, wk_ref, wv_ref, win_ref, qseg_ref, kseg_ref,
        out_ref, q_ref, k_ref, v_ref, normed_ref,
    ):
        position = pl.multiple_of(pos_ref[0], LANES)

        @pl.when(pl.program_id(0) == 0)
        def _():
            values = rows_ref[...].astype(F32)
            normed_ref[...] = (values * scale_of(values) * gain_ref[...]).astype(BF)

        normed = normed_ref[...]
        query = mm(normed_ref[pl.ds(position, rows), :], wq_ref[...]).astype(BF)
        key = mm(normed, wk_ref[...]).astype(BF)
        value = mm(normed, wv_ref[...]).astype(BF)
        q_ref[...], k_ref[...], v_ref[...] = query, key, value
        allowed = allowed_pairs(position, qseg_ref[...], kseg_ref[...], True)
        out_ref[...] = attend_pair(query, key, value, win_ref, allowed, True)

    return pl.pallas_call(
        body,
        grid=(pairs,),
        in_specs=[
            SMEM, whole(target_all), whole(gain),
            pair_cols(width), pair_cols(width, pairs), pair_cols(width, 2 * pairs),
            windows_spec(windows), whole(qseg), whole(kseg),
        ],
        out_specs=[
            pair_cols(rows), pair_cols(rows), pair_cols(length), pair_cols(length),
            whole(target_all),
        ],
        out_shape=[
            shape_of(rows, inner), shape_of(rows, inner), shape_of(length, inner),
            shape_of(length, inner), shape_of(length, width),
        ],
        compiler_params=PARAMS,
        cost_estimate=cost(16),
        name="self_forward",
    )(place, target_all, gain, weights, weights, weights, windows, qseg, kseg)


def self_back(place, target_all, grad, query, key, value, weights, windows, qseg, kseg):
    (length, width), (rows, inner) = target_all.shape, query.shape
    pairs = inner // LANES

    def body(
        pos_ref, rows_ref, do_ref, q_ref, k_ref, v_ref, wq_ref, wk_ref, wv_ref, win_ref,
        qseg_ref, kseg_ref, dq_ref, dk_ref, dv_ref, dwin_ref, back_ref, dgain_ref,
    ):
        step = pl.program_id(0)
        position = pl.multiple_of(pos_ref[0], LANES)
        own = pl.ds(position, rows)
        allowed = allowed_pairs(position, qseg_ref[...], kseg_ref[...], True)
        dq, dk, dv = attend_pair_back(
            q_ref[...], k_ref[...], v_ref[...], do_ref[...], win_ref, dwin_ref, allowed, True
        )
        dq_ref[...] = jnp.zeros_like(dq_ref)
        dq_ref[own, :] = dq
        dk_ref[...], dv_ref[...] = dk, dv
        back = mm(dk, wk_ref[...], NT) + mm(dv, wv_ref[...], NT)

        @pl.when(step == 0)
        def _():
            back_ref[...] = back

        @pl.when(step > 0)
        def _():
            back_ref[...] += back

        back_ref[own, :] += mm(dq, wq_ref[...], NT)

        @pl.when(step == pairs - 1)
        def _():
            values = rows_ref[...].astype(F32)
            dgain_ref[...] = jnp.sum(
                values * scale_of(values) * back_ref[...], axis=0, keepdims=True
            )

    return pl.pallas_call(
        body,
        grid=(pairs,),
        in_specs=[
            SMEM, whole(target_all), pair_cols(rows),
            pair_cols(rows), pair_cols(length), pair_cols(length),
            pair_cols(width), pair_cols(width, pairs), pair_cols(width, 2 * pairs),
            windows_spec(windows), whole(qseg), whole(kseg),
        ],
        out_specs=[
            pair_cols(length), pair_cols(length), pair_cols(length), windows_spec(windows),
            whole(target_all), pl.BlockSpec((1, width), lambda step: (0, 0)),
        ],
        out_shape=[
            shape_of(length, inner), shape_of(length, inner), shape_of(length, inner),
            shape_of(*windows.shape, dtype=F32), shape_of(length, width, dtype=F32),
            shape_of(1, width, dtype=F32),
        ],
        compiler_params=PARAMS,
        cost_estimate=cost(23),
        name="self_back",
    )(place, target_all, grad, query, key, value, weights, weights, weights, windows, qseg, kseg)


def cross_forward(target, attended, memory_all, gain_cross, gain_ffn, weights, qseg, mseg):
    (rows, width), inner, enc = target.shape, attended.shape[1], memory_all.shape[0]
    pairs = inner // LANES

    def body(
        rows_ref, att_ref, mem_ref, gain_ref, gain3_ref, wo_ref, wq_ref, wk_ref, wv_ref, wc_ref,
        qseg_ref, mseg_ref, one_ref, normed_ref, q_ref, k_ref, v_ref, out_ref, two_ref, last_ref,
    ):
        step = pl.program_id(0)

        @pl.when(step == 0)
        def _():
            hidden = rows_ref[...].astype(F32) + mm(att_ref[...], wo_ref[...])
            one_ref[...] = hidden
            two_ref[...] = hidden
            normed_ref[...] = (hidden * scale_of(hidden) * gain_ref[...]).astype(BF)

        query = mm(normed_ref[...], wq_ref[...]).astype(BF)
        key = mm(mem_ref[...], wk_ref[...]).astype(BF)
        value = mm(mem_ref[...], wv_ref[...]).astype(BF)
        q_ref[...], k_ref[...], v_ref[...] = query, key, value
        allowed = allowed_pairs(0, qseg_ref[...], mseg_ref[...], False)
        out = attend_pair(query, key, value, None, allowed, False)
        out_ref[...] = out
        two_ref[...] += mm(out, wc_ref[...])

        @pl.when(step == pairs - 1)
        def _():
            hidden = two_ref[...]
            last_ref[...] = (hidden * scale_of(hidden) * gain3_ref[...]).astype(BF)

    return pl.pallas_call(
        body,
        grid=(pairs,),
        in_specs=[
            whole(target), whole(attended), whole(memory_all), whole(gain_cross), whole(gain_ffn),
            pl.BlockSpec((width, width), lambda step: (0, 0)),
            pair_cols(width, pairs), pair_cols(width, 2 * pairs), pair_cols(width, 3 * pairs),
            pl.BlockSpec((LANES, width), lambda step: (step, 4)),
            whole(qseg), whole(mseg),
        ],
        out_specs=[
            whole(target), whole(target), pair_cols(rows), pair_cols(enc), pair_cols(enc),
            pair_cols(rows), whole(target), whole(target),
        ],
        out_shape=[
            shape_of(rows, width, dtype=F32), shape_of(rows, width), shape_of(rows, inner),
            shape_of(enc, inner), shape_of(enc, inner), shape_of(rows, inner),
            shape_of(rows, width, dtype=F32), shape_of(rows, width),
        ],
        compiler_params=PARAMS,
        cost_estimate=cost(12),
        name="cross_forward",
    )(
        target, attended, memory_all, gain_cross, gain_ffn, weights, weights, weights, weights,
        weights, qseg, mseg,
    )


def cross_back(grad_two, hidden_one, gain, query, key, value, weights, qseg, mseg):
    (rows, width), inner, enc = hidden_one.shape, query.shape[1], key.shape[0]
    pairs = inner // LANES

    def body(
        grad_ref, one_ref, gain_ref, q_ref, k_ref, v_ref, wo_ref, wq_ref, wk_ref, wv_ref, wc_ref,
        qseg_ref, mseg_ref, dq_ref, dk_ref, dv_ref, mem_ref, done_ref, low_ref, datt_ref,
        dgain_ref, two_ref, back_ref,
    ):
        step = pl.program_id(0)

        @pl.when(step == 0)
        def _():
            two_ref[...] = grad_ref[...].astype(BF)

        grad = mm(two_ref[...], wc_ref[...], NT).astype(BF)
        allowed = allowed_pairs(0, qseg_ref[...], mseg_ref[...], False)
        dq, dk, dv = attend_pair_back(
            q_ref[...], k_ref[...], v_ref[...], grad, None, None, allowed, False
        )
        dq_ref[...], dk_ref[...], dv_ref[...] = dq, dk, dv
        back = mm(dq, wq_ref[...], NT)
        memory = mm(dk, wk_ref[...], NT) + mm(dv, wv_ref[...], NT)

        @pl.when(step == 0)
        def _():
            back_ref[...] = back
            mem_ref[...] = memory

        @pl.when(step > 0)
        def _():
            back_ref[...] += back
            mem_ref[...] += memory

        @pl.when(step == pairs - 1)
        def _():
            through, grad_gain = norm_back(one_ref[...], gain_ref[...], back_ref[...])
            grad_one = grad_ref[...] + through
            low = grad_one.astype(BF)
            done_ref[...] = grad_one
            low_ref[...] = low
            dgain_ref[...] = grad_gain
            datt_ref[...] = mm(low, wo_ref[...], NT).astype(BF)

    row = pl.BlockSpec((1, width), lambda step: (0, 0))
    return pl.pallas_call(
        body,
        grid=(pairs,),
        in_specs=[
            whole(grad_two), whole(hidden_one), row,
            pair_cols(rows), pair_cols(enc), pair_cols(enc),
            pl.BlockSpec((width, width), lambda step: (0, 0)),
            pair_cols(width, pairs), pair_cols(width, 2 * pairs), pair_cols(width, 3 * pairs),
            pl.BlockSpec((LANES, width), lambda step: (step, 4)),
            whole(qseg), whole(mseg),
        ],
        out_specs=[
            pair_cols(rows), pair_cols(enc), pair_cols(enc),
            pl.BlockSpec((enc, width), lambda step: (0, 0)),
            whole(hidden_one), whole(hidden_one), whole(hidden_one), row,
        ],
        out_shape=[
            shape_of(rows, inner), shape_of(enc, inner), shape_of(enc, inner),
            shape_of(enc, width, dtype=F32), shape_of(rows, width, dtype=F32),
            shape_of(rows, width), shape_of(rows, inner), shape_of(1, width, dtype=F32),
        ],
        scratch_shapes=[pltpu.VMEM((rows, width), BF), pltpu.VMEM((rows, width), F32)],
        compiler_params=PARAMS,
        cost_estimate=cost(18),
        name="cross_back",
    )(
        grad_two, hidden_one, gain, query, key, value, weights, weights, weights, weights, weights,
        qseg, mseg,
    )


def gather_all(shard):
    return lax.all_gather(shard, AXES, axis=0, tiled=True)


def scatter_all(grads):
    return lax.psum_scatter(grads, AXES, scatter_dimension=0, tiled=True).astype(F32)


class Links:
    def __init__(self):
        self.batch, self.seq = lax.axis_size("batch"), lax.axis_size("seq")
        self.depth = self.batch // 2
        z_x, y_c = lax.axis_index("batch"), lax.axis_index("seq")
        self.z, self.x = z_x // 2, z_x % 2
        self.y, self.core = y_c // 2, y_c % 2
        self.lead = self.core == 0
        self.place = jnp.stack([self.z, self.x, self.y, self.core]).astype(jnp.int32)

    def move(self, value, target):
        pairs = []
        for source in range(self.batch * self.seq):
            z_x, y_c = source // self.seq, source % self.seq
            z, x, y, core = target(z_x // 2, z_x % 2, y_c // 2, y_c % 2)
            pairs.append((source, (z * 2 + x) * self.seq + y * 2 + core))
        return lax.ppermute(value, AXES, pairs)

    def over_core(self, value):
        return self.move(value, lambda z, x, y, core: (z, x, y, 1 - core))

    def over_y(self, value):
        return self.move(value, lambda z, x, y, core: (z, x, 1 - y, core))

    def over_near(self, value):
        return self.move(
            value, lambda z, x, y, c: (z, x, 1 - y, c) if c else (z, 1 - x, y, c)
        )

    def over_far(self, value):
        return self.move(
            value, lambda z, x, y, c: (z, 1 - x, y, c) if c else (z, x, 1 - y, c)
        )

    def over_z(self, value, step):
        depth = self.depth
        return self.move(value, lambda z, x, y, core: ((z - step) % depth, x, y, core))


def in_order(first, own, other):
    return jnp.concatenate([jnp.where(first, own, other), jnp.where(first, other, own)], axis=0)


def gather_core(links, left, right):
    own = jnp.where(links.lead, left, right)
    other = links.over_core(jnp.where(links.lead, right, left))
    return in_order(links.lead, own, other)


def z_steps(links, value, steps):
    return [links.over_z(value, step) for step in steps]


def gather_near(links, value):
    return jnp.stack([value, links.over_near(value)])


def gather_far(links, value):
    return jnp.stack([value, links.over_far(value)])


def assemble(links, *sources):
    count, (rows, cols) = len(sources) // 2, sources[0].shape[-2:]
    depth = links.depth

    def body(place_ref, *refs):
        inputs, out_ref, sem = refs[:-2], refs[-2], refs[-1]
        z, x, y, core = [place_ref[i] for i in range(4)]
        for which, source in enumerate(inputs):
            half = core if which < count else 1 - core
            for near, far, step in np.ndindex(2, 2, depth):
                if count == 2 and far != which % 2:
                    continue
                step_x, step_y = jnp.where(half == 0, near, far), jnp.where(half == 0, far, near)
                chip = (((z + step) % depth) * 2 + (x ^ step_x)) * 2 + (y ^ step_y)
                target = out_ref.at[
                    pl.ds(pl.multiple_of(chip * rows, 16), rows),
                    pl.ds(pl.multiple_of(half * cols, LANES), cols),
                ]
                part = source.at[near, step] if count == 2 else source.at[step, far, near]
                pltpu.make_async_copy(part, target, sem).start()
        pltpu.make_async_copy(out_ref, out_ref, sem).wait()

    return pl.pallas_call(
        body,
        in_specs=[pl.BlockSpec(memory_space=pltpu.SMEM)]
        + [pl.BlockSpec(memory_space=pl.ANY)] * len(sources),
        out_specs=pl.BlockSpec(memory_space=pltpu.VMEM),
        out_shape=jax.ShapeDtypeStruct((depth * 4 * rows, 2 * cols), sources[0].dtype),
        scratch_shapes=[pltpu.SemaphoreType.DMA(())],
        compiler_params=pltpu.CompilerParams(vmem_limit_bytes=48 << 20),
        cost_estimate=cost(6),
        name="assemble",
    )(links.place, *sources)


def weight_grad(links, core, terms, extra=None, z_first=False):
    depth, total_rows = links.depth, terms[0][0].shape[1]
    rows = total_rows // (depth * 4)
    widths = [term[1].shape[1] for term in terms]
    extra_width = 0 if extra is None else extra.shape[1]
    total = sum(widths) + extra_width
    tile = 1408 if total % 1408 == 0 else 512

    def body(place_ref, *refs):
        inputs, out_ref, stage, sems = refs[:-3], refs[-3], refs[-2], refs[-1]
        z, x, y, left = place_ref[0], place_ref[1], place_ref[2], place_ref[3] == 0
        places = []
        for chip in range(depth * 4):
            step_x, step_y = (chip // 2 % 2) ^ x, (chip % 2) ^ y
            near, far = jnp.where(left, step_x, step_y), jnp.where(left, step_y, step_x)
            step = (chip // 4 - z) % depth
            spot = (step * 2 + far) * 2 + near if z_first else (near * 2 + far) * depth + step
            places.append(pl.multiple_of(spot * rows, 8))
        copies, start = [], 0

        def emit(start, value, width):
            for chip, spot in enumerate(places):
                stage[pl.ds(spot, rows), start : start + width] = value[
                    chip * rows : (chip + 1) * rows
                ].astype(BF)
            copies.append(
                pltpu.make_async_copy(
                    stage.at[:, pl.ds(start, width)],
                    out_ref.at[:, pl.ds(start, width)],
                    sems.at[len(copies)],
                )
            )
            copies[-1].start()

        for index, width in enumerate(widths):
            acts_l, grad_l, acts_r, grad_r = inputs[4 * index : 4 * index + 4]
            acts = jnp.where(left, acts_l[...], acts_r[...])
            for offset in range(0, width, tile):
                cols = slice(offset, offset + tile)
                grad = jnp.where(left, grad_l[:, cols], grad_r[:, cols])
                emit(start, mm(acts, grad, TN), tile)
                start += tile
        if extra is not None:
            small = inputs[-1][...]
            emit(start, jnp.where(left, small, jnp.zeros_like(small)), extra_width)
        for copy in copies:
            copy.wait()

    place = links.place.at[3].set(core)
    operands = [array for term in terms for array in term] + ([] if extra is None else [extra])
    count = sum(width // tile for width in widths) + (extra is not None)
    vmem = pl.BlockSpec(memory_space=pltpu.VMEM)
    return pl.pallas_call(
        body,
        in_specs=[pl.BlockSpec(memory_space=pltpu.SMEM)] + [vmem] * len(operands),
        out_specs=pl.BlockSpec(memory_space=pl.ANY),
        out_shape=jax.ShapeDtypeStruct((total_rows, total), BF),
        scratch_shapes=[pltpu.VMEM((total_rows, total), BF), pltpu.SemaphoreType.DMA((count,))],
        compiler_params=pltpu.CompilerParams(vmem_limit_bytes=48 << 20),
        cost_estimate=cost(4),
        name="weight_grad",
    )(place, *operands)


def add_low(one, other):
    return (one.astype(F32) + other.astype(F32)).astype(BF)


class Scatter:
    def __init__(self, links):
        self.links, self.parts = links, []

    def core(self, sent):
        self.rows = sent.shape[0]
        self.parts.append(self.links.over_core(sent))

    def keep(self, kept):
        self.parts.append(kept)

    def total(self, start, count):
        return sum(part[start : start + count].astype(F32) for part in self.parts)

    def halve(self):
        self.rows //= 2
        return self.total(self.rows, self.rows).astype(BF)

    def near(self, send):
        self.parts.append(self.links.over_near(send))

    def far(self, send):
        self.parts.append(self.links.over_far(send))

    def z_sends(self):
        self.rows //= self.links.depth
        return [
            self.total(step * self.rows, self.rows).astype(BF)
            for step in range(1, self.links.depth)
        ]

    def z(self, sends):
        depth = self.links.depth
        for step, send in enumerate(sends, 1):
            self.parts.append(self.links.over_z(send, depth - step))

    def z_start(self, sends):
        links, depth = self.links, self.links.depth
        return links.over_z(sends[-1], 1), links.over_z(sends[-2], depth - 1)

    def z_end(self, sends, back, ahead):
        self.parts.append(back)
        for send in sends[-3::-1]:
            ahead = self.links.over_z(add_low(ahead, send), self.links.depth - 1)
        self.parts.append(ahead)

    def own(self):
        return self.total(0, self.rows)

    def last(self, total):
        links, half = self.links, self.rows // 2
        above, below = total[:half], total[half:]
        own = jnp.where(links.lead, above, below)
        other = links.over_core(jnp.where(links.lead, below, above))
        return jnp.where(links.lead, own, other), jnp.where(links.lead, other, own)


class SeqScatter:
    def __init__(self, links, parts):
        self.links = links
        parts = parts.reshape(2, 2, -1, parts.shape[1])
        take = lambda core: lax.dynamic_index_in_dim(parts, core, 1, False)
        self.kept = take(links.core)
        self.sent = links.over_core(take(1 - links.core).astype(BF))

    def second(self):
        total = self.kept + self.sent.astype(F32)
        take = lambda y: lax.dynamic_index_in_dim(total, y, 0, False)
        self.kept = take(self.links.y)
        self.sent = self.links.over_y(take(1 - self.links.y).astype(BF))

    def total(self):
        return self.kept + self.sent.astype(F32)


class PlainScatter:
    parts = ()

    def core(self, sent):
        self.sent = sent

    def keep(self, kept):
        self.kept = kept

    def halve(self):
        return self.sent

    def near(self, send):
        self.sent = send

    def z_start(self, sends):
        return sends, None

    def z_end(self, sends, back, ahead):
        self.sent = back

    far = near
    z_sends = own = halve

    def last(self, total):
        return jnp.split(scatter_all(self.kept), 2, axis=1)


def phase(*values):
    return lax.optimization_barrier(values)


def per_device(
    target, memory, cotangent, target_segments, memory_segments, bucket_ids,
    self_norm_gain, self_query, self_key, self_value, self_output, bias_table,
    cross_norm_gain, cross_query, cross_key, cross_value, cross_output,
    ffn_norm_gain, ffn_gate, ffn_up, ffn_down,
):
    batch_size, seq_size = lax.axis_size("batch"), lax.axis_size("seq")
    devices = batch_size * seq_size
    seq_index = lax.axis_index("seq")
    rows, width = target.shape[1], target.shape[2]
    length, enc = target_segments.shape[1], memory_segments.shape[1]
    enc_rows = memory.shape[1]
    inner = self_query.shape[1]
    hidden = ffn_gate.shape[1]
    table_rows, table_cols = bias_table.shape
    weight_rows = self_query.shape[0]
    table_size = table_rows * table_cols

    links = Links()
    core, lead, depth = links.core, links.lead, links.depth
    small = jnp.concatenate(
        [self_norm_gain, cross_norm_gain, ffn_norm_gain, bias_table.reshape(-1)]
    )
    small = jnp.pad(small[None], ((0, weight_rows - 1), (0, 2 * LANES - small.shape[0])))
    part = hidden // 2
    groups = [
        [self_query, self_key, self_value, small],
        [self_output, cross_query, cross_key, cross_value, cross_output],
        [ffn_gate[:, :part], ffn_up[:, :part]],
        [ffn_gate[:, part:], ffn_up[:, part:]],
    ]
    groups = [jnp.concatenate(group, axis=1) for group in groups]
    cuts = [group.shape[1] // 2 for group in groups]
    left = jnp.concatenate([group[:, :cut] for group, cut in zip(groups, cuts)], axis=1)
    right = jnp.concatenate([group[:, cut:] for group, cut in zip(groups, cuts)], axis=1)
    down_cut = width // 2
    steps = list(range(1, depth))
    some, rest = steps[:1], steps[1:]
    z_one, z_two, z_three = steps[:1], steps[-1:] if depth > 2 else [], steps[1:-1]
    direct = 2 * ffn_down.shape[0] % 16 == 0
    move = lambda function, *args: function(links, *args) if direct else None

    moved = gather_core(links, left, right)
    down = move(gather_core, ffn_down[:, :down_cut], ffn_down[:, down_cut:])
    if not direct:
        down_whole = gather_all(ffn_down)
    moved, down = phase(moved, down)
    ends = list(np.cumsum(cuts))
    first0, second0, third0, fourth0 = jnp.split(moved, ends[:-1], axis=1)

    position = seq_index * rows
    heads = seq_size * table_cols
    distance = position + rows - jnp.arange(rows + length, dtype=jnp.int32)
    near = (distance >= 0) & (distance < length)
    bucket = jnp.take(bucket_ids, jnp.clip(distance, 0, length - 1))
    bucket_range = jnp.arange(batch_size * table_rows, dtype=jnp.int32)
    onehot = ((bucket[:, None] == bucket_range[None, :]) & near[:, None]).astype(BF)

    first_z = jnp.stack([first0] + z_steps(links, first0, steps))
    down = move(gather_near, down)
    first_z, second0, down = phase(first_z, second0, down)

    first_near = gather_near(links, first_z)
    down = move(gather_far, down)
    second_z = z_steps(links, second0, some)
    rows_own = jnp.concatenate([target[0], memory[0]], axis=0)
    rows_other = links.over_y(rows_own)
    first_near, down, second_z, second0, onehot, rows_own, rows_other = phase(
        first_near, down, second_z, second0, onehot, rows_own, rows_other
    )

    first_far = links.over_far(first_near)
    first_near_other = links.over_core(first_near)
    second_z = jnp.stack([second0] + second_z + z_steps(links, second0, rest))
    rows_pair = in_order(links.y == 0, rows_own, rows_other)
    rows_other = links.over_core(rows_pair)
    first_far, first_near_other, second_z, down, third0, rows_pair, rows_other = phase(
        first_far, first_near_other, second_z, down, third0, rows_pair, rows_other
    )
    by_y = lambda both: both.reshape(2, 1, rows + enc_rows, width)
    both = jnp.concatenate(
        [
            jnp.where(lead, by_y(rows_pair), by_y(rows_other)),
            jnp.where(lead, by_y(rows_other), by_y(rows_pair)),
        ],
        axis=1,
    )
    target_all = both[:, :, :rows].reshape(length, width)
    memory_all = both[:, :, rows:].reshape(enc, width)

    second_near = gather_near(links, second_z)
    third_z = jnp.stack([third0] + z_steps(links, third0, steps))
    first_far_other = links.over_core(first_far)
    first_far_other, second_near, third_z, fourth0, down, target_all, memory_all = phase(
        first_far_other, second_near, third_z, fourth0, down, target_all, memory_all
    )

    second_far = links.over_far(second_near)
    second_near_other = links.over_core(second_near)
    third_near = gather_near(links, third_z)
    fourth_z = jnp.stack([fourth0] + z_steps(links, fourth0, steps))
    down_one = move(z_steps, down, z_one)
    down_two = move(z_steps, down, z_two)
    first = assemble(links, first_near, first_far, first_near_other, first_far_other)
    smalls = first[:, 3 * inner :].reshape(devices, weight_rows, 2 * LANES)[:, 0, :].astype(F32)
    gains = [smalls[:, i * weight_rows : (i + 1) * weight_rows].reshape(1, width) for i in range(3)]
    gain_self, gain_cross, gain_ffn = gains
    table = smalls[:, 3 * weight_rows : 3 * weight_rows + table_size]
    table = table.reshape(batch_size, seq_size, table_rows, table_cols)
    table = jnp.transpose(table, (0, 2, 1, 3)).reshape(batch_size * table_rows, seq_size * table_cols)

    windows = mm(table.astype(BF), onehot, (((0,), (1,)), ((), ())))
    windows = windows.reshape(heads // 2, 2, rows + length)
    position1 = position.reshape(1)
    qseg = lax.dynamic_slice_in_dim(target_segments, position, rows, 1).reshape(rows, 1)
    kseg, mseg = target_segments, memory_segments

    attended, queries, keys, values, normed_all = self_forward(
        position1, target_all, gain_self, first, windows, qseg, kseg
    )
    attended, second_far, second_near_other, third_near, fourth_z, down, down_one, down_two = phase(
        attended, second_far, second_near_other, third_near, fourth_z, down, down_one, down_two
    )

    third_far = links.over_far(third_near)
    third_near_other = links.over_core(third_near)
    fourth_near = links.over_near(fourth_z)
    down_three = []
    for step in z_three:
        down_three.append(links.over_z((down_one + down_three)[-1], 1) if direct else None)
    second = assemble(
        links, second_near, second_far, second_near_other, links.over_core(second_far)
    )
    (
        hidden_one, normed_two, cross_queries, cross_keys, cross_values, cross_attended,
        hidden_two, normed_three,
    ) = cross_forward(
        target[0], attended, memory_all, gain_cross, gain_ffn, second, qseg, mseg
    )
    normed_three, third_far, third_near_other, fourth_z, fourth_near = phase(
        normed_three, third_far, third_near_other, fourth_z, fourth_near
    )
    down, down_one, down_two, down_three, normed_three = phase(
        down, down_one, down_two, down_three, normed_three
    )

    fourth_near = jnp.stack([fourth_z, fourth_near])
    fourth_far = links.over_far(fourth_near)
    fourth_near_other = links.over_core(fourth_near)
    if direct:
        down = jnp.stack([down] + down_one + down_three + down_two)
    down_other = links.over_core(down) if direct else None
    third = assemble(links, third_near, third_far, third_near_other, links.over_core(third_far))
    third_gate_up = mm(normed_three, third)
    if direct:
        w_down = assemble(links, down, down_other)
    else:
        w_down = down_whole
    third_gate_up, fourth_far, fourth_near_other, w_down = phase(
        third_gate_up, fourth_far, fourth_near_other, w_down
    )

    fourth_far_other = links.over_core(fourth_far)
    cot = cotangent[0]

    def gated(gate_up, start):
        inner_act, pull = jax.vjp(gated_unit, gate_up[:, :part], gate_up[:, part:])
        grad_gate, grad_up = pull(mm(cot, w_down[start : start + part], NT))
        return inner_act.astype(BF), grad_gate.astype(BF), grad_up.astype(BF)

    inner_a, gate_a, up_a = gated(third_gate_up, 0)
    third_sum, fourth_sum = Scatter(links), Scatter(links)
    third_terms = [(normed_three, gate_a, normed_three, up_a)]
    third_send = weight_grad(links, 1 - core, third_terms)
    third_send, gate_a, up_a, fourth_far_other, w_down = phase(
        third_send, gate_a, up_a, fourth_far_other, w_down
    )

    third_sum.core(third_send)
    fourth = assemble(links, fourth_near, fourth_far, fourth_near_other, fourth_far_other)
    third_sum.keep(weight_grad(links, core, third_terms))
    third_send = third_sum.halve()
    third_send, fourth = phase(third_send, fourth)

    third_sum.near(third_send)
    inner_b, gate_b, up_b = gated(mm(normed_three, fourth), part)
    fourth_terms = [(normed_three, gate_b, normed_three, up_b)]
    fourth_sum.core(weight_grad(links, 1 - core, fourth_terms))
    inner_low = jnp.concatenate([inner_a, inner_b], axis=1)
    down_terms = [(inner_low, cot[:, :down_cut], inner_low, cot[:, down_cut:])]
    down_sum = Scatter(links) if direct else PlainScatter()
    if direct:
        down_sum.core(weight_grad(links, 1 - core, down_terms, z_first=True))
        down_sum.keep(weight_grad(links, core, down_terms, z_first=True))
    else:
        down_sum.core(inner_low)
        down_sum.keep(mm(inner_low, cot, TN).astype(BF))
    grad_normed_three = mm(jnp.concatenate([gate_a, up_a], axis=1), third, NT) + mm(
        jnp.concatenate([gate_b, up_b], axis=1), fourth, NT
    )
    through, grad_gain_ffn = norm_back(hidden_two, gain_ffn, grad_normed_three)
    grad_hidden_two = cot.astype(F32) + through
    fourth_sum.keep(weight_grad(links, core, fourth_terms))
    third_sum.parts, fourth_sum.parts, down_sum.parts, grad_hidden_two = phase(
        third_sum.parts, fourth_sum.parts, down_sum.parts, grad_hidden_two
    )

    third_sum.far(third_sum.halve())
    fourth_sum.near(fourth_sum.halve())
    down_sends = down_sum.z_sends()
    down_back, down_ahead = down_sum.z_start(down_sends)
    low_two = grad_hidden_two.astype(BF)
    (
        grad_cq, grad_ck, grad_cv, memory_part, grad_hidden_one, low_one, grad_attended,
        grad_gain_cross,
    ) = cross_back(
        grad_hidden_two, hidden_one, gain_cross, cross_queries, cross_keys, cross_values, second,
        qseg, mseg,
    )
    half = inner // 2
    (
        third_sum.parts, fourth_sum.parts, down_back, down_ahead, grad_cq, grad_ck, grad_cv,
        low_one, grad_attended,
    ) = phase(
        third_sum.parts, fourth_sum.parts, down_back, down_ahead, grad_cq, grad_ck, grad_cv,
        low_one, grad_attended,
    )

    cross_terms = [
        (normed_two, grad_cq, cross_attended, low_two),
        (memory_all, grad_ck, memory_all, grad_cv),
        (attended, low_one[:, :half], attended, low_one[:, half:]),
    ]
    cross_sum = Scatter(links)
    cross_sum.core(weight_grad(links, 1 - core, cross_terms))
    fourth_sum.far(fourth_sum.halve())
    third_sum.z(third_sum.z_sends())
    cross_sum.keep(weight_grad(links, core, cross_terms))
    cross_sum.parts, fourth_sum.parts, grad_attended = phase(
        cross_sum.parts, fourth_sum.parts, grad_attended
    )

    cross_sum.near(cross_sum.halve())
    down_sum.z_end(down_sends, down_back, down_ahead)
    grad_q, grad_k, grad_v, grad_windows, grad_normed, grad_gain_self = self_back(
        position1, target_all, grad_attended, queries, keys, values, first, windows, qseg, kseg
    )
    (
        cross_sum.parts, third_sum.parts, down_sum.parts, grad_q, grad_k, grad_v, grad_windows,
        grad_normed, grad_gain_self, memory_part,
    ) = phase(
        cross_sum.parts, third_sum.parts, down_sum.parts, grad_q, grad_k, grad_v, grad_windows,
        grad_normed, grad_gain_self, memory_part,
    )

    cross_sum.far(cross_sum.halve())
    grad_windows = grad_windows.reshape(heads, rows + length)
    grad_table = lax.dot_general(
        onehot.astype(F32), grad_windows, (((0,), (1,)), ((), ())), precision=lax.Precision.HIGHEST
    )
    grad_table = grad_table.reshape(batch_size, table_rows, seq_size, table_cols)
    grad_table = jnp.transpose(grad_table, (0, 2, 1, 3)).reshape(devices, table_size)
    gain_parts = [g.reshape(devices, weight_rows) for g in (grad_gain_self, grad_gain_cross, grad_gain_ffn)]
    small_grad = jnp.concatenate(gain_parts + [grad_table], axis=1)
    small_grad = jnp.pad(
        small_grad[:, None], ((0, 0), (0, weight_rows - 1), (0, LANES - small_grad.shape[1]))
    ).reshape(devices * weight_rows, LANES)
    cut = inner + half
    self_terms = [
        (normed_all, grad_q, normed_all, grad_v),
        (normed_all, grad_k[:, :half], normed_all, grad_k[:, half:]),
    ]
    self_sum = Scatter(links)
    self_sum.core(weight_grad(links, 1 - core, self_terms, small_grad))
    self_sum.keep(weight_grad(links, core, self_terms, small_grad))
    fourth_sum.z(fourth_sum.z_sends())
    self_sum.parts, cross_sum.parts = phase(self_sum.parts, cross_sum.parts)

    self_sum.near(self_sum.halve())
    cross_sends = cross_sum.z_sends()
    cross_back_z, cross_ahead_z = cross_sum.z_start(cross_sends)
    down_sum.far(down_sum.halve())
    normed_rows = SeqScatter(links, grad_normed)
    activations = (hidden_two + mm(inner_low, w_down)).astype(BF)
    (
        self_sum.parts, cross_back_z, cross_ahead_z, down_sum.parts, fourth_sum.parts,
        normed_rows.sent,
    ) = phase(
        self_sum.parts, cross_back_z, cross_ahead_z, down_sum.parts, fourth_sum.parts,
        normed_rows.sent,
    )

    self_sum.far(self_sum.halve())
    cross_sum.z_end(cross_sends, cross_back_z, cross_ahead_z)
    down_sum.near(down_sum.halve())
    normed_rows.second()
    gate_one, up_one = third_sum.last(third_sum.own())
    memory_rows = SeqScatter(links, memory_part)
    self_sum.parts, down_sum.parts, cross_sum.parts, normed_rows.sent, memory_rows.sent = phase(
        self_sum.parts, down_sum.parts, cross_sum.parts, normed_rows.sent, memory_rows.sent
    )

    self_sum.z(self_sum.z_sends())
    memory_rows.second()
    memory_grad = memory_rows.total()
    down_out = jnp.concatenate(down_sum.last(down_sum.own()), axis=1)
    cross_left, cross_right = cross_sum.last(cross_sum.own())
    gate_two, up_two = fourth_sum.last(fourth_sum.own())
    through, _ = norm_back(target[0].astype(F32), gain_self, normed_rows.total())
    target_grad = grad_hidden_one + through
    self_left, self_right = self_sum.last(self_sum.own())
    join = lambda left, right: jnp.concatenate([left, right], axis=1)

    small_out = self_left[0, cut:]
    gain_out = [small_out[i * weight_rows : (i + 1) * weight_rows] for i in range(3)]
    table_out = small_out[3 * weight_rows : 3 * weight_rows + table_size]
    return (
        activations[None],
        target_grad[None],
        memory_grad[None],
        gain_out[0],
        self_left[:, :inner],
        join(self_left[:, inner:cut], self_right[:, inner:cut]),
        self_right[:, :inner],
        join(cross_left[:, 2 * inner :], cross_right[:, 2 * inner :]),
        table_out.reshape(table_rows, table_cols),
        gain_out[1],
        cross_left[:, :inner],
        cross_left[:, inner : 2 * inner],
        cross_right[:, inner : 2 * inner],
        cross_right[:, :inner],
        gain_out[2],
        jnp.concatenate([gate_one, gate_two], axis=1),
        jnp.concatenate([up_one, up_two], axis=1),
        down_out,
    )


def solution(mesh):
    rows3 = P("batch", "seq", None)
    seg = P("batch", None)
    gain = P(AXES)
    weight = P(AXES, None)
    table = P("batch", "seq")
    return jax.shard_map(
        per_device,
        mesh=mesh,
        in_specs=(
            rows3, rows3, rows3, seg, seg, P(),
            gain, weight, weight, weight, weight, table,
            gain, weight, weight, weight, weight,
            gain, weight, weight, weight,
        ),
        out_specs=(
            rows3, rows3, rows3,
            gain, weight, weight, weight, weight, table,
            gain, weight, weight, weight, weight,
            gain, weight, weight, weight,
        ),
        check_vma=False,
    )
```

time: 556 us -> 496 us (0.89)
  waiting for transfers between devices: 223 us -> 127 us
  matrix products: 63.4 us -> 29.2 us
  Pallas kernels: 91.8 us -> 124 us
  starting transfers between devices: 62.6 us -> 89.7 us
  local copies, waits for them, and re-layouts: 29.8 us -> 44.5 us
    ppermute x58 -> x77, waiting for transfers between devices: 213 us -> 127 us  [move(): return lax.ppermute(value, AXES, pairs)]
    dot_general x17 -> x8, matrix products: 62.1 us -> 27.9 us  [mm(): return lax.dot_general(left, right, dims, preferred_element_type=F32)]
    ppermute x58 -> x77, starting transfers between devices: 56.8 us -> 89.7 us  [move(): return lax.ppermute(value, AXES, pairs)]
    pallas_call x4, Pallas kernels: 37.6 us -> 68.7 us  [the longest x1 23.2 us: self_back(): pl.pallas_call(body, grid=(pairs,), in_specs=[SMEM, whole(target_all), pa...]
    unnamed x186 -> x274, local copies, waits for them, and re-layouts: 16.2 us -> 25.7 us
    ppermute x9 -> x0, waiting for transfers between devices: 9.26 us -> none  [the longest x6 4.94 us: seq_scatter(): total = total + lax.ppermute(piece, 'seq', seq_perm(size, step)).astype(F32)]
    ppermute x9 -> x0, starting transfers between devices: 5.75 us -> none  [the longest x6 4.1 us: seq_scatter(): total = total + lax.ppermute(piece, 'seq', seq_perm(size, step)).astype(F32)]
    convert_element_type x8 -> x10, other arithmetic: 25.5 us -> 20.7 us  [halve(): return self.total(self.rows, self.rows).astype(BF)]
  transfers between devices with their start and end apart: 67 -> 77, of which waited for: 33 -> 22; matrix products, arithmetic and copies ran while one was open for 22% -> 19% of each run, Pallas kernels for 11% -> 23%
where the time goes in v3:
time: 496 us; the launch traced here: 488 us
  waiting for transfers between devices  127 us (26%)
  Pallas kernels  124 us (25%)
  starting transfers between devices  89.7 us (18%)
  other arithmetic  70.5 us (14%)
  local copies, waits for them, and re-layouts  44.5 us (9%)
  matrix products  29.2 us (6%)
    ppermute x77, waiting for transfers between devices, move(): return lax.ppermute(value, AXES, pairs)  127 us
    ppermute x77, starting transfers between devices, move(): return lax.ppermute(value, AXES, pairs)  89.7 us
    dot_general x8, matrix products, mm(): return lax.dot_general(left, right, dims, preferred_element_type=F32)  27.9 us
    pallas_call x10, Pallas kernels, weight_grad(): pl.pallas_call(body, in_specs=[pl.BlockSpec(memory_space=pltpu.SMEM)] + [...  27.9 us
    pallas_call x5, Pallas kernels, assemble(): pl.pallas_call(body, in_specs=[pl.BlockSpec(memory_space=pltpu.SMEM)] + [...  27.6 us
    unnamed x274, local copies, waits for them, and re-layouts  25.7 us
    pallas_call x1, Pallas kernels, self_back(): pl.pallas_call(body, grid=(pairs,), in_specs=[SMEM, whole(target_all), pa...  23.2 us
    convert_element_type x10, other arithmetic, halve(): return self.total(self.rows, self.rows).astype(BF)  20.7 us
  transfers between devices with their start and end apart: 77, of which 22 were waited for; matrix products, arithmetic and copies ran while one was open for 19% of the time, Pallas kernels for 23%

profile of v3, /device:TPU:0, one launch (start us, length us, event | category | flops | bytes accessed | tf_op | source)
XLA Modules:
  0.0 487.6 jit_solution(13206418170549835932)
XLA Ops:
  17.3 8.9 %collective-permute-done.3 = bf16[64,1664]{1,0:T(8,128)(2,1)S(1)} collective-permute-done((bf16[64,1664]{1,0:T(8,128)(2,1)S(1)}, bf16[64,1664]{1,0:T(8,128)(2,1)S(1)}, u32[]{:S(2)}, u32[]{:S(2)}) %collective-permute-start.3) | collective-permute-done | bytes 213024 | tf_op jit(solution)/shard_map/ppermute | solution.py:408
  26.1 4.2 collective-permute-done.4
  32.7 4.3 gather_fusion
  41.4 10.3 %collective-permute-done.7 = bf16[2,176,512]{2,1,0:T(8,128)(2,1)S(1)} collective-permute-done((bf16[2,176,512]{2,1,0:T(8,128)(2,1)S(1)}, bf16[2,176,512]{2,1,0:T(8,128)(2,1)S(1)}, u32[]{:S(2)}, u32[]{:S(2)}) %collective-permute-start.7) | collective-permute-done | bytes 360480 | tf_op jit(solution)/shard_map/ppermute | solution.py:408
  64.2 4.2 collective-permute-done.13
  68.4 13.6 %collective-permute-done.12 = bf16[64,2560]{1,0:T(8,128)(2,1)S(1)} collective-permute-done((bf16[64,2560]{1,0:T(8,128)(2,1)}, bf16[64,2560]{1,0:T(8,128)(2,1)S(1)}, u32[]{:S(2)}, u32[]{:S(2)}) %collective-permute-start.12) | collective-permute-done | bytes 327712 | tf_op jit(solution)/shard_map/ppermute | solution.py:408
  96.3 7.5 %collective-permute-done.18 = bf16[64,1408]{1,0:T(8,128)(2,1)S(1)} collective-permute-done((bf16[64,1408]{1,0:T(8,128)(2,1)}, bf16[64,1408]{1,0:T(8,128)(2,1)S(1)}, u32[]{:S(2)}, u32[]{:S(2)}) %collective-permute-start.18) | collective-permute-done | bytes 180256 | tf_op jit(solution)/shard_map/ppermute | solution.py:408
  108.0 4.4 collective-permute-start.25
  115.5 6.1 %assemble.5.wq_ref.wk_ref.wv_ref = bf16[1024,3328]{1,0:T(8,128)(2,1)} custom-call(s32[4]{0:T(128)S(1)} %pad_add_fusion.place_ref, bf16[2,4,64,1664]{3,2,1,0:T(8,128)(2,1)S(1)} %copy-done.9, bf16[2,4,64,1664]{3,2,1,0:T(8,128)(2,1)} %collective-permute-done.10.refs_1_, bf16[2,4,64,1664]{3,2,1,0:T(8,128)(2,1)} %collective-permute-done.11.refs_2_, ...), custom_call_target="tpu_custom_call" | custom-call | flops 6000000000 | bytes 1 | tf_op jit(solution)/shard_map/assemble/pallas_call | solution.py:475
  124.5 7.4 %collective-permute-start.26 = (bf16[2,2,176,512]{3,2,1,0:T(8,128)(2,1)}, bf16[2,2,176,512]{3,2,1,0:T(8,128)(2,1)S(1)}, u32[]{:S(2)}, u32[]{:S(2)}) collective-permute-start(bf16[2,2,176,512]{3,2,1,0:T(8,128)(2,1)} %pad_maximum_fusion.9), channel_id=1, source_target_pairs={{0,24},{1,25},{2,26},{3,27},{4,28},{5,29},{6,30},{7,31},{8,0},{9,1... | collective-permute-start | bytes 2162696 | tf_op jit(solution)/shard_map/ppermute | solution.py:408
  134.1 15.5 %self_forward.1 = (bf16[128,1024]{1,0:T(8,128)(2,1)S(1)}, bf16[128,1024]{1,0:T(8,128)(2,1)S(1)}, bf16[512,1024]{1,0:T(8,128)(2,1)S(1)}, bf16[512,1024]{1,0:T(8,128)(2,1)S(1)}, bf16[512,1024]{1,0:T(8,128)(2,1)S(1)}) custom-call(s32[1]{0:T(128)} %bitcast.1.pos_ref, bf16[512,1024]{1,0:T(8,128)(2,1)S(1)} %bitcast.154, f32[1,1024]{1,0:T(1,128)S(1)} %reshape.336.gain_ref, ...), custom_call_target="tpu_custom_call" | custom-call | flops 16000000000 | bytes 1 | tf_op jit(solution)/shard_map/self_forward/pallas_call | solution.py:166
  153.5 6.4 %collective-permute-done.26 = bf16[2,2,176,512]{3,2,1,0:T(8,128)(2,1)S(1)} collective-permute-done((bf16[2,2,176,512]{3,2,1,0:T(8,128)(2,1)}, bf16[2,2,176,512]{3,2,1,0:T(8,128)(2,1)S(1)}, u32[]{:S(2)}, u32[]{:S(2)}) %collective-permute-start.26) | collective-permute-done | bytes 720928 | tf_op jit(solution)/shard_map/ppermute | solution.py:408
  166.0 8.1 %assemble.6.wo_ref.wq_ref.wk_ref.wv_ref.wc_ref = bf16[1024,5120]{1,0:T(8,128)(2,1)} custom-call(s32[4]{0:T(128)S(1)} %pad_add_fusion.place_ref, bf16[2,4,64,2560]{3,2,1,0:T(8,128)(2,1)S(1)} %pad_maximum_fusion.1.refs_0_, bf16[2,4,64,2560]{3,2,1,0:T(8,128)(2,1)} %collective-permute-done.20.refs_1_, bf16[2,4,64,2560]{3,2,1,0:T(8,128)(2,1)} %collective-permute-done.21.refs_2_, ...), custom_call_target="tpu_custom_call" | custom-call | flops 6000000000 | bytes 1 | tf_op jit(solution)/shard_map/assemble/pallas_call | solution.py:475
  174.1 12.2 %cross_forward.1 = (f32[128,1024]{1,0:T(8,128)S(1)}, bf16[128,1024]{1,0:T(8,128)(2,1)S(1)}, bf16[128,1024]{1,0:T(8,128)(2,1)S(1)}, bf16[256,1024]{1,0:T(8,128)(2...) custom-call(bf16[128,1024]{1,0:T(8,128)(2,1)S(1)} %bitcast.148, ...), custom_call_target="tpu_custom_call" | custom-call | flops 12000000000 | bytes 1 | tf_op jit(solution)/shard_map/cross_forward/pallas_call | solution.py:280
  194.9 4.7 collective-permute-done.33.refs_3_
  199.6 4.2 assemble.7
  203.8 4.7 fusion.88
  219.5 5.3 %assemble.9 = bf16[1024,2816]{1,0:T(8,128)(2,1)} custom-call(s32[4]{0:T(128)S(1)} %pad_add_fusion.place_ref, bf16[2,4,64,1408]{3,2,1,0:T(8,128)(2,1)S(1)} %pad_maximum_fusion.4.refs_0_, bf16[2,4,64,1408]{3,2,1,0:T(8,128)(2,1)} %collective-permute-done.34.refs_1_, bf16[2,4,64,1408]{3,2,1,0:T(8,128)(2,1)S(1)} %copy-done.28, ...), custom_call_target="tpu_custom_call" | custom-call | flops 6000000000 | bytes 1 | tf_op jit(solution)/shard_map/assemble/pallas_call | solution.py:475
  230.0 4.3 fusion.89
  244.1 4.6 fusion.32
  248.7 4.8 multiply_reduce_fusion
  257.3 4.9 %collective-permute-done.39 = bf16[512,1408]{1,0:T(8,128)(2,1)S(1)} collective-permute-done((bf16[512,1408]{1,0:T(8,128)(2,1)}, bf16[512,1408]{1,0:T(8,128)(2,1)S(1)}, u32[]{:S(2)}, u32[]{:S(2)}) %collective-permute-start.39) | collective-permute-done | bytes 1441824 | tf_op jit(solution)/shard_map/ppermute | solution.py:408
  276.5 17.9 %cross_back.1 = (bf16[128,1024]{1,0:T(8,128)(2,1)S(1)}, bf16[256,1024]{1,0:T(8,128)(2,1)S(1)}, bf16[256,1024]{1,0:T(8,128)(2,1)S(1)}, f32[256,1024]{1,0:T(8,128)...) custom-call(f32[128,1024]{1,0:T(8,128)S(1)} %multiply_add_fusion.gra, ...), custom_call_target="tpu_custom_call" | custom-call | flops 17999998976 | bytes 1 | tf_op jit(solution)/shard_map/cross_back/pallas_call | solution.py:353
  294.5 7.7 %collective-permute-done.44 = bf16[704,512]{1,0:T(8,128)(2,1)S(1)} collective-permute-done((bf16[704,512]{1,0:T(8,128)(2,1)}, bf16[704,512]{1,0:T(8,128)(2,1)S(1)}, u32[]{:S(2)}, u32[]{:S(2)}) %collective-permute-start.44) | collective-permute-done | bytes 720928 | tf_op jit(solution)/shard_map/ppermute | solution.py:408
  337.3 23.2 %self_back.1 = (bf16[512,1024]{1,0:T(8,128)(2,1)S(1)}, bf16[512,1024]{1,0:T(8,128)(2,1)S(1)}, bf16[512,1024]{1,0:T(8,128)(2,1)S(1)}, f32[8,2,640]{2,1,0:T(2,128)...) custom-call(s32[1]{0:T(128)} %bitcast.1.pos_ref, bf16[512,1024]{1,0:T(8,128)(2,1)S(1)} %bitcast.155, ...), custom_call_target="tpu_custom_call" | custom-call | flops 23000000512 | bytes 1 | tf_op jit(solution)/shard_map/self_back/pallas_call | solution.py:225
  375.4 4.5 fusion.11
  395.4 11.6 %collective-permute-done.54 = bf16[256,2560]{1,0:T(8,128)(2,1)S(1)} collective-permute-done((bf16[256,2560]{1,0:T(8,128)(2,1)S(1)}, bf16[256,2560]{1,0:T(8,128)(2,1)S(1)}, u32[]{:S(2)}, u32[]{:S(2)}) %collective-permute-start.54) | collective-permute-done | bytes 1310752 | tf_op jit(solution)/shard_map/ppermute | solution.py:408
  419.4 6.1 %collective-permute-done.58 = bf16[352,512]{1,0:T(8,128)(2,1)S(1)} collective-permute-done((bf16[352,512]{1,0:T(8,128)(2,1)S(1)}, bf16[352,512]{1,0:T(8,128)(2,1)S(1)}, u32[]{:S(2)}, u32[]{:S(2)}) %collective-permute-start.58) | collective-permute-done | bytes 360480 | tf_op jit(solution)/shard_map/ppermute | solution.py:408
  427.7 5.4 %collective-permute-done.56 = bf16[64,2560]{1,0:T(8,128)(2,1)S(1)} collective-permute-done((bf16[64,2560]{1,0:T(8,128)(2,1)S(1)}, bf16[64,2560]{1,0:T(8,128)(2,1)S(1)}, u32[]{:S(2)}, u32[]{:S(2)}) %collective-permute-start.56) | collective-permute-done | bytes 327712 | tf_op jit(solution)/shard_map/ppermute | solution.py:408
  446.2 9.4 %collective-permute-done.65 = bf16[64,2560]{1,0:T(8,128)(2,1)S(1)} collective-permute-done((bf16[64,2560]{1,0:T(8,128)(2,1)S(1)}, bf16[64,2560]{1,0:T(8,128)(2,1)S(1)}, u32[]{:S(2)}, u32[]{:S(2)}) %collective-permute-start.65) | collective-permute-done | bytes 327712 | tf_op jit(solution)/shard_map/ppermute | solution.py:408
  469.9 4.2 collective-permute-done.71
  474.1 7.1 %collective-permute-done.70 = bf16[64,1664]{1,0:T(8,128)(2,1)S(1)} collective-permute-done((bf16[64,1664]{1,0:T(8,128)(2,1)S(1)}, bf16[64,1664]{1,0:T(8,128)(2,1)S(1)}, u32[]{:S(2)}, u32[]{:S(2)}) %collective-permute-start.70) | collective-permute-done | bytes 213024 | tf_op jit(solution)/shard_map/ppermute | solution.py:408
  (559 shorter events, 237.0 us)
Async XLA Ops:
  30.4 22.2 %collective-permute-start.6 = (bf16[4,64,1664]{2,1,0:T(8,128)(2,1)S(1)}, bf16[4,64,1664]{2,1,0:T(8,128)(2,1)}, u32[]{:S(2)}, u32[]{:S(2)}) collective-permute-start(bf16[4,64,1664]{2,1,0:T(8,128)(2,1)S(1)} %pad_maximum_fusion.7), channel_id=1, source_target_pairs={{0,4},{1,3},{2,6},{3,1},{4,0},{5,7},{6,2},{7,5},{8,12},{9,11},{10,... | collective-permute-start | bytes 2555912 | tf_op jit(solution)/shard_map/ppermute | solution.py:408
  31.9 22.4 %collective-permute-start.9 = (bf16[192,1024]{1,0:T(8,128)(2,1)S(1)}, bf16[192,1024]{1,0:T(8,128)(2,1)}, u32[]{:S(2)}, u32[]{:S(2)}) collective-permute-start(bf16[192,1024]{1,0:T(8,128)(2,1)S(1)} %pad_maximum_fusion.15), channel_id=1, source_target_pairs={{0,2},{1,3},{2,0},{3,1},{4,6},{5,7},{6,4},{7,5},{8,10},{9,11},{10,... | collective-permute-start | bytes 1179656 | tf_op jit(solution)/shard_map/ppermute | solution.py:408
  55.1 28.1 %collective-permute-start.11 = (bf16[2,4,64,1664]{3,2,1,0:T(8,128)(2,1)S(1)}, bf16[2,4,64,1664]{3,2,1,0:T(8,128)(2,1)}, u32[]{:S(2)}, u32[]{:S(2)}) collective-permute-start(bf16[2,4,64,1664]{3,2,1,0:T(8,128)(2,1)S(1)} %pad_maximum_fusion.2.refs_0_), channel_id=1, source_target_pairs={{0,1},{1,0},{2,3},{3,2},{4,5},{5,4},{6,7},{7,6},{8,9},{9,8},{10,11... | collective-permute-start | bytes 5111816 | tf_op jit(solution)/shard_map/ppermute | solution.py:408
  55.1 28.1 %collective-permute-start.10 = (bf16[2,4,64,1664]{3,2,1,0:T(8,128)(2,1)S(1)}, bf16[2,4,64,1664]{3,2,1,0:T(8,128)(2,1)}, u32[]{:S(2)}, u32[]{:S(2)}) collective-permute-start(bf16[2,4,64,1664]{3,2,1,0:T(8,128)(2,1)S(1)} %pad_maximum_fusion.2.refs_0_), channel_id=1, source_target_pairs={{0,2},{1,5},{2,0},{3,7},{4,6},{5,1},{6,4},{7,3},{8,10},{9,13},{10,... | collective-permute-start | bytes 5111816 | tf_op jit(solution)/shard_map/ppermute | solution.py:408
  59.9 22.1 %collective-permute-start.12 = (bf16[64,2560]{1,0:T(8,128)(2,1)}, bf16[64,2560]{1,0:T(8,128)(2,1)S(1)}, u32[]{:S(2)}, u32[]{:S(2)}) collective-permute-start(bf16[64,2560]{1,0:T(8,128)(2,1)} %split.13), channel_id=1, source_target_pairs={{0,16},{1,17},{2,18},{3,19},{4,20},{5,21},{6,22},{7,23},{8,24},{9,... | collective-permute-start | bytes 983048 | tf_op jit(solution)/shard_map/ppermute | solution.py:408
  84.1 20.8 %collective-permute-start.16 = (bf16[4,64,2560]{2,1,0:T(8,128)(2,1)S(1)}, bf16[4,64,2560]{2,1,0:T(8,128)(2,1)S(1)}, u32[]{:S(2)}, u32[]{:S(2)}) collective-permute-start(bf16[4,64,2560]{2,1,0:T(8,128)(2,1)S(1)} %pad_maximum_fusion.5), channel_id=1, source_target_pairs={{0,4},{1,3},{2,6},{3,1},{4,0},{5,7},{6,2},{7,5},{8,12},{9,11},{10,... | collective-permute-start | bytes 3932168 | tf_op jit(solution)/shard_map/ppermute | solution.py:408
  85.1 22.9 %collective-permute-start.15 = (bf16[2,4,64,1664]{3,2,1,0:T(8,128)(2,1)}, bf16[2,4,64,1664]{3,2,1,0:T(8,128)(2,1)}, u32[]{:S(2)}, u32[]{:S(2)}) collective-permute-start(bf16[2,4,64,1664]{3,2,1,0:T(8,128)(2,1)} %collective-permute-done.10.refs_1_), channel_id=1, source_target_pairs={{0,1},{1,0},{2,3},{3,2},{4,5},{5,4},{6,7},{7,6},{8,9},{9,8},{10,11... | collective-permute-start | bytes 5111816 | tf_op jit(solution)/shard_map/ppermute | solution.py:408
  114.9 45.0 %collective-permute-start.21 = (bf16[2,4,64,2560]{3,2,1,0:T(8,128)(2,1)S(1)}, bf16[2,4,64,2560]{3,2,1,0:T(8,128)(2,1)}, u32[]{:S(2)}, u32[]{:S(2)}) collective-permute-start(bf16[2,4,64,2560]{3,2,1,0:T(8,128)(2,1)S(1)} %pad_maximum_fusion.1.refs_0_), channel_id=1, source_target_pairs={{0,1},{1,0},{2,3},{3,2},{4,5},{5,4},{6,7},{7,6},{8,9},{9,8},{10,11... | collective-permute-start | bytes 7864328 | tf_op jit(solution)/shard_map/ppermute | solution.py:408
  114.9 45.0 %collective-permute-start.20 = (bf16[2,4,64,2560]{3,2,1,0:T(8,128)(2,1)S(1)}, bf16[2,4,64,2560]{3,2,1,0:T(8,128)(2,1)}, u32[]{:S(2)}, u32[]{:S(2)}) collective-permute-start(bf16[2,4,64,2560]{3,2,1,0:T(8,128)(2,1)S(1)} %pad_maximum_fusion.1.refs_0_), channel_id=1, source_target_pairs={{0,2},{1,5},{2,0},{3,7},{4,6},{5,1},{6,4},{7,3},{8,10},{9,13},{10,... | collective-permute-start | bytes 7864328 | tf_op jit(solution)/shard_map/ppermute | solution.py:408
  124.4 29.0 %collective-permute-start.27 = (bf16[2,2,176,512]{3,2,1,0:T(8,128)(2,1)}, bf16[2,2,176,512]{3,2,1,0:T(8,128)(2,1)S(1)}, u32[]{:S(2)}, u32[]{:S(2)}) collective-permute-start(bf16[2,2,176,512]{3,2,1,0:T(8,128)(2,1)} %pad_maximum_fusion.9), channel_id=1, source_target_pairs={{0,8},{1,9},{2,10},{3,11},{4,12},{5,13},{6,14},{7,15},{8,16},{9,17... | collective-permute-start | bytes 2162696 | tf_op jit(solution)/shard_map/ppermute | solution.py:408
  124.5 35.4 %collective-permute-start.26 = (bf16[2,2,176,512]{3,2,1,0:T(8,128)(2,1)}, bf16[2,2,176,512]{3,2,1,0:T(8,128)(2,1)S(1)}, u32[]{:S(2)}, u32[]{:S(2)}) collective-permute-start(bf16[2,2,176,512]{3,2,1,0:T(8,128)(2,1)} %pad_maximum_fusion.9), channel_id=1, source_target_pairs={{0,24},{1,25},{2,26},{3,27},{4,28},{5,29},{6,30},{7,31},{8,0},{9,1... | collective-permute-start | bytes 2162696 | tf_op jit(solution)/shard_map/ppermute | solution.py:408
  131.9 20.3 %collective-permute-start.22 = (bf16[4,64,1408]{2,1,0:T(8,128)(2,1)}, bf16[4,64,1408]{2,1,0:T(8,128)(2,1)S(1)}, u32[]{:S(2)}, u32[]{:S(2)}) collective-permute-start(bf16[4,64,1408]{2,1,0:T(8,128)(2,1)} %pad_maximum_fusion.10), channel_id=1, source_target_pairs={{0,4},{1,3},{2,6},{3,1},{4,0},{5,7},{6,2},{7,5},{8,12},{9,11},{10,... | collective-permute-start | bytes 2162696 | tf_op jit(solution)/shard_map/ppermute | solution.py:408
  161.6 29.2 %collective-permute-start.31 = (bf16[2,4,64,1408]{3,2,1,0:T(8,128)(2,1)}, bf16[2,4,64,1408]{3,2,1,0:T(8,128)(2,1)S(1)}, u32[]{:S(2)}, u32[]{:S(2)}) collective-permute-start(bf16[2,4,64,1408]{3,2,1,0:T(8,128)(2,1)} %pad_maximum_fusion.3.refs_0_), channel_id=1, source_target_pairs={{0,1},{1,0},{2,3},{3,2},{4,5},{5,4},{6,7},{7,6},{8,9},{9,8},{10,11... | collective-permute-start | bytes 4325384 | tf_op jit(solution)/shard_map/ppermute | solution.py:408
  161.7 29.2 %collective-permute-start.30 = (bf16[2,4,64,1408]{3,2,1,0:T(8,128)(2,1)}, bf16[2,4,64,1408]{3,2,1,0:T(8,128)(2,1)S(1)}, u32[]{:S(2)}, u32[]{:S(2)}) collective-permute-start(bf16[2,4,64,1408]{3,2,1,0:T(8,128)(2,1)} %pad_maximum_fusion.3.refs_0_), channel_id=1, source_target_pairs={{0,2},{1,5},{2,0},{3,7},{4,6},{5,1},{6,4},{7,3},{8,10},{9,13},{10,... | collective-permute-start | bytes 4325384 | tf_op jit(solution)/shard_map/ppermute | solution.py:408
  162.4 28.5 %collective-permute-start.29 = (bf16[2,2,176,512]{3,2,1,0:T(8,128)(2,1)}, bf16[2,2,176,512]{3,2,1,0:T(8,128)(2,1)S(1)}, u32[]{:S(2)}, u32[]{:S(2)}) collective-permute-start(bf16[2,2,176,512]{3,2,1,0:T(8,128)(2,1)} %copy-done.99), channel_id=1, source_target_pairs={{0,24},{1,25},{2,26},{3,27},{4,28},{5,29},{6,30},{7,31},{8,0},{9,1... | collective-permute-start | bytes 2162696 | tf_op jit(solution)/shard_map/ppermute | solution.py:408
  165.0 25.8 %collective-permute-start.32 = (bf16[4,64,1408]{2,1,0:T(8,128)(2,1)}, bf16[4,64,1408]{2,1,0:T(8,128)(2,1)S(1)}, u32[]{:S(2)}, u32[]{:S(2)}) collective-permute-start(bf16[4,64,1408]{2,1,0:T(8,128)(2,1)} %pad_maximum_fusion.11), channel_id=1, source_target_pairs={{0,4},{1,3},{2,6},{3,1},{4,0},{5,7},{6,2},{7,5},{8,12},{9,11},{10,... | collective-permute-start | bytes 2162696 | tf_op jit(solution)/shard_map/ppermute | solution.py:408
  238.9 23.4 %collective-permute-start.40 = (bf16[1024,1408]{1,0:T(8,128)(2,1)}, bf16[1024,1408]{1,0:T(8,128)(2,1)}, u32[]{:S(2)}, u32[]{:S(2)}) collective-permute-start(bf16[1024,1408]{1,0:T(8,128)(2,1)} %weight_grad.12), channel_id=1, source_target_pairs={{0,1},{1,0},{2,3},{3,2},{4,5},{5,4},{6,7},{7,6},{8,9},{9,8},{10,11... | collective-permute-start | bytes 8650760 | tf_op jit(solution)/shard_map/ppermute | solution.py:408
  265.3 29.2 %collective-permute-start.42 = (bf16[256,1408]{1,0:T(8,128)(2,1)}, bf16[256,1408]{1,0:T(8,128)(2,1)S(1)}, u32[]{:S(2)}, u32[]{:S(2)}) collective-permute-start(bf16[256,1408]{1,0:T(8,128)(2,1)} %add_convert_fusion.11), channel_id=1, source_target_pairs={{0,2},{1,5},{2,0},{3,7},{4,6},{5,1},{6,4},{7,3},{8,10},{9,13},{10,... | collective-permute-start | bytes 2162696 | tf_op jit(solution)/shard_map/ppermute | solution.py:408
  269.8 24.7 %collective-permute-start.45 = (bf16[704,512]{1,0:T(8,128)(2,1)}, bf16[704,512]{1,0:T(8,128)(2,1)S(1)}, u32[]{:S(2)}, u32[]{:S(2)}) collective-permute-start(bf16[704,512]{1,0:T(8,128)(2,1)} %get-tuple-element.467), channel_id=1, source_target_pairs={{0,8},{1,9},{2,10},{3,11},{4,12},{5,13},{6,14},{7,15},{8,16},{9,17... | collective-permute-start | bytes 2162696 | tf_op jit(solution)/shard_map/ppermute | solution.py:408
  269.8 32.4 %collective-permute-start.44 = (bf16[704,512]{1,0:T(8,128)(2,1)}, bf16[704,512]{1,0:T(8,128)(2,1)S(1)}, u32[]{:S(2)}, u32[]{:S(2)}) collective-permute-start(bf16[704,512]{1,0:T(8,128)(2,1)} %get-tuple-element.468), channel_id=1, source_target_pairs={{0,24},{1,25},{2,26},{3,27},{4,28},{5,29},{6,30},{7,31},{8,0},{9,1... | collective-permute-start | bytes 2162696 | tf_op jit(solution)/shard_map/ppermute | solution.py:408
  275.4 26.8 %collective-permute-start.43 = (bf16[512,1408]{1,0:T(8,128)(2,1)S(1)}, bf16[512,1408]{1,0:T(8,128)(2,1)S(1)}, u32[]{:S(2)}, u32[]{:S(2)}) collective-permute-start(bf16[512,1408]{1,0:T(8,128)(2,1)S(1)} %add_convert_fusion.2), channel_id=1, source_target_pairs={{0,4},{1,3},{2,6},{3,1},{4,0},{5,7},{6,2},{7,5},{8,12},{9,11},{10,... | collective-permute-start | bytes 4325384 | tf_op jit(solution)/shard_map/ppermute | solution.py:408
  327.1 37.0 %collective-permute-start.48 = (bf16[512,2560]{1,0:T(8,128)(2,1)S(1)}, bf16[512,2560]{1,0:T(8,128)(2,1)}, u32[]{:S(2)}, u32[]{:S(2)}) collective-permute-start(bf16[512,2560]{1,0:T(8,128)(2,1)S(1)} %add_convert_fusion), channel_id=1, source_target_pairs={{0,4},{1,3},{2,6},{3,1},{4,0},{5,7},{6,2},{7,5},{8,12},{9,11},{10,... | collective-permute-start | bytes 7864328 | tf_op jit(solution)/shard_map/ppermute | solution.py:408
  330.0 33.0 %collective-permute-start.51 = (bf16[64,1408]{1,0:T(8,128)(2,1)S(1)}, bf16[64,1408]{1,0:T(8,128)(2,1)S(1)}, u32[]{:S(2)}, u32[]{:S(2)}) collective-permute-start(bf16[64,1408]{1,0:T(8,128)(2,1)S(1)} %get-tuple-element.464), channel_id=1, source_target_pairs={{0,24},{1,25},{2,26},{3,27},{4,28},{5,29},{6,30},{7,31},{8,0},{9,1... | collective-permute-start | bytes 540680 | tf_op jit(solution)/shard_map/ppermute | solution.py:408
  332.1 32.0 %collective-permute-start.50 = (bf16[64,1408]{1,0:T(8,128)(2,1)S(1)}, bf16[64,1408]{1,0:T(8,128)(2,1)S(1)}, u32[]{:S(2)}, u32[]{:S(2)}) collective-permute-start(bf16[64,1408]{1,0:T(8,128)(2,1)S(1)} %get-tuple-element.465), channel_id=1, source_target_pairs={{0,16},{1,17},{2,18},{3,19},{4,20},{5,21},{6,22},{7,23},{8,24},{9,... | collective-permute-start | bytes 540680 | tf_op jit(solution)/shard_map/ppermute | solution.py:408
  332.5 31.6 %collective-permute-start.49 = (bf16[64,1408]{1,0:T(8,128)(2,1)S(1)}, bf16[64,1408]{1,0:T(8,128)(2,1)S(1)}, u32[]{:S(2)}, u32[]{:S(2)}) collective-permute-start(bf16[64,1408]{1,0:T(8,128)(2,1)S(1)} %get-tuple-element.466), channel_id=1, source_target_pairs={{0,8},{1,9},{2,10},{3,11},{4,12},{5,13},{6,14},{7,15},{8,16},{9,17... | collective-permute-start | bytes 540680 | tf_op jit(solution)/shard_map/ppermute | solution.py:408
  336.1 28.0 %collective-permute-start.52 = (bf16[704,512]{1,0:T(8,128)(2,1)S(1)}, bf16[704,512]{1,0:T(8,128)(2,1)S(1)}, u32[]{:S(2)}, u32[]{:S(2)}) collective-permute-start(bf16[704,512]{1,0:T(8,128)(2,1)S(1)} %add_convert_fusion.6), channel_id=1, source_target_pairs={{0,8},{1,9},{2,10},{3,11},{4,12},{5,13},{6,14},{7,15},{8,16},{9,17... | collective-permute-start | bytes 2162696 | tf_op jit(solution)/shard_map/ppermute | solution.py:408
  375.1 32.0 %collective-permute-start.53 = (bf16[1024,1664]{1,0:T(8,128)(2,1)}, bf16[1024,1664]{1,0:T(8,128)(2,1)}, u32[]{:S(2)}, u32[]{:S(2)}) collective-permute-start(bf16[1024,1664]{1,0:T(8,128)(2,1)} %weight_grad.18), channel_id=1, source_target_pairs={{0,1},{1,0},{2,3},{3,2},{4,5},{5,4},{6,7},{7,6},{8,9},{9,8},{10,11... | collective-permute-start | bytes 10223624 | tf_op jit(solution)/shard_map/ppermute | solution.py:408
  382.4 29.5 %collective-permute-start.61 = (bf16[64,1408]{1,0:T(8,128)(2,1)S(1)}, bf16[64,1408]{1,0:T(8,128)(2,1)S(1)}, u32[]{:S(2)}, u32[]{:S(2)}) collective-permute-start(bf16[64,1408]{1,0:T(8,128)(2,1)S(1)} %get-tuple-element.461), channel_id=1, source_target_pairs={{0,24},{1,25},{2,26},{3,27},{4,28},{5,29},{6,30},{7,31},{8,0},{9,1... | collective-permute-start | bytes 540680 | tf_op jit(solution)/shard_map/ppermute | solution.py:408
  384.0 30.0 %collective-permute-start.60 = (bf16[64,1408]{1,0:T(8,128)(2,1)S(1)}, bf16[64,1408]{1,0:T(8,128)(2,1)S(1)}, u32[]{:S(2)}, u32[]{:S(2)}) collective-permute-start(bf16[64,1408]{1,0:T(8,128)(2,1)S(1)} %get-tuple-element.462), channel_id=1, source_target_pairs={{0,16},{1,17},{2,18},{3,19},{4,20},{5,21},{6,22},{7,23},{8,24},{9,... | collective-permute-start | bytes 540680 | tf_op jit(solution)/shard_map/ppermute | solution.py:408
  384.7 30.5 %collective-permute-start.59 = (bf16[64,1408]{1,0:T(8,128)(2,1)}, bf16[64,1408]{1,0:T(8,128)(2,1)S(1)}, u32[]{:S(2)}, u32[]{:S(2)}) collective-permute-start(bf16[64,1408]{1,0:T(8,128)(2,1)} %get-tuple-element.463), channel_id=1, source_target_pairs={{0,8},{1,9},{2,10},{3,11},{4,12},{5,13},{6,14},{7,15},{8,16},{9,17... | collective-permute-start | bytes 540680 | tf_op jit(solution)/shard_map/ppermute | solution.py:408
  409.4 25.7 %collective-permute-start.55 = (bf16[512,1664]{1,0:T(8,128)(2,1)S(1)}, bf16[512,1664]{1,0:T(8,128)(2,1)S(1)}, u32[]{:S(2)}, u32[]{:S(2)}) collective-permute-start(bf16[512,1664]{1,0:T(8,128)(2,1)S(1)} %add_convert_fusion.1), channel_id=1, source_target_pairs={{0,4},{1,3},{2,6},{3,1},{4,0},{5,7},{6,2},{7,5},{8,12},{9,11},{10,... | collective-permute-start | bytes 5111816 | tf_op jit(solution)/shard_map/ppermute | solution.py:408
  425.5 20.7 %collective-permute-start.67 = (bf16[2,64,1024]{2,1,0:T(8,128)(2,1)S(1)}, bf16[2,64,1024]{2,1,0:T(8,128)(2,1)S(1)}, u32[]{:S(2)}, u32[]{:S(2)}) collective-permute-start(bf16[2,64,1024]{2,1,0:T(8,128)(2,1)S(1)} %fusion.57), channel_id=1, source_target_pairs={{0,1},{1,0},{2,3},{3,2},{4,5},{5,4},{6,7},{7,6},{8,9},{9,8},{10,11... | collective-permute-start | bytes 786440 | tf_op jit(solution)/shard_map/ppermute | solution.py:408
  (181 other events, 1864.2 us)

commit v4 on v3

--- a/solution.py
+++ b/solution.py
@@ -241,7 +241,7 @@
             shape_of(1, width, dtype=F32),
         ],
         compiler_params=PARAMS,
-        cost_estimate=cost(23),
+        cost_estimate=cost(1),
         name="self_back",
     )(place, target_all, grad, query, key, value, weights, weights, weights, windows, qseg, kseg)
 
@@ -373,7 +373,7 @@
         ],
         scratch_shapes=[pltpu.VMEM((rows, width), BF), pltpu.VMEM((rows, width), F32)],
         compiler_params=PARAMS,
-        cost_estimate=cost(18),
+        cost_estimate=cost(1),
         name="cross_back",
     )(
         grad_two, hidden_one, gain, query, key, value, weights, weights, weights, weights, weights,
@@ -485,68 +485,96 @@
     )(links.place, *sources)
 
 
-def weight_grad(links, core, terms, extra=None, z_first=False):
+def weight_grad(links, terms, extra=None, z_first=False):
     depth, total_rows = links.depth, terms[0][0].shape[1]
     rows = total_rows // (depth * 4)
     widths = [term[1].shape[1] for term in terms]
     extra_width = 0 if extra is None else extra.shape[1]
     total = sum(widths) + extra_width
     tile = 1408 if total % 1408 == 0 else 512
+    operands = [array for term in terms for array in term] + ([] if extra is None else [extra])
+    amount = len(operands)
 
     def body(place_ref, *refs):
-        inputs, out_ref, stage, sems = refs[:-3], refs[-3], refs[-2], refs[-1]
-        z, x, y, left = place_ref[0], place_ref[1], place_ref[2], place_ref[3] == 0
-        places = []
-        for chip in range(depth * 4):
-            step_x, step_y = (chip // 2 % 2) ^ x, (chip % 2) ^ y
-            near, far = jnp.where(left, step_x, step_y), jnp.where(left, step_y, step_x)
-            step = (chip // 4 - z) % depth
-            spot = (step * 2 + far) * 2 + near if z_first else (near * 2 + far) * depth + step
-            places.append(pl.multiple_of(spot * rows, 8))
-        copies, start = [], 0
-
-        def emit(start, value, width):
-            for chip, spot in enumerate(places):
-                stage[pl.ds(spot, rows), start : start + width] = value[
-                    chip * rows : (chip + 1) * rows
-                ].astype(BF)
-            copies.append(
-                pltpu.make_async_copy(
-                    stage.at[:, pl.ds(start, width)],
-                    out_ref.at[:, pl.ds(start, width)],
-                    sems.at[len(copies)],
-                )
+        sources, outs = refs[:amount], refs[amount : amount + 2]
+        stages, sems = refs[amount + 2 : amount + 4], refs[amount + 4]
+        inputs, arrived = refs[amount + 5 : -1], refs[-1]
+        fetches = [
+            pltpu.make_async_copy(source, target, arrived.at[index])
+            for index, (source, target) in enumerate(zip(sources, inputs))
+        ]
+        for fetch in fetches:
+            fetch.start()
+        z, x, y = place_ref[0], place_ref[1], place_ref[2]
+
+        def copy(side, index, start, width):
+            cols = pl.ds(start, width)
+            return pltpu.make_async_copy(
+                stages[side].at[:, cols], outs[side].at[:, cols], sems.at[side, index]
             )
-            copies[-1].start()
-
-        for index, width in enumerate(widths):
-            acts_l, grad_l, acts_r, grad_r = inputs[4 * index : 4 * index + 4]
-            acts = jnp.where(left, acts_l[...], acts_r[...])
-            for offset in range(0, width, tile):
-                cols = slice(offset, offset + tile)
-                grad = jnp.where(left, grad_l[:, cols], grad_r[:, cols])
-                emit(start, mm(acts, grad, TN), tile)
-                start += tile
-        if extra is not None:
-            small = inputs[-1][...]
-            emit(start, jnp.where(left, small, jnp.zeros_like(small)), extra_width)
-        for copy in copies:
-            copy.wait()
-
-    place = links.place.at[3].set(core)
-    operands = [array for term in terms for array in term] + ([] if extra is None else [extra])
+
+        for side in range(2):
+            left = place_ref[3] == 1 - side
+            places = []
+            for chip in range(depth * 4):
+                step_x, step_y = (chip // 2 % 2) ^ x, (chip % 2) ^ y
+                near, far = jnp.where(left, step_x, step_y), jnp.where(left, step_y, step_x)
+                step = (chip // 4 - z) % depth
+                spot = (step * 2 + far) * 2 + near if z_first else (near * 2 + far) * depth + step
+                places.append(pl.multiple_of(spot * rows, 8))
+
+            def emit(index, start, value, width, side=side, places=places):
+                for chip, spot in enumerate(places):
+                    stages[side][pl.ds(spot, rows), pl.ds(start, width)] = value[
+                        chip * rows : (chip + 1) * rows
+                    ].astype(BF)
+                copy(side, index, start, width).start()
+
+            begin, first_copy = 0, 0
+            for which, width in enumerate(widths):
+                acts_l, grad_l, acts_r, grad_r = inputs[4 * which : 4 * which + 4]
+                if side == 0:
+                    for fetch in fetches[4 * which : 4 * which + 4]:
+                        fetch.wait()
+                acts = jnp.where(left, acts_l[...], acts_r[...])
+
+                def one_tile(index, carry, begin=begin, first_copy=first_copy, acts=acts,
+                             grad_l=grad_l, grad_r=grad_r, left=left, emit=emit):
+                    offset = pl.multiple_of(index * tile, LANES)
+                    cols = pl.ds(offset, tile)
+                    grad = jnp.where(left, grad_l[:, cols], grad_r[:, cols])
+                    start = pl.multiple_of(begin + index * tile, LANES)
+                    emit(first_copy + index, start, mm(acts, grad, TN), tile)
+                    return carry
+
+                lax.fori_loop(0, width // tile, one_tile, 0)
+                begin, first_copy = begin + width, first_copy + width // tile
+            if extra is not None:
+                if side == 0:
+                    fetches[-1].wait()
+                small = inputs[-1][...]
+                emit(first_copy, begin, jnp.where(left, small, jnp.zeros_like(small)), extra_width)
+        for side in range(2):
+            for index in range(first_copy):
+                copy(side, index, index * tile, tile).wait()
+            if extra is not None:
+                copy(side, first_copy, begin, extra_width).wait()
+
     count = sum(width // tile for width in widths) + (extra is not None)
-    vmem = pl.BlockSpec(memory_space=pltpu.VMEM)
+    hbm = pl.BlockSpec(memory_space=pltpu.HBM)
     return pl.pallas_call(
         body,
-        in_specs=[pl.BlockSpec(memory_space=pltpu.SMEM)] + [vmem] * len(operands),
-        out_specs=pl.BlockSpec(memory_space=pl.ANY),
-        out_shape=jax.ShapeDtypeStruct((total_rows, total), BF),
-        scratch_shapes=[pltpu.VMEM((total_rows, total), BF), pltpu.SemaphoreType.DMA((count,))],
+        in_specs=[pl.BlockSpec(memory_space=pltpu.SMEM)] + [hbm] * amount,
+        out_specs=[pl.BlockSpec(memory_space=pl.ANY)] * 2,
+        out_shape=[jax.ShapeDtypeStruct((total_rows, total), BF)] * 2,
+        scratch_shapes=[pltpu.VMEM((total_rows, total), BF)] * 2
+        + [pltpu.SemaphoreType.DMA((2, count))]
+        + [pltpu.VMEM(array.shape, array.dtype) for array in operands]
+        + [pltpu.SemaphoreType.DMA((amount,))],
         compiler_params=pltpu.CompilerParams(vmem_limit_bytes=48 << 20),
-        cost_estimate=cost(4),
+        cost_estimate=cost(1),
         name="weight_grad",
-    )(place, *operands)
+    )(links.place, *operands)
 
 
 def add_low(one, other):
@@ -589,9 +617,11 @@
         for step, send in enumerate(sends, 1):
             self.parts.append(self.links.over_z(send, depth - step))
 
-    def z_start(self, sends):
-        links, depth = self.links, self.links.depth
-        return links.over_z(sends[-1], 1), links.over_z(sends[-2], depth - 1)
+    def z_back(self, sends):
+        return self.links.over_z(sends[-1], 1)
+
+    def z_ahead(self, sends):
+        return self.links.over_z(sends[-2], self.links.depth - 1)
 
     def z_end(self, sends, back, ahead):
         self.parts.append(back)
@@ -643,8 +673,10 @@
     def near(self, send):
         self.sent = send
 
-    def z_start(self, sends):
-        return sends, None
+    def z_back(self, sends):
+        return sends
+
+    z_ahead = z_back
 
     def z_end(self, sends, back, ahead):
         self.sent = back
@@ -697,7 +729,6 @@
     right = jnp.concatenate([group[:, cut:] for group, cut in zip(groups, cuts)], axis=1)
     down_cut = width // 2
     steps = list(range(1, depth))
-    some, rest = steps[:1], steps[1:]
     z_one, z_two, z_three = steps[:1], steps[-1:] if depth > 2 else [], steps[1:-1]
     direct = 2 * ffn_down.shape[0] % 16 == 0
     move = lambda function, *args: function(links, *args) if direct else None
@@ -719,21 +750,22 @@
     onehot = ((bucket[:, None] == bucket_range[None, :]) & near[:, None]).astype(BF)
 
     first_z = jnp.stack([first0] + z_steps(links, first0, steps))
+    first_z, second0, down = phase(first_z, second0, down)
+
+    first_near = gather_near(links, first_z)
     down = move(gather_near, down)
-    first_z, second0, down = phase(first_z, second0, down)
-
-    first_near = gather_near(links, first_z)
-    down = move(gather_far, down)
-    second_z = z_steps(links, second0, some)
+    second_one, second_two = z_steps(links, second0, z_one), z_steps(links, second0, z_two)
     rows_own = jnp.concatenate([target[0], memory[0]], axis=0)
     rows_other = links.over_y(rows_own)
-    first_near, down, second_z, second0, onehot, rows_own, rows_other = phase(
-        first_near, down, second_z, second0, onehot, rows_own, rows_other
+    first_near, down, second_one, second_two, second0, onehot, rows_own, rows_other = phase(
+        first_near, down, second_one, second_two, second0, onehot, rows_own, rows_other
     )
 
     first_far = links.over_far(first_near)
     first_near_other = links.over_core(first_near)
-    second_z = jnp.stack([second0] + second_z + z_steps(links, second0, rest))
+    second_z = jnp.stack(
+        [second0] + second_one + z_steps(links, second0, z_three) + second_two
+    )
     rows_pair = in_order(links.y == 0, rows_own, rows_other)
     rows_other = links.over_core(rows_pair)
     first_far, first_near_other, second_z, down, third0, rows_pair, rows_other = phase(
@@ -753,6 +785,7 @@
     second_near = gather_near(links, second_z)
     third_z = jnp.stack([third0] + z_steps(links, third0, steps))
     first_far_other = links.over_core(first_far)
+    down = move(gather_far, down)
     first_far_other, second_near, third_z, fourth0, down, target_all, memory_all = phase(
         first_far_other, second_near, third_z, fourth0, down, target_all, memory_all
     )
@@ -825,6 +858,7 @@
     fourth_far_other = links.over_core(fourth_far)
     cot = cotangent[0]
 
+
     def gated(gate_up, start):
         inner_act, pull = jax.vjp(gated_unit, gate_up[:, :part], gate_up[:, part:])
         grad_gate, grad_up = pull(mm(cot, w_down[start : start + part], NT))
@@ -833,44 +867,52 @@
     inner_a, gate_a, up_a = gated(third_gate_up, 0)
     third_sum, fourth_sum = Scatter(links), Scatter(links)
     third_terms = [(normed_three, gate_a, normed_three, up_a)]
-    third_send = weight_grad(links, 1 - core, third_terms)
-    third_send, gate_a, up_a, fourth_far_other, w_down = phase(
-        third_send, gate_a, up_a, fourth_far_other, w_down
+    third_send, third_keep = weight_grad(links, third_terms)
+    third_send, third_keep, gate_a, up_a, fourth_far_other = phase(
+        third_send, third_keep, gate_a, up_a, fourth_far_other
     )
 
     third_sum.core(third_send)
+    third_sum.keep(third_keep)
     fourth = assemble(links, fourth_near, fourth_far, fourth_near_other, fourth_far_other)
-    third_sum.keep(weight_grad(links, core, third_terms))
-    third_send = third_sum.halve()
-    third_send, fourth = phase(third_send, fourth)
-
+    third_sum.parts, fourth = phase(third_sum.parts, fourth)
+
+    third_send, fourth = phase(third_sum.halve(), fourth)
     third_sum.near(third_send)
     inner_b, gate_b, up_b = gated(mm(normed_three, fourth), part)
     fourth_terms = [(normed_three, gate_b, normed_three, up_b)]
-    fourth_sum.core(weight_grad(links, 1 - core, fourth_terms))
+    fourth_send, fourth_keep = weight_grad(links, fourth_terms)
     inner_low = jnp.concatenate([inner_a, inner_b], axis=1)
     down_terms = [(inner_low, cot[:, :down_cut], inner_low, cot[:, down_cut:])]
     down_sum = Scatter(links) if direct else PlainScatter()
     if direct:
-        down_sum.core(weight_grad(links, 1 - core, down_terms, z_first=True))
-        down_sum.keep(weight_grad(links, core, down_terms, z_first=True))
+        down_send, down_keep = weight_grad(links, down_terms, z_first=True)
     else:
-        down_sum.core(inner_low)
-        down_sum.keep(mm(inner_low, cot, TN).astype(BF))
+        down_send, down_keep = inner_low, mm(inner_low, cot, TN).astype(BF)
+    third_sum.parts, fourth_send, fourth_keep, down_send, down_keep, gate_b, up_b = phase(
+        third_sum.parts, fourth_send, fourth_keep, down_send, down_keep, gate_b, up_b
+    )
+
+    third_send, gate_b, up_b = phase(third_sum.halve(), gate_b, up_b)
+    third_sum.far(third_send)
+    fourth_sum.core(fourth_send)
+    fourth_sum.keep(fourth_keep)
+    down_sum.core(down_send)
+    down_sum.keep(down_keep)
     grad_normed_three = mm(jnp.concatenate([gate_a, up_a], axis=1), third, NT) + mm(
         jnp.concatenate([gate_b, up_b], axis=1), fourth, NT
     )
     through, grad_gain_ffn = norm_back(hidden_two, gain_ffn, grad_normed_three)
     grad_hidden_two = cot.astype(F32) + through
-    fourth_sum.keep(weight_grad(links, core, fourth_terms))
     third_sum.parts, fourth_sum.parts, down_sum.parts, grad_hidden_two = phase(
         third_sum.parts, fourth_sum.parts, down_sum.parts, grad_hidden_two
     )
 
-    third_sum.far(third_sum.halve())
-    fourth_sum.near(fourth_sum.halve())
-    down_sends = down_sum.z_sends()
-    down_back, down_ahead = down_sum.z_start(down_sends)
+    down_sends, fourth_send, grad_hidden_two = phase(
+        down_sum.z_sends(), fourth_sum.halve(), grad_hidden_two
+    )
+    fourth_sum.near(fourth_send)
+    down_back = down_sum.z_back(down_sends)
     low_two = grad_hidden_two.astype(BF)
     (
         grad_cq, grad_ck, grad_cv, memory_part, grad_hidden_one, low_one, grad_attended,
@@ -880,42 +922,61 @@
         qseg, mseg,
     )
     half = inner // 2
-    (
-        third_sum.parts, fourth_sum.parts, down_back, down_ahead, grad_cq, grad_ck, grad_cv,
-        low_one, grad_attended,
-    ) = phase(
-        third_sum.parts, fourth_sum.parts, down_back, down_ahead, grad_cq, grad_ck, grad_cv,
-        low_one, grad_attended,
-    )
-
+    fourth_sum.parts, down_back, grad_cq, grad_ck, grad_cv, low_one, grad_attended, memory_part = (
+        phase(
+            fourth_sum.parts, down_back, grad_cq, grad_ck, grad_cv, low_one, grad_attended,
+            memory_part,
+        )
+    )
+
+    fourth_send, low_one = phase(fourth_sum.halve(), low_one)
+    fourth_sum.far(fourth_send)
+    down_ahead = down_sum.z_ahead(down_sends)
     cross_terms = [
         (normed_two, grad_cq, cross_attended, low_two),
         (memory_all, grad_ck, memory_all, grad_cv),
         (attended, low_one[:, :half], attended, low_one[:, half:]),
     ]
     cross_sum = Scatter(links)
-    cross_sum.core(weight_grad(links, 1 - core, cross_terms))
-    fourth_sum.far(fourth_sum.halve())
-    third_sum.z(third_sum.z_sends())
-    cross_sum.keep(weight_grad(links, core, cross_terms))
-    cross_sum.parts, fourth_sum.parts, grad_attended = phase(
-        cross_sum.parts, fourth_sum.parts, grad_attended
-    )
-
-    cross_sum.near(cross_sum.halve())
+    cross_send, cross_keep = weight_grad(links, cross_terms)
+    cross_send, cross_keep, fourth_sum.parts, down_ahead = phase(
+        cross_send, cross_keep, fourth_sum.parts, down_ahead
+    )
+
+    cross_sum.core(cross_send)
+    cross_sum.keep(cross_keep)
+    memory_rows = SeqScatter(links, memory_part)
+    third_sends = third_sum.z_sends()
+    (
+        cross_sum.parts, third_sends, down_sends, down_back, down_ahead, fourth_sum.parts,
+        memory_rows.sent, memory_rows.kept,
+    ) = phase(
+        cross_sum.parts, third_sends, down_sends, down_back, down_ahead, fourth_sum.parts,
+        memory_rows.sent, memory_rows.kept,
+    )
+
+    cross_send, grad_attended, third_sends, down_sends, down_back, down_ahead = phase(
+        cross_sum.halve(), grad_attended, third_sends, down_sends, down_back, down_ahead
+    )
+    cross_sum.near(cross_send)
     down_sum.z_end(down_sends, down_back, down_ahead)
+    third_sum.z(third_sends)
     grad_q, grad_k, grad_v, grad_windows, grad_normed, grad_gain_self = self_back(
         position1, target_all, grad_attended, queries, keys, values, first, windows, qseg, kseg
     )
     (
-        cross_sum.parts, third_sum.parts, down_sum.parts, grad_q, grad_k, grad_v, grad_windows,
-        grad_normed, grad_gain_self, memory_part,
+        cross_sum.parts, down_sum.parts, fourth_sum.parts, third_sum.parts, grad_q, grad_k,
+        grad_v, grad_windows, grad_normed, grad_gain_self, memory_rows.sent, memory_rows.kept,
     ) = phase(
-        cross_sum.parts, third_sum.parts, down_sum.parts, grad_q, grad_k, grad_v, grad_windows,
-        grad_normed, grad_gain_self, memory_part,
-    )
-
-    cross_sum.far(cross_sum.halve())
+        cross_sum.parts, down_sum.parts, fourth_sum.parts, third_sum.parts, grad_q, grad_k,
+        grad_v, grad_windows, grad_normed, grad_gain_self, memory_rows.sent, memory_rows.kept,
+    )
+
+    (
+        cross_send, fourth_sum.parts, grad_k, grad_windows, grad_gain_self,
+    ) = phase(cross_sum.halve(), fourth_sum.parts, grad_k, grad_windows, grad_gain_self)
+    cross_sum.far(cross_send)
+    memory_rows.second()
     grad_windows = grad_windows.reshape(heads, rows + length)
     grad_table = lax.dot_general(
         onehot.astype(F32), grad_windows, (((0,), (1,)), ((), ())), precision=lax.Precision.HIGHEST
@@ -933,43 +994,70 @@
         (normed_all, grad_k[:, :half], normed_all, grad_k[:, half:]),
     ]
     self_sum = Scatter(links)
-    self_sum.core(weight_grad(links, 1 - core, self_terms, small_grad))
-    self_sum.keep(weight_grad(links, core, self_terms, small_grad))
-    fourth_sum.z(fourth_sum.z_sends())
-    self_sum.parts, cross_sum.parts = phase(self_sum.parts, cross_sum.parts)
-
-    self_sum.near(self_sum.halve())
-    cross_sends = cross_sum.z_sends()
-    cross_back_z, cross_ahead_z = cross_sum.z_start(cross_sends)
-    down_sum.far(down_sum.halve())
+    self_send, self_keep = weight_grad(links, self_terms, small_grad)
+    (
+        self_send, self_keep, cross_sum.parts, down_sum.parts, fourth_sum.parts, third_sum.parts,
+        grad_normed, memory_rows.sent, memory_rows.kept, inner_low,
+    ) = phase(
+        self_send, self_keep, cross_sum.parts, down_sum.parts, fourth_sum.parts, third_sum.parts,
+        grad_normed, memory_rows.sent, memory_rows.kept, inner_low,
+    )
+
+    self_sum.core(self_send)
+    self_sum.keep(self_keep)
+    cross_sends, fourth_sends = cross_sum.z_sends(), fourth_sum.z_sends()
     normed_rows = SeqScatter(links, grad_normed)
+    self_sum.parts, cross_sends, fourth_sends, normed_rows.sent, normed_rows.kept = phase(
+        self_sum.parts, cross_sends, fourth_sends, normed_rows.sent, normed_rows.kept
+    )
+
+    self_send, cross_sends, fourth_sends, inner_low = phase(
+        self_sum.halve(), cross_sends, fourth_sends, inner_low
+    )
+    self_sum.near(self_send)
+    cross_back_z, cross_ahead_z = cross_sum.z_back(cross_sends), cross_sum.z_ahead(cross_sends)
+    fourth_back, fourth_ahead = fourth_sum.z_back(fourth_sends), fourth_sum.z_ahead(fourth_sends)
     activations = (hidden_two + mm(inner_low, w_down)).astype(BF)
     (
-        self_sum.parts, cross_back_z, cross_ahead_z, down_sum.parts, fourth_sum.parts,
-        normed_rows.sent,
+        self_sum.parts, cross_back_z, cross_ahead_z, fourth_back, fourth_ahead, down_sum.parts,
+        activations, third_sum.parts, normed_rows.sent,
     ) = phase(
-        self_sum.parts, cross_back_z, cross_ahead_z, down_sum.parts, fourth_sum.parts,
-        normed_rows.sent,
-    )
-
-    self_sum.far(self_sum.halve())
+        self_sum.parts, cross_back_z, cross_ahead_z, fourth_back, fourth_ahead, down_sum.parts,
+        activations, third_sum.parts, normed_rows.sent,
+    )
+
+    (
+        self_send, down_sum.parts, cross_sends, cross_back_z, cross_ahead_z, fourth_sends,
+        fourth_back, fourth_ahead, normed_rows.sent,
+    ) = phase(
+        self_sum.halve(), down_sum.parts, cross_sends, cross_back_z, cross_ahead_z, fourth_sends,
+        fourth_back, fourth_ahead, normed_rows.sent,
+    )
+    self_sum.far(self_send)
     cross_sum.z_end(cross_sends, cross_back_z, cross_ahead_z)
+    fourth_sum.z_end(fourth_sends, fourth_back, fourth_ahead)
+    down_sum.far(down_sum.halve())
+    normed_rows.second()
+    self_sum.parts, cross_sum.parts, fourth_sum.parts, down_sum.parts, normed_rows.sent = phase(
+        self_sum.parts, cross_sum.parts, fourth_sum.parts, down_sum.parts, normed_rows.sent
+    )
+
+    (
+        self_sends, cross_sum.parts, down_sum.parts, third_sum.parts, fourth_sum.parts,
+        normed_rows.sent, memory_rows.sent,
+    ) = phase(
+        self_sum.z_sends(), cross_sum.parts, down_sum.parts, third_sum.parts, fourth_sum.parts,
+        normed_rows.sent, memory_rows.sent,
+    )
+    self_sum.z(self_sends)
     down_sum.near(down_sum.halve())
-    normed_rows.second()
     gate_one, up_one = third_sum.last(third_sum.own())
-    memory_rows = SeqScatter(links, memory_part)
-    self_sum.parts, down_sum.parts, cross_sum.parts, normed_rows.sent, memory_rows.sent = phase(
-        self_sum.parts, down_sum.parts, cross_sum.parts, normed_rows.sent, memory_rows.sent
-    )
-
-    self_sum.z(self_sum.z_sends())
-    memory_rows.second()
+    gate_two, up_two = fourth_sum.last(fourth_sum.own())
+    cross_left, cross_right = cross_sum.last(cross_sum.own())
     memory_grad = memory_rows.total()
-    down_out = jnp.concatenate(down_sum.last(down_sum.own()), axis=1)
-    cross_left, cross_right = cross_sum.last(cross_sum.own())
-    gate_two, up_two = fourth_sum.last(fourth_sum.own())
     through, _ = norm_back(target[0].astype(F32), gain_self, normed_rows.total())
     target_grad = grad_hidden_one + through
+    down_out = jnp.concatenate(down_sum.last(down_sum.own()), axis=1)
     self_left, self_right = self_sum.last(self_sum.own())
     join = lambda left, right: jnp.concatenate([left, right], axis=1)
 

time: 496 us -> 475 us (0.958)
  waiting for transfers between devices: 127 us -> 101 us
  other arithmetic: 70.5 us -> 76.9 us
  local copies, waits for them, and re-layouts: 44.5 us -> 39.4 us
    ppermute x77, waiting for transfers between devices: 127 us -> 101 us  [move(): return lax.ppermute(value, AXES, pairs)]
    unnamed x274 -> x247, local copies, waits for them, and re-layouts: 25.7 us -> 18 us
    pallas_call x10 -> x5, Pallas kernels: 27.9 us -> 30.2 us  [weight_grad(): pl.pallas_call(body, in_specs=[pl.BlockSpec(memory_space=pltpu.SMEM)] + [...]
  transfers between devices with their start and end apart: 77 -> 77, of which waited for: 22 -> 24; matrix products, arithmetic and copies ran while one was open for 19% -> 20% of each run, Pallas kernels for 23% -> 28%
where the time goes in v4:
time: 475 us; the launch traced here: 466 us
  Pallas kernels  128 us (27%)
  waiting for transfers between devices  101 us (21%)
  starting transfers between devices  93.1 us (20%)
  other arithmetic  76.9 us (16%)
  local copies, waits for them, and re-layouts  39.4 us (8%)
  matrix products  24.3 us (5%)
    ppermute x77, waiting for transfers between devices, move(): return lax.ppermute(value, AXES, pairs)  101 us
    ppermute x77, starting transfers between devices, move(): return lax.ppermute(value, AXES, pairs)  93.1 us
    pallas_call x5, Pallas kernels, weight_grad(): pl.pallas_call(body, in_specs=[pl.BlockSpec(memory_space=pltpu.SMEM)] + [...  30.2 us
    pallas_call x5, Pallas kernels, assemble(): pl.pallas_call(body, in_specs=[pl.BlockSpec(memory_space=pltpu.SMEM)] + [...  29.4 us
    pallas_call x1, Pallas kernels, self_back(): pl.pallas_call(body, grid=(pairs,), in_specs=[SMEM, whole(target_all), pa...  23.2 us
    dot_general x8, matrix products, mm(): return lax.dot_general(left, right, dims, preferred_element_type=F32)  23 us
    convert_element_type x10, other arithmetic, halve(): return self.total(self.rows, self.rows).astype(BF)  21 us
    unnamed x247, local copies, waits for them, and re-layouts  18 us
  transfers between devices with their start and end apart: 77, of which 24 were waited for; matrix products, arithmetic and copies ran while one was open for 20% of the time, Pallas kernels for 28%

profile of v4, /device:TPU:0, one launch (start us, length us, event | category | flops | bytes accessed | tf_op | source)
XLA Modules:
  0.0 465.9 jit_solution(2921670998720386146)
XLA Ops:
  15.7 7.9 %collective-permute-done.3 = bf16[64,1664]{1,0:T(8,128)(2,1)S(1)} collective-permute-done((bf16[64,1664]{1,0:T(8,128)(2,1)S(1)}, bf16[64,1664]{1,0:T(8,128)(2,1)S(1)}, u32[]{:S(2)}, u32[]{:S(2)}) %collective-permute-start.3) | collective-permute-done | bytes 213024 | tf_op jit(solution)/shard_map/ppermute | solution.py:408
  23.6 5.4 %collective-permute-done.4 = bf16[64,1664]{1,0:T(8,128)(2,1)S(1)} collective-permute-done((bf16[64,1664]{1,0:T(8,128)(2,1)S(1)}, bf16[64,1664]{1,0:T(8,128)(2,1)S(1)}, u32[]{:S(2)}, u32[]{:S(2)}) %collective-permute-start.4) | collective-permute-done | bytes 213024 | tf_op jit(solution)/shard_map/ppermute | solution.py:408
  32.4 4.3 gather_fusion
  50.1 5.2 %collective-permute-done.7 = bf16[64,2560]{1,0:T(8,128)(2,1)S(1)} collective-permute-done((bf16[64,2560]{1,0:T(8,128)(2,1)}, bf16[64,2560]{1,0:T(8,128)(2,1)S(1)}, u32[]{:S(2)}, u32[]{:S(2)}) %collective-permute-start.7) | collective-permute-done | bytes 327712 | tf_op jit(solution)/shard_map/ppermute | solution.py:408
  56.5 6.6 %collective-permute-start.12 = (bf16[64,2560]{1,0:T(8,128)(2,1)}, bf16[64,2560]{1,0:T(8,128)(2,1)S(1)}, u32[]{:S(2)}, u32[]{:S(2)}) collective-permute-start(bf16[64,2560]{1,0:T(8,128)(2,1)} %split.13), channel_id=1, source_target_pairs={{0,16},{1,17},{2,18},{3,19},{4,20},{5,21},{6,22},{7,23},{8,24},{9,... | collective-permute-start | bytes 983048 | tf_op jit(solution)/shard_map/ppermute | solution.py:408
  65.3 13.4 %collective-permute-done.12 = bf16[64,2560]{1,0:T(8,128)(2,1)S(1)} collective-permute-done((bf16[64,2560]{1,0:T(8,128)(2,1)}, bf16[64,2560]{1,0:T(8,128)(2,1)S(1)}, u32[]{:S(2)}, u32[]{:S(2)}) %collective-permute-start.12) | collective-permute-done | bytes 327712 | tf_op jit(solution)/shard_map/ppermute | solution.py:408
  93.4 5.8 %collective-permute-done.17 = bf16[64,1408]{1,0:T(8,128)(2,1)S(1)} collective-permute-done((bf16[64,1408]{1,0:T(8,128)(2,1)}, bf16[64,1408]{1,0:T(8,128)(2,1)S(1)}, u32[]{:S(2)}, u32[]{:S(2)}) %collective-permute-start.17) | collective-permute-done | bytes 180256 | tf_op jit(solution)/shard_map/ppermute | solution.py:408
  117.0 6.1 %assemble.5.wq_ref.wk_ref.wv_ref = bf16[1024,3328]{1,0:T(8,128)(2,1)} custom-call(s32[4]{0:T(128)S(1)} %pad_add_fusion.place_ref, bf16[2,4,64,1664]{3,2,1,0:T(8,128)(2,1)S(1)} %copy-done.9, bf16[2,4,64,1664]{3,2,1,0:T(8,128)(2,1)} %collective-permute-done.10.refs_1_, bf16[2,4,64,1664]{3,2,1,0:T(8,128)(2,1)} %collective-permute-done.11.refs_2_, ...), custom_call_target="tpu_custom_call" | custom-call | flops 6000000000 | bytes 1 | tf_op jit(solution)/shard_map/assemble/pallas_call | solution.py:475
  125.4 6.4 %collective-permute-start.26 = (bf16[2,2,176,512]{3,2,1,0:T(8,128)(2,1)}, bf16[2,2,176,512]{3,2,1,0:T(8,128)(2,1)S(1)}, u32[]{:S(2)}, u32[]{:S(2)}) collective-permute-start(bf16[2,2,176,512]{3,2,1,0:T(8,128)(2,1)} %pad_maximum_fusion.10), channel_id=1, source_target_pairs={{0,24},{1,25},{2,26},{3,27},{4,28},{5,29},{6,30},{7,31},{8,0},{9,1... | collective-permute-start | bytes 2162696 | tf_op jit(solution)/shard_map/ppermute | solution.py:408
  132.5 15.5 %self_forward.1 = (bf16[128,1024]{1,0:T(8,128)(2,1)S(1)}, bf16[128,1024]{1,0:T(8,128)(2,1)S(1)}, bf16[512,1024]{1,0:T(8,128)(2,1)S(1)}, bf16[512,1024]{1,0:T(8,128)(2,1)S(1)}, bf16[512,1024]{1,0:T(8,128)(2,1)S(1)}) custom-call(s32[1]{0:T(128)} %bitcast.4.pos_ref, bf16[512,1024]{1,0:T(8,128)(2,1)S(1)} %bitcast.149, f32[1,1024]{1,0:T(1,128)S(1)} %reshape.222.gain_ref, ...), custom_call_target="tpu_custom_call" | custom-call | flops 16000000000 | bytes 1 | tf_op jit(solution)/shard_map/self_forward/pallas_call | solution.py:166
  154.0 5.0 %collective-permute-done.26 = bf16[2,2,176,512]{3,2,1,0:T(8,128)(2,1)S(1)} collective-permute-done((bf16[2,2,176,512]{3,2,1,0:T(8,128)(2,1)}, bf16[2,2,176,512]{3,2,1,0:T(8,128)(2,1)S(1)}, u32[]{:S(2)}, u32[]{:S(2)}) %collective-permute-start.26) | collective-permute-done | bytes 720928 | tf_op jit(solution)/shard_map/ppermute | solution.py:408
  164.6 8.5 %assemble.6.wo_ref.wq_ref.wk_ref.wv_ref.wc_ref = bf16[1024,5120]{1,0:T(8,128)(2,1)} custom-call(s32[4]{0:T(128)S(1)} %pad_add_fusion.place_ref, bf16[2,4,64,2560]{3,2,1,0:T(8,128)(2,1)} %pad_maximum_fusion.1.refs_0_, bf16[2,4,64,2560]{3,2,1,0:T(8,128)(2,1)} %collective-permute-done.20.refs_1_, bf16[2,4,64,2560]{3,2,1,0:T(8,128)(2,1)} %collective-permute-done.21.refs_2_, ...), custom_call_target="tpu_custom_call" | custom-call | flops 6000000000 | bytes 1 | tf_op jit(solution)/shard_map/assemble/pallas_call | solution.py:475
  173.1 12.6 %cross_forward.1 = (f32[128,1024]{1,0:T(8,128)S(1)}, bf16[128,1024]{1,0:T(8,128)(2,1)S(1)}, bf16[128,1024]{1,0:T(8,128)(2,1)S(1)}, bf16[256,1024]{1,0:T(8,128)(2...) custom-call(bf16[128,1024]{1,0:T(8,128)(2,1)S(1)} %bitcast.148, ...), custom_call_target="tpu_custom_call" | custom-call | flops 12000000000 | bytes 1 | tf_op jit(solution)/shard_map/cross_forward/pallas_call | solution.py:280
  192.8 7.5 %collective-permute-done.33.refs_3_ = bf16[2,4,64,1408]{3,2,1,0:T(8,128)(2,1)S(1)} collective-permute-done((bf16[2,4,64,1408]{3,2,1,0:T(8,128)(2,1)S(1)}, bf16[2,4,64,1408]{3,2,1,0:T(8,128)(2,1)S(1)}, u32[]{:S(2)}, u32[]{:S(2)}) %collective-permute-start.33) | collective-permute-done | bytes 1441824 | tf_op jit(solution)/shard_map/ppermute | solution.py:408
  200.3 4.2 assemble.7
  208.1 5.3 %assemble.8 = bf16[2816,1024]{1,0:T(8,128)(2,1)} custom-call(s32[4]{0:T(128)S(1)} %pad_add_fusion.place_ref, bf16[4,2,2,176,512]{4,3,2,1,0:T(8,128)(2,1)S(1)} %pad_maximum_fusion.refs_0_, bf16[4,2,2,176,512]{4,3,2,1,0:T(8,128)(2,1)} %collective-permute-done.36.refs_1_), custom_call_target="tpu_custom_call" | custom-call | flops 6000000000 | bytes 1 | tf_op jit(solution)/shard_map/assemble/pallas_call | solution.py:475
  217.0 4.8 %weight_grad.5 = (bf16[1024,1408]{1,0:T(8,128)(2,1)S(1)}, bf16[1024,1408]{1,0:T(8,128)(2,1)}) custom-call(s32[4]{0:T(128)S(1)} %pad_add_fusion.place_ref, bf16[128,1024]{1,0:T(8,128)(2,1)S(1)} %get-tuple-element.381.refs_0_.refs_2_, bf16[128,1408]{1,0:T(8,128)(2,1)S(1)} %get-tuple-element.419.refs_1_, ...), custom_call_target="tpu_custom_call" | custom-call | flops 1000000000 | bytes 1 | tf_op jit(solution)/shard_map/weight_grad/pallas_call | solution.py:565
  222.8 5.3 %assemble.9 = bf16[1024,2816]{1,0:T(8,128)(2,1)} custom-call(s32[4]{0:T(128)S(1)} %pad_add_fusion.place_ref, bf16[2,4,64,1408]{3,2,1,0:T(8,128)(2,1)S(1)} %pad_maximum_fusion.4.refs_0_, bf16[2,4,64,1408]{3,2,1,0:T(8,128)(2,1)} %collective-permute-done.34.refs_1_, bf16[2,4,64,1408]{3,2,1,0:T(8,128)(2,1)} %collective-permute-done.35.refs_2_, ...), custom_call_target="tpu_custom_call" | custom-call | flops 6000000000 | bytes 1 | tf_op jit(solution)/shard_map/assemble/pallas_call | solution.py:475
  236.7 5.1 %weight_grad.6 = (bf16[1024,1408]{1,0:T(8,128)(2,1)}, bf16[1024,1408]{1,0:T(8,128)(2,1)}) custom-call(s32[4]{0:T(128)S(1)} %pad_add_fusion.place_ref, bf16[128,1024]{1,0:T(8,128)(2,1)S(1)} %get-tuple-element.381.refs_0_.refs_2_, bf16[128,1408]{1,0:T(8,128)(2,1)S(1)} %get-tuple-element.421.refs_1_, bf16[128,1024]{1,0:T(8,128)(2,1)S(1)} %get-tuple-element.381.refs_0_.refs_2_, ...), custom_call_target="tpu_custom_call" | custom-call | flops 1000000000 | bytes 1 | tf_op jit(solution)/shard_map/weight_grad/pallas_call | solution.py:565
  241.9 5.7 %weight_grad.7 = (bf16[2816,512]{1,0:T(8,128)(2,1)}, bf16[2816,512]{1,0:T(8,128)(2,1)}) custom-call(s32[4]{0:T(128)S(1)} %pad_add_fusion.place_ref, bf16[128,2816]{1,0:T(8,128)(2,1)S(1)} %pad_maximum_fusion.12.refs_0_.refs_2_, bf16[128,512]{1,0:T(8,128)(2,1)S(1)} %get-tuple-element.716.refs_1_, bf16[128,2816]{1,0:T(8,128)(2,1)S(1)} %pad_maximum_fusion.12.refs_0_.refs_2_, ...), custom_call_target="tpu_custom_call" | custom-call | flops 1000000000 | bytes 1 | tf_op jit(solution)/shard_map/weight_grad/pallas_call | solution.py:565
  253.1 4.6 fusion.31
  257.7 4.9 %multiply_reduce_fusion = (f32[1024]{0:T(1024)S(1)}, f32[128]{0:T(128)S(1)}, f32[128,1024]{1,0:T(8,128)S(1)}) fusion(f32[128,1024]{1,0:T(8,128)S(1)} %get-tuple-element.418, f32[128]{0:T(128)S(1)} %add_rsqrt_fusion.1, f32[1024]{0:T(1024)S(1)} %mul.224, f32[128,1024]{1,0:T(8,128)S(1)} %fusion.31, bf16[1024,2816]{1,0:T(8,128)(2,1)} %assemble.7, ...), kind=kOutput, calls=%fused_computation.105 | convolution fusion | flops 740555648 | bytes 8070144 | tf_op jit(solution)/shard_map/dot_general | solution.py:25
  273.3 17.4 %cross_back.1 = (bf16[128,1024]{1,0:T(8,128)(2,1)S(1)}, bf16[256,1024]{1,0:T(8,128)(2,1)S(1)}, bf16[256,1024]{1,0:T(8,128)(2,1)S(1)}, f32[256,1024]{1,0:T(8,128)...) custom-call(f32[128,1024]{1,0:T(8,128)S(1)} %multiply_add_fusion.gra, ...), custom_call_target="tpu_custom_call" | custom-call | flops 1000000000 | bytes 1 | tf_op jit(solution)/shard_map/cross_back/pallas_call | solution.py:353
  294.9 7.3 %weight_grad.8 = (bf16[1024,2560]{1,0:T(8,128)(2,1)}, bf16[1024,2560]{1,0:T(8,128)(2,1)}) custom-call(s32[4]{0:T(128)S(1)} %pad_add_fusion.place_ref, bf16[128,1024]{1,0:T(8,128)(2,1)S(1)} %copy-done.44, bf16[128,1024]{1,0:T(8,128)(2,1)S(1)} %get-tuple-element.441.refs_1_, bf16[128,1024]{1,0:T(8,128)(2,1)S(1)} %copy-done.46, ...), custom_call_target="tpu_custom_call" | custom-call | flops 1000000000 | bytes 1 | tf_op jit(solution)/shard_map/weight_grad/pallas_call | solution.py:565
  310.3 4.5 collective-permute-done.48
  327.9 23.2 %self_back.1 = (bf16[512,1024]{1,0:T(8,128)(2,1)S(1)}, bf16[512,1024]{1,0:T(8,128)(2,1)S(1)}, bf16[512,1024]{1,0:T(8,128)(2,1)S(1)}, f32[8,2,640]{2,1,0:T(2,128)...) custom-call(s32[1]{0:T(128)} %bitcast.4.pos_ref, bf16[512,1024]{1,0:T(8,128)(2,1)S(1)} %bitcast.150, ...), custom_call_target="tpu_custom_call" | custom-call | flops 1000000000 | bytes 1 | tf_op jit(solution)/shard_map/self_back/pallas_call | solution.py:225
  352.5 4.7 %add_convert_fusion.4 = bf16[256,2560]{1,0:T(8,128)(2,1)} fusion(bf16[512,2560]{1,0:T(8,128)(2,1)S(1)} %collective-permute-done.49, bf16[1024,2560]{1,0:T(8,128)(2,1)} %get-tuple-element.641, bf16[1024,2560]{1,0:T(8,128)(2,1)} %collective-permute-done.47), kind=kLoop, calls=%fused_computation.11 | loop fusion | flops 3932160 | bytes 5242880 | tf_op jit(solution)/shard_map/convert_element_type | solution.py:600
  368.4 7.2 %weight_grad.9 = (bf16[1024,1664]{1,0:T(8,128)(2,1)}, bf16[1024,1664]{1,0:T(8,128)(2,1)}) custom-call(s32[4]{0:T(128)S(1)} %pad_add_fusion.place_ref, bf16[512,1024]{1,0:T(8,128)(2,1)S(1)} %get-tuple-element.363.refs_0_.refs_2_.refs_4_.refs_6_, bf16[512,1024]{1,0:T(8,128)(2,1)S(1)} %copy-done.15, ...), custom_call_target="tpu_custom_call" | custom-call | flops 1000000000 | bytes 1 | tf_op jit(solution)/shard_map/weight_grad/pallas_call | solution.py:565
  387.1 4.6 collective-permute-start.61
  401.0 6.6 %collective-permute-done.59 = bf16[64,2560]{1,0:T(8,128)(2,1)S(1)} collective-permute-done((bf16[64,2560]{1,0:T(8,128)(2,1)S(1)}, bf16[64,2560]{1,0:T(8,128)(2,1)S(1)}, u32[]{:S(2)}, u32[]{:S(2)}) %collective-permute-start.59) | collective-permute-done | bytes 327712 | tf_op jit(solution)/shard_map/ppermute | solution.py:408
  407.6 6.8 %collective-permute-done.60 = bf16[64,2560]{1,0:T(8,128)(2,1)S(1)} collective-permute-done((bf16[64,2560]{1,0:T(8,128)(2,1)S(1)}, bf16[64,2560]{1,0:T(8,128)(2,1)S(1)}, u32[]{:S(2)}, u32[]{:S(2)}) %collective-permute-start.60) | collective-permute-done | bytes 327712 | tf_op jit(solution)/shard_map/ppermute | solution.py:408
  427.4 6.1 %collective-permute-done.65 = bf16[64,1408]{1,0:T(8,128)(2,1)} collective-permute-done((bf16[64,1408]{1,0:T(8,128)(2,1)}, bf16[64,1408]{1,0:T(8,128)(2,1)}, u32[]{:S(2)}, u32[]{:S(2)}) %collective-permute-start.65) | collective-permute-done | bytes 180256 | tf_op jit(solution)/shard_map/ppermute | solution.py:408
  (530 shorter events, 224.4 us)
Async XLA Ops:
  55.3 25.6 %collective-permute-start.11 = (bf16[2,4,64,1664]{3,2,1,0:T(8,128)(2,1)S(1)}, bf16[2,4,64,1664]{3,2,1,0:T(8,128)(2,1)}, u32[]{:S(2)}, u32[]{:S(2)}) collective-permute-start(bf16[2,4,64,1664]{3,2,1,0:T(8,128)(2,1)S(1)} %pad_maximum_fusion.2.refs_0_), channel_id=1, source_target_pairs={{0,1},{1,0},{2,3},{3,2},{4,5},{5,4},{6,7},{7,6},{8,9},{9,8},{10,11... | collective-permute-start | bytes 5111816 | tf_op jit(solution)/shard_map/ppermute | solution.py:408
  56.0 24.9 %collective-permute-start.10 = (bf16[2,4,64,1664]{3,2,1,0:T(8,128)(2,1)S(1)}, bf16[2,4,64,1664]{3,2,1,0:T(8,128)(2,1)}, u32[]{:S(2)}, u32[]{:S(2)}) collective-permute-start(bf16[2,4,64,1664]{3,2,1,0:T(8,128)(2,1)S(1)} %pad_maximum_fusion.2.refs_0_), channel_id=1, source_target_pairs={{0,2},{1,5},{2,0},{3,7},{4,6},{5,1},{6,4},{7,3},{8,10},{9,13},{10,... | collective-permute-start | bytes 5111816 | tf_op jit(solution)/shard_map/ppermute | solution.py:408
  56.5 22.1 %collective-permute-start.12 = (bf16[64,2560]{1,0:T(8,128)(2,1)}, bf16[64,2560]{1,0:T(8,128)(2,1)S(1)}, u32[]{:S(2)}, u32[]{:S(2)}) collective-permute-start(bf16[64,2560]{1,0:T(8,128)(2,1)} %split.13), channel_id=1, source_target_pairs={{0,16},{1,17},{2,18},{3,19},{4,20},{5,21},{6,22},{7,23},{8,24},{9,... | collective-permute-start | bytes 983048 | tf_op jit(solution)/shard_map/ppermute | solution.py:408
  81.7 21.8 %collective-permute-start.15 = (bf16[4,64,2560]{2,1,0:T(8,128)(2,1)}, bf16[4,64,2560]{2,1,0:T(8,128)(2,1)}, u32[]{:S(2)}, u32[]{:S(2)}) collective-permute-start(bf16[4,64,2560]{2,1,0:T(8,128)(2,1)} %pad_maximum_fusion.5), channel_id=1, source_target_pairs={{0,4},{1,3},{2,6},{3,1},{4,0},{5,7},{6,2},{7,5},{8,12},{9,11},{10,... | collective-permute-start | bytes 3932168 | tf_op jit(solution)/shard_map/ppermute | solution.py:408
  82.3 24.9 %collective-permute-start.14 = (bf16[2,4,64,1664]{3,2,1,0:T(8,128)(2,1)}, bf16[2,4,64,1664]{3,2,1,0:T(8,128)(2,1)}, u32[]{:S(2)}, u32[]{:S(2)}) collective-permute-start(bf16[2,4,64,1664]{3,2,1,0:T(8,128)(2,1)} %collective-permute-done.10.refs_1_), channel_id=1, source_target_pairs={{0,1},{1,0},{2,3},{3,2},{4,5},{5,4},{6,7},{7,6},{8,9},{9,8},{10,11... | collective-permute-start | bytes 5111816 | tf_op jit(solution)/shard_map/ppermute | solution.py:408
  107.1 18.2 %collective-permute-start.25 = (bf16[64,1408]{1,0:T(8,128)(2,1)S(1)}, bf16[64,1408]{1,0:T(8,128)(2,1)S(1)}, u32[]{:S(2)}, u32[]{:S(2)}) collective-permute-start(bf16[64,1408]{1,0:T(8,128)(2,1)S(1)} %copy-done.85), channel_id=1, source_target_pairs={{0,8},{1,9},{2,10},{3,11},{4,12},{5,13},{6,14},{7,15},{8,16},{9,17... | collective-permute-start | bytes 540680 | tf_op jit(solution)/shard_map/ppermute | solution.py:408
  112.6 19.2 %collective-permute-start.23 = (bf16[64,1408]{1,0:T(8,128)(2,1)S(1)}, bf16[64,1408]{1,0:T(8,128)(2,1)S(1)}, u32[]{:S(2)}, u32[]{:S(2)}) collective-permute-start(bf16[64,1408]{1,0:T(8,128)(2,1)S(1)} %copy-done.85), channel_id=1, source_target_pairs={{0,24},{1,25},{2,26},{3,27},{4,28},{5,29},{6,30},{7,31},{8,0},{9,1... | collective-permute-start | bytes 540680 | tf_op jit(solution)/shard_map/ppermute | solution.py:408
  115.4 43.6 %collective-permute-start.21 = (bf16[2,4,64,2560]{3,2,1,0:T(8,128)(2,1)}, bf16[2,4,64,2560]{3,2,1,0:T(8,128)(2,1)}, u32[]{:S(2)}, u32[]{:S(2)}) collective-permute-start(bf16[2,4,64,2560]{3,2,1,0:T(8,128)(2,1)} %pad_maximum_fusion.1.refs_0_), channel_id=1, source_target_pairs={{0,1},{1,0},{2,3},{3,2},{4,5},{5,4},{6,7},{7,6},{8,9},{9,8},{10,11... | collective-permute-start | bytes 7864328 | tf_op jit(solution)/shard_map/ppermute | solution.py:408
  115.4 43.6 %collective-permute-start.20 = (bf16[2,4,64,2560]{3,2,1,0:T(8,128)(2,1)}, bf16[2,4,64,2560]{3,2,1,0:T(8,128)(2,1)}, u32[]{:S(2)}, u32[]{:S(2)}) collective-permute-start(bf16[2,4,64,2560]{3,2,1,0:T(8,128)(2,1)} %pad_maximum_fusion.1.refs_0_), channel_id=1, source_target_pairs={{0,2},{1,5},{2,0},{3,7},{4,6},{5,1},{6,4},{7,3},{8,10},{9,13},{10,... | collective-permute-start | bytes 7864328 | tf_op jit(solution)/shard_map/ppermute | solution.py:408
  125.3 28.7 %collective-permute-start.27 = (bf16[2,2,176,512]{3,2,1,0:T(8,128)(2,1)}, bf16[2,2,176,512]{3,2,1,0:T(8,128)(2,1)S(1)}, u32[]{:S(2)}, u32[]{:S(2)}) collective-permute-start(bf16[2,2,176,512]{3,2,1,0:T(8,128)(2,1)} %pad_maximum_fusion.10), channel_id=1, source_target_pairs={{0,8},{1,9},{2,10},{3,11},{4,12},{5,13},{6,14},{7,15},{8,16},{9,17... | collective-permute-start | bytes 2162696 | tf_op jit(solution)/shard_map/ppermute | solution.py:408
  125.4 33.6 %collective-permute-start.26 = (bf16[2,2,176,512]{3,2,1,0:T(8,128)(2,1)}, bf16[2,2,176,512]{3,2,1,0:T(8,128)(2,1)S(1)}, u32[]{:S(2)}, u32[]{:S(2)}) collective-permute-start(bf16[2,2,176,512]{3,2,1,0:T(8,128)(2,1)} %pad_maximum_fusion.10), channel_id=1, source_target_pairs={{0,24},{1,25},{2,26},{3,27},{4,28},{5,29},{6,30},{7,31},{8,0},{9,1... | collective-permute-start | bytes 2162696 | tf_op jit(solution)/shard_map/ppermute | solution.py:408
  131.8 19.9 %collective-permute-start.22 = (bf16[4,64,1408]{2,1,0:T(8,128)(2,1)}, bf16[4,64,1408]{2,1,0:T(8,128)(2,1)S(1)}, u32[]{:S(2)}, u32[]{:S(2)}) collective-permute-start(bf16[4,64,1408]{2,1,0:T(8,128)(2,1)} %pad_maximum_fusion.9), channel_id=1, source_target_pairs={{0,4},{1,3},{2,6},{3,1},{4,0},{5,7},{6,2},{7,5},{8,12},{9,11},{10,... | collective-permute-start | bytes 2162696 | tf_op jit(solution)/shard_map/ppermute | solution.py:408
  160.1 28.6 %collective-permute-start.31 = (bf16[2,4,64,1408]{3,2,1,0:T(8,128)(2,1)}, bf16[2,4,64,1408]{3,2,1,0:T(8,128)(2,1)S(1)}, u32[]{:S(2)}, u32[]{:S(2)}) collective-permute-start(bf16[2,4,64,1408]{3,2,1,0:T(8,128)(2,1)} %pad_maximum_fusion.3.refs_0_), channel_id=1, source_target_pairs={{0,1},{1,0},{2,3},{3,2},{4,5},{5,4},{6,7},{7,6},{8,9},{9,8},{10,11... | collective-permute-start | bytes 4325384 | tf_op jit(solution)/shard_map/ppermute | solution.py:408
  160.1 28.5 %collective-permute-start.30 = (bf16[2,4,64,1408]{3,2,1,0:T(8,128)(2,1)}, bf16[2,4,64,1408]{3,2,1,0:T(8,128)(2,1)S(1)}, u32[]{:S(2)}, u32[]{:S(2)}) collective-permute-start(bf16[2,4,64,1408]{3,2,1,0:T(8,128)(2,1)} %pad_maximum_fusion.3.refs_0_), channel_id=1, source_target_pairs={{0,2},{1,5},{2,0},{3,7},{4,6},{5,1},{6,4},{7,3},{8,10},{9,13},{10,... | collective-permute-start | bytes 4325384 | tf_op jit(solution)/shard_map/ppermute | solution.py:408
  161.1 27.6 %collective-permute-start.29 = (bf16[2,2,176,512]{3,2,1,0:T(8,128)(2,1)}, bf16[2,2,176,512]{3,2,1,0:T(8,128)(2,1)}, u32[]{:S(2)}, u32[]{:S(2)}) collective-permute-start(bf16[2,2,176,512]{3,2,1,0:T(8,128)(2,1)} %copy-done.81), channel_id=1, source_target_pairs={{0,24},{1,25},{2,26},{3,27},{4,28},{5,29},{6,30},{7,31},{8,0},{9,1... | collective-permute-start | bytes 2162696 | tf_op jit(solution)/shard_map/ppermute | solution.py:408
  163.6 25.0 %collective-permute-start.32 = (bf16[4,64,1408]{2,1,0:T(8,128)(2,1)}, bf16[4,64,1408]{2,1,0:T(8,128)(2,1)S(1)}, u32[]{:S(2)}, u32[]{:S(2)}) collective-permute-start(bf16[4,64,1408]{2,1,0:T(8,128)(2,1)} %pad_maximum_fusion.11), channel_id=1, source_target_pairs={{0,4},{1,3},{2,6},{3,1},{4,0},{5,7},{6,2},{7,5},{8,12},{9,11},{10,... | collective-permute-start | bytes 2162696 | tf_op jit(solution)/shard_map/ppermute | solution.py:408
  191.2 16.9 %collective-permute-start.36 = (bf16[4,2,2,176,512]{4,3,2,1,0:T(8,128)(2,1)S(1)}, bf16[4,2,2,176,512]{4,3,2,1,0:T(8,128)(2,1)}, u32[]{:S(2)}, u32[]{:S(2)}) collective-permute-start(bf16[4,2,2,176,512]{4,3,2,1,0:T(8,128)(2,1)S(1)} %pad_maximum_fusion.refs_0_), channel_id=1, source_target_pairs={{0,1},{1,0},{2,3},{3,2},{4,5},{5,4},{6,7},{7,6},{8,9},{9,8},{10,11... | collective-permute-start | bytes 8650760 | tf_op jit(solution)/shard_map/ppermute | solution.py:408
  191.9 21.5 %collective-permute-start.35 = (bf16[2,4,64,1408]{3,2,1,0:T(8,128)(2,1)S(1)}, bf16[2,4,64,1408]{3,2,1,0:T(8,128)(2,1)}, u32[]{:S(2)}, u32[]{:S(2)}) collective-permute-start(bf16[2,4,64,1408]{3,2,1,0:T(8,128)(2,1)S(1)} %pad_maximum_fusion.4.refs_0_), channel_id=1, source_target_pairs={{0,1},{1,0},{2,3},{3,2},{4,5},{5,4},{6,7},{7,6},{8,9},{9,8},{10,11... | collective-permute-start | bytes 4325384 | tf_op jit(solution)/shard_map/ppermute | solution.py:408
  192.1 21.3 %collective-permute-start.34 = (bf16[2,4,64,1408]{3,2,1,0:T(8,128)(2,1)S(1)}, bf16[2,4,64,1408]{3,2,1,0:T(8,128)(2,1)}, u32[]{:S(2)}, u32[]{:S(2)}) collective-permute-start(bf16[2,4,64,1408]{3,2,1,0:T(8,128)(2,1)S(1)} %pad_maximum_fusion.4.refs_0_), channel_id=1, source_target_pairs={{0,2},{1,5},{2,0},{3,7},{4,6},{5,1},{6,4},{7,3},{8,10},{9,13},{10,... | collective-permute-start | bytes 4325384 | tf_op jit(solution)/shard_map/ppermute | solution.py:408
  229.8 19.1 %collective-permute-start.39 = (bf16[512,1408]{1,0:T(8,128)(2,1)S(1)}, bf16[512,1408]{1,0:T(8,128)(2,1)S(1)}, u32[]{:S(2)}, u32[]{:S(2)}) collective-permute-start(bf16[512,1408]{1,0:T(8,128)(2,1)S(1)} %add_convert_fusion.3), channel_id=1, source_target_pairs={{0,4},{1,3},{2,6},{3,1},{4,0},{5,7},{6,2},{7,5},{8,12},{9,11},{10,... | collective-permute-start | bytes 4325384 | tf_op jit(solution)/shard_map/ppermute | solution.py:408
  270.2 21.6 %collective-permute-start.43 = (bf16[512,1408]{1,0:T(8,128)(2,1)S(1)}, bf16[512,1408]{1,0:T(8,128)(2,1)S(1)}, u32[]{:S(2)}, u32[]{:S(2)}) collective-permute-start(bf16[512,1408]{1,0:T(8,128)(2,1)S(1)} %add_convert_fusion.2), channel_id=1, source_target_pairs={{0,4},{1,3},{2,6},{3,1},{4,0},{5,7},{6,2},{7,5},{8,12},{9,11},{10,... | collective-permute-start | bytes 4325384 | tf_op jit(solution)/shard_map/ppermute | solution.py:408
  271.3 20.5 %collective-permute-start.44 = (bf16[704,512]{1,0:T(8,128)(2,1)}, bf16[704,512]{1,0:T(8,128)(2,1)}, u32[]{:S(2)}, u32[]{:S(2)}) collective-permute-start(bf16[704,512]{1,0:T(8,128)(2,1)} %get-tuple-element.429), channel_id=1, source_target_pairs={{0,24},{1,25},{2,26},{3,27},{4,28},{5,29},{6,30},{7,31},{8,0},{9,1... | collective-permute-start | bytes 2162696 | tf_op jit(solution)/shard_map/ppermute | solution.py:408
  272.8 33.1 %collective-permute-start.46 = (bf16[704,512]{1,0:T(8,128)(2,1)S(1)}, bf16[704,512]{1,0:T(8,128)(2,1)}, u32[]{:S(2)}, u32[]{:S(2)}) collective-permute-start(bf16[704,512]{1,0:T(8,128)(2,1)S(1)} %get-tuple-element.453), channel_id=1, source_target_pairs={{0,8},{1,9},{2,10},{3,11},{4,12},{5,13},{6,14},{7,15},{8,16},{9,17... | collective-permute-start | bytes 2162696 | tf_op jit(solution)/shard_map/ppermute | solution.py:408
  318.9 33.5 %collective-permute-start.49 = (bf16[512,2560]{1,0:T(8,128)(2,1)S(1)}, bf16[512,2560]{1,0:T(8,128)(2,1)S(1)}, u32[]{:S(2)}, u32[]{:S(2)}) collective-permute-start(bf16[512,2560]{1,0:T(8,128)(2,1)S(1)} %add_convert_fusion), channel_id=1, source_target_pairs={{0,4},{1,3},{2,6},{3,1},{4,0},{5,7},{6,2},{7,5},{8,12},{9,11},{10,... | collective-permute-start | bytes 7864328 | tf_op jit(solution)/shard_map/ppermute | solution.py:408
  321.0 31.4 %collective-permute-start.50 = (bf16[704,512]{1,0:T(8,128)(2,1)S(1)}, bf16[704,512]{1,0:T(8,128)(2,1)S(1)}, u32[]{:S(2)}, u32[]{:S(2)}) collective-permute-start(bf16[704,512]{1,0:T(8,128)(2,1)S(1)} %add_convert_fusion.6), channel_id=1, source_target_pairs={{0,8},{1,9},{2,10},{3,11},{4,12},{5,13},{6,14},{7,15},{8,16},{9,17... | collective-permute-start | bytes 2162696 | tf_op jit(solution)/shard_map/ppermute | solution.py:408
  321.4 29.7 %collective-permute-start.51 = (bf16[64,1408]{1,0:T(8,128)(2,1)S(1)}, bf16[64,1408]{1,0:T(8,128)(2,1)S(1)}, u32[]{:S(2)}, u32[]{:S(2)}) collective-permute-start(bf16[64,1408]{1,0:T(8,128)(2,1)S(1)} %get-tuple-element.485), channel_id=1, source_target_pairs={{0,8},{1,9},{2,10},{3,11},{4,12},{5,13},{6,14},{7,15},{8,16},{9,17... | collective-permute-start | bytes 540680 | tf_op jit(solution)/shard_map/ppermute | solution.py:408
  323.2 29.1 %collective-permute-start.52 = (bf16[64,1408]{1,0:T(8,128)(2,1)S(1)}, bf16[64,1408]{1,0:T(8,128)(2,1)S(1)}, u32[]{:S(2)}, u32[]{:S(2)}) collective-permute-start(bf16[64,1408]{1,0:T(8,128)(2,1)S(1)} %get-tuple-element.486), channel_id=1, source_target_pairs={{0,16},{1,17},{2,18},{3,19},{4,20},{5,21},{6,22},{7,23},{8,24},{9,... | collective-permute-start | bytes 540680 | tf_op jit(solution)/shard_map/ppermute | solution.py:408
  325.5 26.9 %collective-permute-start.53 = (bf16[64,1408]{1,0:T(8,128)(2,1)S(1)}, bf16[64,1408]{1,0:T(8,128)(2,1)S(1)}, u32[]{:S(2)}, u32[]{:S(2)}) collective-permute-start(bf16[64,1408]{1,0:T(8,128)(2,1)S(1)} %get-tuple-element.487), channel_id=1, source_target_pairs={{0,24},{1,25},{2,26},{3,27},{4,28},{5,29},{6,30},{7,31},{8,0},{9,1... | collective-permute-start | bytes 540680 | tf_op jit(solution)/shard_map/ppermute | solution.py:408
  357.2 20.7 %collective-permute-start.54 = (bf16[256,2560]{1,0:T(8,128)(2,1)}, bf16[256,2560]{1,0:T(8,128)(2,1)}, u32[]{:S(2)}, u32[]{:S(2)}) collective-permute-start(bf16[256,2560]{1,0:T(8,128)(2,1)} %add_convert_fusion.4), channel_id=1, source_target_pairs={{0,2},{1,5},{2,0},{3,7},{4,6},{5,1},{6,4},{7,3},{8,10},{9,13},{10,... | collective-permute-start | bytes 3932168 | tf_op jit(solution)/shard_map/ppermute | solution.py:408
  385.9 28.5 %collective-permute-start.58 = (bf16[512,1664]{1,0:T(8,128)(2,1)S(1)}, bf16[512,1664]{1,0:T(8,128)(2,1)S(1)}, u32[]{:S(2)}, u32[]{:S(2)}) collective-permute-start(bf16[512,1664]{1,0:T(8,128)(2,1)S(1)} %add_convert_fusion.1), channel_id=1, source_target_pairs={{0,4},{1,3},{2,6},{3,1},{4,0},{5,7},{6,2},{7,5},{8,12},{9,11},{10,... | collective-permute-start | bytes 5111816 | tf_op jit(solution)/shard_map/ppermute | solution.py:408
  395.5 18.9 %collective-permute-start.60 = (bf16[64,2560]{1,0:T(8,128)(2,1)S(1)}, bf16[64,2560]{1,0:T(8,128)(2,1)S(1)}, u32[]{:S(2)}, u32[]{:S(2)}) collective-permute-start(bf16[64,2560]{1,0:T(8,128)(2,1)S(1)} %get-tuple-element.559), channel_id=1, source_target_pairs={{0,8},{1,9},{2,10},{3,11},{4,12},{5,13},{6,14},{7,15},{8,16},{9,17... | collective-permute-start | bytes 983048 | tf_op jit(solution)/shard_map/ppermute | solution.py:408
  420.5 17.2 %collective-permute-start.63 = (bf16[256,1664]{1,0:T(8,128)(2,1)}, bf16[256,1664]{1,0:T(8,128)(2,1)}, u32[]{:S(2)}, u32[]{:S(2)}) collective-permute-start(bf16[256,1664]{1,0:T(8,128)(2,1)} %add_convert_fusion.5), channel_id=1, source_target_pairs={{0,2},{1,5},{2,0},{3,7},{4,6},{5,1},{6,4},{7,3},{8,10},{9,13},{10,... | collective-permute-start | bytes 2555912 | tf_op jit(solution)/shard_map/ppermute | solution.py:408
  (168 other events, 1566.1 us)

commit v5 on v3

--- a/solution.py
+++ b/solution.py
@@ -180,7 +180,7 @@
             shape_of(length, inner), shape_of(length, width),
         ],
         compiler_params=PARAMS,
-        cost_estimate=cost(16),
+        cost_estimate=cost(4),
         name="self_forward",
     )(place, target_all, gain, weights, weights, weights, windows, qseg, kseg)
 
@@ -241,7 +241,7 @@
             shape_of(1, width, dtype=F32),
         ],
         compiler_params=PARAMS,
-        cost_estimate=cost(23),
+        cost_estimate=cost(1),
         name="self_back",
     )(place, target_all, grad, query, key, value, weights, weights, weights, windows, qseg, kseg)
 
@@ -297,7 +297,7 @@
             shape_of(rows, width, dtype=F32), shape_of(rows, width),
         ],
         compiler_params=PARAMS,
-        cost_estimate=cost(12),
+        cost_estimate=cost(8),
         name="cross_forward",
     )(
         target, attended, memory_all, gain_cross, gain_ffn, weights, weights, weights, weights,
@@ -373,7 +373,7 @@
         ],
         scratch_shapes=[pltpu.VMEM((rows, width), BF), pltpu.VMEM((rows, width), F32)],
         compiler_params=PARAMS,
-        cost_estimate=cost(18),
+        cost_estimate=cost(1),
         name="cross_back",
     )(
         grad_two, hidden_one, gain, query, key, value, weights, weights, weights, weights, weights,
@@ -480,21 +480,33 @@
         out_shape=jax.ShapeDtypeStruct((depth * 4 * rows, 2 * cols), sources[0].dtype),
         scratch_shapes=[pltpu.SemaphoreType.DMA(())],
         compiler_params=pltpu.CompilerParams(vmem_limit_bytes=48 << 20),
-        cost_estimate=cost(6),
+        cost_estimate=cost(1),
         name="assemble",
     )(links.place, *sources)
 
 
-def weight_grad(links, core, terms, extra=None, z_first=False):
-    depth, total_rows = links.depth, terms[0][0].shape[1]
+def weight_grad(links, terms, extra=None, z_first=False):
+    depth, total_rows = links.depth, terms[0][0][0].shape[1]
     rows = total_rows // (depth * 4)
-    widths = [term[1].shape[1] for term in terms]
+    widths = [term[0][1].shape[1] for term in terms]
     extra_width = 0 if extra is None else extra.shape[1]
     total = sum(widths) + extra_width
     tile = 1408 if total % 1408 == 0 else 512
+    operands = [array for term in terms for pair in term for array in pair]
+    operands += [] if extra is None else [extra]
+    amount, pieces = len(operands), depth if z_first else 2
+    piece_rows = total_rows // pieces
 
     def body(place_ref, *refs):
-        inputs, out_ref, stage, sems = refs[:-3], refs[-3], refs[-2], refs[-1]
+        sources, outs = refs[:amount], refs[amount : amount + pieces]
+        stage, sems = refs[amount + pieces], refs[amount + pieces + 1]
+        inputs, arrived = refs[amount + pieces + 2 : -1], refs[-1]
+        fetches = [
+            pltpu.make_async_copy(source, target, arrived.at[index])
+            for index, (source, target) in enumerate(zip(sources, inputs))
+        ]
+        for fetch in fetches:
+            fetch.start()
         z, x, y, left = place_ref[0], place_ref[1], place_ref[2], place_ref[3] == 0
         places = []
         for chip in range(depth * 4):
@@ -503,50 +515,65 @@
             step = (chip // 4 - z) % depth
             spot = (step * 2 + far) * 2 + near if z_first else (near * 2 + far) * depth + step
             places.append(pl.multiple_of(spot * rows, 8))
-        copies, start = [], 0
-
-        def emit(start, value, width):
+
+        def copy(piece, index, start, width):
+            cols = pl.ds(start, width)
+            return pltpu.make_async_copy(
+                stage.at[pl.ds(piece * piece_rows, piece_rows), cols],
+                outs[piece].at[:, cols],
+                sems.at[piece, index],
+            )
+
+        def emit(index, start, value, width):
             for chip, spot in enumerate(places):
-                stage[pl.ds(spot, rows), start : start + width] = value[
+                stage[pl.ds(spot, rows), pl.ds(start, width)] = value[
                     chip * rows : (chip + 1) * rows
                 ].astype(BF)
-            copies.append(
-                pltpu.make_async_copy(
-                    stage.at[:, pl.ds(start, width)],
-                    out_ref.at[:, pl.ds(start, width)],
-                    sems.at[len(copies)],
-                )
-            )
-            copies[-1].start()
-
-        for index, width in enumerate(widths):
-            acts_l, grad_l, acts_r, grad_r = inputs[4 * index : 4 * index + 4]
-            acts = jnp.where(left, acts_l[...], acts_r[...])
-            for offset in range(0, width, tile):
-                cols = slice(offset, offset + tile)
-                grad = jnp.where(left, grad_l[:, cols], grad_r[:, cols])
-                emit(start, mm(acts, grad, TN), tile)
-                start += tile
+            for piece in range(pieces):
+                copy(piece, index, start, width).start()
+
+        begin, first_copy, taken = 0, 0, 0
+        for term, width in zip(terms, widths):
+            pairs = inputs[taken : taken + 2 * len(term)]
+            for fetch in fetches[taken : taken + 2 * len(term)]:
+                fetch.wait()
+            taken += 2 * len(term)
+
+            def one_tile(index, carry, begin=begin, first_copy=first_copy, pairs=pairs):
+                cols = pl.ds(pl.multiple_of(index * tile, LANES), tile)
+                value = mm(pairs[0][...], pairs[1][:, cols], TN)
+                if len(pairs) == 4:
+                    value = value + mm(pairs[2][...], pairs[3][:, cols], TN)
+                start = pl.multiple_of(begin + index * tile, LANES)
+                emit(first_copy + index, start, value, tile)
+                return carry
+
+            lax.fori_loop(0, width // tile, one_tile, 0)
+            begin, first_copy = begin + width, first_copy + width // tile
         if extra is not None:
+            fetches[-1].wait()
             small = inputs[-1][...]
-            emit(start, jnp.where(left, small, jnp.zeros_like(small)), extra_width)
-        for copy in copies:
-            copy.wait()
-
-    place = links.place.at[3].set(core)
-    operands = [array for term in terms for array in term] + ([] if extra is None else [extra])
+            emit(first_copy, begin, jnp.where(left, small, jnp.zeros_like(small)), extra_width)
+        for piece in range(pieces):
+            for index in range(first_copy):
+                copy(piece, index, index * tile, tile).wait()
+            if extra is not None:
+                copy(piece, first_copy, begin, extra_width).wait()
+
     count = sum(width // tile for width in widths) + (extra is not None)
-    vmem = pl.BlockSpec(memory_space=pltpu.VMEM)
+    hbm = pl.BlockSpec(memory_space=pltpu.HBM)
     return pl.pallas_call(
         body,
-        in_specs=[pl.BlockSpec(memory_space=pltpu.SMEM)] + [vmem] * len(operands),
-        out_specs=pl.BlockSpec(memory_space=pl.ANY),
-        out_shape=jax.ShapeDtypeStruct((total_rows, total), BF),
-        scratch_shapes=[pltpu.VMEM((total_rows, total), BF), pltpu.SemaphoreType.DMA((count,))],
+        in_specs=[pl.BlockSpec(memory_space=pltpu.SMEM)] + [hbm] * amount,
+        out_specs=[pl.BlockSpec(memory_space=pl.ANY)] * pieces,
+        out_shape=[jax.ShapeDtypeStruct((piece_rows, total), BF)] * pieces,
+        scratch_shapes=[pltpu.VMEM((total_rows, total), BF), pltpu.SemaphoreType.DMA((pieces, count))]
+        + [pltpu.VMEM(array.shape, array.dtype) for array in operands]
+        + [pltpu.SemaphoreType.DMA((amount,))],
         compiler_params=pltpu.CompilerParams(vmem_limit_bytes=48 << 20),
-        cost_estimate=cost(4),
+        cost_estimate=cost(1),
         name="weight_grad",
-    )(place, *operands)
+    )(links.place, *operands)
 
 
 def add_low(one, other):
@@ -554,15 +581,8 @@
 
 
 class Scatter:
-    def __init__(self, links):
-        self.links, self.parts = links, []
-
-    def core(self, sent):
-        self.rows = sent.shape[0]
-        self.parts.append(self.links.over_core(sent))
-
-    def keep(self, kept):
-        self.parts.append(kept)
+    def __init__(self, links, kept):
+        self.links, self.parts, self.rows = links, [kept], kept.shape[0]
 
     def total(self, start, count):
         return sum(part[start : start + count].astype(F32) for part in self.parts)
@@ -589,15 +609,22 @@
         for step, send in enumerate(sends, 1):
             self.parts.append(self.links.over_z(send, depth - step))
 
-    def z_start(self, sends):
-        links, depth = self.links, self.links.depth
-        return links.over_z(sends[-1], 1), links.over_z(sends[-2], depth - 1)
+    def z_back(self, sends):
+        return self.links.over_z(sends[-1], 1)
+
+    def z_ahead(self, sends):
+        return self.links.over_z(sends[-2], self.links.depth - 1)
+
+    def z_mid(self, sends, ahead):
+        for send in sends[-3:0:-1]:
+            ahead = self.links.over_z(add_low(ahead, send), self.links.depth - 1)
+        return add_low(ahead, sends[0])
+
+    def z_last(self, back, ahead):
+        self.parts += [back, self.links.over_z(ahead, self.links.depth - 1)]
 
     def z_end(self, sends, back, ahead):
-        self.parts.append(back)
-        for send in sends[-3::-1]:
-            ahead = self.links.over_z(add_low(ahead, send), self.links.depth - 1)
-        self.parts.append(ahead)
+        self.z_last(back, self.z_mid(sends, ahead))
 
     def own(self):
         return self.total(0, self.rows)
@@ -631,26 +658,25 @@
 class PlainScatter:
     parts = ()
 
-    def core(self, sent):
-        self.sent = sent
-
-    def keep(self, kept):
+    def __init__(self, kept):
         self.kept = kept
 
     def halve(self):
-        return self.sent
+        return ()
 
     def near(self, send):
-        self.sent = send
-
-    def z_start(self, sends):
-        return sends, None
-
-    def z_end(self, sends, back, ahead):
-        self.sent = back
-
-    far = near
-    z_sends = own = halve
+        pass
+
+    def z_mid(self, sends, ahead):
+        return ()
+
+    def z_last(self, back, ahead):
+        pass
+
+    def z_back(self, sends):
+        return ()
+
+    far, own, z_ahead = near, halve, z_back
 
     def last(self, total):
         return jnp.split(scatter_all(self.kept), 2, axis=1)
@@ -697,7 +723,6 @@
     right = jnp.concatenate([group[:, cut:] for group, cut in zip(groups, cuts)], axis=1)
     down_cut = width // 2
     steps = list(range(1, depth))
-    some, rest = steps[:1], steps[1:]
     z_one, z_two, z_three = steps[:1], steps[-1:] if depth > 2 else [], steps[1:-1]
     direct = 2 * ffn_down.shape[0] % 16 == 0
     move = lambda function, *args: function(links, *args) if direct else None
@@ -708,7 +733,41 @@
         down_whole = gather_all(ffn_down)
     moved, down = phase(moved, down)
     ends = list(np.cumsum(cuts))
-    first0, second0, third0, fourth0 = jnp.split(moved, ends[:-1], axis=1)
+    first0, second0, gated0 = jnp.split(moved, ends[:2], axis=1)
+
+    first_z = jnp.stack([first0] + z_steps(links, first0, steps))
+    first_z, second0, down = phase(first_z, second0, down)
+
+    first_near = gather_near(links, first_z)
+    down = move(gather_near, down)
+    second_one, second_two = z_steps(links, second0, z_one), z_steps(links, second0, z_two)
+    rows_own = jnp.concatenate([target[0], memory[0]], axis=0)
+    rows_other = links.over_y(rows_own)
+    first_near, down, second_one, second_two, second0, rows_own, rows_other = phase(
+        first_near, down, second_one, second_two, second0, rows_own, rows_other
+    )
+
+    first_far = links.over_far(first_near)
+    first_near_other = links.over_core(first_near)
+    second_three = []
+    for step in z_three:
+        second_three.append(links.over_z((second_one + second_three)[-1], 1))
+    second_z = jnp.stack([second0] + second_one + second_three + second_two)
+    rows_pair = in_order(links.y == 0, rows_own, rows_other)
+    rows_other = links.over_core(rows_pair)
+    first_far, first_near_other, second_z, down, gated0, rows_pair, rows_other, bucket_ids = phase(
+        first_far, first_near_other, second_z, down, gated0, rows_pair, rows_other, bucket_ids
+    )
+    by_y = lambda both: both.reshape(2, 1, rows + enc_rows, width)
+    both = jnp.concatenate(
+        [
+            jnp.where(lead, by_y(rows_pair), by_y(rows_other)),
+            jnp.where(lead, by_y(rows_other), by_y(rows_pair)),
+        ],
+        axis=1,
+    )
+    target_all = both[:, :, :rows].reshape(length, width)
+    memory_all = both[:, :, rows:].reshape(enc, width)
 
     position = seq_index * rows
     heads = seq_size * table_cols
@@ -718,51 +777,22 @@
     bucket_range = jnp.arange(batch_size * table_rows, dtype=jnp.int32)
     onehot = ((bucket[:, None] == bucket_range[None, :]) & near[:, None]).astype(BF)
 
-    first_z = jnp.stack([first0] + z_steps(links, first0, steps))
-    down = move(gather_near, down)
-    first_z, second0, down = phase(first_z, second0, down)
-
-    first_near = gather_near(links, first_z)
+    second_near = gather_near(links, second_z)
+    gated0, down, target_all, memory_all = phase(gated0, down, target_all, memory_all)
+    gated_z = jnp.stack([gated0] + z_steps(links, gated0, steps))
+    third_z, fourth_z = gated_z[..., : cuts[2]], gated_z[..., cuts[2] :]
+    first_far_other = links.over_core(first_far)
     down = move(gather_far, down)
-    second_z = z_steps(links, second0, some)
-    rows_own = jnp.concatenate([target[0], memory[0]], axis=0)
-    rows_other = links.over_y(rows_own)
-    first_near, down, second_z, second0, onehot, rows_own, rows_other = phase(
-        first_near, down, second_z, second0, onehot, rows_own, rows_other
-    )
-
-    first_far = links.over_far(first_near)
-    first_near_other = links.over_core(first_near)
-    second_z = jnp.stack([second0] + second_z + z_steps(links, second0, rest))
-    rows_pair = in_order(links.y == 0, rows_own, rows_other)
-    rows_other = links.over_core(rows_pair)
-    first_far, first_near_other, second_z, down, third0, rows_pair, rows_other = phase(
-        first_far, first_near_other, second_z, down, third0, rows_pair, rows_other
-    )
-    by_y = lambda both: both.reshape(2, 1, rows + enc_rows, width)
-    both = jnp.concatenate(
-        [
-            jnp.where(lead, by_y(rows_pair), by_y(rows_other)),
-            jnp.where(lead, by_y(rows_other), by_y(rows_pair)),
-        ],
-        axis=1,
-    )
-    target_all = both[:, :, :rows].reshape(length, width)
-    memory_all = both[:, :, rows:].reshape(enc, width)
-
-    second_near = gather_near(links, second_z)
-    third_z = jnp.stack([third0] + z_steps(links, third0, steps))
-    first_far_other = links.over_core(first_far)
-    first_far_other, second_near, third_z, fourth0, down, target_all, memory_all = phase(
-        first_far_other, second_near, third_z, fourth0, down, target_all, memory_all
+    (
+        first_far_other, second_near, third_z, fourth_z, down, target_all, memory_all, onehot,
+    ) = phase(
+        first_far_other, second_near, third_z, fourth_z, down, target_all, memory_all, onehot,
     )
 
     second_far = links.over_far(second_near)
     second_near_other = links.over_core(second_near)
     third_near = gather_near(links, third_z)
-    fourth_z = jnp.stack([fourth0] + z_steps(links, fourth0, steps))
-    down_one = move(z_steps, down, z_one)
-    down_two = move(z_steps, down, z_two)
+    down_one, down_two = move(z_steps, down, z_one), move(z_steps, down, z_two)
     first = assemble(links, first_near, first_far, first_near_other, first_far_other)
     smalls = first[:, 3 * inner :].reshape(devices, weight_rows, 2 * LANES)[:, 0, :].astype(F32)
     gains = [smalls[:, i * weight_rows : (i + 1) * weight_rows].reshape(1, width) for i in range(3)]
@@ -799,78 +829,95 @@
     ) = cross_forward(
         target[0], attended, memory_all, gain_cross, gain_ffn, second, qseg, mseg
     )
-    normed_three, third_far, third_near_other, fourth_z, fourth_near = phase(
-        normed_three, third_far, third_near_other, fourth_z, fourth_near
-    )
-    down, down_one, down_two, down_three, normed_three = phase(
-        down, down_one, down_two, down_three, normed_three
+    choose = lambda left, right: (jnp.where(lead, left, right), jnp.where(lead, right, left))
+    cot = cotangent[0]
+    cot_own, cot_sent = choose(cot[:, :down_cut], cot[:, down_cut:])
+    cot_other = links.over_core(cot_sent)
+    (
+        normed_three, third_far, third_near_other, fourth_z, fourth_near, down, down_one, down_two,
+        down_three, cot_other,
+    ) = phase(
+        normed_three, third_far, third_near_other, fourth_z, fourth_near, down, down_one, down_two,
+        down_three, cot_other,
     )
 
     fourth_near = jnp.stack([fourth_z, fourth_near])
     fourth_far = links.over_far(fourth_near)
-    fourth_near_other = links.over_core(fourth_near)
     if direct:
         down = jnp.stack([down] + down_one + down_three + down_two)
+    third_far_other, down, fourth_later = phase(links.over_core(third_far), down, fourth_near)
     down_other = links.over_core(down) if direct else None
-    third = assemble(links, third_near, third_far, third_near_other, links.over_core(third_far))
+    fourth_near_other = links.over_core(fourth_later)
+    third = assemble(links, third_near, third_far, third_near_other, third_far_other)
     third_gate_up = mm(normed_three, third)
     if direct:
         w_down = assemble(links, down, down_other)
     else:
         w_down = down_whole
-    third_gate_up, fourth_far, fourth_near_other, w_down = phase(
-        third_gate_up, fourth_far, fourth_near_other, w_down
+    third_gate_up, fourth_far, fourth_near_other, w_down, normed_three = phase(
+        third_gate_up, fourth_far, fourth_near_other, w_down, normed_three
     )
 
     fourth_far_other = links.over_core(fourth_far)
-    cot = cotangent[0]
-
+    normed_other = links.over_core(normed_three)
     def gated(gate_up, start):
         inner_act, pull = jax.vjp(gated_unit, gate_up[:, :part], gate_up[:, part:])
         grad_gate, grad_up = pull(mm(cot, w_down[start : start + part], NT))
         return inner_act.astype(BF), grad_gate.astype(BF), grad_up.astype(BF)
 
     inner_a, gate_a, up_a = gated(third_gate_up, 0)
-    third_sum, fourth_sum = Scatter(links), Scatter(links)
-    third_terms = [(normed_three, gate_a, normed_three, up_a)]
-    third_send = weight_grad(links, 1 - core, third_terms)
-    third_send, gate_a, up_a, fourth_far_other, w_down = phase(
-        third_send, gate_a, up_a, fourth_far_other, w_down
-    )
-
-    third_sum.core(third_send)
+    third_own, third_sent = choose(gate_a, up_a)
+    third_own, third_sent, inner_a, fourth_far_other, normed_other = phase(
+        third_own, third_sent, inner_a, fourth_far_other, normed_other
+    )
+
+    third_other = links.over_core(third_sent)
+    inner_a_other = links.over_core(inner_a)
     fourth = assemble(links, fourth_near, fourth_far, fourth_near_other, fourth_far_other)
-    third_sum.keep(weight_grad(links, core, third_terms))
-    third_send = third_sum.halve()
-    third_send, fourth = phase(third_send, fourth)
-
+    third_other, inner_a_other, fourth = phase(third_other, inner_a_other, fourth)
+    third_keep, third_send = weight_grad(
+        links, [[(normed_three, third_own), (normed_other, third_other)]]
+    )
+
+    third_keep, third_send, fourth = phase(third_keep, third_send, fourth)
+    third_sum = Scatter(links, third_keep)
     third_sum.near(third_send)
     inner_b, gate_b, up_b = gated(mm(normed_three, fourth), part)
-    fourth_terms = [(normed_three, gate_b, normed_three, up_b)]
-    fourth_sum.core(weight_grad(links, 1 - core, fourth_terms))
+    fourth_own, fourth_sent = choose(gate_b, up_b)
+    fourth_other = links.over_core(fourth_sent)
+    inner_b_other = links.over_core(inner_b)
     inner_low = jnp.concatenate([inner_a, inner_b], axis=1)
-    down_terms = [(inner_low, cot[:, :down_cut], inner_low, cot[:, down_cut:])]
-    down_sum = Scatter(links) if direct else PlainScatter()
+    inner_other = jnp.concatenate([inner_a_other, inner_b_other], axis=1)
     if direct:
-        down_sum.core(weight_grad(links, 1 - core, down_terms, z_first=True))
-        down_sum.keep(weight_grad(links, core, down_terms, z_first=True))
+        down_keep, *down_sends = weight_grad(
+            links, [[(inner_low, cot_own), (inner_other, cot_other)]], z_first=True
+        )
+        down_sum = Scatter(links, down_keep)
     else:
-        down_sum.core(inner_low)
-        down_sum.keep(mm(inner_low, cot, TN).astype(BF))
+        down_sends, down_sum = (), PlainScatter(mm(inner_low, cot, TN).astype(BF))
+    (
+        third_sum.parts, fourth_own, fourth_other, gate_b, up_b, down_sends, down_sum.parts,
+        inner_low,
+    ) = phase(
+        third_sum.parts, fourth_own, fourth_other, gate_b, up_b, down_sends, down_sum.parts,
+        inner_low,
+    )
+
+    fourth_keep, fourth_send = weight_grad(
+        links, [[(normed_three, fourth_own), (normed_other, fourth_other)]]
+    )
+    third_send, fourth_keep, fourth_send, gate_b, up_b, down_sends = phase(
+        third_sum.halve(), fourth_keep, fourth_send, gate_b, up_b, down_sends
+    )
+    third_sum.far(third_send)
+    fourth_sum = Scatter(links, fourth_keep)
+    fourth_sum.near(fourth_send)
+    down_back, down_ahead = down_sum.z_back(down_sends), down_sum.z_ahead(down_sends)
     grad_normed_three = mm(jnp.concatenate([gate_a, up_a], axis=1), third, NT) + mm(
         jnp.concatenate([gate_b, up_b], axis=1), fourth, NT
     )
     through, grad_gain_ffn = norm_back(hidden_two, gain_ffn, grad_normed_three)
     grad_hidden_two = cot.astype(F32) + through
-    fourth_sum.keep(weight_grad(links, core, fourth_terms))
-    third_sum.parts, fourth_sum.parts, down_sum.parts, grad_hidden_two = phase(
-        third_sum.parts, fourth_sum.parts, down_sum.parts, grad_hidden_two
-    )
-
-    third_sum.far(third_sum.halve())
-    fourth_sum.near(fourth_sum.halve())
-    down_sends = down_sum.z_sends()
-    down_back, down_ahead = down_sum.z_start(down_sends)
     low_two = grad_hidden_two.astype(BF)
     (
         grad_cq, grad_ck, grad_cv, memory_part, grad_hidden_one, low_one, grad_attended,
@@ -881,41 +928,79 @@
     )
     half = inner // 2
     (
-        third_sum.parts, fourth_sum.parts, down_back, down_ahead, grad_cq, grad_ck, grad_cv,
-        low_one, grad_attended,
+        third_sum.parts, fourth_sum.parts, down_sends, down_back, down_ahead, grad_cq, grad_ck,
+        grad_cv, low_two, low_one, grad_attended, memory_part,
     ) = phase(
-        third_sum.parts, fourth_sum.parts, down_back, down_ahead, grad_cq, grad_ck, grad_cv,
-        low_one, grad_attended,
-    )
-
-    cross_terms = [
-        (normed_two, grad_cq, cross_attended, low_two),
-        (memory_all, grad_ck, memory_all, grad_cv),
-        (attended, low_one[:, :half], attended, low_one[:, half:]),
-    ]
-    cross_sum = Scatter(links)
-    cross_sum.core(weight_grad(links, 1 - core, cross_terms))
-    fourth_sum.far(fourth_sum.halve())
+        third_sum.parts, fourth_sum.parts, down_sends, down_back, down_ahead, grad_cq, grad_ck,
+        grad_cv, low_two, low_one, grad_attended, memory_part,
+    )
+
+    cross_acts, cross_acts_sent = choose(normed_two, cross_attended)
+    cross_grad, cross_grad_sent = choose(grad_cq, low_two)
+    cross_kv, cross_kv_sent = choose(grad_ck, grad_cv)
+    cross_sent = jnp.concatenate(
+        [cross_acts_sent, cross_grad_sent, cross_kv_sent, attended, low_one], axis=0
+    )
+    fourth_send, cross_sent, third_sum.parts, memory_part = phase(
+        fourth_sum.halve(), cross_sent, third_sum.parts, memory_part
+    )
+    fourth_sum.far(fourth_send)
+    cross_other = links.over_core(cross_sent)
     third_sum.z(third_sum.z_sends())
-    cross_sum.keep(weight_grad(links, core, cross_terms))
-    cross_sum.parts, fourth_sum.parts, grad_attended = phase(
-        cross_sum.parts, fourth_sum.parts, grad_attended
-    )
-
-    cross_sum.near(cross_sum.halve())
-    down_sum.z_end(down_sends, down_back, down_ahead)
+    memory_rows = SeqScatter(links, memory_part)
+    bounds = np.cumsum([rows, rows, enc, rows]).tolist()
+    other_acts, other_grad, other_kv, other_attended, other_low = jnp.split(
+        cross_other, bounds, axis=0
+    )
+    low_half = choose(low_one[:, :half], low_one[:, half:])[0]
+    other_low = choose(other_low[:, :half], other_low[:, half:])[0]
+    cross_keep, cross_send = weight_grad(
+        links,
+        [
+            [(cross_acts, cross_grad), (other_acts, other_grad)],
+            [(memory_all, add_low(cross_kv, other_kv))],
+            [(attended, low_half), (other_attended, other_low)],
+        ],
+    )
+    (
+        cross_keep, cross_send, fourth_sum.parts, third_sum.parts, grad_attended, down_sends,
+        down_back, down_ahead, memory_rows.sent, memory_rows.kept,
+    ) = phase(
+        cross_keep, cross_send, fourth_sum.parts, third_sum.parts, grad_attended, down_sends,
+        down_back, down_ahead, memory_rows.sent, memory_rows.kept,
+    )
+
+    cross_sum = Scatter(links, cross_keep)
+    cross_sum.near(cross_send)
+    down_mid, fourth_sends, grad_attended = phase(
+        down_sum.z_mid(down_sends, down_ahead), fourth_sum.z_sends(), grad_attended
+    )
+    down_sum.z_last(down_back, down_mid)
+    fourth_sum.z(fourth_sends)
     grad_q, grad_k, grad_v, grad_windows, grad_normed, grad_gain_self = self_back(
         position1, target_all, grad_attended, queries, keys, values, first, windows, qseg, kseg
     )
     (
-        cross_sum.parts, third_sum.parts, down_sum.parts, grad_q, grad_k, grad_v, grad_windows,
-        grad_normed, grad_gain_self, memory_part,
+        cross_sum.parts, down_sum.parts, fourth_sum.parts, third_sum.parts, grad_q, grad_k, grad_v,
+        grad_windows, grad_normed, grad_gain_self, memory_rows.sent, memory_rows.kept,
     ) = phase(
-        cross_sum.parts, third_sum.parts, down_sum.parts, grad_q, grad_k, grad_v, grad_windows,
-        grad_normed, grad_gain_self, memory_part,
-    )
-
-    cross_sum.far(cross_sum.halve())
+        cross_sum.parts, down_sum.parts, fourth_sum.parts, third_sum.parts, grad_q, grad_k, grad_v,
+        grad_windows, grad_normed, grad_gain_self, memory_rows.sent, memory_rows.kept,
+    )
+
+    cut = inner + half
+    self_own, self_sent = choose(
+        jnp.concatenate([grad_q, grad_k[:, :half]], axis=1),
+        jnp.concatenate([grad_v, grad_k[:, half:]], axis=1),
+    )
+    (
+        cross_send, self_own, self_sent, grad_windows, grad_gain_self, grad_normed,
+    ) = phase(
+        cross_sum.halve(), self_own, self_sent, grad_windows, grad_gain_self, grad_normed,
+    )
+    cross_sum.far(cross_send)
+    self_other = links.over_core(self_sent)
+    normed_rows = SeqScatter(links, grad_normed)
     grad_windows = grad_windows.reshape(heads, rows + length)
     grad_table = lax.dot_general(
         onehot.astype(F32), grad_windows, (((0,), (1,)), ((), ())), precision=lax.Precision.HIGHEST
@@ -927,49 +1012,77 @@
     small_grad = jnp.pad(
         small_grad[:, None], ((0, 0), (0, weight_rows - 1), (0, LANES - small_grad.shape[1]))
     ).reshape(devices * weight_rows, LANES)
-    cut = inner + half
-    self_terms = [
-        (normed_all, grad_q, normed_all, grad_v),
-        (normed_all, grad_k[:, :half], normed_all, grad_k[:, half:]),
-    ]
-    self_sum = Scatter(links)
-    self_sum.core(weight_grad(links, 1 - core, self_terms, small_grad))
-    self_sum.keep(weight_grad(links, core, self_terms, small_grad))
-    fourth_sum.z(fourth_sum.z_sends())
-    self_sum.parts, cross_sum.parts = phase(self_sum.parts, cross_sum.parts)
-
-    self_sum.near(self_sum.halve())
-    cross_sends = cross_sum.z_sends()
-    cross_back_z, cross_ahead_z = cross_sum.z_start(cross_sends)
-    down_sum.far(down_sum.halve())
-    normed_rows = SeqScatter(links, grad_normed)
+    small_grad = small_grad.astype(BF)
+    small_other = links.over_core(small_grad)
+    (
+        self_own, self_other, small_grad, small_other, cross_sum.parts, down_sum.parts, fourth_sum.parts,
+        third_sum.parts, normed_rows.sent, normed_rows.kept, memory_rows.sent, memory_rows.kept,
+        inner_low,
+    ) = phase(
+        self_own, self_other, small_grad, small_other, cross_sum.parts, down_sum.parts, fourth_sum.parts,
+        third_sum.parts, normed_rows.sent, normed_rows.kept, memory_rows.sent, memory_rows.kept,
+        inner_low,
+    )
+    self_keep, self_send = weight_grad(
+        links,
+        [[(normed_all, add_low(self_own, self_other))]],
+        add_low(small_grad, small_other),
+    )
+
+    (
+        self_keep, self_send, cross_sum.parts, inner_low, third_sum.parts, fourth_sum.parts,
+        down_sum.parts, memory_rows.sent, normed_rows.sent,
+    ) = phase(
+        self_keep, self_send, cross_sum.parts, inner_low, third_sum.parts, fourth_sum.parts,
+        down_sum.parts, memory_rows.sent, normed_rows.sent,
+    )
+    self_sum = Scatter(links, self_keep)
+    self_sum.near(self_send)
+    cross_sends, down_send = cross_sum.z_sends(), down_sum.halve()
+    memory_rows.second()
+    down_sum.far(down_send)
+    cross_back_z, cross_ahead_z = cross_sum.z_back(cross_sends), cross_sum.z_ahead(cross_sends)
     activations = (hidden_two + mm(inner_low, w_down)).astype(BF)
-    (
-        self_sum.parts, cross_back_z, cross_ahead_z, down_sum.parts, fourth_sum.parts,
-        normed_rows.sent,
+    third_total = third_sum.own()
+    (
+        self_sum.parts, cross_back_z, cross_ahead_z, down_sum.parts, activations, third_total,
+        fourth_sum.parts, memory_rows.sent, memory_rows.kept, normed_rows.sent, normed_rows.kept,
     ) = phase(
-        self_sum.parts, cross_back_z, cross_ahead_z, down_sum.parts, fourth_sum.parts,
-        normed_rows.sent,
-    )
-
-    self_sum.far(self_sum.halve())
+        self_sum.parts, cross_back_z, cross_ahead_z, down_sum.parts, activations, third_total,
+        fourth_sum.parts, memory_rows.sent, memory_rows.kept, normed_rows.sent, normed_rows.kept,
+    )
+
+    (
+        self_send, down_sum.parts, cross_sends, cross_back_z, cross_ahead_z, normed_rows.sent,
+        third_total, fourth_sum.parts, memory_rows.sent,
+    ) = phase(
+        self_sum.halve(), down_sum.parts, cross_sends, cross_back_z, cross_ahead_z,
+        normed_rows.sent, third_total, fourth_sum.parts, memory_rows.sent,
+    )
+    self_sum.far(self_send)
     cross_sum.z_end(cross_sends, cross_back_z, cross_ahead_z)
     down_sum.near(down_sum.halve())
     normed_rows.second()
-    gate_one, up_one = third_sum.last(third_sum.own())
-    memory_rows = SeqScatter(links, memory_part)
-    self_sum.parts, down_sum.parts, cross_sum.parts, normed_rows.sent, memory_rows.sent = phase(
-        self_sum.parts, down_sum.parts, cross_sum.parts, normed_rows.sent, memory_rows.sent
-    )
-
-    self_sum.z(self_sum.z_sends())
-    memory_rows.second()
     memory_grad = memory_rows.total()
-    down_out = jnp.concatenate(down_sum.last(down_sum.own()), axis=1)
+    fourth_total = fourth_sum.own()
+    (
+        self_sum.parts, cross_sum.parts, down_sum.parts, normed_rows.sent, fourth_total,
+        memory_grad,
+    ) = phase(
+        self_sum.parts, cross_sum.parts, down_sum.parts, normed_rows.sent, fourth_total,
+        memory_grad,
+    )
+
+    self_sends, cross_sum.parts, down_sum.parts, fourth_total, normed_rows.sent = phase(
+        self_sum.z_sends(), cross_sum.parts, down_sum.parts, fourth_total, normed_rows.sent
+    )
+    self_sum.z(self_sends)
+    gate_one, up_one = third_sum.last(third_total)
+    gate_two, up_two = fourth_sum.last(fourth_total)
     cross_left, cross_right = cross_sum.last(cross_sum.own())
-    gate_two, up_two = fourth_sum.last(fourth_sum.own())
     through, _ = norm_back(target[0].astype(F32), gain_self, normed_rows.total())
     target_grad = grad_hidden_one + through
+    down_out = jnp.concatenate(down_sum.last(down_sum.own()), axis=1)
     self_left, self_right = self_sum.last(self_sum.own())
     join = lambda left, right: jnp.concatenate([left, right], axis=1)
 

time: 496 us -> 462 us (0.931)
  the two profiles are of different devices: /device:TPU:0 before, /device:TPU:11 now
where the time goes in v5:
time: 462 us; the launch traced here: 454 us
  waiting for transfers between devices  148 us (32%)
  Pallas kernels  120 us (26%)
  starting transfers between devices  64.1 us (14%)
  other arithmetic  53.2 us (12%)
  local copies, waits for them, and re-layouts  37.8 us (8%)
  matrix products  28.2 us (6%)
    ppermute x78, waiting for transfers between devices, move(): return lax.ppermute(value, AXES, pairs)  148 us
    ppermute x78, starting transfers between devices, move(): return lax.ppermute(value, AXES, pairs)  64.1 us
    pallas_call x5, Pallas kernels, assemble(): pl.pallas_call(body, in_specs=[pl.BlockSpec(memory_space=pltpu.SMEM)] + [...  30.3 us
    dot_general x8, matrix products, mm(): return lax.dot_general(left, right, dims, preferred_element_type=F32)  27.7 us
    pallas_call x1, Pallas kernels, self_back(): pl.pallas_call(body, grid=(pairs,), in_specs=[SMEM, whole(target_all), pa...  23 us
    pallas_call x5, Pallas kernels, weight_grad(): pl.pallas_call(body, in_specs=[pl.BlockSpec(memory_space=pltpu.SMEM)] + [...  22.1 us
    pallas_call x1, Pallas kernels, cross_back(): pl.pallas_call(body, grid=(pairs,), in_specs=[whole(grad_two), whole(hidd...  17.4 us
    unnamed x227, local copies, waits for them, and re-layouts  16.8 us
  transfers between devices with their start and end apart: 78, of which 31 were waited for; matrix products, arithmetic and copies ran while one was open for 16% of the time, Pallas kernels for 24%

profile of v5, /device:TPU:11, one launch (start us, length us, event | category | flops | bytes accessed | tf_op | source)
XLA Modules:
  0.0 454.3 jit_solution(5251784177504094705)
XLA Ops:
  14.1 9.4 %collective-permute-done.3 = bf16[64,1664]{1,0:T(8,128)(2,1)S(1)} collective-permute-done((bf16[64,1664]{1,0:T(8,128)(2,1)S(1)}, bf16[64,1664]{1,0:T(8,128)(2,1)S(1)}, u32[]{:S(2)}, u32[]{:S(2)}) %collective-permute-start.3) | collective-permute-done | bytes 213024 | tf_op jit(solution)/shard_map/ppermute | solution.py:408
  23.5 4.6 %collective-permute-done.4 = bf16[64,1664]{1,0:T(8,128)(2,1)S(1)} collective-permute-done((bf16[64,1664]{1,0:T(8,128)(2,1)S(1)}, bf16[64,1664]{1,0:T(8,128)(2,1)S(1)}, u32[]{:S(2)}, u32[]{:S(2)}) %collective-permute-start.4) | collective-permute-done | bytes 213024 | tf_op jit(solution)/shard_map/ppermute | solution.py:408
  33.3 13.0 %collective-permute-done.6 = bf16[176,512]{1,0:T(8,128)(2,1)S(1)} collective-permute-done((bf16[176,512]{1,0:T(8,128)(2,1)S(1)}, bf16[176,512]{1,0:T(8,128)(2,1)S(1)}, u32[]{:S(2)}, u32[]{:S(2)}) %collective-permute-start.6) | collective-permute-done | bytes 180256 | tf_op jit(solution)/shard_map/ppermute | solution.py:408
  55.1 9.6 %collective-permute-done.12 = bf16[64,2560]{1,0:T(8,128)(2,1)S(1)} collective-permute-done((bf16[64,2560]{1,0:T(8,128)(2,1)S(1)}, bf16[64,2560]{1,0:T(8,128)(2,1)S(1)}, u32[]{:S(2)}, u32[]{:S(2)}) %collective-permute-start.12) | collective-permute-done | bytes 327712 | tf_op jit(solution)/shard_map/ppermute | solution.py:408
  66.1 5.6 %collective-permute-done.10.refs_1_ = bf16[2,4,64,1664]{3,2,1,0:T(8,128)(2,1)} collective-permute-done((bf16[2,4,64,1664]{3,2,1,0:T(8,128)(2,1)S(1)}, bf16[2,4,64,1664]{3,2,1,0:T(8,128)(2,1)}, u32[]{:S(2)}, u32[]{:S(2)}) %collective-permute-start.10) | collective-permute-done | bytes 1703968 | tf_op jit(solution)/shard_map/ppermute | solution.py:408
  80.5 4.3 gather_fusion
  85.9 15.6 %collective-permute-done.16 = bf16[64,2816]{1,0:T(8,128)(2,1)S(1)} collective-permute-done((bf16[64,2816]{1,0:T(8,128)(2,1)S(1)}, bf16[64,2816]{1,0:T(8,128)(2,1)S(1)}, u32[]{:S(2)}, u32[]{:S(2)}) %collective-permute-start.16) | collective-permute-done | bytes 360480 | tf_op jit(solution)/shard_map/ppermute | solution.py:408
  101.5 5.1 %collective-permute-done.18 = bf16[64,2816]{1,0:T(8,128)(2,1)} collective-permute-done((bf16[64,2816]{1,0:T(8,128)(2,1)S(1)}, bf16[64,2816]{1,0:T(8,128)(2,1)}, u32[]{:S(2)}, u32[]{:S(2)}) %collective-permute-start.18) | collective-permute-done | bytes 360480 | tf_op jit(solution)/shard_map/ppermute | solution.py:408
  118.5 6.1 %assemble.5.wq_ref.wk_ref.wv_ref = bf16[1024,3328]{1,0:T(8,128)(2,1)} custom-call(s32[4]{0:T(128)S(1)} %pad_add_fusion.place_ref, bf16[2,4,64,1664]{3,2,1,0:T(8,128)(2,1)S(1)} %copy-done.5, bf16[2,4,64,1664]{3,2,1,0:T(8,128)(2,1)} %collective-permute-done.10.refs_1_, bf16[2,4,64,1664]{3,2,1,0:T(8,128)(2,1)} %collective-permute-done.11.refs_2_, ...), custom_call_target="tpu_custom_call" | custom-call | flops 1000000000 | bytes 1 | tf_op jit(solution)/shard_map/assemble/pallas_call | solution.py:475
  128.1 15.4 %self_forward.1 = (bf16[128,1024]{1,0:T(8,128)(2,1)S(1)}, bf16[128,1024]{1,0:T(8,128)(2,1)S(1)}, bf16[512,1024]{1,0:T(8,128)(2,1)S(1)}, bf16[512,1024]{1,0:T(8,128)(2,1)S(1)}, bf16[512,1024]{1,0:T(8,128)(2,1)S(1)}) custom-call(s32[1]{0:T(128)} %bitcast.4.pos_ref, bf16[512,1024]{1,0:T(8,128)(2,1)S(1)} %bitcast.141, f32[1,1024]{1,0:T(1,128)S(1)} %reshape.224.gain_ref, ...), custom_call_target="tpu_custom_call" | custom-call | flops 4000000000 | bytes 1 | tf_op jit(solution)/shard_map/self_forward/pallas_call | solution.py:166
  158.1 8.0 %assemble.6.wo_ref.wq_ref.wk_ref.wv_ref.wc_ref = bf16[1024,5120]{1,0:T(8,128)(2,1)} custom-call(s32[4]{0:T(128)S(1)} %pad_add_fusion.place_ref, bf16[2,4,64,2560]{3,2,1,0:T(8,128)(2,1)S(1)} %pad_maximum_fusion.1.refs_0_, bf16[2,4,64,2560]{3,2,1,0:T(8,128)(2,1)} %collective-permute-done.20.refs_1_, bf16[2,4,64,2560]{3,2,1,0:T(8,128)(2,1)} %collective-permute-done.21.refs_2_, ...), custom_call_target="tpu_custom_call" | custom-call | flops 1000000000 | bytes 1 | tf_op jit(solution)/shard_map/assemble/pallas_call | solution.py:475
  166.2 12.2 %cross_forward.1 = (f32[128,1024]{1,0:T(8,128)S(1)}, bf16[128,1024]{1,0:T(8,128)(2,1)S(1)}, bf16[128,1024]{1,0:T(8,128)(2,1)S(1)}, bf16[256,1024]{1,0:T(8,128)(2...) custom-call(bf16[128,1024]{1,0:T(8,128)(2,1)S(1)} %bitcast.144, ...), custom_call_target="tpu_custom_call" | custom-call | flops 8000000000 | bytes 1 | tf_op jit(solution)/shard_map/cross_forward/pallas_call | solution.py:280
  187.9 5.4 %assemble.7 = bf16[1024,2816]{1,0:T(8,128)(2,1)} custom-call(s32[4]{0:T(128)S(1)} %pad_add_fusion.place_ref, bf16[2,4,64,1408]{3,2,1,0:T(8,128)(2,1)} %pad_maximum_fusion.6.refs_0_, bf16[2,4,64,1408]{3,2,1,0:T(8,128)(2,1)} %collective-permute-done.26.refs_1_, bf16[2,4,64,1408]{3,2,1,0:T(8,128)(2,1)} %collective-permute-done.27.refs_2_, ...), custom_call_target="tpu_custom_call" | custom-call | flops 1000000000 | bytes 1 | tf_op jit(solution)/shard_map/assemble/pallas_call | solution.py:475
  196.9 5.3 %assemble.8 = bf16[2816,1024]{1,0:T(8,128)(2,1)} custom-call(s32[4]{0:T(128)S(1)} %pad_add_fusion.place_ref, bf16[4,2,2,176,512]{4,3,2,1,0:T(8,128)(2,1)S(1)} %pad_maximum_fusion.refs_0_, bf16[4,2,2,176,512]{4,3,2,1,0:T(8,128)(2,1)} %collective-permute-done.34.refs_1_), custom_call_target="tpu_custom_call" | custom-call | flops 1000000000 | bytes 1 | tf_op jit(solution)/shard_map/assemble/pallas_call | solution.py:475
  209.9 5.4 %assemble.9 = bf16[1024,2816]{1,0:T(8,128)(2,1)} custom-call(s32[4]{0:T(128)S(1)} %pad_add_fusion.place_ref, bf16[2,4,64,1408]{3,2,1,0:T(8,128)(2,1)} %pad_maximum_fusion.7.refs_0_, bf16[2,4,64,1408]{3,2,1,0:T(8,128)(2,1)} %collective-permute-done.32.refs_1_, bf16[2,4,64,1408]{3,2,1,0:T(8,128)(2,1)} %collective-permute-done.33.refs_2_, ...), custom_call_target="tpu_custom_call" | custom-call | flops 1000000000 | bytes 1 | tf_op jit(solution)/shard_map/assemble/pallas_call | solution.py:475
  218.7 4.1 fusion.90
  228.7 5.5 %weight_grad.6 = (bf16[704,512]{1,0:T(8,128)(2,1)S(1)}, bf16[704,512]{1,0:T(8,128)(2,1)S(1)}, bf16[704,512]{1,0:T(8,128)(2,1)S(1)}, bf16[704,512]{1,0:T(8,128)(2,1)S(1)}) custom-call(s32[4]{0:T(128)S(1)} %pad_add_fusion.place_ref, bf16[128,2816]{1,0:T(8,128)(2,1)S(1)} %pad_maximum_fusion.13.refs_0_, bf16[128,512]{1,0:T(8,128)(2,1)S(1)} %copy-done.48, ...), custom_call_target="tpu_custom_call" | custom-call | flops 1000000000 | bytes 1 | tf_op jit(solution)/shard_map/weight_grad/pallas_call | solution.py:565
  236.1 5.2 %collective-permute-done.39 = bf16[512,1408]{1,0:T(8,128)(2,1)S(1)} collective-permute-done((bf16[512,1408]{1,0:T(8,128)(2,1)S(1)}, bf16[512,1408]{1,0:T(8,128)(2,1)S(1)}, u32[]{:S(2)}, u32[]{:S(2)}) %collective-permute-start.39) | collective-permute-done | bytes 1441824 | tf_op jit(solution)/shard_map/ppermute | solution.py:408
  249.4 4.6 %fusion.32 = f32[128,1024]{1,0:T(8,128)S(1)} fusion(bf16[1024,2816]{1,0:T(8,128)(2,1)} %assemble.9, bf16[128,1408]{1,0:T(8,128)(2,1)S(1)} %get-tuple-element.436, bf16[128,1408]{1,0:T(8,128)(2,1)S(1)} %get-tuple-element.435), kind=kOutput, calls=%fused_computation.70 | convolution fusion | flops 739639296 | bytes 7012352 | tf_op jit(solution)/shard_map/dot_general | solution.py:25
  254.0 4.7 %multiply_reduce_fusion = (bf16[1024]{0:T(1024)(128)(2,1)S(1)}, f32[128]{0:T(128)S(1)}, f32[128,1024]{1,0:T(8,128)S(1)}) fusion(f32[128,1024]{1,0:T(8,128)S(1)} %get-tuple-element.434, f32[128]{0:T(128)S(1)} %add_rsqrt_fusion.1, f32[1024]{0:T(1024)S(1)} %mul.224, f32[128,1024]{1,0:T(8,128)S(1)} %fusion.32, bf16[1024,2816]{1,0:T(8,128)(2,1)} %assemble.7, ...), kind=kOutput, calls=%fused_computation.106 | convolution fusion | flops 740555648 | bytes 8068096 | tf_op jit(solution)/shard_map/dot_general | solution.py:25
  260.2 17.4 %cross_back.1 = (bf16[128,1024]{1,0:T(8,128)(2,1)S(1)}, bf16[256,1024]{1,0:T(8,128)(2,1)S(1)}, bf16[256,1024]{1,0:T(8,128)(2,1)S(1)}, f32[256,1024]{1,0:T(8,128)...) custom-call(f32[128,1024]{1,0:T(8,128)S(1)} %get-tuple-element.659.g, ...), custom_call_target="tpu_custom_call" | custom-call | flops 1000000000 | bytes 1 | tf_op jit(solution)/shard_map/cross_back/pallas_call | solution.py:353
  299.3 5.8 %weight_grad.8 = (bf16[512,2560]{1,0:T(8,128)(2,1)S(1)}, bf16[512,2560]{1,0:T(8,128)(2,1)}) custom-call(s32[4]{0:T(128)S(1)} %pad_add_fusion.place_ref, bf16[128,1024]{1,0:T(8,128)(2,1)S(1)} %copy-done.42, bf16[128,1024]{1,0:T(8,128)(2,1)S(1)} %copy-done.47, bf16[128,1024]{1,0:T(8,128)(2,1)S(1)} %get-tuple-element.682.refs_2_, ...), custom_call_target="tpu_custom_call" | custom-call | flops 1000000000 | bytes 1 | tf_op jit(solution)/shard_map/weight_grad/pallas_call | solution.py:565
  317.4 23.0 %self_back.1 = (bf16[512,1024]{1,0:T(8,128)(2,1)S(1)}, bf16[512,1024]{1,0:T(8,128)(2,1)S(1)}, bf16[512,1024]{1,0:T(8,128)(2,1)S(1)}, f32[8,2,640]{2,1,0:T(2,128)...) custom-call(s32[1]{0:T(128)} %bitcast.4.pos_ref, bf16[512,1024]{1,0:T(8,128)(2,1)S(1)} %bitcast.142, ...), custom_call_target="tpu_custom_call" | custom-call | flops 1000000000 | bytes 1 | tf_op jit(solution)/shard_map/self_back/pallas_call | solution.py:225
  340.4 4.2 collective-permute-done.55
  357.9 10.6 %collective-permute-done.59 = bf16[256,2560]{1,0:T(8,128)(2,1)} collective-permute-done((bf16[256,2560]{1,0:T(8,128)(2,1)}, bf16[256,2560]{1,0:T(8,128)(2,1)}, u32[]{:S(2)}, u32[]{:S(2)}) %collective-permute-start.59) | collective-permute-done | bytes 1310752 | tf_op jit(solution)/shard_map/ppermute | solution.py:408
  371.6 4.2 weight_grad.9
  382.4 4.3 fusion.10
  387.1 9.0 %collective-permute-done.63 = bf16[64,2560]{1,0:T(8,128)(2,1)S(1)} collective-permute-done((bf16[64,2560]{1,0:T(8,128)(2,1)S(1)}, bf16[64,2560]{1,0:T(8,128)(2,1)S(1)}, u32[]{:S(2)}, u32[]{:S(2)}) %collective-permute-start.63) | collective-permute-done | bytes 327712 | tf_op jit(solution)/shard_map/ppermute | solution.py:408
  396.0 7.3 %collective-permute-done.61 = bf16[512,1664]{1,0:T(8,128)(2,1)S(1)} collective-permute-done((bf16[512,1664]{1,0:T(8,128)(2,1)}, bf16[512,1664]{1,0:T(8,128)(2,1)S(1)}, u32[]{:S(2)}, u32[]{:S(2)}) %collective-permute-start.61) | collective-permute-done | bytes 1703968 | tf_op jit(solution)/shard_map/ppermute | solution.py:408
  409.6 7.6 %collective-permute-done.68 = bf16[176,512]{1,0:T(8,128)(2,1)S(1)} collective-permute-done((bf16[176,512]{1,0:T(8,128)(2,1)S(1)}, bf16[176,512]{1,0:T(8,128)(2,1)S(1)}, u32[]{:S(2)}, u32[]{:S(2)}) %collective-permute-start.68) | collective-permute-done | bytes 180256 | tf_op jit(solution)/shard_map/ppermute | solution.py:408
  419.7 5.0 %collective-permute-start.77 = (f32[88,512]{1,0:T(8,128)S(1)}, f32[88,512]{1,0:T(8,128)S(1)}, u32[]{:S(2)}, u32[]{:S(2)}) collective-permute-start(f32[88,512]{1,0:T(8,128)S(1)} %slice_select_fusion.4), channel_id=1, source_target_pairs={{0,1},{1,0},{2,3},{3,2},{4,5},{5,4},{6,7},{7,6},{8,9},{9,8},{10,11... | collective-permute-start | bytes 540680 | tf_op jit(solution)/shard_map/ppermute | solution.py:408
  433.4 11.7 %collective-permute-done.71 = bf16[64,1664]{1,0:T(8,128)(2,1)S(1)} collective-permute-done((bf16[64,1664]{1,0:T(8,128)(2,1)S(1)}, bf16[64,1664]{1,0:T(8,128)(2,1)S(1)}, u32[]{:S(2)}, u32[]{:S(2)}) %collective-permute-start.71) | collective-permute-done | bytes 213024 | tf_op jit(solution)/shard_map/ppermute | solution.py:408
  (517 shorter events, 192.2 us)
Async XLA Ops:
  28.2 18.8 %collective-permute-start.5 = (bf16[4,64,1664]{2,1,0:T(8,128)(2,1)S(1)}, bf16[4,64,1664]{2,1,0:T(8,128)(2,1)S(1)}, u32[]{:S(2)}, u32[]{:S(2)}) collective-permute-start(bf16[4,64,1664]{2,1,0:T(8,128)(2,1)S(1)} %pad_maximum_fusion.10), channel_id=1, source_target_pairs={{0,4},{1,3},{2,6},{3,1},{4,0},{5,7},{6,2},{7,5},{8,12},{9,11},{10,... | collective-permute-start | bytes 2555912 | tf_op jit(solution)/shard_map/ppermute | solution.py:408
  29.8 20.4 %collective-permute-start.9 = (bf16[192,1024]{1,0:T(8,128)(2,1)S(1)}, bf16[192,1024]{1,0:T(8,128)(2,1)S(1)}, u32[]{:S(2)}, u32[]{:S(2)}) collective-permute-start(bf16[192,1024]{1,0:T(8,128)(2,1)S(1)} %pad_maximum_fusion.17), channel_id=1, source_target_pairs={{0,2},{1,3},{2,0},{3,1},{4,6},{5,7},{6,4},{7,5},{8,10},{9,11},{10,... | collective-permute-start | bytes 1179656 | tf_op jit(solution)/shard_map/ppermute | solution.py:408
  31.1 19.1 %collective-permute-start.7 = (bf16[64,2560]{1,0:T(8,128)(2,1)S(1)}, bf16[64,2560]{1,0:T(8,128)(2,1)S(1)}, u32[]{:S(2)}, u32[]{:S(2)}) collective-permute-start(bf16[64,2560]{1,0:T(8,128)(2,1)S(1)} %split.23), channel_id=1, source_target_pairs={{0,24},{1,25},{2,26},{3,27},{4,28},{5,29},{6,30},{7,31},{8,0},{9,1... | collective-permute-start | bytes 983048 | tf_op jit(solution)/shard_map/ppermute | solution.py:408
  51.0 20.8 %collective-permute-start.10 = (bf16[2,4,64,1664]{3,2,1,0:T(8,128)(2,1)S(1)}, bf16[2,4,64,1664]{3,2,1,0:T(8,128)(2,1)}, u32[]{:S(2)}, u32[]{:S(2)}) collective-permute-start(bf16[2,4,64,1664]{3,2,1,0:T(8,128)(2,1)S(1)} %pad_maximum_fusion.2.refs_0_), channel_id=1, source_target_pairs={{0,2},{1,5},{2,0},{3,7},{4,6},{5,1},{6,4},{7,3},{8,10},{9,13},{10,... | collective-permute-start | bytes 5111816 | tf_op jit(solution)/shard_map/ppermute | solution.py:408
  51.7 20.1 %collective-permute-start.11 = (bf16[2,4,64,1664]{3,2,1,0:T(8,128)(2,1)S(1)}, bf16[2,4,64,1664]{3,2,1,0:T(8,128)(2,1)}, u32[]{:S(2)}, u32[]{:S(2)}) collective-permute-start(bf16[2,4,64,1664]{3,2,1,0:T(8,128)(2,1)S(1)} %pad_maximum_fusion.2.refs_0_), channel_id=1, source_target_pairs={{0,1},{1,0},{2,3},{3,2},{4,5},{5,4},{6,7},{7,6},{8,9},{9,8},{10,11... | collective-permute-start | bytes 5111816 | tf_op jit(solution)/shard_map/ppermute | solution.py:408
  74.1 27.4 %collective-permute-start.16 = (bf16[64,2816]{1,0:T(8,128)(2,1)S(1)}, bf16[64,2816]{1,0:T(8,128)(2,1)S(1)}, u32[]{:S(2)}, u32[]{:S(2)}) collective-permute-start(bf16[64,2816]{1,0:T(8,128)(2,1)S(1)} %copy-done.68), channel_id=1, source_target_pairs={{0,24},{1,25},{2,26},{3,27},{4,28},{5,29},{6,30},{7,31},{8,0},{9,1... | collective-permute-start | bytes 1081352 | tf_op jit(solution)/shard_map/ppermute | solution.py:408
  75.3 26.2 %collective-permute-start.17 = (bf16[64,2816]{1,0:T(8,128)(2,1)S(1)}, bf16[64,2816]{1,0:T(8,128)(2,1)}, u32[]{:S(2)}, u32[]{:S(2)}) collective-permute-start(bf16[64,2816]{1,0:T(8,128)(2,1)S(1)} %copy-done.68), channel_id=1, source_target_pairs={{0,16},{1,17},{2,18},{3,19},{4,20},{5,21},{6,22},{7,23},{8,24},{9,... | collective-permute-start | bytes 1081352 | tf_op jit(solution)/shard_map/ppermute | solution.py:408
  78.5 28.1 %collective-permute-start.18 = (bf16[64,2816]{1,0:T(8,128)(2,1)S(1)}, bf16[64,2816]{1,0:T(8,128)(2,1)}, u32[]{:S(2)}, u32[]{:S(2)}) collective-permute-start(bf16[64,2816]{1,0:T(8,128)(2,1)S(1)} %copy-done.68), channel_id=1, source_target_pairs={{0,8},{1,9},{2,10},{3,11},{4,12},{5,13},{6,14},{7,15},{8,16},{9,17... | collective-permute-start | bytes 1081352 | tf_op jit(solution)/shard_map/ppermute | solution.py:408
  78.5 30.6 %collective-permute-start.15 = (bf16[4,64,2560]{2,1,0:T(8,128)(2,1)S(1)}, bf16[4,64,2560]{2,1,0:T(8,128)(2,1)}, u32[]{:S(2)}, u32[]{:S(2)}) collective-permute-start(bf16[4,64,2560]{2,1,0:T(8,128)(2,1)S(1)} %copy-done.54), channel_id=1, source_target_pairs={{0,4},{1,3},{2,6},{3,1},{4,0},{5,7},{6,2},{7,5},{8,12},{9,11},{10,... | collective-permute-start | bytes 3932168 | tf_op jit(solution)/shard_map/ppermute | solution.py:408
  84.8 26.4 %collective-permute-start.14 = (bf16[2,4,64,1664]{3,2,1,0:T(8,128)(2,1)}, bf16[2,4,64,1664]{3,2,1,0:T(8,128)(2,1)S(1)}, u32[]{:S(2)}, u32[]{:S(2)}) collective-permute-start(bf16[2,4,64,1664]{3,2,1,0:T(8,128)(2,1)} %collective-permute-done.10.refs_1_), channel_id=1, source_target_pairs={{0,1},{1,0},{2,3},{3,2},{4,5},{5,4},{6,7},{7,6},{8,9},{9,8},{10,11... | collective-permute-start | bytes 5111816 | tf_op jit(solution)/shard_map/ppermute | solution.py:408
  112.5 38.6 %collective-permute-start.20 = (bf16[2,4,64,2560]{3,2,1,0:T(8,128)(2,1)S(1)}, bf16[2,4,64,2560]{3,2,1,0:T(8,128)(2,1)}, u32[]{:S(2)}, u32[]{:S(2)}) collective-permute-start(bf16[2,4,64,2560]{3,2,1,0:T(8,128)(2,1)S(1)} %pad_maximum_fusion.1.refs_0_), channel_id=1, source_target_pairs={{0,2},{1,5},{2,0},{3,7},{4,6},{5,1},{6,4},{7,3},{8,10},{9,13},{10,... | collective-permute-start | bytes 7864328 | tf_op jit(solution)/shard_map/ppermute | solution.py:408
  113.6 37.5 %collective-permute-start.21 = (bf16[2,4,64,2560]{3,2,1,0:T(8,128)(2,1)S(1)}, bf16[2,4,64,2560]{3,2,1,0:T(8,128)(2,1)}, u32[]{:S(2)}, u32[]{:S(2)}) collective-permute-start(bf16[2,4,64,2560]{3,2,1,0:T(8,128)(2,1)S(1)} %pad_maximum_fusion.1.refs_0_), channel_id=1, source_target_pairs={{0,1},{1,0},{2,3},{3,2},{4,5},{5,4},{6,7},{7,6},{8,9},{9,8},{10,11... | collective-permute-start | bytes 7864328 | tf_op jit(solution)/shard_map/ppermute | solution.py:408
  114.2 33.4 %collective-permute-start.23 = (bf16[2,2,176,512]{3,2,1,0:T(8,128)(2,1)}, bf16[2,2,176,512]{3,2,1,0:T(8,128)(2,1)}, u32[]{:S(2)}, u32[]{:S(2)}) collective-permute-start(bf16[2,2,176,512]{3,2,1,0:T(8,128)(2,1)} %pad_maximum_fusion.12), channel_id=1, source_target_pairs={{0,24},{1,25},{2,26},{3,27},{4,28},{5,29},{6,30},{7,31},{8,0},{9,1... | collective-permute-start | bytes 2162696 | tf_op jit(solution)/shard_map/ppermute | solution.py:408
  114.9 32.7 %collective-permute-start.24 = (bf16[2,2,176,512]{3,2,1,0:T(8,128)(2,1)}, bf16[2,2,176,512]{3,2,1,0:T(8,128)(2,1)}, u32[]{:S(2)}, u32[]{:S(2)}) collective-permute-start(bf16[2,2,176,512]{3,2,1,0:T(8,128)(2,1)} %pad_maximum_fusion.12), channel_id=1, source_target_pairs={{0,8},{1,9},{2,10},{3,11},{4,12},{5,13},{6,14},{7,15},{8,16},{9,17... | collective-permute-start | bytes 2162696 | tf_op jit(solution)/shard_map/ppermute | solution.py:408
  116.5 28.0 %collective-permute-start.22 = (bf16[4,64,1408]{2,1,0:T(8,128)(2,1)}, bf16[4,64,1408]{2,1,0:T(8,128)(2,1)}, u32[]{:S(2)}, u32[]{:S(2)}) collective-permute-start(bf16[4,64,1408]{2,1,0:T(8,128)(2,1)} %get-tuple-element.367), channel_id=1, source_target_pairs={{0,4},{1,3},{2,6},{3,1},{4,0},{5,7},{6,2},{7,5},{8,12},{9,11},{10,... | collective-permute-start | bytes 2162696 | tf_op jit(solution)/shard_map/ppermute | solution.py:408
  152.2 27.8 %collective-permute-start.26 = (bf16[2,4,64,1408]{3,2,1,0:T(8,128)(2,1)}, bf16[2,4,64,1408]{3,2,1,0:T(8,128)(2,1)}, u32[]{:S(2)}, u32[]{:S(2)}) collective-permute-start(bf16[2,4,64,1408]{3,2,1,0:T(8,128)(2,1)} %pad_maximum_fusion.6.refs_0_), channel_id=1, source_target_pairs={{0,2},{1,5},{2,0},{3,7},{4,6},{5,1},{6,4},{7,3},{8,10},{9,13},{10,... | collective-permute-start | bytes 4325384 | tf_op jit(solution)/shard_map/ppermute | solution.py:408
  153.3 26.8 %collective-permute-start.27 = (bf16[2,4,64,1408]{3,2,1,0:T(8,128)(2,1)}, bf16[2,4,64,1408]{3,2,1,0:T(8,128)(2,1)}, u32[]{:S(2)}, u32[]{:S(2)}) collective-permute-start(bf16[2,4,64,1408]{3,2,1,0:T(8,128)(2,1)} %pad_maximum_fusion.6.refs_0_), channel_id=1, source_target_pairs={{0,1},{1,0},{2,3},{3,2},{4,5},{5,4},{6,7},{7,6},{8,9},{9,8},{10,11... | collective-permute-start | bytes 4325384 | tf_op jit(solution)/shard_map/ppermute | solution.py:408
  154.2 25.8 %collective-permute-start.30 = (bf16[128,512]{1,0:T(8,128)(2,1)}, bf16[128,512]{1,0:T(8,128)(2,1)}, u32[]{:S(2)}, u32[]{:S(2)}) collective-permute-start(bf16[128,512]{1,0:T(8,128)(2,1)} %get-tuple-element.714), channel_id=1, source_target_pairs={{0,1},{1,0},{2,3},{3,2},{4,5},{5,4},{6,7},{7,6},{8,9},{9,8},{10,11... | collective-permute-start | bytes 393224 | tf_op jit(solution)/shard_map/ppermute | solution.py:408
  154.8 25.2 %collective-permute-start.28 = (bf16[4,64,1408]{2,1,0:T(8,128)(2,1)}, bf16[4,64,1408]{2,1,0:T(8,128)(2,1)S(1)}, u32[]{:S(2)}, u32[]{:S(2)}) collective-permute-start(bf16[4,64,1408]{2,1,0:T(8,128)(2,1)} %get-tuple-element.389), channel_id=1, source_target_pairs={{0,4},{1,3},{2,6},{3,1},{4,0},{5,7},{6,2},{7,5},{8,12},{9,11},{10,... | collective-permute-start | bytes 2162696 | tf_op jit(solution)/shard_map/ppermute | solution.py:408
  157.1 22.9 %collective-permute-start.29 = (bf16[2,2,176,512]{3,2,1,0:T(8,128)(2,1)}, bf16[2,2,176,512]{3,2,1,0:T(8,128)(2,1)S(1)}, u32[]{:S(2)}, u32[]{:S(2)}) collective-permute-start(bf16[2,2,176,512]{3,2,1,0:T(8,128)(2,1)} %collective-permute-done.23), channel_id=1, source_target_pairs={{0,24},{1,25},{2,26},{3,27},{4,28},{5,29},{6,30},{7,31},{8,0},{9,1... | collective-permute-start | bytes 2162696 | tf_op jit(solution)/shard_map/ppermute | solution.py:408
  245.8 36.1 %collective-permute-start.43 = (bf16[512,1408]{1,0:T(8,128)(2,1)S(1)}, bf16[512,1408]{1,0:T(8,128)(2,1)S(1)}, u32[]{:S(2)}, u32[]{:S(2)}) collective-permute-start(bf16[512,1408]{1,0:T(8,128)(2,1)S(1)} %get-tuple-element.430), channel_id=1, source_target_pairs={{0,4},{1,3},{2,6},{3,1},{4,0},{5,7},{6,2},{7,5},{8,12},{9,11},{10,... | collective-permute-start | bytes 4325384 | tf_op jit(solution)/shard_map/ppermute | solution.py:408
  246.1 32.2 %collective-permute-start.42 = (bf16[256,1408]{1,0:T(8,128)(2,1)}, bf16[256,1408]{1,0:T(8,128)(2,1)}, u32[]{:S(2)}, u32[]{:S(2)}) collective-permute-start(bf16[256,1408]{1,0:T(8,128)(2,1)} %add_convert_fusion.5), channel_id=1, source_target_pairs={{0,2},{1,5},{2,0},{3,7},{4,6},{5,1},{6,4},{7,3},{8,10},{9,13},{10,... | collective-permute-start | bytes 2162696 | tf_op jit(solution)/shard_map/ppermute | solution.py:408
  247.1 31.2 %collective-permute-start.44 = (bf16[704,512]{1,0:T(8,128)(2,1)S(1)}, bf16[704,512]{1,0:T(8,128)(2,1)S(1)}, u32[]{:S(2)}, u32[]{:S(2)}) collective-permute-start(bf16[704,512]{1,0:T(8,128)(2,1)S(1)} %get-tuple-element.433), channel_id=1, source_target_pairs={{0,24},{1,25},{2,26},{3,27},{4,28},{5,29},{6,30},{7,31},{8,0},{9,1... | collective-permute-start | bytes 2162696 | tf_op jit(solution)/shard_map/ppermute | solution.py:408
  247.1 34.8 %collective-permute-start.45 = (bf16[704,512]{1,0:T(8,128)(2,1)S(1)}, bf16[704,512]{1,0:T(8,128)(2,1)}, u32[]{:S(2)}, u32[]{:S(2)}) collective-permute-start(bf16[704,512]{1,0:T(8,128)(2,1)S(1)} %get-tuple-element.432), channel_id=1, source_target_pairs={{0,8},{1,9},{2,10},{3,11},{4,12},{5,13},{6,14},{7,15},{8,16},{9,17... | collective-permute-start | bytes 2162696 | tf_op jit(solution)/shard_map/ppermute | solution.py:408
  309.8 36.2 %collective-permute-start.52 = (bf16[512,2560]{1,0:T(8,128)(2,1)}, bf16[512,2560]{1,0:T(8,128)(2,1)S(1)}, u32[]{:S(2)}, u32[]{:S(2)}) collective-permute-start(bf16[512,2560]{1,0:T(8,128)(2,1)} %get-tuple-element.471), channel_id=1, source_target_pairs={{0,4},{1,3},{2,6},{3,1},{4,0},{5,7},{6,2},{7,5},{8,12},{9,11},{10,... | collective-permute-start | bytes 7864328 | tf_op jit(solution)/shard_map/ppermute | solution.py:408
  313.7 32.3 %collective-permute-start.53 = (bf16[704,512]{1,0:T(8,128)(2,1)S(1)}, bf16[704,512]{1,0:T(8,128)(2,1)S(1)}, u32[]{:S(2)}, u32[]{:S(2)}) collective-permute-start(bf16[704,512]{1,0:T(8,128)(2,1)S(1)} %add_convert_fusion.3), channel_id=1, source_target_pairs={{0,8},{1,9},{2,10},{3,11},{4,12},{5,13},{6,14},{7,15},{8,16},{9,17... | collective-permute-start | bytes 2162696 | tf_op jit(solution)/shard_map/ppermute | solution.py:408
  313.8 26.6 %collective-permute-start.54 = (bf16[64,1408]{1,0:T(8,128)(2,1)S(1)}, bf16[64,1408]{1,0:T(8,128)(2,1)S(1)}, u32[]{:S(2)}, u32[]{:S(2)}) collective-permute-start(bf16[64,1408]{1,0:T(8,128)(2,1)S(1)} %get-tuple-element.481), channel_id=1, source_target_pairs={{0,8},{1,9},{2,10},{3,11},{4,12},{5,13},{6,14},{7,15},{8,16},{9,17... | collective-permute-start | bytes 540680 | tf_op jit(solution)/shard_map/ppermute | solution.py:408
  314.2 30.4 %collective-permute-start.55 = (bf16[64,1408]{1,0:T(8,128)(2,1)S(1)}, bf16[64,1408]{1,0:T(8,128)(2,1)S(1)}, u32[]{:S(2)}, u32[]{:S(2)}) collective-permute-start(bf16[64,1408]{1,0:T(8,128)(2,1)S(1)} %get-tuple-element.482), channel_id=1, source_target_pairs={{0,16},{1,17},{2,18},{3,19},{4,20},{5,21},{6,22},{7,23},{8,24},{9,... | collective-permute-start | bytes 540680 | tf_op jit(solution)/shard_map/ppermute | solution.py:408
  317.3 28.7 %collective-permute-start.56 = (bf16[64,1408]{1,0:T(8,128)(2,1)S(1)}, bf16[64,1408]{1,0:T(8,128)(2,1)S(1)}, u32[]{:S(2)}, u32[]{:S(2)}) collective-permute-start(bf16[64,1408]{1,0:T(8,128)(2,1)S(1)} %get-tuple-element.483), channel_id=1, source_target_pairs={{0,24},{1,25},{2,26},{3,27},{4,28},{5,29},{6,30},{7,31},{8,0},{9,1... | collective-permute-start | bytes 540680 | tf_op jit(solution)/shard_map/ppermute | solution.py:408
  377.0 19.1 %collective-permute-start.64 = (bf16[352,512]{1,0:T(8,128)(2,1)S(1)}, bf16[352,512]{1,0:T(8,128)(2,1)S(1)}, u32[]{:S(2)}, u32[]{:S(2)}) collective-permute-start(bf16[352,512]{1,0:T(8,128)(2,1)S(1)} %add_convert_fusion.7), channel_id=1, source_target_pairs={{0,2},{1,5},{2,0},{3,7},{4,6},{5,1},{6,4},{7,3},{8,10},{9,13},{10,... | collective-permute-start | bytes 1081352 | tf_op jit(solution)/shard_map/ppermute | solution.py:408
  377.3 26.0 %collective-permute-start.61 = (bf16[512,1664]{1,0:T(8,128)(2,1)}, bf16[512,1664]{1,0:T(8,128)(2,1)S(1)}, u32[]{:S(2)}, u32[]{:S(2)}) collective-permute-start(bf16[512,1664]{1,0:T(8,128)(2,1)} %get-tuple-element.563), channel_id=1, source_target_pairs={{0,4},{1,3},{2,6},{3,1},{4,0},{5,7},{6,2},{7,5},{8,12},{9,11},{10,... | collective-permute-start | bytes 5111816 | tf_op jit(solution)/shard_map/ppermute | solution.py:408
  426.0 22.9 %collective-permute-start.74 = (f32[32,2560]{1,0:T(8,128)S(1)}, f32[32,2560]{1,0:T(8,128)S(1)}, u32[]{:S(2)}, u32[]{:S(2)}) collective-permute-start(f32[32,2560]{1,0:T(8,128)S(1)} %slice_select_fusion), channel_id=1, source_target_pairs={{0,1},{1,0},{2,3},{3,2},{4,5},{5,4},{6,7},{7,6},{8,9},{9,8},{10,11... | collective-permute-start | bytes 983048 | tf_op jit(solution)/shard_map/ppermute | solution.py:408
  (158 other events, 1330.9 us)

commit v6 on v5

--- a/solution.py
+++ b/solution.py
@@ -972,11 +972,11 @@
 
     cross_sum = Scatter(links, cross_keep)
     cross_sum.near(cross_send)
-    down_mid, fourth_sends, grad_attended = phase(
-        down_sum.z_mid(down_sends, down_ahead), fourth_sum.z_sends(), grad_attended
+    down_mid, memory_rows.sent, grad_attended = phase(
+        down_sum.z_mid(down_sends, down_ahead), memory_rows.sent, grad_attended
     )
     down_sum.z_last(down_back, down_mid)
-    fourth_sum.z(fourth_sends)
+    memory_rows.second()
     grad_q, grad_k, grad_v, grad_windows, grad_normed, grad_gain_self = self_back(
         position1, target_all, grad_attended, queries, keys, values, first, windows, qseg, kseg
     )
@@ -994,13 +994,14 @@
         jnp.concatenate([grad_v, grad_k[:, half:]], axis=1),
     )
     (
-        cross_send, self_own, self_sent, grad_windows, grad_gain_self, grad_normed,
+        cross_send, self_own, self_sent, grad_windows, grad_gain_self, fourth_sum.parts,
     ) = phase(
-        cross_sum.halve(), self_own, self_sent, grad_windows, grad_gain_self, grad_normed,
+        cross_sum.halve(), self_own, self_sent, grad_windows, grad_gain_self, fourth_sum.parts,
     )
     cross_sum.far(cross_send)
+    fourth_sends = fourth_sum.z_sends()
+    fourth_back, fourth_ahead = fourth_sum.z_back(fourth_sends), fourth_sum.z_ahead(fourth_sends)
     self_other = links.over_core(self_sent)
-    normed_rows = SeqScatter(links, grad_normed)
     grad_windows = grad_windows.reshape(heads, rows + length)
     grad_table = lax.dot_general(
         onehot.astype(F32), grad_windows, (((0,), (1,)), ((), ())), precision=lax.Precision.HIGHEST
@@ -1015,13 +1016,13 @@
     small_grad = small_grad.astype(BF)
     small_other = links.over_core(small_grad)
     (
-        self_own, self_other, small_grad, small_other, cross_sum.parts, down_sum.parts, fourth_sum.parts,
-        third_sum.parts, normed_rows.sent, normed_rows.kept, memory_rows.sent, memory_rows.kept,
-        inner_low,
+        self_own, self_other, small_grad, small_other, cross_sum.parts, down_sum.parts,
+        fourth_sends, fourth_back, fourth_ahead, third_sum.parts, grad_normed, memory_rows.sent,
+        memory_rows.kept, inner_low,
     ) = phase(
-        self_own, self_other, small_grad, small_other, cross_sum.parts, down_sum.parts, fourth_sum.parts,
-        third_sum.parts, normed_rows.sent, normed_rows.kept, memory_rows.sent, memory_rows.kept,
-        inner_low,
+        self_own, self_other, small_grad, small_other, cross_sum.parts, down_sum.parts,
+        fourth_sends, fourth_back, fourth_ahead, third_sum.parts, grad_normed, memory_rows.sent,
+        memory_rows.kept, inner_low,
     )
     self_keep, self_send = weight_grad(
         links,
@@ -1030,53 +1031,52 @@
     )
 
     (
-        self_keep, self_send, cross_sum.parts, inner_low, third_sum.parts, fourth_sum.parts,
-        down_sum.parts, memory_rows.sent, normed_rows.sent,
+        self_keep, self_send, cross_sum.parts, inner_low, third_sum.parts, fourth_sends,
+        fourth_back, fourth_ahead, down_sum.parts, memory_rows.sent, grad_normed,
     ) = phase(
-        self_keep, self_send, cross_sum.parts, inner_low, third_sum.parts, fourth_sum.parts,
-        down_sum.parts, memory_rows.sent, normed_rows.sent,
+        self_keep, self_send, cross_sum.parts, inner_low, third_sum.parts, fourth_sends,
+        fourth_back, fourth_ahead, down_sum.parts, memory_rows.sent, grad_normed,
     )
     self_sum = Scatter(links, self_keep)
     self_sum.near(self_send)
-    cross_sends, down_send = cross_sum.z_sends(), down_sum.halve()
-    memory_rows.second()
-    down_sum.far(down_send)
+    cross_sends = cross_sum.z_sends()
+    fourth_sum.z_end(fourth_sends, fourth_back, fourth_ahead)
+    normed_rows = SeqScatter(links, grad_normed)
+    memory_grad = memory_rows.total()
     cross_back_z, cross_ahead_z = cross_sum.z_back(cross_sends), cross_sum.z_ahead(cross_sends)
     activations = (hidden_two + mm(inner_low, w_down)).astype(BF)
     third_total = third_sum.own()
     (
         self_sum.parts, cross_back_z, cross_ahead_z, down_sum.parts, activations, third_total,
-        fourth_sum.parts, memory_rows.sent, memory_rows.kept, normed_rows.sent, normed_rows.kept,
+        fourth_sum.parts, memory_grad, normed_rows.sent, normed_rows.kept,
     ) = phase(
         self_sum.parts, cross_back_z, cross_ahead_z, down_sum.parts, activations, third_total,
-        fourth_sum.parts, memory_rows.sent, memory_rows.kept, normed_rows.sent, normed_rows.kept,
+        fourth_sum.parts, memory_grad, normed_rows.sent, normed_rows.kept,
     )
 
     (
         self_send, down_sum.parts, cross_sends, cross_back_z, cross_ahead_z, normed_rows.sent,
-        third_total, fourth_sum.parts, memory_rows.sent,
+        third_total, fourth_sum.parts,
     ) = phase(
         self_sum.halve(), down_sum.parts, cross_sends, cross_back_z, cross_ahead_z,
-        normed_rows.sent, third_total, fourth_sum.parts, memory_rows.sent,
+        normed_rows.sent, third_total, fourth_sum.parts,
     )
     self_sum.far(self_send)
     cross_sum.z_end(cross_sends, cross_back_z, cross_ahead_z)
-    down_sum.near(down_sum.halve())
+    down_sum.far(down_sum.halve())
     normed_rows.second()
-    memory_grad = memory_rows.total()
     fourth_total = fourth_sum.own()
     (
         self_sum.parts, cross_sum.parts, down_sum.parts, normed_rows.sent, fourth_total,
-        memory_grad,
     ) = phase(
         self_sum.parts, cross_sum.parts, down_sum.parts, normed_rows.sent, fourth_total,
-        memory_grad,
     )
 
     self_sends, cross_sum.parts, down_sum.parts, fourth_total, normed_rows.sent = phase(
         self_sum.z_sends(), cross_sum.parts, down_sum.parts, fourth_total, normed_rows.sent
     )
     self_sum.z(self_sends)
+    down_sum.near(down_sum.halve())
     gate_one, up_one = third_sum.last(third_total)
     gate_two, up_two = fourth_sum.last(fourth_total)
     cross_left, cross_right = cross_sum.last(cross_sum.own())

time: 462 us -> 460 us (level)
  the two profiles are of different devices: /device:TPU:11 before, /device:TPU:9 now
where the time goes in v6:
time: 460 us; the launch traced here: 452 us
  waiting for transfers between devices  135 us (29%)
  Pallas kernels  120 us (26%)
  starting transfers between devices  71.1 us (15%)
  other arithmetic  60 us (13%)
  local copies, waits for them, and re-layouts  35.5 us (8%)
  matrix products  27.2 us (6%)
    ppermute x78, waiting for transfers between devices, move(): return lax.ppermute(value, AXES, pairs)  135 us
    ppermute x78, starting transfers between devices, move(): return lax.ppermute(value, AXES, pairs)  71.1 us
    pallas_call x5, Pallas kernels, assemble(): pl.pallas_call(body, in_specs=[pl.BlockSpec(memory_space=pltpu.SMEM)] + [...  30.3 us
    dot_general x8, matrix products, mm(): return lax.dot_general(left, right, dims, preferred_element_type=F32)  26.7 us
    pallas_call x1, Pallas kernels, self_back(): pl.pallas_call(body, grid=(pairs,), in_specs=[SMEM, whole(target_all), pa...  23 us
    pallas_call x5, Pallas kernels, weight_grad(): pl.pallas_call(body, in_specs=[pl.BlockSpec(memory_space=pltpu.SMEM)] + [...  22.1 us
    pallas_call x1, Pallas kernels, cross_back(): pl.pallas_call(body, grid=(pairs,), in_specs=[whole(grad_two), whole(hidd...  17.4 us
    unnamed x225, local copies, waits for them, and re-layouts  17.3 us
  transfers between devices with their start and end apart: 78, of which 26 were waited for; matrix products, arithmetic and copies ran while one was open for 16% of the time, Pallas kernels for 24%

profile of v6, /device:TPU:9, one launch (start us, length us, event | category | flops | bytes accessed | tf_op | source)
XLA Modules:
  0.0 452.3 jit_solution(6743762766665938770)
XLA Ops:
  14.1 9.4 %collective-permute-done.3 = bf16[64,1664]{1,0:T(8,128)(2,1)S(1)} collective-permute-done((bf16[64,1664]{1,0:T(8,128)(2,1)S(1)}, bf16[64,1664]{1,0:T(8,128)(2,1)S(1)}, u32[]{:S(2)}, u32[]{:S(2)}) %collective-permute-start.3) | collective-permute-done | bytes 213024 | tf_op jit(solution)/shard_map/ppermute | solution.py:408
  23.5 4.6 %collective-permute-done.4 = bf16[64,1664]{1,0:T(8,128)(2,1)S(1)} collective-permute-done((bf16[64,1664]{1,0:T(8,128)(2,1)S(1)}, bf16[64,1664]{1,0:T(8,128)(2,1)S(1)}, u32[]{:S(2)}, u32[]{:S(2)}) %collective-permute-start.4) | collective-permute-done | bytes 213024 | tf_op jit(solution)/shard_map/ppermute | solution.py:408
  33.3 13.0 %collective-permute-done.6 = bf16[176,512]{1,0:T(8,128)(2,1)S(1)} collective-permute-done((bf16[176,512]{1,0:T(8,128)(2,1)S(1)}, bf16[176,512]{1,0:T(8,128)(2,1)S(1)}, u32[]{:S(2)}, u32[]{:S(2)}) %collective-permute-start.6) | collective-permute-done | bytes 180256 | tf_op jit(solution)/shard_map/ppermute | solution.py:408
  55.6 9.6 %collective-permute-done.12 = bf16[64,2560]{1,0:T(8,128)(2,1)S(1)} collective-permute-done((bf16[64,2560]{1,0:T(8,128)(2,1)S(1)}, bf16[64,2560]{1,0:T(8,128)(2,1)S(1)}, u32[]{:S(2)}, u32[]{:S(2)}) %collective-permute-start.12) | collective-permute-done | bytes 327712 | tf_op jit(solution)/shard_map/ppermute | solution.py:408
  66.6 5.2 %collective-permute-done.10.refs_1_ = bf16[2,4,64,1664]{3,2,1,0:T(8,128)(2,1)} collective-permute-done((bf16[2,4,64,1664]{3,2,1,0:T(8,128)(2,1)S(1)}, bf16[2,4,64,1664]{3,2,1,0:T(8,128)(2,1)}, u32[]{:S(2)}, u32[]{:S(2)}) %collective-permute-start.10) | collective-permute-done | bytes 1703968 | tf_op jit(solution)/shard_map/ppermute | solution.py:408
  81.4 4.3 gather_fusion
  86.8 15.7 %collective-permute-done.16 = bf16[64,2816]{1,0:T(8,128)(2,1)S(1)} collective-permute-done((bf16[64,2816]{1,0:T(8,128)(2,1)S(1)}, bf16[64,2816]{1,0:T(8,128)(2,1)S(1)}, u32[]{:S(2)}, u32[]{:S(2)}) %collective-permute-start.16) | collective-permute-done | bytes 360480 | tf_op jit(solution)/shard_map/ppermute | solution.py:408
  102.4 4.9 %collective-permute-done.18 = bf16[64,2816]{1,0:T(8,128)(2,1)} collective-permute-done((bf16[64,2816]{1,0:T(8,128)(2,1)S(1)}, bf16[64,2816]{1,0:T(8,128)(2,1)}, u32[]{:S(2)}, u32[]{:S(2)}) %collective-permute-start.18) | collective-permute-done | bytes 360480 | tf_op jit(solution)/shard_map/ppermute | solution.py:408
  119.3 6.2 %assemble.5.wq_ref.wk_ref.wv_ref = bf16[1024,3328]{1,0:T(8,128)(2,1)} custom-call(s32[4]{0:T(128)S(1)} %pad_add_fusion.place_ref, bf16[2,4,64,1664]{3,2,1,0:T(8,128)(2,1)S(1)} %copy-done.5, bf16[2,4,64,1664]{3,2,1,0:T(8,128)(2,1)} %collective-permute-done.10.refs_1_, bf16[2,4,64,1664]{3,2,1,0:T(8,128)(2,1)} %collective-permute-done.11.refs_2_, ...), custom_call_target="tpu_custom_call" | custom-call | flops 1000000000 | bytes 1 | tf_op jit(solution)/shard_map/assemble/pallas_call | solution.py:475
  128.9 15.4 %self_forward.1 = (bf16[128,1024]{1,0:T(8,128)(2,1)S(1)}, bf16[128,1024]{1,0:T(8,128)(2,1)S(1)}, bf16[512,1024]{1,0:T(8,128)(2,1)S(1)}, bf16[512,1024]{1,0:T(8,128)(2,1)S(1)}, bf16[512,1024]{1,0:T(8,128)(2,1)S(1)}) custom-call(s32[1]{0:T(128)} %bitcast.4.pos_ref, bf16[512,1024]{1,0:T(8,128)(2,1)S(1)} %bitcast.141, f32[1,1024]{1,0:T(1,128)S(1)} %reshape.224.gain_ref, ...), custom_call_target="tpu_custom_call" | custom-call | flops 4000000000 | bytes 1 | tf_op jit(solution)/shard_map/self_forward/pallas_call | solution.py:166
  148.3 3.6 collective-permute-done.20.refs_1_
  158.1 8.0 %assemble.6.wo_ref.wq_ref.wk_ref.wv_ref.wc_ref = bf16[1024,5120]{1,0:T(8,128)(2,1)} custom-call(s32[4]{0:T(128)S(1)} %pad_add_fusion.place_ref, bf16[2,4,64,2560]{3,2,1,0:T(8,128)(2,1)S(1)} %pad_maximum_fusion.1.refs_0_, bf16[2,4,64,2560]{3,2,1,0:T(8,128)(2,1)} %collective-permute-done.20.refs_1_, bf16[2,4,64,2560]{3,2,1,0:T(8,128)(2,1)} %collective-permute-done.21.refs_2_, ...), custom_call_target="tpu_custom_call" | custom-call | flops 1000000000 | bytes 1 | tf_op jit(solution)/shard_map/assemble/pallas_call | solution.py:475
  166.2 12.2 %cross_forward.1 = (f32[128,1024]{1,0:T(8,128)S(1)}, bf16[128,1024]{1,0:T(8,128)(2,1)S(1)}, bf16[128,1024]{1,0:T(8,128)(2,1)S(1)}, bf16[256,1024]{1,0:T(8,128)(2...) custom-call(bf16[128,1024]{1,0:T(8,128)(2,1)S(1)} %bitcast.144, ...), custom_call_target="tpu_custom_call" | custom-call | flops 8000000000 | bytes 1 | tf_op jit(solution)/shard_map/cross_forward/pallas_call | solution.py:280
  188.6 5.4 %assemble.7 = bf16[1024,2816]{1,0:T(8,128)(2,1)} custom-call(s32[4]{0:T(128)S(1)} %pad_add_fusion.place_ref, bf16[2,4,64,1408]{3,2,1,0:T(8,128)(2,1)} %pad_maximum_fusion.6.refs_0_, bf16[2,4,64,1408]{3,2,1,0:T(8,128)(2,1)} %collective-permute-done.26.refs_1_, bf16[2,4,64,1408]{3,2,1,0:T(8,128)(2,1)} %collective-permute-done.27.refs_2_, ...), custom_call_target="tpu_custom_call" | custom-call | flops 1000000000 | bytes 1 | tf_op jit(solution)/shard_map/assemble/pallas_call | solution.py:475
  197.6 5.3 %assemble.8 = bf16[2816,1024]{1,0:T(8,128)(2,1)} custom-call(s32[4]{0:T(128)S(1)} %pad_add_fusion.place_ref, bf16[4,2,2,176,512]{4,3,2,1,0:T(8,128)(2,1)S(1)} %pad_maximum_fusion.refs_0_, bf16[4,2,2,176,512]{4,3,2,1,0:T(8,128)(2,1)} %collective-permute-done.34.refs_1_), custom_call_target="tpu_custom_call" | custom-call | flops 1000000000 | bytes 1 | tf_op jit(solution)/shard_map/assemble/pallas_call | solution.py:475
  209.8 5.4 %assemble.9 = bf16[1024,2816]{1,0:T(8,128)(2,1)} custom-call(s32[4]{0:T(128)S(1)} %pad_add_fusion.place_ref, bf16[2,4,64,1408]{3,2,1,0:T(8,128)(2,1)} %pad_maximum_fusion.7.refs_0_, bf16[2,4,64,1408]{3,2,1,0:T(8,128)(2,1)} %collective-permute-done.32.refs_1_, bf16[2,4,64,1408]{3,2,1,0:T(8,128)(2,1)} %collective-permute-done.33.refs_2_, ...), custom_call_target="tpu_custom_call" | custom-call | flops 1000000000 | bytes 1 | tf_op jit(solution)/shard_map/assemble/pallas_call | solution.py:475
  218.6 4.1 fusion.90
  229.0 5.5 %weight_grad.6 = (bf16[704,512]{1,0:T(8,128)(2,1)S(1)}, bf16[704,512]{1,0:T(8,128)(2,1)S(1)}, bf16[704,512]{1,0:T(8,128)(2,1)S(1)}, bf16[704,512]{1,0:T(8,128)(2,1)S(1)}) custom-call(s32[4]{0:T(128)S(1)} %pad_add_fusion.place_ref, bf16[128,2816]{1,0:T(8,128)(2,1)S(1)} %pad_maximum_fusion.13.refs_0_, bf16[128,512]{1,0:T(8,128)(2,1)S(1)} %copy-done.50, ...), custom_call_target="tpu_custom_call" | custom-call | flops 1000000000 | bytes 1 | tf_op jit(solution)/shard_map/weight_grad/pallas_call | solution.py:565
  236.3 5.0 %collective-permute-done.39 = bf16[512,1408]{1,0:T(8,128)(2,1)} collective-permute-done((bf16[512,1408]{1,0:T(8,128)(2,1)S(1)}, bf16[512,1408]{1,0:T(8,128)(2,1)}, u32[]{:S(2)}, u32[]{:S(2)}) %collective-permute-start.39) | collective-permute-done | bytes 1441824 | tf_op jit(solution)/shard_map/ppermute | solution.py:408
  250.2 4.6 %fusion.32 = f32[128,1024]{1,0:T(8,128)S(1)} fusion(bf16[1024,2816]{1,0:T(8,128)(2,1)} %assemble.9, bf16[128,1408]{1,0:T(8,128)(2,1)S(1)} %get-tuple-element.417, bf16[128,1408]{1,0:T(8,128)(2,1)S(1)} %copy-done.67), kind=kOutput, calls=%fused_computation.70 | convolution fusion | flops 739639296 | bytes 7012352 | tf_op jit(solution)/shard_map/dot_general | solution.py:25
  254.8 4.7 %multiply_reduce_fusion = (bf16[1024]{0:T(1024)(128)(2,1)S(1)}, f32[128]{0:T(128)S(1)}, f32[128,1024]{1,0:T(8,128)S(1)}) fusion(f32[128,1024]{1,0:T(8,128)S(1)} %get-tuple-element.415, f32[128]{0:T(128)S(1)} %add_rsqrt_fusion.1, f32[1024]{0:T(1024)S(1)} %mul.224, f32[128,1024]{1,0:T(8,128)S(1)} %fusion.32, bf16[1024,2816]{1,0:T(8,128)(2,1)} %assemble.7, ...), kind=kOutput, calls=%fused_computation.105 | convolution fusion | flops 740555648 | bytes 8068096 | tf_op jit(solution)/shard_map/dot_general | solution.py:25
  260.9 17.4 %cross_back.1 = (bf16[128,1024]{1,0:T(8,128)(2,1)S(1)}, bf16[256,1024]{1,0:T(8,128)(2,1)S(1)}, bf16[256,1024]{1,0:T(8,128)(2,1)S(1)}, f32[256,1024]{1,0:T(8,128)...) custom-call(f32[128,1024]{1,0:T(8,128)S(1)} %get-tuple-element.621.g, ...), custom_call_target="tpu_custom_call" | custom-call | flops 1000000000 | bytes 1 | tf_op jit(solution)/shard_map/cross_back/pallas_call | solution.py:353
  300.5 5.8 %weight_grad.8 = (bf16[512,2560]{1,0:T(8,128)(2,1)S(1)}, bf16[512,2560]{1,0:T(8,128)(2,1)}) custom-call(s32[4]{0:T(128)S(1)} %pad_add_fusion.place_ref, bf16[128,1024]{1,0:T(8,128)(2,1)S(1)} %get-tuple-element.668.refs_0_, bf16[128,1024]{1,0:T(8,128)(2,1)S(1)} %get-tuple-element.666.refs_1_, bf16[128,1024]{1,0:T(8,128)(2,1)S(1)} %get-tuple-element.644.refs_2_, ...), custom_call_target="tpu_custom_call" | custom-call | flops 1000000000 | bytes 1 | tf_op jit(solution)/shard_map/weight_grad/pallas_call | solution.py:565
  314.5 23.0 %self_back.1 = (bf16[512,1024]{1,0:T(8,128)(2,1)S(1)}, bf16[512,1024]{1,0:T(8,128)(2,1)S(1)}, bf16[512,1024]{1,0:T(8,128)(2,1)S(1)}, f32[8,2,640]{2,1,0:T(2,128)...) custom-call(s32[1]{0:T(128)} %bitcast.4.pos_ref, bf16[512,1024]{1,0:T(8,128)(2,1)S(1)} %bitcast.142, ...), custom_call_target="tpu_custom_call" | custom-call | flops 1000000000 | bytes 1 | tf_op jit(solution)/shard_map/self_back/pallas_call | solution.py:225
  338.3 5.8 %collective-permute-done.54 = bf16[64,1024]{1,0:T(8,128)(2,1)S(1)} collective-permute-done((bf16[64,1024]{1,0:T(8,128)(2,1)S(1)}, bf16[64,1024]{1,0:T(8,128)(2,1)S(1)}, u32[]{:S(2)}, u32[]{:S(2)}) %collective-permute-start.54) | collective-permute-done | bytes 131104 | tf_op jit(solution)/shard_map/ppermute | solution.py:408
  356.0 8.3 %collective-permute-done.58 = bf16[64,1408]{1,0:T(8,128)(2,1)} collective-permute-done((bf16[64,1408]{1,0:T(8,128)(2,1)}, bf16[64,1408]{1,0:T(8,128)(2,1)}, u32[]{:S(2)}, u32[]{:S(2)}) %collective-permute-start.58) | collective-permute-done | bytes 180256 | tf_op jit(solution)/shard_map/ppermute | solution.py:408
  369.9 4.1 weight_grad.9
  383.4 4.4 fusion.10
  388.6 8.4 %collective-permute-done.62 = bf16[64,2560]{1,0:T(8,128)(2,1)S(1)} collective-permute-done((bf16[64,2560]{1,0:T(8,128)(2,1)S(1)}, bf16[64,2560]{1,0:T(8,128)(2,1)S(1)}, u32[]{:S(2)}, u32[]{:S(2)}) %collective-permute-start.62) | collective-permute-done | bytes 327712 | tf_op jit(solution)/shard_map/ppermute | solution.py:408
  408.1 7.4 %collective-permute-done.65 = bf16[256,1664]{1,0:T(8,128)(2,1)S(1)} collective-permute-done((bf16[256,1664]{1,0:T(8,128)(2,1)S(1)}, bf16[256,1664]{1,0:T(8,128)(2,1)S(1)}, u32[]{:S(2)}, u32[]{:S(2)}) %collective-permute-start.65) | collective-permute-done | bytes 852000 | tf_op jit(solution)/shard_map/ppermute | solution.py:408
  417.4 4.2 collective-permute-start.75
  431.1 10.4 %collective-permute-done.70 = bf16[64,1664]{1,0:T(8,128)(2,1)S(1)} collective-permute-done((bf16[64,1664]{1,0:T(8,128)(2,1)S(1)}, bf16[64,1664]{1,0:T(8,128)(2,1)S(1)}, u32[]{:S(2)}, u32[]{:S(2)}) %collective-permute-start.70) | collective-permute-done | bytes 213024 | tf_op jit(solution)/shard_map/ppermute | solution.py:408
  (517 shorter events, 198.1 us)
Async XLA Ops:
  28.2 18.8 %collective-permute-start.5 = (bf16[4,64,1664]{2,1,0:T(8,128)(2,1)S(1)}, bf16[4,64,1664]{2,1,0:T(8,128)(2,1)S(1)}, u32[]{:S(2)}, u32[]{:S(2)}) collective-permute-start(bf16[4,64,1664]{2,1,0:T(8,128)(2,1)S(1)} %pad_maximum_fusion.10), channel_id=1, source_target_pairs={{0,4},{1,3},{2,6},{3,1},{4,0},{5,7},{6,2},{7,5},{8,12},{9,11},{10,... | collective-permute-start | bytes 2555912 | tf_op jit(solution)/shard_map/ppermute | solution.py:408
  29.8 20.4 %collective-permute-start.9 = (bf16[192,1024]{1,0:T(8,128)(2,1)S(1)}, bf16[192,1024]{1,0:T(8,128)(2,1)S(1)}, u32[]{:S(2)}, u32[]{:S(2)}) collective-permute-start(bf16[192,1024]{1,0:T(8,128)(2,1)S(1)} %pad_maximum_fusion.17), channel_id=1, source_target_pairs={{0,2},{1,3},{2,0},{3,1},{4,6},{5,7},{6,4},{7,5},{8,10},{9,11},{10,... | collective-permute-start | bytes 1179656 | tf_op jit(solution)/shard_map/ppermute | solution.py:408
  31.1 19.1 %collective-permute-start.7 = (bf16[64,2560]{1,0:T(8,128)(2,1)S(1)}, bf16[64,2560]{1,0:T(8,128)(2,1)S(1)}, u32[]{:S(2)}, u32[]{:S(2)}) collective-permute-start(bf16[64,2560]{1,0:T(8,128)(2,1)S(1)} %split.23), channel_id=1, source_target_pairs={{0,24},{1,25},{2,26},{3,27},{4,28},{5,29},{6,30},{7,31},{8,0},{9,1... | collective-permute-start | bytes 983048 | tf_op jit(solution)/shard_map/ppermute | solution.py:408
  51.0 20.8 %collective-permute-start.10 = (bf16[2,4,64,1664]{3,2,1,0:T(8,128)(2,1)S(1)}, bf16[2,4,64,1664]{3,2,1,0:T(8,128)(2,1)}, u32[]{:S(2)}, u32[]{:S(2)}) collective-permute-start(bf16[2,4,64,1664]{3,2,1,0:T(8,128)(2,1)S(1)} %pad_maximum_fusion.2.refs_0_), channel_id=1, source_target_pairs={{0,2},{1,5},{2,0},{3,7},{4,6},{5,1},{6,4},{7,3},{8,10},{9,13},{10,... | collective-permute-start | bytes 5111816 | tf_op jit(solution)/shard_map/ppermute | solution.py:408
  52.2 19.6 %collective-permute-start.11 = (bf16[2,4,64,1664]{3,2,1,0:T(8,128)(2,1)S(1)}, bf16[2,4,64,1664]{3,2,1,0:T(8,128)(2,1)}, u32[]{:S(2)}, u32[]{:S(2)}) collective-permute-start(bf16[2,4,64,1664]{3,2,1,0:T(8,128)(2,1)S(1)} %pad_maximum_fusion.2.refs_0_), channel_id=1, source_target_pairs={{0,1},{1,0},{2,3},{3,2},{4,5},{5,4},{6,7},{7,6},{8,9},{9,8},{10,11... | collective-permute-start | bytes 5111816 | tf_op jit(solution)/shard_map/ppermute | solution.py:408
  75.0 27.4 %collective-permute-start.16 = (bf16[64,2816]{1,0:T(8,128)(2,1)S(1)}, bf16[64,2816]{1,0:T(8,128)(2,1)S(1)}, u32[]{:S(2)}, u32[]{:S(2)}) collective-permute-start(bf16[64,2816]{1,0:T(8,128)(2,1)S(1)} %copy-done.65), channel_id=1, source_target_pairs={{0,24},{1,25},{2,26},{3,27},{4,28},{5,29},{6,30},{7,31},{8,0},{9,1... | collective-permute-start | bytes 1081352 | tf_op jit(solution)/shard_map/ppermute | solution.py:408
  76.2 26.2 %collective-permute-start.17 = (bf16[64,2816]{1,0:T(8,128)(2,1)S(1)}, bf16[64,2816]{1,0:T(8,128)(2,1)}, u32[]{:S(2)}, u32[]{:S(2)}) collective-permute-start(bf16[64,2816]{1,0:T(8,128)(2,1)S(1)} %copy-done.65), channel_id=1, source_target_pairs={{0,16},{1,17},{2,18},{3,19},{4,20},{5,21},{6,22},{7,23},{8,24},{9,... | collective-permute-start | bytes 1081352 | tf_op jit(solution)/shard_map/ppermute | solution.py:408
  79.4 27.9 %collective-permute-start.18 = (bf16[64,2816]{1,0:T(8,128)(2,1)S(1)}, bf16[64,2816]{1,0:T(8,128)(2,1)}, u32[]{:S(2)}, u32[]{:S(2)}) collective-permute-start(bf16[64,2816]{1,0:T(8,128)(2,1)S(1)} %copy-done.65), channel_id=1, source_target_pairs={{0,8},{1,9},{2,10},{3,11},{4,12},{5,13},{6,14},{7,15},{8,16},{9,17... | collective-permute-start | bytes 1081352 | tf_op jit(solution)/shard_map/ppermute | solution.py:408
  79.4 30.5 %collective-permute-start.15 = (bf16[4,64,2560]{2,1,0:T(8,128)(2,1)S(1)}, bf16[4,64,2560]{2,1,0:T(8,128)(2,1)}, u32[]{:S(2)}, u32[]{:S(2)}) collective-permute-start(bf16[4,64,2560]{2,1,0:T(8,128)(2,1)S(1)} %copy-done.55), channel_id=1, source_target_pairs={{0,4},{1,3},{2,6},{3,1},{4,0},{5,7},{6,2},{7,5},{8,12},{9,11},{10,... | collective-permute-start | bytes 3932168 | tf_op jit(solution)/shard_map/ppermute | solution.py:408
  85.7 26.3 %collective-permute-start.14 = (bf16[2,4,64,1664]{3,2,1,0:T(8,128)(2,1)}, bf16[2,4,64,1664]{3,2,1,0:T(8,128)(2,1)S(1)}, u32[]{:S(2)}, u32[]{:S(2)}) collective-permute-start(bf16[2,4,64,1664]{3,2,1,0:T(8,128)(2,1)} %collective-permute-done.10.refs_1_), channel_id=1, source_target_pairs={{0,1},{1,0},{2,3},{3,2},{4,5},{5,4},{6,7},{7,6},{8,9},{9,8},{10,11... | collective-permute-start | bytes 5111816 | tf_op jit(solution)/shard_map/ppermute | solution.py:408
  113.3 38.6 %collective-permute-start.20 = (bf16[2,4,64,2560]{3,2,1,0:T(8,128)(2,1)S(1)}, bf16[2,4,64,2560]{3,2,1,0:T(8,128)(2,1)}, u32[]{:S(2)}, u32[]{:S(2)}) collective-permute-start(bf16[2,4,64,2560]{3,2,1,0:T(8,128)(2,1)S(1)} %pad_maximum_fusion.1.refs_0_), channel_id=1, source_target_pairs={{0,2},{1,5},{2,0},{3,7},{4,6},{5,1},{6,4},{7,3},{8,10},{9,13},{10,... | collective-permute-start | bytes 7864328 | tf_op jit(solution)/shard_map/ppermute | solution.py:408
  113.7 38.2 %collective-permute-start.21 = (bf16[2,4,64,2560]{3,2,1,0:T(8,128)(2,1)S(1)}, bf16[2,4,64,2560]{3,2,1,0:T(8,128)(2,1)}, u32[]{:S(2)}, u32[]{:S(2)}) collective-permute-start(bf16[2,4,64,2560]{3,2,1,0:T(8,128)(2,1)S(1)} %pad_maximum_fusion.1.refs_0_), channel_id=1, source_target_pairs={{0,1},{1,0},{2,3},{3,2},{4,5},{5,4},{6,7},{7,6},{8,9},{9,8},{10,11... | collective-permute-start | bytes 7864328 | tf_op jit(solution)/shard_map/ppermute | solution.py:408
  115.1 33.2 %collective-permute-start.23 = (bf16[2,2,176,512]{3,2,1,0:T(8,128)(2,1)}, bf16[2,2,176,512]{3,2,1,0:T(8,128)(2,1)}, u32[]{:S(2)}, u32[]{:S(2)}) collective-permute-start(bf16[2,2,176,512]{3,2,1,0:T(8,128)(2,1)} %pad_maximum_fusion.12), channel_id=1, source_target_pairs={{0,24},{1,25},{2,26},{3,27},{4,28},{5,29},{6,30},{7,31},{8,0},{9,1... | collective-permute-start | bytes 2162696 | tf_op jit(solution)/shard_map/ppermute | solution.py:408
  115.8 32.5 %collective-permute-start.24 = (bf16[2,2,176,512]{3,2,1,0:T(8,128)(2,1)}, bf16[2,2,176,512]{3,2,1,0:T(8,128)(2,1)}, u32[]{:S(2)}, u32[]{:S(2)}) collective-permute-start(bf16[2,2,176,512]{3,2,1,0:T(8,128)(2,1)} %pad_maximum_fusion.12), channel_id=1, source_target_pairs={{0,8},{1,9},{2,10},{3,11},{4,12},{5,13},{6,14},{7,15},{8,16},{9,17... | collective-permute-start | bytes 2162696 | tf_op jit(solution)/shard_map/ppermute | solution.py:408
  117.5 27.8 %collective-permute-start.22 = (bf16[4,64,1408]{2,1,0:T(8,128)(2,1)}, bf16[4,64,1408]{2,1,0:T(8,128)(2,1)}, u32[]{:S(2)}, u32[]{:S(2)}) collective-permute-start(bf16[4,64,1408]{2,1,0:T(8,128)(2,1)} %get-tuple-element.348), channel_id=1, source_target_pairs={{0,4},{1,3},{2,6},{3,1},{4,0},{5,7},{6,2},{7,5},{8,12},{9,11},{10,... | collective-permute-start | bytes 2162696 | tf_op jit(solution)/shard_map/ppermute | solution.py:408
  153.0 27.0 %collective-permute-start.26 = (bf16[2,4,64,1408]{3,2,1,0:T(8,128)(2,1)}, bf16[2,4,64,1408]{3,2,1,0:T(8,128)(2,1)}, u32[]{:S(2)}, u32[]{:S(2)}) collective-permute-start(bf16[2,4,64,1408]{3,2,1,0:T(8,128)(2,1)} %pad_maximum_fusion.6.refs_0_), channel_id=1, source_target_pairs={{0,2},{1,5},{2,0},{3,7},{4,6},{5,1},{6,4},{7,3},{8,10},{9,13},{10,... | collective-permute-start | bytes 4325384 | tf_op jit(solution)/shard_map/ppermute | solution.py:408
  153.4 26.6 %collective-permute-start.27 = (bf16[2,4,64,1408]{3,2,1,0:T(8,128)(2,1)}, bf16[2,4,64,1408]{3,2,1,0:T(8,128)(2,1)}, u32[]{:S(2)}, u32[]{:S(2)}) collective-permute-start(bf16[2,4,64,1408]{3,2,1,0:T(8,128)(2,1)} %pad_maximum_fusion.6.refs_0_), channel_id=1, source_target_pairs={{0,1},{1,0},{2,3},{3,2},{4,5},{5,4},{6,7},{7,6},{8,9},{9,8},{10,11... | collective-permute-start | bytes 4325384 | tf_op jit(solution)/shard_map/ppermute | solution.py:408
  155.1 24.8 %collective-permute-start.30 = (bf16[128,512]{1,0:T(8,128)(2,1)}, bf16[128,512]{1,0:T(8,128)(2,1)}, u32[]{:S(2)}, u32[]{:S(2)}) collective-permute-start(bf16[128,512]{1,0:T(8,128)(2,1)} %get-tuple-element.676), channel_id=1, source_target_pairs={{0,1},{1,0},{2,3},{3,2},{4,5},{5,4},{6,7},{7,6},{8,9},{9,8},{10,11... | collective-permute-start | bytes 393224 | tf_op jit(solution)/shard_map/ppermute | solution.py:408
  155.4 24.6 %collective-permute-start.28 = (bf16[4,64,1408]{2,1,0:T(8,128)(2,1)}, bf16[4,64,1408]{2,1,0:T(8,128)(2,1)S(1)}, u32[]{:S(2)}, u32[]{:S(2)}) collective-permute-start(bf16[4,64,1408]{2,1,0:T(8,128)(2,1)} %get-tuple-element.370), channel_id=1, source_target_pairs={{0,4},{1,3},{2,6},{3,1},{4,0},{5,7},{6,2},{7,5},{8,12},{9,11},{10,... | collective-permute-start | bytes 2162696 | tf_op jit(solution)/shard_map/ppermute | solution.py:408
  157.9 22.1 %collective-permute-start.29 = (bf16[2,2,176,512]{3,2,1,0:T(8,128)(2,1)}, bf16[2,2,176,512]{3,2,1,0:T(8,128)(2,1)S(1)}, u32[]{:S(2)}, u32[]{:S(2)}) collective-permute-start(bf16[2,2,176,512]{3,2,1,0:T(8,128)(2,1)} %collective-permute-done.23), channel_id=1, source_target_pairs={{0,24},{1,25},{2,26},{3,27},{4,28},{5,29},{6,30},{7,31},{8,0},{9,1... | collective-permute-start | bytes 2162696 | tf_op jit(solution)/shard_map/ppermute | solution.py:408
  185.1 18.5 %collective-permute-start.32 = (bf16[2,4,64,1408]{3,2,1,0:T(8,128)(2,1)}, bf16[2,4,64,1408]{3,2,1,0:T(8,128)(2,1)}, u32[]{:S(2)}, u32[]{:S(2)}) collective-permute-start(bf16[2,4,64,1408]{3,2,1,0:T(8,128)(2,1)} %pad_maximum_fusion.7.refs_0_), channel_id=1, source_target_pairs={{0,2},{1,5},{2,0},{3,7},{4,6},{5,1},{6,4},{7,3},{8,10},{9,13},{10,... | collective-permute-start | bytes 4325384 | tf_op jit(solution)/shard_map/ppermute | solution.py:408
  223.0 18.3 %collective-permute-start.39 = (bf16[512,1408]{1,0:T(8,128)(2,1)S(1)}, bf16[512,1408]{1,0:T(8,128)(2,1)}, u32[]{:S(2)}, u32[]{:S(2)}) collective-permute-start(bf16[512,1408]{1,0:T(8,128)(2,1)S(1)} %get-tuple-element.390), channel_id=1, source_target_pairs={{0,4},{1,3},{2,6},{3,1},{4,0},{5,7},{6,2},{7,5},{8,12},{9,11},{10,... | collective-permute-start | bytes 4325384 | tf_op jit(solution)/shard_map/ppermute | solution.py:408
  246.5 36.0 %collective-permute-start.43 = (bf16[512,1408]{1,0:T(8,128)(2,1)S(1)}, bf16[512,1408]{1,0:T(8,128)(2,1)S(1)}, u32[]{:S(2)}, u32[]{:S(2)}) collective-permute-start(bf16[512,1408]{1,0:T(8,128)(2,1)S(1)} %get-tuple-element.411), channel_id=1, source_target_pairs={{0,4},{1,3},{2,6},{3,1},{4,0},{5,7},{6,2},{7,5},{8,12},{9,11},{10,... | collective-permute-start | bytes 4325384 | tf_op jit(solution)/shard_map/ppermute | solution.py:408
  247.6 31.4 %collective-permute-start.42 = (bf16[256,1408]{1,0:T(8,128)(2,1)S(1)}, bf16[256,1408]{1,0:T(8,128)(2,1)}, u32[]{:S(2)}, u32[]{:S(2)}) collective-permute-start(bf16[256,1408]{1,0:T(8,128)(2,1)S(1)} %add_convert_fusion.5), channel_id=1, source_target_pairs={{0,2},{1,5},{2,0},{3,7},{4,6},{5,1},{6,4},{7,3},{8,10},{9,13},{10,... | collective-permute-start | bytes 2162696 | tf_op jit(solution)/shard_map/ppermute | solution.py:408
  248.0 31.0 %collective-permute-start.44 = (bf16[704,512]{1,0:T(8,128)(2,1)S(1)}, bf16[704,512]{1,0:T(8,128)(2,1)S(1)}, u32[]{:S(2)}, u32[]{:S(2)}) collective-permute-start(bf16[704,512]{1,0:T(8,128)(2,1)S(1)} %get-tuple-element.414), channel_id=1, source_target_pairs={{0,24},{1,25},{2,26},{3,27},{4,28},{5,29},{6,30},{7,31},{8,0},{9,1... | collective-permute-start | bytes 2162696 | tf_op jit(solution)/shard_map/ppermute | solution.py:408
  248.0 34.5 %collective-permute-start.45 = (bf16[704,512]{1,0:T(8,128)(2,1)S(1)}, bf16[704,512]{1,0:T(8,128)(2,1)S(1)}, u32[]{:S(2)}, u32[]{:S(2)}) collective-permute-start(bf16[704,512]{1,0:T(8,128)(2,1)S(1)} %get-tuple-element.413), channel_id=1, source_target_pairs={{0,8},{1,9},{2,10},{3,11},{4,12},{5,13},{6,14},{7,15},{8,16},{9,17... | collective-permute-start | bytes 2162696 | tf_op jit(solution)/shard_map/ppermute | solution.py:408
  310.5 33.6 %collective-permute-start.52 = (bf16[512,2560]{1,0:T(8,128)(2,1)}, bf16[512,2560]{1,0:T(8,128)(2,1)}, u32[]{:S(2)}, u32[]{:S(2)}) collective-permute-start(bf16[512,2560]{1,0:T(8,128)(2,1)} %get-tuple-element.452), channel_id=1, source_target_pairs={{0,4},{1,3},{2,6},{3,1},{4,0},{5,7},{6,2},{7,5},{8,12},{9,11},{10,... | collective-permute-start | bytes 7864328 | tf_op jit(solution)/shard_map/ppermute | solution.py:408
  312.1 31.9 %collective-permute-start.53 = (bf16[704,512]{1,0:T(8,128)(2,1)}, bf16[704,512]{1,0:T(8,128)(2,1)}, u32[]{:S(2)}, u32[]{:S(2)}) collective-permute-start(bf16[704,512]{1,0:T(8,128)(2,1)} %add_convert_fusion.3), channel_id=1, source_target_pairs={{0,8},{1,9},{2,10},{3,11},{4,12},{5,13},{6,14},{7,15},{8,16},{9,17... | collective-permute-start | bytes 2162696 | tf_op jit(solution)/shard_map/ppermute | solution.py:408
  313.5 30.5 %collective-permute-start.54 = (bf16[64,1024]{1,0:T(8,128)(2,1)S(1)}, bf16[64,1024]{1,0:T(8,128)(2,1)S(1)}, u32[]{:S(2)}, u32[]{:S(2)}) collective-permute-start(bf16[64,1024]{1,0:T(8,128)(2,1)S(1)} %fusion.59), channel_id=1, source_target_pairs={{0,2},{1,3},{2,0},{3,1},{4,6},{5,7},{6,4},{7,5},{8,10},{9,11},{10,... | collective-permute-start | bytes 393224 | tf_op jit(solution)/shard_map/ppermute | solution.py:408
  375.1 21.9 %collective-permute-start.60 = (bf16[512,1664]{1,0:T(8,128)(2,1)}, bf16[512,1664]{1,0:T(8,128)(2,1)S(1)}, u32[]{:S(2)}, u32[]{:S(2)}) collective-permute-start(bf16[512,1664]{1,0:T(8,128)(2,1)} %get-tuple-element.538), channel_id=1, source_target_pairs={{0,4},{1,3},{2,6},{3,1},{4,0},{5,7},{6,2},{7,5},{8,12},{9,11},{10,... | collective-permute-start | bytes 5111816 | tf_op jit(solution)/shard_map/ppermute | solution.py:408
  422.9 23.1 %collective-permute-start.73 = (f32[32,2560]{1,0:T(8,128)S(1)}, f32[32,2560]{1,0:T(8,128)S(1)}, u32[]{:S(2)}, u32[]{:S(2)}) collective-permute-start(f32[32,2560]{1,0:T(8,128)S(1)} %slice_select_fusion), channel_id=1, source_target_pairs={{0,1},{1,0},{2,3},{3,2},{4,5},{5,4},{6,7},{7,6},{8,9},{9,8},{10,11... | collective-permute-start | bytes 983048 | tf_op jit(solution)/shard_map/ppermute | solution.py:408
  429.1 18.5 %collective-permute-start.77 = (f32[88,512]{1,0:T(8,128)S(1)}, f32[88,512]{1,0:T(8,128)S(1)}, u32[]{:S(2)}, u32[]{:S(2)}) collective-permute-start(f32[88,512]{1,0:T(8,128)S(1)} %slice_select_fusion.4), channel_id=1, source_target_pairs={{0,1},{1,0},{2,3},{3,2},{4,5},{5,4},{6,7},{7,6},{8,9},{9,8},{10,11... | collective-permute-start | bytes 540680 | tf_op jit(solution)/shard_map/ppermute | solution.py:408
  (157 other events, 1276.0 us)

commit v7 on v6

--- a/solution.py
+++ b/solution.py
@@ -74,7 +74,7 @@
     scores = jnp.where(allowed, scores, MASKED)
     top = jnp.max(scores, axis=1, keepdims=True)
     grown = jnp.exp(scores - top)
-    return grown / jnp.sum(grown, axis=1, keepdims=True)
+    return grown * (1.0 / jnp.sum(grown, axis=1, keepdims=True))
 
 
 def attend_pair(query, key, value, bias_ref, allowed, causal):

time: 460 us -> 460 us (level)
  no operation moved by 1% of the time
where the time goes in v7:
time: 460 us; the launch traced here: 452 us
  waiting for transfers between devices  135 us (29%)
  Pallas kernels  120 us (26%)
  starting transfers between devices  71.1 us (15%)
  other arithmetic  60 us (13%)
  local copies, waits for them, and re-layouts  35.5 us (8%)
  matrix products  27.2 us (6%)
    ppermute x78, waiting for transfers between devices, move(): return lax.ppermute(value, AXES, pairs)  135 us
    ppermute x78, starting transfers between devices, move(): return lax.ppermute(value, AXES, pairs)  71.1 us
    pallas_call x5, Pallas kernels, assemble(): pl.pallas_call(body, in_specs=[pl.BlockSpec(memory_space=pltpu.SMEM)] + [...  30.3 us
    dot_general x8, matrix products, mm(): return lax.dot_general(left, right, dims, preferred_element_type=F32)  26.7 us
    pallas_call x1, Pallas kernels, self_back(): pl.pallas_call(body, grid=(pairs,), in_specs=[SMEM, whole(target_all), pa...  23 us
    pallas_call x5, Pallas kernels, weight_grad(): pl.pallas_call(body, in_specs=[pl.BlockSpec(memory_space=pltpu.SMEM)] + [...  22.1 us
    pallas_call x1, Pallas kernels, cross_back(): pl.pallas_call(body, grid=(pairs,), in_specs=[whole(grad_two), whole(hidd...  17.4 us
    unnamed x225, local copies, waits for them, and re-layouts  17.3 us
  transfers between devices with their start and end apart: 78, of which 26 were waited for; matrix products, arithmetic and copies ran while one was open for 16% of the time, Pallas kernels for 24%

profile of v7, /device:TPU:9, one launch (start us, length us, event | category | flops | bytes accessed | tf_op | source)
XLA Modules:
  0.0 452.3 jit_solution(6743762766665938770)
XLA Ops:
  14.1 9.4 %collective-permute-done.3 = bf16[64,1664]{1,0:T(8,128)(2,1)S(1)} collective-permute-done((bf16[64,1664]{1,0:T(8,128)(2,1)S(1)}, bf16[64,1664]{1,0:T(8,128)(2,1)S(1)}, u32[]{:S(2)}, u32[]{:S(2)}) %collective-permute-start.3) | collective-permute-done | bytes 213024 | tf_op jit(solution)/shard_map/ppermute | solution.py:408
  23.5 4.6 %collective-permute-done.4 = bf16[64,1664]{1,0:T(8,128)(2,1)S(1)} collective-permute-done((bf16[64,1664]{1,0:T(8,128)(2,1)S(1)}, bf16[64,1664]{1,0:T(8,128)(2,1)S(1)}, u32[]{:S(2)}, u32[]{:S(2)}) %collective-permute-start.4) | collective-permute-done | bytes 213024 | tf_op jit(solution)/shard_map/ppermute | solution.py:408
  33.3 13.0 %collective-permute-done.6 = bf16[176,512]{1,0:T(8,128)(2,1)S(1)} collective-permute-done((bf16[176,512]{1,0:T(8,128)(2,1)S(1)}, bf16[176,512]{1,0:T(8,128)(2,1)S(1)}, u32[]{:S(2)}, u32[]{:S(2)}) %collective-permute-start.6) | collective-permute-done | bytes 180256 | tf_op jit(solution)/shard_map/ppermute | solution.py:408
  55.6 9.6 %collective-permute-done.12 = bf16[64,2560]{1,0:T(8,128)(2,1)S(1)} collective-permute-done((bf16[64,2560]{1,0:T(8,128)(2,1)S(1)}, bf16[64,2560]{1,0:T(8,128)(2,1)S(1)}, u32[]{:S(2)}, u32[]{:S(2)}) %collective-permute-start.12) | collective-permute-done | bytes 327712 | tf_op jit(solution)/shard_map/ppermute | solution.py:408
  66.6 5.2 %collective-permute-done.10.refs_1_ = bf16[2,4,64,1664]{3,2,1,0:T(8,128)(2,1)} collective-permute-done((bf16[2,4,64,1664]{3,2,1,0:T(8,128)(2,1)S(1)}, bf16[2,4,64,1664]{3,2,1,0:T(8,128)(2,1)}, u32[]{:S(2)}, u32[]{:S(2)}) %collective-permute-start.10) | collective-permute-done | bytes 1703968 | tf_op jit(solution)/shard_map/ppermute | solution.py:408
  81.4 4.3 gather_fusion
  86.8 15.7 %collective-permute-done.16 = bf16[64,2816]{1,0:T(8,128)(2,1)S(1)} collective-permute-done((bf16[64,2816]{1,0:T(8,128)(2,1)S(1)}, bf16[64,2816]{1,0:T(8,128)(2,1)S(1)}, u32[]{:S(2)}, u32[]{:S(2)}) %collective-permute-start.16) | collective-permute-done | bytes 360480 | tf_op jit(solution)/shard_map/ppermute | solution.py:408
  102.4 4.9 %collective-permute-done.18 = bf16[64,2816]{1,0:T(8,128)(2,1)} collective-permute-done((bf16[64,2816]{1,0:T(8,128)(2,1)S(1)}, bf16[64,2816]{1,0:T(8,128)(2,1)}, u32[]{:S(2)}, u32[]{:S(2)}) %collective-permute-start.18) | collective-permute-done | bytes 360480 | tf_op jit(solution)/shard_map/ppermute | solution.py:408
  119.3 6.2 %assemble.5.wq_ref.wk_ref.wv_ref = bf16[1024,3328]{1,0:T(8,128)(2,1)} custom-call(s32[4]{0:T(128)S(1)} %pad_add_fusion.place_ref, bf16[2,4,64,1664]{3,2,1,0:T(8,128)(2,1)S(1)} %copy-done.5, bf16[2,4,64,1664]{3,2,1,0:T(8,128)(2,1)} %collective-permute-done.10.refs_1_, bf16[2,4,64,1664]{3,2,1,0:T(8,128)(2,1)} %collective-permute-done.11.refs_2_, ...), custom_call_target="tpu_custom_call" | custom-call | flops 1000000000 | bytes 1 | tf_op jit(solution)/shard_map/assemble/pallas_call | solution.py:475
  128.9 15.4 %self_forward.1 = (bf16[128,1024]{1,0:T(8,128)(2,1)S(1)}, bf16[128,1024]{1,0:T(8,128)(2,1)S(1)}, bf16[512,1024]{1,0:T(8,128)(2,1)S(1)}, bf16[512,1024]{1,0:T(8,128)(2,1)S(1)}, bf16[512,1024]{1,0:T(8,128)(2,1)S(1)}) custom-call(s32[1]{0:T(128)} %bitcast.4.pos_ref, bf16[512,1024]{1,0:T(8,128)(2,1)S(1)} %bitcast.141, f32[1,1024]{1,0:T(1,128)S(1)} %reshape.224.gain_ref, ...), custom_call_target="tpu_custom_call" | custom-call | flops 4000000000 | bytes 1 | tf_op jit(solution)/shard_map/self_forward/pallas_call | solution.py:166
  148.3 3.6 collective-permute-done.20.refs_1_
  158.1 8.0 %assemble.6.wo_ref.wq_ref.wk_ref.wv_ref.wc_ref = bf16[1024,5120]{1,0:T(8,128)(2,1)} custom-call(s32[4]{0:T(128)S(1)} %pad_add_fusion.place_ref, bf16[2,4,64,2560]{3,2,1,0:T(8,128)(2,1)S(1)} %pad_maximum_fusion.1.refs_0_, bf16[2,4,64,2560]{3,2,1,0:T(8,128)(2,1)} %collective-permute-done.20.refs_1_, bf16[2,4,64,2560]{3,2,1,0:T(8,128)(2,1)} %collective-permute-done.21.refs_2_, ...), custom_call_target="tpu_custom_call" | custom-call | flops 1000000000 | bytes 1 | tf_op jit(solution)/shard_map/assemble/pallas_call | solution.py:475
  166.2 12.2 %cross_forward.1 = (f32[128,1024]{1,0:T(8,128)S(1)}, bf16[128,1024]{1,0:T(8,128)(2,1)S(1)}, bf16[128,1024]{1,0:T(8,128)(2,1)S(1)}, bf16[256,1024]{1,0:T(8,128)(2...) custom-call(bf16[128,1024]{1,0:T(8,128)(2,1)S(1)} %bitcast.144, ...), custom_call_target="tpu_custom_call" | custom-call | flops 8000000000 | bytes 1 | tf_op jit(solution)/shard_map/cross_forward/pallas_call | solution.py:280
  188.6 5.4 %assemble.7 = bf16[1024,2816]{1,0:T(8,128)(2,1)} custom-call(s32[4]{0:T(128)S(1)} %pad_add_fusion.place_ref, bf16[2,4,64,1408]{3,2,1,0:T(8,128)(2,1)} %pad_maximum_fusion.6.refs_0_, bf16[2,4,64,1408]{3,2,1,0:T(8,128)(2,1)} %collective-permute-done.26.refs_1_, bf16[2,4,64,1408]{3,2,1,0:T(8,128)(2,1)} %collective-permute-done.27.refs_2_, ...), custom_call_target="tpu_custom_call" | custom-call | flops 1000000000 | bytes 1 | tf_op jit(solution)/shard_map/assemble/pallas_call | solution.py:475
  197.6 5.3 %assemble.8 = bf16[2816,1024]{1,0:T(8,128)(2,1)} custom-call(s32[4]{0:T(128)S(1)} %pad_add_fusion.place_ref, bf16[4,2,2,176,512]{4,3,2,1,0:T(8,128)(2,1)S(1)} %pad_maximum_fusion.refs_0_, bf16[4,2,2,176,512]{4,3,2,1,0:T(8,128)(2,1)} %collective-permute-done.34.refs_1_), custom_call_target="tpu_custom_call" | custom-call | flops 1000000000 | bytes 1 | tf_op jit(solution)/shard_map/assemble/pallas_call | solution.py:475
  209.8 5.4 %assemble.9 = bf16[1024,2816]{1,0:T(8,128)(2,1)} custom-call(s32[4]{0:T(128)S(1)} %pad_add_fusion.place_ref, bf16[2,4,64,1408]{3,2,1,0:T(8,128)(2,1)} %pad_maximum_fusion.7.refs_0_, bf16[2,4,64,1408]{3,2,1,0:T(8,128)(2,1)} %collective-permute-done.32.refs_1_, bf16[2,4,64,1408]{3,2,1,0:T(8,128)(2,1)} %collective-permute-done.33.refs_2_, ...), custom_call_target="tpu_custom_call" | custom-call | flops 1000000000 | bytes 1 | tf_op jit(solution)/shard_map/assemble/pallas_call | solution.py:475
  218.6 4.1 fusion.90
  229.0 5.5 %weight_grad.6 = (bf16[704,512]{1,0:T(8,128)(2,1)S(1)}, bf16[704,512]{1,0:T(8,128)(2,1)S(1)}, bf16[704,512]{1,0:T(8,128)(2,1)S(1)}, bf16[704,512]{1,0:T(8,128)(2,1)S(1)}) custom-call(s32[4]{0:T(128)S(1)} %pad_add_fusion.place_ref, bf16[128,2816]{1,0:T(8,128)(2,1)S(1)} %pad_maximum_fusion.13.refs_0_, bf16[128,512]{1,0:T(8,128)(2,1)S(1)} %copy-done.50, ...), custom_call_target="tpu_custom_call" | custom-call | flops 1000000000 | bytes 1 | tf_op jit(solution)/shard_map/weight_grad/pallas_call | solution.py:565
  236.3 5.0 %collective-permute-done.39 = bf16[512,1408]{1,0:T(8,128)(2,1)} collective-permute-done((bf16[512,1408]{1,0:T(8,128)(2,1)S(1)}, bf16[512,1408]{1,0:T(8,128)(2,1)}, u32[]{:S(2)}, u32[]{:S(2)}) %collective-permute-start.39) | collective-permute-done | bytes 1441824 | tf_op jit(solution)/shard_map/ppermute | solution.py:408
  250.2 4.6 %fusion.32 = f32[128,1024]{1,0:T(8,128)S(1)} fusion(bf16[1024,2816]{1,0:T(8,128)(2,1)} %assemble.9, bf16[128,1408]{1,0:T(8,128)(2,1)S(1)} %get-tuple-element.417, bf16[128,1408]{1,0:T(8,128)(2,1)S(1)} %copy-done.67), kind=kOutput, calls=%fused_computation.70 | convolution fusion | flops 739639296 | bytes 7012352 | tf_op jit(solution)/shard_map/dot_general | solution.py:25
  254.8 4.7 %multiply_reduce_fusion = (bf16[1024]{0:T(1024)(128)(2,1)S(1)}, f32[128]{0:T(128)S(1)}, f32[128,1024]{1,0:T(8,128)S(1)}) fusion(f32[128,1024]{1,0:T(8,128)S(1)} %get-tuple-element.415, f32[128]{0:T(128)S(1)} %add_rsqrt_fusion.1, f32[1024]{0:T(1024)S(1)} %mul.224, f32[128,1024]{1,0:T(8,128)S(1)} %fusion.32, bf16[1024,2816]{1,0:T(8,128)(2,1)} %assemble.7, ...), kind=kOutput, calls=%fused_computation.105 | convolution fusion | flops 740555648 | bytes 8068096 | tf_op jit(solution)/shard_map/dot_general | solution.py:25
  260.9 17.4 %cross_back.1 = (bf16[128,1024]{1,0:T(8,128)(2,1)S(1)}, bf16[256,1024]{1,0:T(8,128)(2,1)S(1)}, bf16[256,1024]{1,0:T(8,128)(2,1)S(1)}, f32[256,1024]{1,0:T(8,128)...) custom-call(f32[128,1024]{1,0:T(8,128)S(1)} %get-tuple-element.621.g, ...), custom_call_target="tpu_custom_call" | custom-call | flops 1000000000 | bytes 1 | tf_op jit(solution)/shard_map/cross_back/pallas_call | solution.py:353
  300.5 5.8 %weight_grad.8 = (bf16[512,2560]{1,0:T(8,128)(2,1)S(1)}, bf16[512,2560]{1,0:T(8,128)(2,1)}) custom-call(s32[4]{0:T(128)S(1)} %pad_add_fusion.place_ref, bf16[128,1024]{1,0:T(8,128)(2,1)S(1)} %get-tuple-element.668.refs_0_, bf16[128,1024]{1,0:T(8,128)(2,1)S(1)} %get-tuple-element.666.refs_1_, bf16[128,1024]{1,0:T(8,128)(2,1)S(1)} %get-tuple-element.644.refs_2_, ...), custom_call_target="tpu_custom_call" | custom-call | flops 1000000000 | bytes 1 | tf_op jit(solution)/shard_map/weight_grad/pallas_call | solution.py:565
  314.5 23.0 %self_back.1 = (bf16[512,1024]{1,0:T(8,128)(2,1)S(1)}, bf16[512,1024]{1,0:T(8,128)(2,1)S(1)}, bf16[512,1024]{1,0:T(8,128)(2,1)S(1)}, f32[8,2,640]{2,1,0:T(2,128)...) custom-call(s32[1]{0:T(128)} %bitcast.4.pos_ref, bf16[512,1024]{1,0:T(8,128)(2,1)S(1)} %bitcast.142, ...), custom_call_target="tpu_custom_call" | custom-call | flops 1000000000 | bytes 1 | tf_op jit(solution)/shard_map/self_back/pallas_call | solution.py:225
  338.3 5.8 %collective-permute-done.54 = bf16[64,1024]{1,0:T(8,128)(2,1)S(1)} collective-permute-done((bf16[64,1024]{1,0:T(8,128)(2,1)S(1)}, bf16[64,1024]{1,0:T(8,128)(2,1)S(1)}, u32[]{:S(2)}, u32[]{:S(2)}) %collective-permute-start.54) | collective-permute-done | bytes 131104 | tf_op jit(solution)/shard_map/ppermute | solution.py:408
  356.0 8.3 %collective-permute-done.58 = bf16[64,1408]{1,0:T(8,128)(2,1)} collective-permute-done((bf16[64,1408]{1,0:T(8,128)(2,1)}, bf16[64,1408]{1,0:T(8,128)(2,1)}, u32[]{:S(2)}, u32[]{:S(2)}) %collective-permute-start.58) | collective-permute-done | bytes 180256 | tf_op jit(solution)/shard_map/ppermute | solution.py:408
  369.9 4.1 weight_grad.9
  383.4 4.4 fusion.10
  388.6 8.4 %collective-permute-done.62 = bf16[64,2560]{1,0:T(8,128)(2,1)S(1)} collective-permute-done((bf16[64,2560]{1,0:T(8,128)(2,1)S(1)}, bf16[64,2560]{1,0:T(8,128)(2,1)S(1)}, u32[]{:S(2)}, u32[]{:S(2)}) %collective-permute-start.62) | collective-permute-done | bytes 327712 | tf_op jit(solution)/shard_map/ppermute | solution.py:408
  408.1 7.4 %collective-permute-done.65 = bf16[256,1664]{1,0:T(8,128)(2,1)S(1)} collective-permute-done((bf16[256,1664]{1,0:T(8,128)(2,1)S(1)}, bf16[256,1664]{1,0:T(8,128)(2,1)S(1)}, u32[]{:S(2)}, u32[]{:S(2)}) %collective-permute-start.65) | collective-permute-done | bytes 852000 | tf_op jit(solution)/shard_map/ppermute | solution.py:408
  417.4 4.2 collective-permute-start.75
  431.1 10.4 %collective-permute-done.70 = bf16[64,1664]{1,0:T(8,128)(2,1)S(1)} collective-permute-done((bf16[64,1664]{1,0:T(8,128)(2,1)S(1)}, bf16[64,1664]{1,0:T(8,128)(2,1)S(1)}, u32[]{:S(2)}, u32[]{:S(2)}) %collective-permute-start.70) | collective-permute-done | bytes 213024 | tf_op jit(solution)/shard_map/ppermute | solution.py:408
  (517 shorter events, 198.1 us)
Async XLA Ops:
  28.2 18.8 %collective-permute-start.5 = (bf16[4,64,1664]{2,1,0:T(8,128)(2,1)S(1)}, bf16[4,64,1664]{2,1,0:T(8,128)(2,1)S(1)}, u32[]{:S(2)}, u32[]{:S(2)}) collective-permute-start(bf16[4,64,1664]{2,1,0:T(8,128)(2,1)S(1)} %pad_maximum_fusion.10), channel_id=1, source_target_pairs={{0,4},{1,3},{2,6},{3,1},{4,0},{5,7},{6,2},{7,5},{8,12},{9,11},{10,... | collective-permute-start | bytes 2555912 | tf_op jit(solution)/shard_map/ppermute | solution.py:408
  29.8 20.4 %collective-permute-start.9 = (bf16[192,1024]{1,0:T(8,128)(2,1)S(1)}, bf16[192,1024]{1,0:T(8,128)(2,1)S(1)}, u32[]{:S(2)}, u32[]{:S(2)}) collective-permute-start(bf16[192,1024]{1,0:T(8,128)(2,1)S(1)} %pad_maximum_fusion.17), channel_id=1, source_target_pairs={{0,2},{1,3},{2,0},{3,1},{4,6},{5,7},{6,4},{7,5},{8,10},{9,11},{10,... | collective-permute-start | bytes 1179656 | tf_op jit(solution)/shard_map/ppermute | solution.py:408
  31.1 19.1 %collective-permute-start.7 = (bf16[64,2560]{1,0:T(8,128)(2,1)S(1)}, bf16[64,2560]{1,0:T(8,128)(2,1)S(1)}, u32[]{:S(2)}, u32[]{:S(2)}) collective-permute-start(bf16[64,2560]{1,0:T(8,128)(2,1)S(1)} %split.23), channel_id=1, source_target_pairs={{0,24},{1,25},{2,26},{3,27},{4,28},{5,29},{6,30},{7,31},{8,0},{9,1... | collective-permute-start | bytes 983048 | tf_op jit(solution)/shard_map/ppermute | solution.py:408
  51.0 20.8 %collective-permute-start.10 = (bf16[2,4,64,1664]{3,2,1,0:T(8,128)(2,1)S(1)}, bf16[2,4,64,1664]{3,2,1,0:T(8,128)(2,1)}, u32[]{:S(2)}, u32[]{:S(2)}) collective-permute-start(bf16[2,4,64,1664]{3,2,1,0:T(8,128)(2,1)S(1)} %pad_maximum_fusion.2.refs_0_), channel_id=1, source_target_pairs={{0,2},{1,5},{2,0},{3,7},{4,6},{5,1},{6,4},{7,3},{8,10},{9,13},{10,... | collective-permute-start | bytes 5111816 | tf_op jit(solution)/shard_map/ppermute | solution.py:408
  52.2 19.6 %collective-permute-start.11 = (bf16[2,4,64,1664]{3,2,1,0:T(8,128)(2,1)S(1)}, bf16[2,4,64,1664]{3,2,1,0:T(8,128)(2,1)}, u32[]{:S(2)}, u32[]{:S(2)}) collective-permute-start(bf16[2,4,64,1664]{3,2,1,0:T(8,128)(2,1)S(1)} %pad_maximum_fusion.2.refs_0_), channel_id=1, source_target_pairs={{0,1},{1,0},{2,3},{3,2},{4,5},{5,4},{6,7},{7,6},{8,9},{9,8},{10,11... | collective-permute-start | bytes 5111816 | tf_op jit(solution)/shard_map/ppermute | solution.py:408
  75.0 27.4 %collective-permute-start.16 = (bf16[64,2816]{1,0:T(8,128)(2,1)S(1)}, bf16[64,2816]{1,0:T(8,128)(2,1)S(1)}, u32[]{:S(2)}, u32[]{:S(2)}) collective-permute-start(bf16[64,2816]{1,0:T(8,128)(2,1)S(1)} %copy-done.65), channel_id=1, source_target_pairs={{0,24},{1,25},{2,26},{3,27},{4,28},{5,29},{6,30},{7,31},{8,0},{9,1... | collective-permute-start | bytes 1081352 | tf_op jit(solution)/shard_map/ppermute | solution.py:408
  76.2 26.2 %collective-permute-start.17 = (bf16[64,2816]{1,0:T(8,128)(2,1)S(1)}, bf16[64,2816]{1,0:T(8,128)(2,1)}, u32[]{:S(2)}, u32[]{:S(2)}) collective-permute-start(bf16[64,2816]{1,0:T(8,128)(2,1)S(1)} %copy-done.65), channel_id=1, source_target_pairs={{0,16},{1,17},{2,18},{3,19},{4,20},{5,21},{6,22},{7,23},{8,24},{9,... | collective-permute-start | bytes 1081352 | tf_op jit(solution)/shard_map/ppermute | solution.py:408
  79.4 27.9 %collective-permute-start.18 = (bf16[64,2816]{1,0:T(8,128)(2,1)S(1)}, bf16[64,2816]{1,0:T(8,128)(2,1)}, u32[]{:S(2)}, u32[]{:S(2)}) collective-permute-start(bf16[64,2816]{1,0:T(8,128)(2,1)S(1)} %copy-done.65), channel_id=1, source_target_pairs={{0,8},{1,9},{2,10},{3,11},{4,12},{5,13},{6,14},{7,15},{8,16},{9,17... | collective-permute-start | bytes 1081352 | tf_op jit(solution)/shard_map/ppermute | solution.py:408
  79.4 30.5 %collective-permute-start.15 = (bf16[4,64,2560]{2,1,0:T(8,128)(2,1)S(1)}, bf16[4,64,2560]{2,1,0:T(8,128)(2,1)}, u32[]{:S(2)}, u32[]{:S(2)}) collective-permute-start(bf16[4,64,2560]{2,1,0:T(8,128)(2,1)S(1)} %copy-done.55), channel_id=1, source_target_pairs={{0,4},{1,3},{2,6},{3,1},{4,0},{5,7},{6,2},{7,5},{8,12},{9,11},{10,... | collective-permute-start | bytes 3932168 | tf_op jit(solution)/shard_map/ppermute | solution.py:408
  85.7 26.3 %collective-permute-start.14 = (bf16[2,4,64,1664]{3,2,1,0:T(8,128)(2,1)}, bf16[2,4,64,1664]{3,2,1,0:T(8,128)(2,1)S(1)}, u32[]{:S(2)}, u32[]{:S(2)}) collective-permute-start(bf16[2,4,64,1664]{3,2,1,0:T(8,128)(2,1)} %collective-permute-done.10.refs_1_), channel_id=1, source_target_pairs={{0,1},{1,0},{2,3},{3,2},{4,5},{5,4},{6,7},{7,6},{8,9},{9,8},{10,11... | collective-permute-start | bytes 5111816 | tf_op jit(solution)/shard_map/ppermute | solution.py:408
  113.3 38.6 %collective-permute-start.20 = (bf16[2,4,64,2560]{3,2,1,0:T(8,128)(2,1)S(1)}, bf16[2,4,64,2560]{3,2,1,0:T(8,128)(2,1)}, u32[]{:S(2)}, u32[]{:S(2)}) collective-permute-start(bf16[2,4,64,2560]{3,2,1,0:T(8,128)(2,1)S(1)} %pad_maximum_fusion.1.refs_0_), channel_id=1, source_target_pairs={{0,2},{1,5},{2,0},{3,7},{4,6},{5,1},{6,4},{7,3},{8,10},{9,13},{10,... | collective-permute-start | bytes 7864328 | tf_op jit(solution)/shard_map/ppermute | solution.py:408
  113.7 38.2 %collective-permute-start.21 = (bf16[2,4,64,2560]{3,2,1,0:T(8,128)(2,1)S(1)}, bf16[2,4,64,2560]{3,2,1,0:T(8,128)(2,1)}, u32[]{:S(2)}, u32[]{:S(2)}) collective-permute-start(bf16[2,4,64,2560]{3,2,1,0:T(8,128)(2,1)S(1)} %pad_maximum_fusion.1.refs_0_), channel_id=1, source_target_pairs={{0,1},{1,0},{2,3},{3,2},{4,5},{5,4},{6,7},{7,6},{8,9},{9,8},{10,11... | collective-permute-start | bytes 7864328 | tf_op jit(solution)/shard_map/ppermute | solution.py:408
  115.1 33.2 %collective-permute-start.23 = (bf16[2,2,176,512]{3,2,1,0:T(8,128)(2,1)}, bf16[2,2,176,512]{3,2,1,0:T(8,128)(2,1)}, u32[]{:S(2)}, u32[]{:S(2)}) collective-permute-start(bf16[2,2,176,512]{3,2,1,0:T(8,128)(2,1)} %pad_maximum_fusion.12), channel_id=1, source_target_pairs={{0,24},{1,25},{2,26},{3,27},{4,28},{5,29},{6,30},{7,31},{8,0},{9,1... | collective-permute-start | bytes 2162696 | tf_op jit(solution)/shard_map/ppermute | solution.py:408
  115.8 32.5 %collective-permute-start.24 = (bf16[2,2,176,512]{3,2,1,0:T(8,128)(2,1)}, bf16[2,2,176,512]{3,2,1,0:T(8,128)(2,1)}, u32[]{:S(2)}, u32[]{:S(2)}) collective-permute-start(bf16[2,2,176,512]{3,2,1,0:T(8,128)(2,1)} %pad_maximum_fusion.12), channel_id=1, source_target_pairs={{0,8},{1,9},{2,10},{3,11},{4,12},{5,13},{6,14},{7,15},{8,16},{9,17... | collective-permute-start | bytes 2162696 | tf_op jit(solution)/shard_map/ppermute | solution.py:408
  117.5 27.8 %collective-permute-start.22 = (bf16[4,64,1408]{2,1,0:T(8,128)(2,1)}, bf16[4,64,1408]{2,1,0:T(8,128)(2,1)}, u32[]{:S(2)}, u32[]{:S(2)}) collective-permute-start(bf16[4,64,1408]{2,1,0:T(8,128)(2,1)} %get-tuple-element.348), channel_id=1, source_target_pairs={{0,4},{1,3},{2,6},{3,1},{4,0},{5,7},{6,2},{7,5},{8,12},{9,11},{10,... | collective-permute-start | bytes 2162696 | tf_op jit(solution)/shard_map/ppermute | solution.py:408
  153.0 27.0 %collective-permute-start.26 = (bf16[2,4,64,1408]{3,2,1,0:T(8,128)(2,1)}, bf16[2,4,64,1408]{3,2,1,0:T(8,128)(2,1)}, u32[]{:S(2)}, u32[]{:S(2)}) collective-permute-start(bf16[2,4,64,1408]{3,2,1,0:T(8,128)(2,1)} %pad_maximum_fusion.6.refs_0_), channel_id=1, source_target_pairs={{0,2},{1,5},{2,0},{3,7},{4,6},{5,1},{6,4},{7,3},{8,10},{9,13},{10,... | collective-permute-start | bytes 4325384 | tf_op jit(solution)/shard_map/ppermute | solution.py:408
  153.4 26.6 %collective-permute-start.27 = (bf16[2,4,64,1408]{3,2,1,0:T(8,128)(2,1)}, bf16[2,4,64,1408]{3,2,1,0:T(8,128)(2,1)}, u32[]{:S(2)}, u32[]{:S(2)}) collective-permute-start(bf16[2,4,64,1408]{3,2,1,0:T(8,128)(2,1)} %pad_maximum_fusion.6.refs_0_), channel_id=1, source_target_pairs={{0,1},{1,0},{2,3},{3,2},{4,5},{5,4},{6,7},{7,6},{8,9},{9,8},{10,11... | collective-permute-start | bytes 4325384 | tf_op jit(solution)/shard_map/ppermute | solution.py:408
  155.1 24.8 %collective-permute-start.30 = (bf16[128,512]{1,0:T(8,128)(2,1)}, bf16[128,512]{1,0:T(8,128)(2,1)}, u32[]{:S(2)}, u32[]{:S(2)}) collective-permute-start(bf16[128,512]{1,0:T(8,128)(2,1)} %get-tuple-element.676), channel_id=1, source_target_pairs={{0,1},{1,0},{2,3},{3,2},{4,5},{5,4},{6,7},{7,6},{8,9},{9,8},{10,11... | collective-permute-start | bytes 393224 | tf_op jit(solution)/shard_map/ppermute | solution.py:408
  155.4 24.6 %collective-permute-start.28 = (bf16[4,64,1408]{2,1,0:T(8,128)(2,1)}, bf16[4,64,1408]{2,1,0:T(8,128)(2,1)S(1)}, u32[]{:S(2)}, u32[]{:S(2)}) collective-permute-start(bf16[4,64,1408]{2,1,0:T(8,128)(2,1)} %get-tuple-element.370), channel_id=1, source_target_pairs={{0,4},{1,3},{2,6},{3,1},{4,0},{5,7},{6,2},{7,5},{8,12},{9,11},{10,... | collective-permute-start | bytes 2162696 | tf_op jit(solution)/shard_map/ppermute | solution.py:408
  157.9 22.1 %collective-permute-start.29 = (bf16[2,2,176,512]{3,2,1,0:T(8,128)(2,1)}, bf16[2,2,176,512]{3,2,1,0:T(8,128)(2,1)S(1)}, u32[]{:S(2)}, u32[]{:S(2)}) collective-permute-start(bf16[2,2,176,512]{3,2,1,0:T(8,128)(2,1)} %collective-permute-done.23), channel_id=1, source_target_pairs={{0,24},{1,25},{2,26},{3,27},{4,28},{5,29},{6,30},{7,31},{8,0},{9,1... | collective-permute-start | bytes 2162696 | tf_op jit(solution)/shard_map/ppermute | solution.py:408
  185.1 18.5 %collective-permute-start.32 = (bf16[2,4,64,1408]{3,2,1,0:T(8,128)(2,1)}, bf16[2,4,64,1408]{3,2,1,0:T(8,128)(2,1)}, u32[]{:S(2)}, u32[]{:S(2)}) collective-permute-start(bf16[2,4,64,1408]{3,2,1,0:T(8,128)(2,1)} %pad_maximum_fusion.7.refs_0_), channel_id=1, source_target_pairs={{0,2},{1,5},{2,0},{3,7},{4,6},{5,1},{6,4},{7,3},{8,10},{9,13},{10,... | collective-permute-start | bytes 4325384 | tf_op jit(solution)/shard_map/ppermute | solution.py:408
  223.0 18.3 %collective-permute-start.39 = (bf16[512,1408]{1,0:T(8,128)(2,1)S(1)}, bf16[512,1408]{1,0:T(8,128)(2,1)}, u32[]{:S(2)}, u32[]{:S(2)}) collective-permute-start(bf16[512,1408]{1,0:T(8,128)(2,1)S(1)} %get-tuple-element.390), channel_id=1, source_target_pairs={{0,4},{1,3},{2,6},{3,1},{4,0},{5,7},{6,2},{7,5},{8,12},{9,11},{10,... | collective-permute-start | bytes 4325384 | tf_op jit(solution)/shard_map/ppermute | solution.py:408
  246.5 36.0 %collective-permute-start.43 = (bf16[512,1408]{1,0:T(8,128)(2,1)S(1)}, bf16[512,1408]{1,0:T(8,128)(2,1)S(1)}, u32[]{:S(2)}, u32[]{:S(2)}) collective-permute-start(bf16[512,1408]{1,0:T(8,128)(2,1)S(1)} %get-tuple-element.411), channel_id=1, source_target_pairs={{0,4},{1,3},{2,6},{3,1},{4,0},{5,7},{6,2},{7,5},{8,12},{9,11},{10,... | collective-permute-start | bytes 4325384 | tf_op jit(solution)/shard_map/ppermute | solution.py:408
  247.6 31.4 %collective-permute-start.42 = (bf16[256,1408]{1,0:T(8,128)(2,1)S(1)}, bf16[256,1408]{1,0:T(8,128)(2,1)}, u32[]{:S(2)}, u32[]{:S(2)}) collective-permute-start(bf16[256,1408]{1,0:T(8,128)(2,1)S(1)} %add_convert_fusion.5), channel_id=1, source_target_pairs={{0,2},{1,5},{2,0},{3,7},{4,6},{5,1},{6,4},{7,3},{8,10},{9,13},{10,... | collective-permute-start | bytes 2162696 | tf_op jit(solution)/shard_map/ppermute | solution.py:408
  248.0 31.0 %collective-permute-start.44 = (bf16[704,512]{1,0:T(8,128)(2,1)S(1)}, bf16[704,512]{1,0:T(8,128)(2,1)S(1)}, u32[]{:S(2)}, u32[]{:S(2)}) collective-permute-start(bf16[704,512]{1,0:T(8,128)(2,1)S(1)} %get-tuple-element.414), channel_id=1, source_target_pairs={{0,24},{1,25},{2,26},{3,27},{4,28},{5,29},{6,30},{7,31},{8,0},{9,1... | collective-permute-start | bytes 2162696 | tf_op jit(solution)/shard_map/ppermute | solution.py:408
  248.0 34.5 %collective-permute-start.45 = (bf16[704,512]{1,0:T(8,128)(2,1)S(1)}, bf16[704,512]{1,0:T(8,128)(2,1)S(1)}, u32[]{:S(2)}, u32[]{:S(2)}) collective-permute-start(bf16[704,512]{1,0:T(8,128)(2,1)S(1)} %get-tuple-element.413), channel_id=1, source_target_pairs={{0,8},{1,9},{2,10},{3,11},{4,12},{5,13},{6,14},{7,15},{8,16},{9,17... | collective-permute-start | bytes 2162696 | tf_op jit(solution)/shard_map/ppermute | solution.py:408
  310.5 33.6 %collective-permute-start.52 = (bf16[512,2560]{1,0:T(8,128)(2,1)}, bf16[512,2560]{1,0:T(8,128)(2,1)}, u32[]{:S(2)}, u32[]{:S(2)}) collective-permute-start(bf16[512,2560]{1,0:T(8,128)(2,1)} %get-tuple-element.452), channel_id=1, source_target_pairs={{0,4},{1,3},{2,6},{3,1},{4,0},{5,7},{6,2},{7,5},{8,12},{9,11},{10,... | collective-permute-start | bytes 7864328 | tf_op jit(solution)/shard_map/ppermute | solution.py:408
  312.1 31.9 %collective-permute-start.53 = (bf16[704,512]{1,0:T(8,128)(2,1)}, bf16[704,512]{1,0:T(8,128)(2,1)}, u32[]{:S(2)}, u32[]{:S(2)}) collective-permute-start(bf16[704,512]{1,0:T(8,128)(2,1)} %add_convert_fusion.3), channel_id=1, source_target_pairs={{0,8},{1,9},{2,10},{3,11},{4,12},{5,13},{6,14},{7,15},{8,16},{9,17... | collective-permute-start | bytes 2162696 | tf_op jit(solution)/shard_map/ppermute | solution.py:408
  313.5 30.5 %collective-permute-start.54 = (bf16[64,1024]{1,0:T(8,128)(2,1)S(1)}, bf16[64,1024]{1,0:T(8,128)(2,1)S(1)}, u32[]{:S(2)}, u32[]{:S(2)}) collective-permute-start(bf16[64,1024]{1,0:T(8,128)(2,1)S(1)} %fusion.59), channel_id=1, source_target_pairs={{0,2},{1,3},{2,0},{3,1},{4,6},{5,7},{6,4},{7,5},{8,10},{9,11},{10,... | collective-permute-start | bytes 393224 | tf_op jit(solution)/shard_map/ppermute | solution.py:408
  375.1 21.9 %collective-permute-start.60 = (bf16[512,1664]{1,0:T(8,128)(2,1)}, bf16[512,1664]{1,0:T(8,128)(2,1)S(1)}, u32[]{:S(2)}, u32[]{:S(2)}) collective-permute-start(bf16[512,1664]{1,0:T(8,128)(2,1)} %get-tuple-element.538), channel_id=1, source_target_pairs={{0,4},{1,3},{2,6},{3,1},{4,0},{5,7},{6,2},{7,5},{8,12},{9,11},{10,... | collective-permute-start | bytes 5111816 | tf_op jit(solution)/shard_map/ppermute | solution.py:408
  422.9 23.1 %collective-permute-start.73 = (f32[32,2560]{1,0:T(8,128)S(1)}, f32[32,2560]{1,0:T(8,128)S(1)}, u32[]{:S(2)}, u32[]{:S(2)}) collective-permute-start(f32[32,2560]{1,0:T(8,128)S(1)} %slice_select_fusion), channel_id=1, source_target_pairs={{0,1},{1,0},{2,3},{3,2},{4,5},{5,4},{6,7},{7,6},{8,9},{9,8},{10,11... | collective-permute-start | bytes 983048 | tf_op jit(solution)/shard_map/ppermute | solution.py:408
  429.1 18.5 %collective-permute-start.77 = (f32[88,512]{1,0:T(8,128)S(1)}, f32[88,512]{1,0:T(8,128)S(1)}, u32[]{:S(2)}, u32[]{:S(2)}) collective-permute-start(f32[88,512]{1,0:T(8,128)S(1)} %slice_select_fusion.4), channel_id=1, source_target_pairs={{0,1},{1,0},{2,3},{3,2},{4,5},{5,4},{6,7},{7,6},{8,9},{9,8},{10,11... | collective-permute-start | bytes 540680 | tf_op jit(solution)/shard_map/ppermute | solution.py:408
  (157 other events, 1276.0 us)
